TPU v7x, 32 devices: a whole 2x2x4 slice. The times are simulated.
32 devices in a mesh: seq: 4 (over x, core), fsdp: 8 (over z, y).
Axes of the slice: x: 2, y: 2, z: 4, core: 2. Of those that a mesh axis runs over, the one named last changes fastest.
Arguments:
- patches: bfloat16 [24, 1024, 1152], P('fsdp', 'seq'), may hold values from -6 to 6
- lengths: int32 [24, 4], P('fsdp'), may hold values from 0 to 1024, as said below
- first_gain: bfloat16 [1152], P('fsdp'), may hold values from 0.5 to 1.5
- first_shift: bfloat16 [1152], P('fsdp'), may hold values from -3 to 3
- query_weight: bfloat16 [1152, 1152], P('fsdp'), may hold values from -0.1875 to 0.1875
- query_bias: bfloat16 [1152], P('fsdp'), may hold values from -3 to 3
- key_weight: bfloat16 [1152, 1152], P('fsdp'), may hold values from -0.1875 to 0.1875
- value_weight: bfloat16 [1152, 1152], P('fsdp'), may hold values from -0.1875 to 0.1875
- value_bias: bfloat16 [1152], P('fsdp'), may hold values from -3 to 3
- output_weight: bfloat16 [1152, 1152], P('fsdp'), may hold values from -0.75 to 0.75
- output_bias: bfloat16 [1152], P('fsdp'), may hold values from -3 to 3
- second_gain: bfloat16 [1152], P('fsdp'), may hold values from 0.5 to 1.5
- second_shift: bfloat16 [1152], P('fsdp'), may hold values from -3 to 3
- hidden_weight: bfloat16 [1152, 4304], P('fsdp'), may hold values from -0.1875 to 0.1875
- hidden_bias: bfloat16 [4304], replicated, may hold values from -3 to 3
- down_weight: bfloat16 [4304, 1152], P(None, 'fsdp'), may hold values from -0.09375 to 0.09375
- down_bias: bfloat16 [1152], P('fsdp'), may hold values from -3 to 3
- cotangent: bfloat16 [24, 1024, 1152], P('fsdp', 'seq'), may hold values from -6 to 6
Outputs:
- layer_output: bfloat16 [24, 1024, 1152], P('fsdp', 'seq')
- grad_patches: float32 [24, 1024, 1152], P('fsdp', 'seq')
- grad_first_gain: float32 [1152], P('fsdp')
- grad_first_shift: float32 [1152], P('fsdp')
- grad_query_weight: float32 [1152, 1152], P('fsdp')
- grad_query_bias: float32 [1152], P('fsdp')
- grad_key_weight: float32 [1152, 1152], P('fsdp')
- grad_value_weight: float32 [1152, 1152], P('fsdp')
- grad_value_bias: float32 [1152], P('fsdp')
- grad_output_weight: float32 [1152, 1152], P('fsdp')
- grad_output_bias: float32 [1152], P('fsdp')
- grad_second_gain: float32 [1152], P('fsdp')
- grad_second_shift: float32 [1152], P('fsdp')
- grad_hidden_weight: float32 [1152, 4304], P('fsdp')
- grad_hidden_bias: float32 [4304], replicated
- grad_down_weight: float32 [4304, 1152], P(None, 'fsdp')
- grad_down_bias: float32 [1152], P('fsdp')
Inputs may be any that keep to these rules, and one draw needn't show every extreme that they name: `lengths`: each row lists its pictures' patch counts in its first slots: 1 to 4 pictures of 100 or more patches each, summing to at most 1024; the remaining slots are 0 and the rest of the row is padding. Some row holds one picture of 1024 patches.
All inputs are finite; a program needn't handle non-finite values.
Results may differ from a plain program's by a relative error of at most 0.013.
Values may be sent and summed in bfloat16 or wider, within the bound.
No kernel may reach another device: no remote copies, remote signals or barrier semaphores. Data moves between devices by JAX's collectives and lax.ppermute only.
A program may use at most 320 MiB of HBM per device.

v0:
```python
from functools import partial
import math

import jax
import jax.numpy as jnp
from jax import lax
from jax.sharding import PartitionSpec as P

HEAD_DIM = 72
MB = 3


EPS = 1e-06
GELU_COEF = math.sqrt(2.0 / math.pi)
MASKED = -1e30


def for_sending(array):
    return jax.tree.map(lambda a: a.astype(jnp.bfloat16) if a.dtype == jnp.float32 else a, array)


def layer_norm(values, gain, shift):
    center = values - jnp.mean(values, axis=-1, keepdims=True)
    spread = jnp.mean(center * center, axis=-1, keepdims=True)
    return center * lax.rsqrt(spread + EPS) * gain + shift


def gelu_tanh(inner):
    return 0.5 * inner * (1.0 + jnp.tanh(GELU_COEF * (inner + 0.044715 * inner * inner * inner)))


def across_rows(left, right):
    return lax.dot_general(
        left, right, (((0,), (0,)), ((), ())), preferred_element_type=jnp.float32
    )


def times_transposed(left, right):
    return lax.dot_general(
        left, right, (((1,), (1,)), ((), ())), preferred_element_type=jnp.float32
    )


def picture_ids(lengths, seq_len):
    position = jnp.arange(seq_len, dtype=jnp.int32)
    picture_ends = jnp.cumsum(lengths, axis=-1)
    picture = jnp.sum(
        (position[None, :, None] >= picture_ends[:, None, :]).astype(jnp.int32), axis=-1
    )
    usable = position[None, :] < picture_ends[:, -1:]
    return (picture, usable)


def block_scores(query_block, key_heads, picture, usable, block_start, block_rows, score_scale):
    position = jnp.arange(picture.shape[0], dtype=jnp.int32)
    own_picture = picture[block_start : block_start + block_rows]
    own_position = position[block_start : block_start + block_rows]
    allowed = (own_picture[:, None] == picture[None, :]) & usable[None, :] | (
        own_position[:, None] == position[None, :]
    )
    scores = (
        jnp.einsum("qhd,khd->hqk", query_block, key_heads, preferred_element_type=jnp.float32)
        * score_scale
    )
    return jnp.where(allowed[None], scores, MASKED)


def attend_row(packed, head_dim):
    queries, key_rows, value_rows, picture, usable = packed
    seq_len, head_width = queries.shape
    heads_here = head_width // head_dim
    block_rows = min(512, seq_len)
    score_scale = 1.0 / math.sqrt(head_dim)
    key_heads = key_rows.reshape(seq_len, heads_here, head_dim)
    value_heads = value_rows.reshape(seq_len, heads_here, head_dim)
    pieces_out = []
    pieces_lse = []
    for block_start in range(0, seq_len, block_rows):
        query_block = queries[block_start : block_start + block_rows].reshape(
            block_rows, heads_here, head_dim
        )
        scores = block_scores(
            query_block, key_heads, picture, usable, block_start, block_rows, score_scale
        )
        row_peak = jnp.max(scores, axis=-1, keepdims=True)
        exponent = jnp.exp(scores - row_peak)
        row_total = jnp.sum(exponent, axis=-1, keepdims=True)
        soft_weights = (exponent / row_total).astype(jnp.bfloat16)
        attended = jnp.einsum(
            "hqk,khd->qhd", soft_weights, value_heads, preferred_element_type=jnp.float32
        )
        pieces_out.append(attended.reshape(block_rows, head_width).astype(jnp.bfloat16))
        pieces_lse.append((row_peak + jnp.log(row_total))[..., 0])
    return (jnp.concatenate(pieces_out, axis=0), jnp.concatenate(pieces_lse, axis=1))


def attend_row_back(packed, head_dim):
    queries, key_rows, value_rows, grad_rows, log_total, picture, usable = packed
    seq_len, head_width = queries.shape
    heads_here = head_width // head_dim
    block_rows = min(512, seq_len)
    score_scale = 1.0 / math.sqrt(head_dim)
    key_heads = key_rows.reshape(seq_len, heads_here, head_dim)
    value_heads = value_rows.reshape(seq_len, heads_here, head_dim)
    grad_keys = jnp.zeros((seq_len, heads_here, head_dim), jnp.float32)
    grad_values = jnp.zeros((seq_len, heads_here, head_dim), jnp.float32)
    pieces_query = []
    for block_start in range(0, seq_len, block_rows):
        query_block = queries[block_start : block_start + block_rows].reshape(
            block_rows, heads_here, head_dim
        )
        grad_block = grad_rows[block_start : block_start + block_rows].reshape(
            block_rows, heads_here, head_dim
        )
        scores = block_scores(
            query_block, key_heads, picture, usable, block_start, block_rows, score_scale
        )
        soft_weights = jnp.exp(scores - log_total[:, block_start : block_start + block_rows, None])
        grad_probs = jnp.einsum(
            "qhd,khd->hqk", grad_block, value_heads, preferred_element_type=jnp.float32
        )
        row_inner = jnp.sum(soft_weights * grad_probs, axis=-1, keepdims=True)
        grad_scores = (soft_weights * (grad_probs - row_inner)).astype(jnp.bfloat16)
        grad_query_block = (
            jnp.einsum("hqk,khd->qhd", grad_scores, key_heads, preferred_element_type=jnp.float32)
            * score_scale
        )
        pieces_query.append(grad_query_block.reshape(block_rows, head_width).astype(jnp.bfloat16))
        grad_keys = grad_keys + jnp.einsum(
            "hqk,qhd->khd", grad_scores, query_block, preferred_element_type=jnp.float32
        )
        grad_values = grad_values + jnp.einsum(
            "hqk,qhd->khd",
            soft_weights.astype(jnp.bfloat16),
            grad_block,
            preferred_element_type=jnp.float32,
        )
    grad_keys = (grad_keys * score_scale).reshape(seq_len, head_width).astype(jnp.bfloat16)
    grad_values = grad_values.reshape(seq_len, head_width).astype(jnp.bfloat16)
    return (jnp.concatenate(pieces_query, axis=0), grad_keys, grad_values)


def local(
    patches,
    lengths,
    first_gain,
    first_shift,
    query_weight,
    query_bias,
    key_weight,
    value_weight,
    value_bias,
    output_weight,
    output_bias,
    second_gain,
    second_shift,
    hidden_weight,
    hidden_bias,
    down_weight,
    down_bias,
    cotangent,
):
    seq_count = lax.axis_size("seq")
    row_dev, tok_seq, width = patches.shape
    seq_len = tok_seq * seq_count
    per_micro = row_dev // MB
    flat_rows = per_micro * tok_seq
    picture, usable = picture_ids(lengths, seq_len)
    hidden_shift = hidden_bias.astype(jnp.float32)
    forward_run = partial(attend_row, head_dim=HEAD_DIM)
    backward_run = partial(attend_row_back, head_dim=HEAD_DIM)
    stored = []
    output_parts = []
    for micro in range(MB):
        low_row = micro * per_micro
        gathered = (
            lax.all_gather(query_weight, "fsdp", axis=0, tiled=True),
            lax.all_gather(key_weight, "fsdp", axis=0, tiled=True),
            lax.all_gather(value_weight, "fsdp", axis=0, tiled=True),
            lax.all_gather(output_weight, "fsdp", axis=0, tiled=True),
            lax.all_gather(hidden_weight, "fsdp", axis=0, tiled=True),
            lax.all_gather(down_weight, "fsdp", axis=1, tiled=True),
            lax.all_gather(first_gain, "fsdp", axis=0, tiled=True),
            lax.all_gather(first_shift, "fsdp", axis=0, tiled=True),
            lax.all_gather(query_bias, "fsdp", axis=0, tiled=True),
            lax.all_gather(value_bias, "fsdp", axis=0, tiled=True),
            lax.all_gather(output_bias, "fsdp", axis=0, tiled=True),
            lax.all_gather(second_gain, "fsdp", axis=0, tiled=True),
            lax.all_gather(second_shift, "fsdp", axis=0, tiled=True),
            lax.all_gather(down_bias, "fsdp", axis=0, tiled=True),
        )
        (
            w_query,
            w_key,
            w_value,
            w_output,
            w_hidden,
            w_down,
            gain_one,
            shift_one,
            bias_query,
            bias_value,
            bias_output,
            gain_two,
            shift_two,
            bias_down,
        ) = gathered
        inputs = (
            patches[low_row : low_row + per_micro].reshape(flat_rows, width).astype(jnp.float32)
        )
        normed = layer_norm(
            inputs, gain_one.astype(jnp.float32), shift_one.astype(jnp.float32)
        ).astype(jnp.bfloat16)
        queries = (
            jnp.dot(normed, w_query, preferred_element_type=jnp.float32)
            + bias_query.astype(jnp.float32)
        ).astype(jnp.bfloat16)
        key_rows = jnp.dot(normed, w_key, preferred_element_type=jnp.float32).astype(jnp.bfloat16)
        value_rows = (
            jnp.dot(normed, w_value, preferred_element_type=jnp.float32)
            + bias_value.astype(jnp.float32)
        ).astype(jnp.bfloat16)
        head_query, head_key, head_value = (
            lax.all_to_all(
                queries.reshape(per_micro, tok_seq, width),
                "seq",
                split_axis=2,
                concat_axis=1,
                tiled=True,
            ),
            lax.all_to_all(
                key_rows.reshape(per_micro, tok_seq, width),
                "seq",
                split_axis=2,
                concat_axis=1,
                tiled=True,
            ),
            lax.all_to_all(
                value_rows.reshape(per_micro, tok_seq, width),
                "seq",
                split_axis=2,
                concat_axis=1,
                tiled=True,
            ),
        )
        picture_micro = picture[low_row : low_row + per_micro]
        usable_micro = usable[low_row : low_row + per_micro]
        head_out, log_total = lax.map(
            forward_run, (head_query, head_key, head_value, picture_micro, usable_micro)
        )
        attended = jax.tree.map(
            lambda part, own: part.astype(own.dtype),
            lax.all_to_all(for_sending(head_out), "seq", split_axis=1, concat_axis=2, tiled=True),
            head_out,
        ).reshape(flat_rows, width)
        middle = (
            inputs
            + jnp.dot(attended, w_output, preferred_element_type=jnp.float32)
            + bias_output.astype(jnp.float32)
        )
        second_normed = layer_norm(
            middle, gain_two.astype(jnp.float32), shift_two.astype(jnp.float32)
        ).astype(jnp.bfloat16)
        pre_act = (
            jnp.dot(second_normed, w_hidden, preferred_element_type=jnp.float32) + hidden_shift
        )
        activated = gelu_tanh(pre_act).astype(jnp.bfloat16)
        result = (
            middle
            + jnp.dot(activated, w_down, preferred_element_type=jnp.float32)
            + bias_down.astype(jnp.float32)
        )
        output_parts.append(result.astype(jnp.bfloat16).reshape(per_micro, tok_seq, width))
        stored.append(
            (
                gathered,
                inputs,
                normed,
                head_query,
                head_key,
                head_value,
                log_total,
                attended,
                middle,
                second_normed,
                pre_act,
                activated,
            )
        )
    sums_list = [jnp.zeros(piece.shape, jnp.float32) for piece in stored[0][0]]
    hidden_bias_sum = jnp.zeros(hidden_bias.shape, jnp.float32)
    grad_parts = []
    for micro in range(MB):
        low_row = micro * per_micro
        (
            kept_weights,
            inputs,
            normed,
            head_query,
            head_key,
            head_value,
            log_total,
            attended,
            middle,
            second_normed,
            pre_act,
            activated,
        ) = stored[micro]
        weights_now = (
            lax.all_gather(query_weight, "fsdp", axis=0, tiled=True),
            lax.all_gather(key_weight, "fsdp", axis=0, tiled=True),
            lax.all_gather(value_weight, "fsdp", axis=0, tiled=True),
            lax.all_gather(output_weight, "fsdp", axis=0, tiled=True),
            lax.all_gather(hidden_weight, "fsdp", axis=0, tiled=True),
            lax.all_gather(down_weight, "fsdp", axis=1, tiled=True),
            lax.all_gather(first_gain, "fsdp", axis=0, tiled=True),
            lax.all_gather(first_shift, "fsdp", axis=0, tiled=True),
            lax.all_gather(query_bias, "fsdp", axis=0, tiled=True),
            lax.all_gather(value_bias, "fsdp", axis=0, tiled=True),
            lax.all_gather(output_bias, "fsdp", axis=0, tiled=True),
            lax.all_gather(second_gain, "fsdp", axis=0, tiled=True),
            lax.all_gather(second_shift, "fsdp", axis=0, tiled=True),
            lax.all_gather(down_bias, "fsdp", axis=0, tiled=True),
        )
        (
            w_query,
            w_key,
            w_value,
            w_output,
            w_hidden,
            w_down,
            gain_one,
            shift_one,
            bias_query,
            bias_value,
            bias_output,
            gain_two,
            shift_two,
            bias_down,
        ) = weights_now
        incoming = cotangent[low_row : low_row + per_micro].reshape(flat_rows, width)
        incoming_wide = incoming.astype(jnp.float32)
        grad_down = across_rows(activated, incoming)
        grad_bias_down = jnp.sum(incoming_wide, axis=0)
        grad_act = times_transposed(incoming, w_down)
        _, gelu_pull = jax.vjp(gelu_tanh, pre_act)
        grad_pre = gelu_pull(grad_act)[0].astype(jnp.bfloat16)
        grad_hidden = across_rows(second_normed, grad_pre)
        grad_hidden_bias = jnp.sum(grad_pre.astype(jnp.float32), axis=0)
        grad_second = times_transposed(grad_pre, w_hidden)
        _, second_pull = jax.vjp(
            layer_norm, middle, gain_two.astype(jnp.float32), shift_two.astype(jnp.float32)
        )
        grad_mid_norm, grad_gain_two, grad_shift_two = second_pull(grad_second)
        grad_middle = incoming_wide + grad_mid_norm
        grad_branch = grad_middle.astype(jnp.bfloat16)
        grad_output = across_rows(attended, grad_branch)
        grad_bias_output = jnp.sum(grad_branch.astype(jnp.float32), axis=0)
        grad_attended = (
            times_transposed(grad_branch, w_output)
            .astype(jnp.bfloat16)
            .reshape(per_micro, tok_seq, width)
        )
        head_grad = lax.all_to_all(grad_attended, "seq", split_axis=2, concat_axis=1, tiled=True)
        picture_micro = picture[low_row : low_row + per_micro]
        usable_micro = usable[low_row : low_row + per_micro]
        grad_head_query, grad_head_key, grad_head_value = lax.map(
            backward_run,
            (head_query, head_key, head_value, head_grad, log_total, picture_micro, usable_micro),
        )
        grad_queries, grad_key_rows, grad_value_rows = (
            lax.all_to_all(
                for_sending(grad_head_query), "seq", split_axis=1, concat_axis=2, tiled=True
            ).astype(grad_head_query.dtype),
            lax.all_to_all(
                for_sending(grad_head_key), "seq", split_axis=1, concat_axis=2, tiled=True
            ).astype(grad_head_key.dtype),
            lax.all_to_all(
                for_sending(grad_head_value), "seq", split_axis=1, concat_axis=2, tiled=True
            ).astype(grad_head_value.dtype),
        )
        grad_queries = grad_queries.reshape(flat_rows, width)
        grad_key_rows = grad_key_rows.reshape(flat_rows, width)
        grad_value_rows = grad_value_rows.reshape(flat_rows, width)
        grad_query = across_rows(normed, grad_queries)
        grad_key = across_rows(normed, grad_key_rows)
        grad_value = across_rows(normed, grad_value_rows)
        grad_bias_query = jnp.sum(grad_queries.astype(jnp.float32), axis=0)
        grad_bias_value = jnp.sum(grad_value_rows.astype(jnp.float32), axis=0)
        grad_normed = (
            times_transposed(grad_queries, w_query)
            + times_transposed(grad_key_rows, w_key)
            + times_transposed(grad_value_rows, w_value)
        )
        _, first_pull = jax.vjp(
            layer_norm, inputs, gain_one.astype(jnp.float32), shift_one.astype(jnp.float32)
        )
        grad_in_norm, grad_gain_one, grad_shift_one = first_pull(grad_normed)
        grad_parts.append((grad_middle + grad_in_norm).reshape(per_micro, tok_seq, width))
        terms = (
            grad_query,
            grad_key,
            grad_value,
            grad_output,
            grad_hidden,
            grad_down,
            grad_gain_one,
            grad_shift_one,
            grad_bias_query,
            grad_bias_value,
            grad_bias_output,
            grad_gain_two,
            grad_shift_two,
            grad_bias_down,
        )
        sums_list = [running + term for running, term in zip(sums_list, terms)]
        hidden_bias_sum = hidden_bias_sum + grad_hidden_bias
    owned = (
        lax.psum_scatter(sums_list[0], "fsdp", scatter_dimension=0, tiled=True),
        lax.psum_scatter(sums_list[1], "fsdp", scatter_dimension=0, tiled=True),
        lax.psum_scatter(sums_list[2], "fsdp", scatter_dimension=0, tiled=True),
        lax.psum_scatter(sums_list[3], "fsdp", scatter_dimension=0, tiled=True),
        lax.psum_scatter(sums_list[4], "fsdp", scatter_dimension=0, tiled=True),
        lax.psum_scatter(sums_list[5], "fsdp", scatter_dimension=1, tiled=True),
    )
    shares = (
        lax.psum_scatter(owned[0], "seq", scatter_dimension=1, tiled=True),
        lax.psum_scatter(owned[1], "seq", scatter_dimension=1, tiled=True),
        lax.psum_scatter(owned[2], "seq", scatter_dimension=1, tiled=True),
        lax.psum_scatter(owned[3], "seq", scatter_dimension=1, tiled=True),
        lax.psum_scatter(owned[4], "seq", scatter_dimension=1, tiled=True),
        lax.psum_scatter(owned[5], "seq", scatter_dimension=0, tiled=True),
    )
    matrices = (
        lax.all_gather(shares[0], "seq", axis=1, tiled=True),
        lax.all_gather(shares[1], "seq", axis=1, tiled=True),
        lax.all_gather(shares[2], "seq", axis=1, tiled=True),
        lax.all_gather(shares[3], "seq", axis=1, tiled=True),
        lax.all_gather(shares[4], "seq", axis=1, tiled=True),
        lax.all_gather(shares[5], "seq", axis=0, tiled=True),
    )
    stacked = jnp.stack(sums_list[6:14], axis=0)
    vector_total, hidden_total = lax.psum((stacked, hidden_bias_sum), ("seq", "fsdp"))
    own_width = width // lax.axis_size("fsdp")
    own_vectors = lax.dynamic_slice_in_dim(
        vector_total, lax.axis_index("fsdp") * own_width, own_width, 1
    )
    owned_sums = list(matrices) + [own_vectors[member] for member in range(8)]
    layer_output = jnp.concatenate(output_parts, axis=0)
    grad_patches = jnp.concatenate(grad_parts, axis=0)
    return (
        layer_output,
        grad_patches,
        owned_sums[6],
        owned_sums[7],
        owned_sums[0],
        owned_sums[8],
        owned_sums[1],
        owned_sums[2],
        owned_sums[9],
        owned_sums[3],
        owned_sums[10],
        owned_sums[11],
        owned_sums[12],
        owned_sums[4],
        hidden_total,
        owned_sums[5],
        owned_sums[13],
    )


def solution(mesh):
    in_specs = (
        P("fsdp", "seq", None),
        P("fsdp", None),
        P("fsdp"),
        P("fsdp"),
        P("fsdp", None),
        P("fsdp"),
        P("fsdp", None),
        P("fsdp", None),
        P("fsdp"),
        P("fsdp", None),
        P("fsdp"),
        P("fsdp"),
        P("fsdp"),
        P("fsdp", None),
        P(),
        P(None, "fsdp"),
        P("fsdp"),
        P("fsdp", "seq", None),
    )
    out_specs = (
        P("fsdp", "seq", None),
        P("fsdp", "seq", None),
        P("fsdp"),
        P("fsdp"),
        P("fsdp", None),
        P("fsdp"),
        P("fsdp", None),
        P("fsdp", None),
        P("fsdp"),
        P("fsdp", None),
        P("fsdp"),
        P("fsdp"),
        P("fsdp"),
        P("fsdp", None),
        P(),
        P(None, "fsdp"),
        P("fsdp"),
    )
    return jax.shard_map(local, mesh=mesh, in_specs=in_specs, out_specs=out_specs, check_vma=False)
```

profile of v0, /device:TPU:0, one launch (start us, length us, event | category | flops | bytes accessed | tf_op | source)
XLA Modules:
  0.0 2415.3 jit_solution(9907811332257995592)
XLA Ops:
  19.0 40.2 %all-reduce.12 = (bf16[1152]{0:T(1024)(128)(2,1)}, bf16[1152]{0:T(1024)(128)(2,1)S(1)}, bf16[1152]{0:T(1024)(128)(2,1)S(1)}, bf16[1152]{0:T(1024)(128)(2,1)S(1)}...) all-reduce(bf16[1152]{0:T(1024)(128)(2,1)S(1)} %dynamic-update-slic, ...), channel_id=1, replica_groups=mesh['seq'=4,'fsdp'=8] {'fsdp'}, use_global_device_ids=true, to_apply=%add.2 | all-reduce | flops 9216 | bytes 36864
  106.5 17.9 all-gather.19.cloned.1.call-done
  344.2 37.6 %all-gather.23.cloned.1.call-done = bf16[1152,4304]{1,0:T(8,128)(2,1)} async-done(((bf16[144,4304]{1,0:T(8,128)(2,1)}), bf16[1152,4304]{1,0:T(8,128)(2,1)}) %all-gather.23.cloned.1.call-update) | async-done | bytes 9916432 | tf_op jit(solution)/shard_map/all_gather | solution.py:181
  399.7 127.6 %all-gather.25.cloned.1.call-done = bf16[4304,1152]{0,1:T(8,128)(2,1)} async-done(((bf16[4304,144]{0,1:T(8,128)(2,1)}), bf16[4304,1152]{0,1:T(8,128)(2,1)}) %all-gather.25.cloned.1.call-update) | async-done | bytes 9916432 | tf_op jit(solution)/shard_map/all_gather | solution.py:182
  538.8 12.0 convert_reduce_fusion.1
  959.5 13.1 all_to_all.360
  1002.8 12.4 convolution_add_fusion.3
  1015.1 17.7 convolution_add_fusion.2
  1054.7 17.5 convolution_add_fusion.1
  1072.2 13.6 convolution_add_fusion
  1153.7 12.1 all_to_all.361
  1219.3 14.0 all_to_all.362
  1275.2 13.8 all_to_all.363
  1308.8 52.6 %reduce-scatter.31.cloned.1.call-done = f32[4304,144]{0,1:T(8,128)} async-done(((f32[4304,1152]{0,1:T(8,128)}), f32[4304,144]{0,1:T(8,128)}) %reduce-scatter.31.cloned.1.call-update) | async-done | bytes 2479120 | tf_op jit(solution)/shard_map/reduce_scatter | solution.py:424
  1361.4 334.2 %reduce-scatter.29.cloned.1.call-done = f32[144,4304]{1,0:T(8,128)} async-done(((f32[1152,4304]{1,0:T(8,128)}), f32[144,4304]{1,0:T(8,128)}) %reduce-scatter.29.cloned.1.call-update) | async-done | bytes 2479120 | tf_op jit(solution)/shard_map/reduce_scatter | solution.py:423
  1695.6 106.9 %reduce-scatter.27.cloned.1.call-done = f32[144,1152]{1,0:T(8,128)} async-done(((f32[1152,1152]{1,0:T(8,128)}), f32[144,1152]{1,0:T(8,128)}) %reduce-scatter.27.cloned.1.call-update) | async-done | bytes 663568 | tf_op jit(solution)/shard_map/reduce_scatter | solution.py:422
  1805.2 105.1 %reduce-scatter.25.cloned.1.call-done = f32[144,1152]{1,0:T(8,128)} async-done(((f32[1152,1152]{1,0:T(8,128)}), f32[144,1152]{1,0:T(8,128)}) %reduce-scatter.25.cloned.1.call-update) | async-done | bytes 663568 | tf_op jit(solution)/shard_map/reduce_scatter | solution.py:421
  1925.0 92.9 %reduce-scatter.23.cloned.1.call-done = f32[144,1152]{1,0:T(8,128)} async-done(((f32[1152,1152]{1,0:T(8,128)}), f32[144,1152]{1,0:T(8,128)}) %reduce-scatter.23.cloned.1.call-update) | async-done | bytes 663568 | tf_op jit(solution)/shard_map/reduce_scatter | solution.py:420
  2036.2 89.5 %reduce-scatter.21.cloned.1.call-done = f32[144,1152]{1,0:T(8,128)} async-done(((f32[1152,1152]{1,0:T(8,128)}), f32[144,1152]{1,0:T(8,128)}) %reduce-scatter.21.cloned.1.call-update) | async-done | bytes 663568 | tf_op jit(solution)/shard_map/reduce_scatter | solution.py:419
  2138.8 88.1 %all-reduce.15.cloned.1.call-done = (f32[144,4304]{1,0:T(8,128)}, f32[4304,144]{0,1:T(8,128)}) async-done(((f32[144,4304]{1,0:T(8,128)}, f32[4304,144]{0,1:T(8,128)}), (f32[144,4304]{1,0:T(8,128)}, f32[4304,144]{0,1:T(8,128)})) %all-reduce.15.cloned.1.call-update) | async-done | bytes 4958224
  2266.0 41.1 %all-reduce.10 = (f32[8,1152]{1,0:T(8,128)}, f32[4304]{0:T(1024)}) all-reduce(f32[8,1152]{1,0:T(8,128)} %stack.2, f32[4304]{0:T(1024)} %add_add_fusion.8), channel_id=1, replica_groups=mesh['seq'=4,'fsdp'=8] {'seq','fsdp'}, use_global_device_ids=true, to_apply=%region_68.69 | all-reduce | flops 13520 | bytes 108160 | tf_op jit(solution)/shard_map/psum | solution.py:443
  2329.1 14.0 all-gather.2
  2357.8 14.4 all-gather
  2381.0 22.1 all-gather.27.cloned.1.call-done
  (1077 shorter events, 1085.2 us)
Async XLA Ops:
  7.2 61.2 %all-gather.17.cloned.1.call-start = ((), (), s32[]{:S(2)}) async-start(), calls=%async_computation.35 | async-start | bytes 2985984 | tf_op jit(solution)/shard_map/all_gather | solution.py:177
  7.9 116.4 %all-gather.19.cloned.1.call-start = ((), (), s32[]{:S(2)}) async-start(), calls=%async_computation.36 | async-start | bytes 2985984 | tf_op jit(solution)/shard_map/all_gather | solution.py:178
  8.7 171.5 %all-gather.15.cloned.1.call-start = ((), (), s32[]{:S(2)}) async-start(), calls=%async_computation.34 | async-start | bytes 2985984 | tf_op jit(solution)/shard_map/all_gather | solution.py:179
  9.4 329.3 %all-gather.21.cloned.1.call-start = ((), (), s32[]{:S(2)}) async-start(), calls=%async_computation.37 | async-start | bytes 2985984 | tf_op jit(solution)/shard_map/all_gather | solution.py:180
  10.0 371.7 %all-gather.23.cloned.1.call-start = ((), (), s32[]{:S(2)}) async-start(), calls=%async_computation.38 | async-start | bytes 11280384 | tf_op jit(solution)/shard_map/all_gather | solution.py:181
  10.7 516.6 %all-gather.25.cloned.1.call-start = ((), (), s32[]{:S(2)}) async-start(), calls=%async_computation.39 | async-start | bytes 11280384 | tf_op jit(solution)/shard_map/all_gather | solution.py:182
  102.3 38.2 %all-to-all-start.9 = ((bf16[4,2,36864]{2,1,0:T(2,128)(2,1)}), bf16[4,2,36864]{2,1,0:T(2,128)(2,1)S(1)}, u32[]{:S(2)}, u32[]{:S(2)}) async-start(bf16[4,2,36864]{2,1,0:T(2,128)(2,1)} %reshape.1571), calls=%async_computation.9 | async-start | bytes 1179648 | tf_op jit(solution)/shard_map/all_to_all | solution.py:224
  163.5 32.8 %all-to-all-start.10 = ((bf16[4,2,36864]{2,1,0:T(2,128)(2,1)}), bf16[4,2,36864]{2,1,0:T(2,128)(2,1)}, u32[]{:S(2)}, u32[]{:S(2)}) async-start(bf16[4,2,36864]{2,1,0:T(2,128)(2,1)} %reshape.1573), calls=%async_computation.10 | async-start | bytes 1179648 | tf_op jit(solution)/shard_map/all_to_all | solution.py:231
  282.7 33.5 %all-to-all-start.11 = ((bf16[4,2,36864]{2,1,0:T(2,128)(2,1)}), bf16[4,2,36864]{2,1,0:T(2,128)(2,1)}, u32[]{:S(2)}, u32[]{:S(2)}) async-start(bf16[4,2,36864]{2,1,0:T(2,128)(2,1)} %reshape.1575), calls=%async_computation.11 | async-start | bytes 1179648 | tf_op jit(solution)/shard_map/all_to_all | solution.py:253
  659.6 56.7 %all-to-all-start.19 = ((bf16[4,2,36864]{2,1,0:T(2,128)(2,1)}), bf16[4,2,36864]{2,1,0:T(2,128)(2,1)}, u32[]{:S(2)}, u32[]{:S(2)}) async-start(bf16[4,2,36864]{2,1,0:T(2,128)(2,1)} %reshape.1591), calls=%async_computation.19 | async-start | bytes 1179648 | tf_op jit(solution)/shard_map/all_to_all | solution.py:378
  794.0 39.9 %all-to-all-start.17 = ((bf16[4,2,36864]{2,1,0:T(2,128)(2,1)}), bf16[4,2,36864]{2,1,0:T(2,128)(2,1)}, u32[]{:S(2)}, u32[]{:S(2)}) async-start(bf16[4,2,36864]{2,1,0:T(2,128)(2,1)} %reshape.1587), calls=%async_computation.17 | async-start | bytes 1179648 | tf_op jit(solution)/shard_map/all_to_all | solution.py:372
  911.4 450.0 %reduce-scatter.31.cloned.1.call-start = ((), (), s32[]{:S(2)}) async-start(), calls=%async_computation.45 | async-start | bytes 22560768 | tf_op jit(solution)/shard_map/reduce_scatter | solution.py:424
  1032.9 662.7 %reduce-scatter.29.cloned.1.call-start = ((), (), s32[]{:S(2)}) async-start(), calls=%async_computation.44 | async-start | bytes 22560768 | tf_op jit(solution)/shard_map/reduce_scatter | solution.py:423
  1085.8 716.7 %reduce-scatter.27.cloned.1.call-start = ((), (), s32[]{:S(2)}) async-start(), calls=%async_computation.43 | async-start | bytes 5971968 | tf_op jit(solution)/shard_map/reduce_scatter | solution.py:422
  1118.3 792.0 %reduce-scatter.25.cloned.1.call-start = ((), (), s32[]{:S(2)}) async-start(), calls=%async_computation.42 | async-start | bytes 5971968 | tf_op jit(solution)/shard_map/reduce_scatter | solution.py:421
  1184.3 833.6 %reduce-scatter.23.cloned.1.call-start = ((), (), s32[]{:S(2)}) async-start(), calls=%async_computation.41 | async-start | bytes 5971968 | tf_op jit(solution)/shard_map/reduce_scatter | solution.py:420
  1253.1 872.6 %reduce-scatter.21.cloned.1.call-start = ((), (), s32[]{:S(2)}) async-start(), calls=%async_computation.40 | async-start | bytes 5971968 | tf_op jit(solution)/shard_map/reduce_scatter | solution.py:419
  1308.7 918.2 %all-reduce.15.cloned.1.call-start = ((), (), s32[]{:S(2)}) async-start(), calls=%async_computation.52 | async-start | bytes 10027008
  1695.6 619.6 %reduce-scatter.39.cloned.1.call-start = ((), (), s32[]{:S(2)}) async-start(), calls=%async_computation.51 | async-start | bytes 1474560
  1805.0 523.0 %reduce-scatter.37.cloned.1.call-start = ((), (), s32[]{:S(2)}) async-start(), calls=%async_computation.50 | async-start | bytes 1474560
  1912.8 431.9 %reduce-scatter.35.cloned.1.call-start = ((), (), s32[]{:S(2)}) async-start(), calls=%async_computation.49 | async-start | bytes 1474560
  2020.4 336.3 %reduce-scatter.33.cloned.1.call-start = ((), (), s32[]{:S(2)}) async-start(), calls=%async_computation.48 | async-start | bytes 1474560
  2128.3 247.6 %all-gather.29.cloned.1.call-start = ((), (), s32[]{:S(2)}) async-start(), calls=%async_computation.47 | async-start | bytes 3317760 | tf_op jit(solution)/shard_map/all_gather | solution.py:440
  2229.1 174.0 %all-gather.27.cloned.1.call-start = ((), (), s32[]{:S(2)}) async-start(), calls=%async_computation.46 | async-start | bytes 3317760 | tf_op jit(solution)/shard_map/all_gather | solution.py:439
  (297 other events, 3936.4 us)
Sparse Core Ops, SparseCore 0:
  10.2 58.1 all-gather.16
  70.6 53.7 all-gather.18
  126.5 53.5 all-gather.14
  182.2 53.5 all-gather.20
  237.9 143.8 all-gather.22
  383.8 143.4 all-gather.24
  1033.0 328.3 reduce-scatter.30
  1365.3 330.2 reduce-scatter.28
  1699.2 103.2 reduce-scatter.26
  1806.4 103.9 reduce-scatter.24
  1913.9 103.9 reduce-scatter.22
  2021.8 103.8 reduce-scatter.20
  2128.1 98.7 all-reduce.14
  2229.3 25.8 reduce-scatter.38
  2257.8 25.8 reduce-scatter.36
  2286.2 26.0 reduce-scatter.34
  2314.9 29.9 reduce-scatter.32
  2346.2 29.5 all-gather.28
  2377.4 25.7 all-gather.26
where the time goes:
time: 2430 us; the launch traced here: 2420 us
  waiting for transfers between devices  1110 us (46%)
  matrix products  405 us (17%)
  local copies, waits for them, and re-layouts  372 us (15%)
  other arithmetic  243 us (10%)
  blocking collectives  182 us (7%)
  starting transfers between devices  83.7 us (3%)
    reduce_scatter x1, waiting for transfers between devices, local(): lax.psum_scatter(sums_list[4], 'fsdp', scatter_dimension=0, tiled=True)  334 us
    unnamed x657, local copies, waits for them, and re-layouts  184 us
    unnamed x30, other arithmetic  158 us
    all_gather x1, waiting for transfers between devices, local(): lax.all_gather(down_weight, 'fsdp', axis=1, tiled=True)  128 us
    reduce_scatter x1, waiting for transfers between devices, local(): lax.psum_scatter(sums_list[3], 'fsdp', scatter_dimension=0, tiled=True)  107 us
    reduce_scatter x1, waiting for transfers between devices, local(): lax.psum_scatter(sums_list[2], 'fsdp', scatter_dimension=0, tiled=True)  105 us
    dot_general x18, matrix products, across_rows(): lax.dot_general(left, right, (((0,), (0,)), ((), ())), preferred_element_...  103 us
    reduce_scatter x1, waiting for transfers between devices, local(): lax.psum_scatter(sums_list[1], 'fsdp', scatter_dimension=0, tiled=True)  92.9 us
  transfers between devices with their start and end apart: 39, of which 15 were waited for; matrix products, arithmetic and copies ran while one was open for 31% of the time, Pallas kernels for 0%

commit v1 on v0

v1 whole, which is shorter than its diff:
```python
import functools
import math

import jax
import jax.numpy as jnp
from jax import lax
from jax.experimental import pallas as pl
from jax.experimental.pallas import tpu as pltpu
from jax.sharding import PartitionSpec as P

HEAD_DIM = 72
EPS = 1e-06
GELU_COEF = math.sqrt(2.0 / math.pi)
MASKED = -1e30
F32 = jnp.float32
BF16 = jnp.bfloat16
SCALE = 1.0 / math.sqrt(HEAD_DIM)
WIN = 256
VMEM = 60 << 20


def round_up(value, step):
    return (value + step - 1) // step * step


def dot(left, right, dims=((1,), (0,))):
    return lax.dot_general(left, right, (dims, ((), ())), preferred_element_type=F32)


NT = ((1,), (1,))
TN = ((0,), (0,))


def params(semantics):
    return pltpu.CompilerParams(dimension_semantics=semantics, vmem_limit_bytes=VMEM)


def swap(array, axis, bit):
    size = lax.axis_size(axis)
    return lax.ppermute(array, axis, [(i, i ^ bit) for i in range(size)])


def bits_of(size):
    return [1 << k for k in reversed(range(size.bit_length() - 1))]


def after(value, *earlier):
    return lax.optimization_barrier((value,) + tuple(earlier))[0]


def gather_shards(shard, gate=None):
    parts = {0: shard}
    first = {}
    for bit in bits_of(lax.axis_size("fsdp")):
        fresh = {}
        for distance, part in parts.items():
            if gate and bit in gate and distance == 0:
                part = after(part, gate[bit])
            fresh[distance | bit] = swap(part, "fsdp", bit)
        first[bit] = fresh[bit]
        parts.update(fresh)
    return parts, first


def rel_position(distance, count):
    width = count.bit_length() - 1
    return sum(((distance >> k) & 1) << (width - 1 - k) for k in range(width))


def assemble_kernel(count, rows, off_ref, *refs):
    out_ref = refs[count]
    for distance in range(count):
        start = pl.multiple_of(off_ref[distance], 16)
        out_ref[pl.ds(start, rows), :] = refs[distance][...]


def assemble(parts, me):
    count = len(parts)
    rows, cols = parts[0].shape
    if rows % 16:
        stacked = jnp.stack([parts[d] for d in range(count)])
        return jnp.take(stacked, me ^ jnp.arange(count), axis=0).reshape(count * rows, cols)
    offsets = ((me ^ jnp.arange(count, dtype=jnp.int32)) * rows).astype(jnp.int32)
    tile = cols
    for candidate in (640, 384, 128):
        if cols % candidate == 0:
            tile = candidate
            break
    return pl.pallas_call(
        functools.partial(assemble_kernel, count, rows),
        out_shape=jax.ShapeDtypeStruct((count * rows, cols), parts[0].dtype),
        grid_spec=pltpu.PrefetchScalarGridSpec(
            num_scalar_prefetch=1,
            grid=(cols // tile,),
            in_specs=[pl.BlockSpec((rows, tile), lambda n, off: (0, n))] * count,
            out_specs=pl.BlockSpec((count * rows, tile), lambda n, off: (0, n)),
        ),
        compiler_params=params(("arbitrary",)),
        cost_estimate=pl.CostEstimate(
            flops=0, transcendentals=0, bytes_accessed=4 * count * rows * cols
        ),
        name="assemble",
    )(offsets, *[parts[d] for d in range(count)])


def weight_grad_kernel(pairs, count, rows, pos_ref, *refs):
    lefts, rights = refs[:pairs], refs[pairs : 2 * pairs]
    out_ref, turned = refs[2 * pairs], refs[2 * pairs + 1]
    tokens = lefts[0].shape[0]

    @pl.when(pl.program_id(0) == 0)
    def _():
        for i in range(pairs):
            turned[:, i * tokens : (i + 1) * tokens] = lefts[i][...].T

    total = dot(turned[:, :tokens], rights[0][...])
    for i in range(1, pairs):
        total += dot(turned[:, i * tokens : (i + 1) * tokens], rights[i][...])
    for shard in range(count):
        start = pl.multiple_of(pos_ref[shard], 16)
        out_ref[pl.ds(start, rows), :] = total[shard * rows : (shard + 1) * rows].astype(BF16)


def weight_grad(lefts, rights, me, count, first_col=0, cols=None):
    tokens, width = lefts[0].shape
    cols = cols or rights[0].shape[1]
    rows = width // count
    order = me ^ jnp.arange(count, dtype=jnp.int32)
    table = jnp.array([rel_position(d, count) for d in range(count)], jnp.int32)
    if rows % 16:
        total = sum(dot(a, b[:, first_col : first_col + cols], TN) for a, b in zip(lefts, rights))
        by_distance = jnp.take(total.astype(BF16).reshape(count, rows, cols), order, axis=0)
        back = [0] * count
        for d in range(count):
            back[rel_position(d, count)] = d
        return jnp.take(by_distance, jnp.array(back), axis=0)
    positions = (table[order] * rows).astype(jnp.int32)
    tile = 256 if first_col % 256 == 0 else 128
    pairs = len(lefts)
    base = first_col // tile
    return pl.pallas_call(
        functools.partial(weight_grad_kernel, pairs, count, rows),
        out_shape=jax.ShapeDtypeStruct((width, cols), BF16),
        grid_spec=pltpu.PrefetchScalarGridSpec(
            num_scalar_prefetch=1,
            grid=(pl.cdiv(cols, tile),),
            in_specs=[
                pl.BlockSpec((tokens, width), lambda n, off: (0, 0), pipeline_mode=pl.Buffered(1))
            ]
            * pairs
            + [pl.BlockSpec((tokens, tile), lambda n, off: (0, n + base))] * pairs,
            out_specs=pl.BlockSpec((width, tile), lambda n, off: (0, n)),
            scratch_shapes=[pltpu.VMEM((width, pairs * tokens), BF16)],
        ),
        compiler_params=params(("arbitrary",)),
        cost_estimate=pl.CostEstimate(
            flops=2 * pairs * tokens * width * cols,
            transcendentals=0,
            bytes_accessed=2 * (pairs * tokens * (width + cols) + width * cols),
        ),
        name="weight_grad",
    )(positions, *lefts, *rights).reshape(count, rows, cols)


def scatter_sum(blocks):
    for bit in reversed(bits_of(lax.axis_size("fsdp"))):
        half = blocks.shape[0] // 2
        arrived = swap(blocks[half:], "fsdp", bit)
        blocks = (blocks[:half].astype(F32) + arrived.astype(F32)).astype(BF16)
    mine = blocks[0]
    for bit in bits_of(lax.axis_size("seq"))[:-1]:
        arrived = swap(mine, "seq", bit)
        total = mine.astype(F32) + arrived.astype(F32)
        mine = total.astype(BF16)
    return total


def norm_kernel(x_ref, gain_ref, shift_ref, out_ref):
    values = x_ref[...].astype(F32)
    center = values - jnp.mean(values, axis=-1, keepdims=True)
    spread = jnp.mean(center * center, axis=-1, keepdims=True)
    out_ref[...] = (center * lax.rsqrt(spread + EPS) * gain_ref[...] + shift_ref[...]).astype(BF16)


def norm(values, gain, shift):
    rows, width = values.shape
    block = 256 if rows % 256 == 0 else rows
    return pl.pallas_call(
        norm_kernel,
        out_shape=jax.ShapeDtypeStruct((rows, width), BF16),
        grid=(rows // block,),
        in_specs=[
            pl.BlockSpec((block, width), lambda i: (i, 0)),
            pl.BlockSpec((1, width), lambda i: (0, 0)),
            pl.BlockSpec((1, width), lambda i: (0, 0)),
        ],
        out_specs=pl.BlockSpec((block, width), lambda i: (i, 0)),
        compiler_params=params(("arbitrary",)),
        cost_estimate=pl.CostEstimate(
            flops=10 * rows * width, transcendentals=0, bytes_accessed=6 * rows * width
        ),
        name="norm",
    )(values, gain, shift)


def norm_back_kernel(x_ref, own_ref, other_ref, gain_ref, add_ref, dx_ref, low_ref, dg_ref, ds_ref):
    values = x_ref[...].astype(F32)
    center = values - jnp.mean(values, axis=-1, keepdims=True)
    spread = jnp.mean(center * center, axis=-1, keepdims=True)
    inverse = lax.rsqrt(spread + EPS)
    hat = center * inverse
    grad = own_ref[...].astype(F32) + other_ref[...].astype(F32)
    scaled = grad * gain_ref[...]
    first = jnp.mean(scaled, axis=-1, keepdims=True)
    second = jnp.mean(scaled * hat, axis=-1, keepdims=True)
    total = add_ref[...].astype(F32) + inverse * (scaled - first - hat * second)
    dx_ref[...] = total
    low_ref[...] = total.astype(BF16)

    @pl.when(pl.program_id(0) == 0)
    def _():
        dg_ref[...] = jnp.zeros_like(dg_ref)
        ds_ref[...] = jnp.zeros_like(ds_ref)

    dg_ref[...] += jnp.sum(grad * hat, axis=0, keepdims=True)
    ds_ref[...] += jnp.sum(grad, axis=0, keepdims=True)


def norm_back(values, own, other, gain, add):
    rows, width = values.shape
    block = 256 if rows % 256 == 0 else rows
    wide = pl.BlockSpec((block, width), lambda i: (i, 0))
    line = pl.BlockSpec((1, width), lambda i: (0, 0))
    return pl.pallas_call(
        norm_back_kernel,
        out_shape=(
            jax.ShapeDtypeStruct((rows, width), F32),
            jax.ShapeDtypeStruct((rows, width), BF16),
            jax.ShapeDtypeStruct((1, width), F32),
            jax.ShapeDtypeStruct((1, width), F32),
        ),
        grid=(rows // block,),
        in_specs=[wide, wide, wide, line, wide],
        out_specs=(wide, wide, line, line),
        compiler_params=params(("arbitrary",)),
        cost_estimate=pl.CostEstimate(
            flops=20 * rows * width, transcendentals=0, bytes_accessed=18 * rows * width
        ),
        name="norm_back",
    )(values, own, other, gain, add)


def hidden_kernel(x_ref, w_ref, b_ref, act_ref, slope_ref):
    pre = dot(x_ref[...], w_ref[...]) + b_ref[...]
    square = pre * pre
    turn = jnp.tanh(GELU_COEF * (pre + 0.044715 * square * pre))
    act_ref[...] = (0.5 * pre * (1.0 + turn)).astype(BF16)
    inner = GELU_COEF * (1.0 + 3.0 * 0.044715 * square)
    slope_ref[...] = (0.5 * (1.0 + turn) + 0.5 * pre * (1.0 - turn * turn) * inner).astype(BF16)


def hidden(x, weight, bias):
    rows, width = x.shape
    cols = weight.shape[1]
    block = 128
    out = pl.BlockSpec((block, cols), lambda i: (i, 0))
    return pl.pallas_call(
        hidden_kernel,
        out_shape=(jax.ShapeDtypeStruct((rows, cols), BF16),) * 2,
        grid=(rows // block,),
        in_specs=[
            pl.BlockSpec((block, width), lambda i: (i, 0)),
            pl.BlockSpec((width, cols), lambda i: (0, 0), pipeline_mode=pl.Buffered(1)),
            pl.BlockSpec((1, cols), lambda i: (0, 0)),
        ],
        out_specs=(out, out),
        compiler_params=params(("arbitrary",)),
        cost_estimate=pl.CostEstimate(
            flops=2 * rows * width * cols,
            transcendentals=rows * cols,
            bytes_accessed=2 * (rows * width + width * cols + 2 * rows * cols),
        ),
        name="hidden",
    )(x, weight, bias)


def head_window(head, padded):
    tile = jnp.minimum((head * HEAD_DIM) >> 7, (padded - WIN) >> 7)
    return pl.multiple_of(tile * 128, 128), head * HEAD_DIM - tile * 128


def only_head(block, lane, low):
    return jnp.where((lane >= low) & (lane < low + HEAD_DIM), block.astype(F32), 0.0).astype(BF16)


def attend_kernel(which, heads, blocks, padded, need_ref, col_ref, row_ref, *refs):
    sides = refs[:blocks]
    out_ref, lse_ref, score, peak, total, acc = refs[blocks:]
    row = pl.program_id(0)
    tokens = out_ref.shape[1]
    lane = lax.broadcasted_iota(jnp.int32, (tokens, WIN), 1)
    slot = lax.broadcasted_iota(jnp.int32, (tokens, 128), 1)
    out_ref[...] = jnp.zeros_like(out_ref)
    lse_ref[...] = jnp.zeros_like(lse_ref)

    def one_head(head, carry):
        start, low = head_window(head, padded)
        query = only_head(sides[which][0, :, pl.ds(start, WIN)], lane, low)
        peak[...] = jnp.full_like(peak, MASKED)
        total[...] = jnp.zeros_like(total)
        acc[...] = jnp.zeros_like(acc)
        for block in range(blocks):

            @pl.when(need_ref[row, which, block] != 0)
            def _():
                key = sides[block][0, :, pl.ds(padded + start, WIN)]
                found = jnp.where(
                    col_ref[0, which] == row_ref[0, block : block + 1], dot(query, key, NT), MASKED
                )
                score[block] = found
                peak[...] = jnp.maximum(peak[...], jnp.max(found, axis=-1, keepdims=True))

        for block in range(blocks):

            @pl.when(need_ref[row, which, block] != 0)
            def _():
                weight = jnp.exp((score[block] - peak[:, :1]) * SCALE)
                total[...] += jnp.sum(weight, axis=-1, keepdims=True)
                value = sides[block][0, :, pl.ds(2 * padded + start, WIN)]
                acc[...] += dot(weight.astype(BF16), value)

        result = acc[...] / total[:, :1]
        kept = out_ref[0, :, pl.ds(start, WIN)].astype(F32)
        mine = (lane >= low) & (lane < low + HEAD_DIM)
        out_ref[0, :, pl.ds(start, WIN)] = jnp.where(mine, result, kept).astype(BF16)
        lse = peak[...] * SCALE + jnp.log(total[...])
        lse_ref[0] = jnp.where(slot == head, lse, lse_ref[0])
        return carry

    lax.fori_loop(0, heads, one_head, 0)


def attend(which, sides, need, seg_col, seg_row, heads):
    rows, tokens, wide = sides[0].shape
    blocks, padded = len(sides), wide // 3
    cost = rows * heads * blocks * tokens * tokens
    return pl.pallas_call(
        functools.partial(attend_kernel, which, heads, blocks, padded),
        out_shape=(
            jax.ShapeDtypeStruct((rows, tokens, padded), BF16),
            jax.ShapeDtypeStruct((rows, tokens, 128), F32),
        ),
        grid_spec=pltpu.PrefetchScalarGridSpec(
            num_scalar_prefetch=1,
            grid=(rows,),
            in_specs=[
                pl.BlockSpec((1, blocks, tokens, 1), lambda r, need: (r, 0, 0, 0)),
                pl.BlockSpec((1, blocks, tokens), lambda r, need: (r, 0, 0)),
            ]
            + [pl.BlockSpec((1, tokens, wide), lambda r, need: (r, 0, 0))] * blocks,
            out_specs=(
                pl.BlockSpec((1, tokens, padded), lambda r, need: (r, 0, 0)),
                pl.BlockSpec((1, tokens, 128), lambda r, need: (r, 0, 0)),
            ),
            scratch_shapes=[
                pltpu.VMEM((blocks, tokens, tokens), F32),
                pltpu.VMEM((tokens, 128), F32),
                pltpu.VMEM((tokens, 128), F32),
                pltpu.VMEM((tokens, WIN), F32),
            ],
        ),
        compiler_params=params(("arbitrary",)),
        cost_estimate=pl.CostEstimate(
            flops=4 * cost * WIN, transcendentals=cost, bytes_accessed=2 * rows * tokens * wide * blocks
        ),
        name="attend",
    )(need, seg_col, seg_row, *sides)


def attend_back_kernel(heads, blocks, padded, need_ref, col_ref, row_ref, pick_ref, *refs):
    sides = refs[:blocks]
    grads, outs, lses = refs[blocks : blocks + 2], refs[blocks + 2 : blocks + 4], refs[blocks + 4 : blocks + 6]
    results = refs[blocks + 6 : 2 * blocks + 6]
    sums, lse_turn, inner_turn, dq = refs[2 * blocks + 6 :]
    row = pl.program_id(0)
    tokens = grads[0].shape[1]
    lane = lax.broadcasted_iota(jnp.int32, (tokens, WIN), 1)
    sums[...] = jnp.zeros_like(sums)
    for which in range(2):
        results[which][0, :, :padded] = jnp.zeros((tokens, padded), BF16)
        lse_turn[...] = lses[which][0].T
        product = grads[which][0].astype(F32) * outs[which][0].astype(F32)
        high = product.astype(BF16)
        rest = (product - high.astype(F32)).astype(BF16)
        inner_turn[...] = dot(pick_ref[...], high, NT) + dot(pick_ref[...], rest, NT)

        def one_head(head, carry, which=which):
            start, low = head_window(head, padded)
            query = only_head(sides[which][0, :, pl.ds(start, WIN)], lane, low)
            grad = only_head(grads[which][0, :, pl.ds(start, WIN)], lane, low)
            lse = lse_turn[pl.ds(head, 1), :]
            inner = inner_turn[pl.ds(head, 1), :]
            dq[...] = jnp.zeros_like(dq)
            for block in range(blocks):

                @pl.when(need_ref[row, which, block] != 0)
                def _():
                    key = sides[block][0, :, pl.ds(padded + start, WIN)]
                    value = sides[block][0, :, pl.ds(2 * padded + start, WIN)]
                    seen = col_ref[0, block] == row_ref[0, which : which + 1]
                    prob = jnp.where(seen, jnp.exp(dot(key, query, NT) * SCALE - lse), 0.0)
                    slope = (prob * (dot(value, grad, NT) - inner)).astype(BF16)
                    sums[block, :, pl.ds(start, WIN)] += dot(slope, query)
                    sums[block, :, pl.ds(padded + start, WIN)] += dot(prob.astype(BF16), grad)
                    dq[...] += dot(slope, key, TN)

            kept = results[which][0, :, pl.ds(start, WIN)].astype(F32)
            mine = (lane >= low) & (lane < low + HEAD_DIM)
            results[which][0, :, pl.ds(start, WIN)] = jnp.where(mine, dq[...] * SCALE, kept).astype(BF16)
            return carry

        lax.fori_loop(0, heads, one_head, 0)
    for block in range(blocks):
        skip = padded if block < 2 else 0
        results[block][0, :, skip : skip + padded] = (sums[block, :, :padded] * SCALE).astype(BF16)
        results[block][0, :, skip + padded :] = sums[block, :, padded:].astype(BF16)


def attend_back(sides, grads, outs, lses, need, seg_col, seg_row, heads):
    rows, tokens, wide = sides[0].shape
    blocks, padded = len(sides), wide // 3
    cost = 2 * rows * heads * blocks * tokens * tokens
    column = lax.broadcasted_iota(jnp.int32, (128, padded), 1)
    pick = (column // HEAD_DIM == lax.broadcasted_iota(jnp.int32, (128, padded), 0)).astype(BF16)
    narrow = pl.BlockSpec((1, tokens, padded), lambda r, need: (r, 0, 0))
    line = pl.BlockSpec((1, tokens, 128), lambda r, need: (r, 0, 0))
    widths = [wide if block < 2 else 2 * padded for block in range(blocks)]
    return pl.pallas_call(
        functools.partial(attend_back_kernel, heads, blocks, padded),
        out_shape=tuple(jax.ShapeDtypeStruct((rows, tokens, w), BF16) for w in widths),
        grid_spec=pltpu.PrefetchScalarGridSpec(
            num_scalar_prefetch=1,
            grid=(rows,),
            in_specs=[
                pl.BlockSpec((1, blocks, tokens, 1), lambda r, need: (r, 0, 0, 0)),
                pl.BlockSpec((1, blocks, tokens), lambda r, need: (r, 0, 0)),
                pl.BlockSpec((128, padded), lambda r, need: (0, 0)),
            ]
            + [pl.BlockSpec((1, tokens, wide), lambda r, need: (r, 0, 0))] * blocks
            + [narrow] * 4
            + [line] * 2,
            out_specs=tuple(pl.BlockSpec((1, tokens, w), lambda r, need: (r, 0, 0)) for w in widths),
            scratch_shapes=[
                pltpu.VMEM((blocks, tokens, 2 * padded), F32),
                pltpu.VMEM((128, tokens), F32),
                pltpu.VMEM((128, tokens), F32),
                pltpu.VMEM((tokens, WIN), F32),
            ],
        ),
        compiler_params=params(("arbitrary",)),
        cost_estimate=pl.CostEstimate(
            flops=10 * cost * WIN,
            transcendentals=cost,
            bytes_accessed=4 * rows * tokens * wide * blocks,
        ),
        name="attend_back",
    )(need, seg_col, seg_row, pick, *sides, *grads, *outs, *lses)


def column_sum(array):
    ones = jnp.ones((8, array.shape[0]), BF16)
    return dot(ones, array)[0]


def local(
    patches,
    lengths,
    first_gain,
    first_shift,
    query_weight,
    query_bias,
    key_weight,
    value_weight,
    value_bias,
    output_weight,
    output_bias,
    second_gain,
    second_shift,
    hidden_weight,
    hidden_bias,
    down_weight,
    down_bias,
    cotangent,
):
    seq_count, shards = lax.axis_size("seq"), lax.axis_size("fsdp")
    place, me = lax.axis_index("seq"), lax.axis_index("fsdp")
    core = place & 1
    is_first = core == 0
    rows, tokens, width = patches.shape
    flat = rows * tokens
    heads = width // HEAD_DIM // 2
    half = heads * HEAD_DIM
    padded = round_up(half, 128)
    ff = hidden_bias.shape[0]
    ff_half = round_up(ff, 256) // 2
    out_cols = padded
    out_cut = width - padded

    def my_half(array, size, padded_size):
        first, second = array[..., :size], array[..., size:]
        grow = [(0, 0)] * (array.ndim - 1)
        first = jnp.pad(first, grow + [(0, padded_size - size)])
        second = jnp.pad(second, grow + [(0, padded_size - second.shape[-1])])
        return jnp.where(is_first, first, second)

    vectors = jnp.stack(
        [
            first_gain,
            first_shift,
            query_bias,
            value_bias,
            output_bias,
            second_gain,
            second_shift,
            down_bias,
        ]
    )
    vector_parts, _ = gather_shards(vectors)
    stacked = jnp.stack([vector_parts[d] for d in range(shards)])
    stacked = jnp.take(stacked, me ^ jnp.arange(shards), axis=0)
    stacked = stacked.transpose(1, 0, 2).reshape(8, width).astype(F32)
    gain_one, shift_one, bias_query, bias_value, bias_output, gain_two, shift_two, bias_down = [
        stacked[i : i + 1] for i in range(8)
    ]

    shard_qkv = jnp.concatenate(
        [my_half(w, half, padded) for w in (query_weight, key_weight, value_weight)], axis=1
    )
    shard_out = jnp.where(is_first, output_weight[:, :out_cols], output_weight[:, out_cut:])
    shard_hidden = my_half(hidden_weight, ff_half, ff_half)
    shard_down = my_half(down_weight.T, ff_half, ff_half)
    parts_qkv, first_qkv = gather_shards(shard_qkv)
    parts_out, first_out = gather_shards(shard_out, first_qkv)
    parts_hidden, first_hidden = gather_shards(shard_hidden, first_out)
    parts_down, _ = gather_shards(shard_down, first_hidden)

    block_of = place ^ jnp.arange(seq_count, dtype=jnp.int32)
    position = block_of[:, None] * tokens + jnp.arange(tokens, dtype=jnp.int32)[None, :]
    ends = jnp.cumsum(lengths, axis=-1)
    picture = jnp.sum(
        (position[None, :, :, None] >= ends[:, None, None, :]).astype(jnp.int32), axis=-1
    )
    usable = position[None] < ends[:, -1][:, None, None]
    segment = jnp.where(usable, picture, 1000 + position[None])
    seg_row = segment
    seg_col = segment[..., None]
    low_id = jnp.min(jnp.where(usable, picture, 1 << 20), axis=-1)
    high_id = jnp.max(jnp.where(usable, picture, -1), axis=-1)
    need = (low_id[:, :2, None] <= high_id[:, None, :]) & (low_id[:, None, :] <= high_id[:, :2, None])
    need = need | jnp.eye(2, seq_count, dtype=jnp.bool_)[None]
    need = need.astype(jnp.int32)

    inputs = patches.reshape(flat, width)
    incoming = cotangent.reshape(flat, width)
    incoming_pair = swap(incoming, "seq", 1)
    normed = {0: norm(inputs, gain_one, shift_one)}
    for bit in bits_of(seq_count):
        normed.update({j | bit: swap(part, "seq", bit) for j, part in list(normed.items())})
    w_qkv = assemble(parts_qkv, me)
    zeros = jnp.zeros((1, padded), F32)
    bias_qkv = jnp.concatenate(
        [my_half(bias_query, half, padded), zeros, my_half(bias_value, half, padded)], axis=1
    )
    sides = [
        (dot(normed[j], w_qkv) + bias_qkv).astype(BF16).reshape(rows, tokens, 3 * padded)
        for j in range(seq_count)
    ]
    out_pair, lse_pair = attend(1, sides, need, seg_col, seg_row, heads)
    other_half = swap(out_pair, "seq", 1)
    out_own, lse_own = attend(0, sides, need, seg_col, seg_row, heads)
    own_cut = out_own.reshape(flat, padded)[:, :half]
    other_cut = other_half.reshape(flat, padded)[:, :half]
    attended = jnp.where(
        is_first,
        jnp.concatenate([own_cut, other_cut], axis=1),
        jnp.concatenate([other_cut, own_cut], axis=1),
    )
    w_out_mine = assemble(parts_out, me)
    w_out_other = swap(w_out_mine, "seq", 1)
    w_out = jnp.where(
        is_first,
        jnp.concatenate([w_out_mine[:, :out_cut], w_out_other], axis=1),
        jnp.concatenate([w_out_other[:, :out_cut], w_out_mine], axis=1),
    )
    middle = inputs.astype(F32) + dot(attended, w_out) + bias_output
    second = norm(middle, gain_two, shift_two)
    second_pair = swap(second, "seq", 1)
    w_hidden = assemble(parts_hidden, me)
    bias_hidden = my_half(hidden_bias.astype(F32)[None], ff_half, ff_half)
    act_own, slope_own = hidden(second, w_hidden, bias_hidden)
    act_pair, slope_pair = hidden(second_pair, w_hidden, bias_hidden)
    w_down = assemble(parts_down, me)
    down_pair = dot(act_pair, w_down, NT).astype(BF16)
    down_back = swap(down_pair, "seq", 1)
    result = middle + dot(act_own, w_down, NT) + down_back.astype(F32) + bias_down
    layer_output = result.astype(BF16).reshape(rows, tokens, width)

    grad_down = weight_grad([incoming, incoming_pair], [act_own, act_pair], me, shards)
    pre_pair = (dot(incoming_pair, w_down) * slope_pair.astype(F32)).astype(BF16)
    back_pair = dot(pre_pair, w_hidden, NT).astype(BF16)
    back_other = swap(back_pair, "seq", 1)
    pre_own = (dot(incoming, w_down) * slope_own.astype(F32)).astype(BF16)
    back_own = dot(pre_own, w_hidden, NT)
    sum_down = scatter_sum(grad_down)
    grad_hidden = weight_grad([second, second_pair], [pre_own, pre_pair], me, shards)
    sum_hidden = scatter_sum(grad_hidden)
    grad_hidden_bias = column_sum(pre_own) + column_sum(pre_pair)
    grad_middle, branch, grad_gain_two, grad_shift_two = norm_back(
        middle, back_own, back_other, gain_two, incoming
    )
    grad_attended = dot(branch, w_out, NT).astype(BF16)
    grad_first, grad_second = grad_attended[:, :half], grad_attended[:, half:]
    grow = ((0, 0), (0, padded - half))
    grad_mine = jnp.pad(jnp.where(is_first, grad_first, grad_second), grow)
    grad_send = jnp.pad(jnp.where(is_first, grad_second, grad_first), grow)
    grad_pair = swap(grad_send, "seq", 1)
    partial_out = weight_grad([attended], [branch], me, shards)
    out_mine = jnp.where(is_first, partial_out[..., :out_cols], partial_out[..., out_cut:])
    out_send = jnp.where(is_first, partial_out[..., out_cut:], partial_out[..., :out_cols])
    out_back = swap(out_send, "seq", 1)
    grad_out = (out_mine.astype(F32) + out_back.astype(F32)).astype(BF16)
    sum_out = scatter_sum(grad_out)
    shape = (rows, tokens, padded)
    grad_sides = attend_back(
        sides,
        [grad_mine.reshape(shape), grad_pair.reshape(shape)],
        [out_own, out_pair],
        [lse_own, lse_pair],
        need,
        seg_col,
        seg_row,
        heads,
    )
    grad_sides = [g.reshape(flat, g.shape[-1]) for g in grad_sides]
    w_kv = w_qkv[:, padded:]
    grad_query = weight_grad(
        [normed[0], normed[1]], [grad_sides[0], grad_sides[1]], me, shards, 0, padded
    )
    far = [jnp.pad(grad_sides[j], ((0, 0), (padded, 0))) for j in range(2, seq_count)]
    grad_kv = weight_grad(
        [normed[j] for j in range(seq_count)], grad_sides[:2] + far, me, shards, padded, 2 * padded
    )
    sum_query = scatter_sum(grad_query)
    sum_kv = scatter_sum(grad_kv)
    back = {
        j: dot(grad_sides[j], w_qkv if j < 2 else w_kv, NT) for j in reversed(range(seq_count))
    }
    for bit in reversed(bits_of(seq_count)):
        kept = {j: part for j, part in back.items() if not j & bit}
        if bit == bits_of(seq_count)[0]:
            last = swap(back[bit].astype(BF16), "seq", bit)
            back = kept
        else:
            back = {j: part + swap(back[j | bit].astype(BF16), "seq", bit) for j, part in kept.items()}
    grad_patches, _, grad_gain_one, grad_shift_one = norm_back(
        inputs, back[0], last, gain_one, grad_middle
    )

    def widen(vector, size):
        own = vector[None, :size]
        none = jnp.zeros_like(own)
        return jnp.where(
            is_first, jnp.concatenate([own, none], axis=1), jnp.concatenate([none, own], axis=1)
        )

    grad_bias_query = sum(column_sum(grad_sides[j][:, :padded]) for j in range(2))
    grad_bias_value = sum(column_sum(grad_sides[j][:, -padded:]) for j in range(seq_count))
    lines = [
        grad_gain_one,
        grad_shift_one,
        widen(grad_bias_query, half),
        widen(grad_bias_value, half),
        column_sum(branch)[None],
        grad_gain_two,
        grad_shift_two,
        column_sum(incoming)[None],
    ]
    bundle = jnp.concatenate(
        [jnp.concatenate(lines, axis=1), widen(grad_hidden_bias, ff_half)], axis=1
    )
    for axis in ("seq", "fsdp"):
        for bit in bits_of(lax.axis_size(axis)):
            bundle = bundle + swap(bundle, axis, bit)
    own_width = width // shards
    own_vectors = [
        lax.dynamic_slice_in_dim(bundle[0, i * width : (i + 1) * width], me * own_width, own_width, 0)
        for i in range(8)
    ]
    hidden_total = bundle[0, 8 * width : 8 * width + ff]

    def whole(mine, size, total):
        other = swap(mine, "seq", 1)
        return jnp.where(
            is_first,
            jnp.concatenate([mine[:, :size], other[:, : total - size]], axis=1),
            jnp.concatenate([other[:, :size], mine[:, : total - size]], axis=1),
        )

    full_query = whole(sum_query, half, width)
    full_key = whole(sum_kv[:, :padded], half, width)
    full_value = whole(sum_kv[:, padded:], half, width)
    full_hidden = whole(sum_hidden, ff_half, ff)
    full_down = whole(sum_down, ff_half, ff).T
    other_out = swap(sum_out, "seq", 1)
    full_out = jnp.where(
        is_first,
        jnp.concatenate([sum_out[:, :out_cut], other_out], axis=1),
        jnp.concatenate([other_out[:, :out_cut], sum_out], axis=1),
    )
    return (
        layer_output,
        grad_patches.reshape(rows, tokens, width),
        own_vectors[0],
        own_vectors[1],
        full_query,
        own_vectors[2],
        full_key,
        full_value,
        own_vectors[3],
        full_out,
        own_vectors[4],
        own_vectors[5],
        own_vectors[6],
        full_hidden,
        hidden_total,
        full_down,
        own_vectors[7],
    )


def solution(mesh):
    shard, line, tokens = P("fsdp", None), P("fsdp"), P("fsdp", "seq", None)
    in_specs = (
        tokens,
        shard,
        line,
        line,
        shard,
        line,
        shard,
        shard,
        line,
        shard,
        line,
        line,
        line,
        shard,
        P(),
        P(None, "fsdp"),
        line,
        tokens,
    )
    out_specs = (
        tokens,
        tokens,
        line,
        line,
        shard,
        line,
        shard,
        shard,
        line,
        shard,
        line,
        line,
        line,
        shard,
        P(),
        P(None, "fsdp"),
        line,
    )
    return jax.shard_map(local, mesh=mesh, in_specs=in_specs, out_specs=out_specs, check_vma=False)
```

time: 2430 us -> 966 us (0.40)
  waiting for transfers between devices: 1110 us -> 329 us
  Pallas kernels: 0 us -> 350 us
  local copies, waits for them, and re-layouts: 372 us -> 53.9 us
  matrix products: 405 us -> 114 us
  other arithmetic: 243 us -> 41.6 us
  blocking collectives: 182 us -> 0 us
    reduce_scatter x6 -> x0, waiting for transfers between devices: 781 us -> none  [the longest x1 334 us: local(): lax.psum_scatter(sums_list[4], 'fsdp', scatter_dimension=0, tiled=True)]
    pallas_call x0 -> x18, Pallas kernels: none -> 350 us  [the longest x2 100 us: attend(): pl.pallas_call(functools.partial(attend_kernel, which, heads, blocks, pad...]
    ppermute x0 -> x80, waiting for transfers between devices: none -> 329 us  [swap(): return lax.ppermute(array, axis, [(i, i ^ bit) for i in range(size)])]
    dot_general x90 -> x26, matrix products: 405 us -> 114 us  [dot(): lax.dot_general(left, right, (dims, ((), ())), preferred_element_type=F32)]
    all_gather x8 -> x0, waiting for transfers between devices: 228 us -> none  [the longest x1 128 us: local(): lax.all_gather(down_weight, 'fsdp', axis=1, tiled=True)]
    unnamed x657 -> x153, local copies, waits for them, and re-layouts: 184 us -> 10 us
    unnamed x30 -> x5, other arithmetic: 158 us -> 0.16 us
    unnamed x24 -> x0, waiting for transfers between devices: 92 us -> none
  transfers between devices with their start and end apart: 39 -> 80, of which waited for: 15 -> 30; matrix products, arithmetic and copies ran while one was open for 31% -> 19% of each run, Pallas kernels for 0% -> 35%
where the time goes in v1:
time: 966 us; the launch traced here: 959 us
  Pallas kernels  350 us (36%)
  waiting for transfers between devices  329 us (34%)
  matrix products  114 us (12%)
  starting transfers between devices  68 us (7%)
  local copies, waits for them, and re-layouts  53.9 us (6%)
  other arithmetic  41.6 us (4%)
    ppermute x80, waiting for transfers between devices, swap(): return lax.ppermute(array, axis, [(i, i ^ bit) for i in range(size)])  329 us
    dot_general x26, matrix products, dot(): lax.dot_general(left, right, (dims, ((), ())), preferred_element_type=F32)  114 us
    pallas_call x2, Pallas kernels, attend(): pl.pallas_call(functools.partial(attend_kernel, which, heads, blocks, pad...  100 us
    pallas_call x1, Pallas kernels, attend_back(): pl.pallas_call(functools.partial(attend_back_kernel, heads, blocks, padde...  92 us
    pallas_call x5, Pallas kernels, weight_grad(): pl.pallas_call(functools.partial(weight_grad_kernel, pairs, count, rows),...  75 us
    ppermute x80, starting transfers between devices, swap(): return lax.ppermute(array, axis, [(i, i ^ bit) for i in range(size)])  68 us
    pallas_call x4, Pallas kernels, assemble(): pl.pallas_call(functools.partial(assemble_kernel, count, rows), out_shape...  32.6 us
    pallas_call x2, Pallas kernels, hidden(): pl.pallas_call(hidden_kernel, out_shape=(jax.ShapeDtypeStruct((rows, cols...  24.7 us
  transfers between devices with their start and end apart: 80, of which 30 were waited for; matrix products, arithmetic and copies ran while one was open for 19% of the time, Pallas kernels for 35%

profile of v1, /device:TPU:0, one launch (start us, length us, event | category | flops | bytes accessed | tf_op | source)
XLA Modules:
  0.0 959.1 jit_solution(13865158765442182855)
XLA Ops:
  25.4 9.1 collective-permute-done.1
  54.6 12.0 %collective-permute-done.19.refs_2_ = bf16[144,640]{1,0:T(8,128)(2,1)} collective-permute-done((bf16[144,640]{1,0:T(8,128)(2,1)S(1)}, bf16[144,640]{1,0:T(8,128)(2,1)}, u32[]{:S(2)}, u32[]{:S(2)}) %collective-permute-start.19) | collective-permute-done | bytes 184352 | tf_op jit(solution)/shard_map/ppermute | solution.py:40
  102.2 11.8 %collective-permute-done.11.refs_5_ = bf16[144,1920]{1,0:T(8,128)(2,1)} collective-permute-done((bf16[144,1920]{1,0:T(8,128)(2,1)}, bf16[144,1920]{1,0:T(8,128)(2,1)}, u32[]{:S(2)}, u32[]{:S(2)}) %collective-permute-start.11) | collective-permute-done | bytes 552992 | tf_op jit(solution)/shard_map/ppermute | solution.py:40
  114.0 11.8 %collective-permute-done.9.refs_3_ = bf16[144,1920]{1,0:T(8,128)(2,1)} collective-permute-done((bf16[144,1920]{1,0:T(8,128)(2,1)}, bf16[144,1920]{1,0:T(8,128)(2,1)}, u32[]{:S(2)}, u32[]{:S(2)}) %collective-permute-start.9) | collective-permute-done | bytes 552992 | tf_op jit(solution)/shard_map/ppermute | solution.py:40
  192.6 56.6 %attend.3 = (bf16[3,256,640]{2,1,0:T(8,128)(2,1)}, f32[3,256,128]{2,1,0:T(8,128)}) custom-call(s32[3,2,4]{2,1,0:T(2,128)} %or_convert_fusion.need_ref, s32[3,4,256,1]{3,2,1,0:T(8,128)} %compare_select_fusion.col_ref, s32[3,4,256]{2,1,0:T(4,128)} %get-tuple-element.107.row_ref, bf16[3,256,1920]{2,1,0:T(8,128)(2,1)} %bitcast.182, ...), custom_call_target="tpu_custom_call" | custom-call | flops 6442450944 | bytes 11796480 | tf_op jit(solution)/shard_map/attend/pallas_call | solution.py:347
  255.9 11.6 %assemble.6.w_ref = bf16[1152,2176]{1,0:T(8,128)(2,1)} custom-call(s32[8]{0:T(128)} %fusion.51.off_ref, bf16[144,2176]{1,0:T(8,128)(2,1)} %copy-done.22, bf16[144,2176]{1,0:T(8,128)(2,1)} %collective-permute-done.26.refs_1_, bf16[144,2176]{1,0:T(8,128)(2,1)} %collective-permute-done.27.refs_2_, bf16[144,2176]{1,0:T(8,128)(2,1)} %copy-done.37, ...), custom_call_target="tpu_custom_call" | custom-call | bytes 10027008 | tf_op jit(solution)/shard_map/assemble/pallas_call | solution.py:89
  268.1 11.6 %assemble.7 = bf16[1152,2176]{1,0:T(8,128)(2,1)} custom-call(s32[8]{0:T(128)} %fusion.51.off_ref, bf16[144,2176]{1,0:T(8,128)(2,1)} %slice_select_fusion.refs_0_, bf16[144,2176]{1,0:T(8,128)(2,1)} %collective-permute-done.33.refs_1_, bf16[144,2176]{1,0:T(8,128)(2,1)} %copy-done.35, bf16[144,2176]{1,0:T(8,128)(2,1)} %collective-permute-done.35.refs_3_, ...), custom_call_target="tpu_custom_call" | custom-call | bytes 10027008 | tf_op jit(solution)/shard_map/assemble/pallas_call | solution.py:89
  279.7 43.5 %attend.2 = (bf16[3,256,640]{2,1,0:T(8,128)(2,1)}, f32[3,256,128]{2,1,0:T(8,128)}) custom-call(s32[3,2,4]{2,1,0:T(2,128)} %or_convert_fusion.need_ref, s32[3,4,256,1]{3,2,1,0:T(8,128)} %compare_select_fusion.col_ref, s32[3,4,256]{2,1,0:T(4,128)} %get-tuple-element.107.row_ref, bf16[3,256,1920]{2,1,0:T(8,128)(2,1)} %bitcast.183, ...), custom_call_target="tpu_custom_call" | custom-call | flops 6442450944 | bytes 11796480 | tf_op jit(solution)/shard_map/attend/pallas_call | solution.py:347
  338.8 13.2 %collective-permute-start.40 = (bf16[768,1152]{1,0:T(8,128)(2,1)}, bf16[768,1152]{1,0:T(8,128)(2,1)}, u32[]{:S(2)}, u32[]{:S(2)}) collective-permute-start(bf16[768,1152]{1,0:T(8,128)(2,1)} %norm.3.x_ref.refs_0_), channel_id=1, source_target_pairs={{0,8},{8,0},{16,24},{24,16},{1,9},{9,1},{17,25},{25,17},{2,10},{10... | collective-permute-start | bytes 5308424 | tf_op jit(solution)/shard_map/ppermute | solution.py:40
  352.0 12.1 %hidden.2 = (bf16[768,2176]{1,0:T(8,128)(2,1)}, bf16[768,2176]{1,0:T(8,128)(2,1)}) custom-call(bf16[768,1152]{1,0:T(8,128)(2,1)} %norm.3.x_ref.refs_0_, bf16[1152,2176]{1,0:T(8,128)(2,1)} %assemble.6.w_ref, f32[1,2176]{1,0:T(1,128)} %broadcast_select_fusion.4.b_ref), custom_call_target="tpu_custom_call" | custom-call | flops 3850371072 | bytes 13467648 | tf_op jit(solution)/shard_map/hidden/pallas_call | solution.py:267
  371.9 10.2 %fusion.70.own_ref = f32[768,1152]{1,0:T(8,128)} fusion(bf16[768,2176]{1,0:T(8,128)(2,1)S(1)} %fusion.1.refs_2_, bf16[1152,2176]{1,0:T(8,128)(2,1)} %assemble.6.w_ref), kind=kOutput, calls=%fused_computation.193 | convolution fusion | flops 3850371072 | bytes 11894784 | tf_op jit(solution)/shard_map/dot_general | solution.py:27
  382.7 12.5 %hidden.3 = (bf16[768,2176]{1,0:T(8,128)(2,1)}, bf16[768,2176]{1,0:T(8,128)(2,1)}) custom-call(bf16[768,1152]{1,0:T(8,128)(2,1)} %collective-permute-done.40.x_ref.refs_1_, bf16[1152,2176]{1,0:T(8,128)(2,1)} %assemble.6.w_ref, f32[1,2176]{1,0:T(1,128)} %broadcast_select_fusion.4.b_ref), custom_call_target="tpu_custom_call" | custom-call | flops 3850371072 | bytes 13467648 | tf_op jit(solution)/shard_map/hidden/pallas_call | solution.py:267
  395.2 9.4 convolution_convert_fusion.4
  404.6 15.5 %weight_grad.9 = bf16[1152,2176]{1,0:T(8,128)(2,1)} custom-call(s32[8]{0:T(128)} %broadcast_multiply_fusion.pos_ref, bf16[768,1152]{1,0:T(8,128)(2,1)} %bitcast.142, bf16[768,1152]{1,0:T(8,128)(2,1)} %collective-permute-done.42.refs_1_, bf16[768,2176]{1,0:T(8,128)(2,1)} %get-tuple-element.53.refs_2_, bf16[768,2176]{1,0:T(8,128)(2,1)} %get-tuple-element.57.refs_3_), custom_call_target="tpu_custom_call" | custom-call | flops 7700742144 | bytes 15237120 | tf_op jit(solution)/shard_map/weight_grad/pallas_call | solution.py:141
  439.8 15.6 %weight_grad.8 = bf16[1152,2176]{1,0:T(8,128)(2,1)} custom-call(s32[8]{0:T(128)} %broadcast_multiply_fusion.pos_ref, bf16[768,1152]{1,0:T(8,128)(2,1)} %norm.3.x_ref.refs_0_, bf16[768,1152]{1,0:T(8,128)(2,1)} %collective-permute-done.40.x_ref.refs_1_, bf16[768,2176]{1,0:T(8,128)(2,1)} %copy-done.18, bf16[768,2176]{1,0:T(8,128)(2,1)} %copy-done.19), custom_call_target="tpu_custom_call" | custom-call | flops 7700742144 | bytes 15237120 | tf_op jit(solution)/shard_map/weight_grad/pallas_call | solution.py:141
  502.8 33.2 %collective-permute-done.70 = bf16[4,144,2176]{2,1,0:T(8,128)(2,1)} collective-permute-done((bf16[4,144,2176]{2,1,0:T(8,128)(2,1)}, bf16[4,144,2176]{2,1,0:T(8,128)(2,1)}, u32[]{:S(2)}, u32[]{:S(2)}) %collective-permute-start.70) | collective-permute-done | bytes 2506784 | tf_op jit(solution)/shard_map/ppermute | solution.py:40
  541.9 92.0 %attend_back.1 = (bf16[3,256,1920]{2,1,0:T(8,128)(2,1)}, bf16[3,256,1920]{2,1,0:T(8,128)(2,1)}, bf16[3,256,1280]{2,1,0:T(8,128)(2,1)}, bf16[3,256,1280]{2,1,0:T(8,128)(2,1)}) custom-call(s32[3,2,4]{2,1,0:T(2,128)} %or_convert_fusion.need_ref, s32[3,4,256,1]{3,2,1,0:T(8,128)} %compare_select_fusion.col_ref, s32[3,4,256]{2,1,0:T(4,128)} %get-tuple-element.107.row_ref, ...), custom_call_target="tpu_custom_call" | custom-call | flops 32212254720 | bytes 23592960 | tf_op jit(solution)/shard_map/attend_back/pallas_call | solution.py:438
  648.2 27.5 %weight_grad.6 = bf16[1152,1280]{1,0:T(8,128)(2,1)} custom-call(s32[8]{0:T(128)} %broadcast_multiply_fusion.pos_ref, bf16[768,1152]{1,0:T(8,128)(2,1)} %norm.2.refs_0_, bf16[768,1152]{1,0:T(8,128)(2,1)} %copy-done.27, bf16[768,1152]{1,0:T(8,128)(2,1)} %collective-permute-done.15.refs_2_, bf16[768,1152]{1,0:T(8,128)(2,1)} %copy-done.52, ...), custom_call_target="tpu_custom_call" | custom-call | flops 9059696640 | bytes 17891328 | tf_op jit(solution)/shard_map/weight_grad/pallas_call | solution.py:141
  700.2 28.1 %collective-permute-done.53 = bf16[4,144,640]{2,1,0:T(8,128)(2,1)S(1)} collective-permute-done((bf16[4,144,640]{2,1,0:T(8,128)(2,1)S(1)}, bf16[4,144,640]{2,1,0:T(8,128)(2,1)S(1)}, u32[]{:S(2)}, u32[]{:S(2)}) %collective-permute-start.53) | collective-permute-done | bytes 737312 | tf_op jit(solution)/shard_map/ppermute | solution.py:40
  732.5 8.9 collective-permute-done.54
  747.8 31.3 %collective-permute-done.55 = bf16[1,144,640]{2,1,0:T(8,128)(2,1)S(1)} collective-permute-done((bf16[1,144,640]{2,1,0:T(8,128)(2,1)S(1)}, bf16[1,144,640]{2,1,0:T(8,128)(2,1)S(1)}, u32[]{:S(2)}, u32[]{:S(2)}) %collective-permute-start.55) | collective-permute-done | bytes 184352 | tf_op jit(solution)/shard_map/ppermute | solution.py:40
  790.9 24.4 %collective-permute-done.72 = bf16[1,144,2176]{2,1,0:T(8,128)(2,1)S(1)} collective-permute-done((bf16[1,144,2176]{2,1,0:T(8,128)(2,1)S(1)}, bf16[1,144,2176]{2,1,0:T(8,128)(2,1)S(1)}, u32[]{:S(2)}, u32[]{:S(2)}) %collective-permute-start.72) | collective-permute-done | bytes 626720 | tf_op jit(solution)/shard_map/ppermute | solution.py:40
  829.7 56.2 %collective-permute-done.68 = bf16[144,640]{1,0:T(8,128)(2,1)S(1)} collective-permute-done((bf16[144,640]{1,0:T(8,128)(2,1)S(1)}, bf16[144,640]{1,0:T(8,128)(2,1)S(1)}, u32[]{:S(2)}, u32[]{:S(2)}) %collective-permute-start.68) | collective-permute-done | bytes 184352 | tf_op jit(solution)/shard_map/ppermute | solution.py:40
  889.6 16.7 %collective-permute-done.60 = bf16[1,144,1280]{2,1,0:T(8,128)(2,1)S(1)} collective-permute-done((bf16[1,144,1280]{2,1,0:T(8,128)(2,1)S(1)}, bf16[1,144,1280]{2,1,0:T(8,128)(2,1)S(1)}, u32[]{:S(2)}, u32[]{:S(2)}) %collective-permute-start.60) | collective-permute-done | bytes 368672 | tf_op jit(solution)/shard_map/ppermute | solution.py:40
  (470 shorter events, 381.9 us)
Async XLA Ops:
  79.3 68.3 %collective-permute-start.15 = (bf16[768,1152]{1,0:T(8,128)(2,1)}, bf16[768,1152]{1,0:T(8,128)(2,1)}, u32[]{:S(2)}, u32[]{:S(2)}) collective-permute-start(bf16[768,1152]{1,0:T(8,128)(2,1)} %norm.2.refs_0_), channel_id=1, source_target_pairs={{0,16},{8,24},{16,0},{24,8},{1,17},{9,25},{17,1},{25,9},{2,18},{10... | collective-permute-start | bytes 5308424 | tf_op jit(solution)/shard_map/ppermute | solution.py:40
  102.2 52.5 %collective-permute-start.14 = (bf16[768,1152]{1,0:T(8,128)(2,1)S(1)}, bf16[768,1152]{1,0:T(8,128)(2,1)S(1)}, u32[]{:S(2)}, u32[]{:S(2)}) collective-permute-start(bf16[768,1152]{1,0:T(8,128)(2,1)S(1)} %copy-done.12), channel_id=1, source_target_pairs={{0,8},{8,0},{16,24},{24,16},{1,9},{9,1},{17,25},{25,17},{2,10},{10... | collective-permute-start | bytes 5308424 | tf_op jit(solution)/shard_map/ppermute | solution.py:40
  114.0 76.5 %collective-permute-start.25 = (bf16[1152,640]{1,0:T(8,128)(2,1)}, bf16[1152,640]{1,0:T(8,128)(2,1)}, u32[]{:S(2)}, u32[]{:S(2)}) collective-permute-start(bf16[1152,640]{1,0:T(8,128)(2,1)} %assemble.5), channel_id=1, source_target_pairs={{0,8},{8,0},{16,24},{24,16},{1,9},{9,1},{17,25},{25,17},{2,10},{10... | collective-permute-start | bytes 4423688 | tf_op jit(solution)/shard_map/ppermute | solution.py:40
  171.5 77.7 %collective-permute-start.32 = (bf16[144,2176]{1,0:T(8,128)(2,1)}, bf16[144,2176]{1,0:T(8,128)(2,1)S(1)}, u32[]{:S(2)}, u32[]{:S(2)}) collective-permute-start(bf16[144,2176]{1,0:T(8,128)(2,1)} %collective-permute-done.31.refs_6_), channel_id=1, source_target_pairs={{0,1},{1,0},{2,3},{3,2},{4,5},{5,4},{6,7},{7,6},{8,9},{9,8},{10,11... | collective-permute-start | bytes 1880072 | tf_op jit(solution)/shard_map/ppermute | solution.py:40
  188.5 79.0 %collective-permute-start.33 = (bf16[144,2176]{1,0:T(8,128)(2,1)}, bf16[144,2176]{1,0:T(8,128)(2,1)}, u32[]{:S(2)}, u32[]{:S(2)}) collective-permute-start(bf16[144,2176]{1,0:T(8,128)(2,1)} %slice_select_fusion.refs_0_), channel_id=1, source_target_pairs={{0,1},{1,0},{2,3},{3,2},{4,5},{5,4},{6,7},{7,6},{8,9},{9,8},{10,11... | collective-permute-start | bytes 1880072 | tf_op jit(solution)/shard_map/ppermute | solution.py:40
  188.8 79.3 %collective-permute-start.37 = (bf16[144,2176]{1,0:T(8,128)(2,1)}, bf16[144,2176]{1,0:T(8,128)(2,1)}, u32[]{:S(2)}, u32[]{:S(2)}) collective-permute-start(bf16[144,2176]{1,0:T(8,128)(2,1)} %collective-permute-done.36.refs_4_), channel_id=1, source_target_pairs={{0,1},{1,0},{2,3},{3,2},{4,5},{5,4},{6,7},{7,6},{8,9},{9,8},{10,11... | collective-permute-start | bytes 1880072 | tf_op jit(solution)/shard_map/ppermute | solution.py:40
  190.5 77.6 %collective-permute-start.35 = (bf16[144,2176]{1,0:T(8,128)(2,1)S(1)}, bf16[144,2176]{1,0:T(8,128)(2,1)}, u32[]{:S(2)}, u32[]{:S(2)}) collective-permute-start(bf16[144,2176]{1,0:T(8,128)(2,1)S(1)} %collective-permute-done.34.refs_2_), channel_id=1, source_target_pairs={{0,1},{1,0},{2,3},{3,2},{4,5},{5,4},{6,7},{7,6},{8,9},{9,8},{10,11... | collective-permute-start | bytes 1880072 | tf_op jit(solution)/shard_map/ppermute | solution.py:40
  190.8 77.3 %collective-permute-start.39 = (bf16[144,2176]{1,0:T(8,128)(2,1)}, bf16[144,2176]{1,0:T(8,128)(2,1)}, u32[]{:S(2)}, u32[]{:S(2)}) collective-permute-start(bf16[144,2176]{1,0:T(8,128)(2,1)} %collective-permute-done.38.refs_6_), channel_id=1, source_target_pairs={{0,1},{1,0},{2,3},{3,2},{4,5},{5,4},{6,7},{7,6},{8,9},{9,8},{10,11... | collective-permute-start | bytes 1880072 | tf_op jit(solution)/shard_map/ppermute | solution.py:40
  250.0 73.2 %collective-permute-start.17 = (bf16[3,256,640]{2,1,0:T(8,128)(2,1)}, bf16[3,256,640]{2,1,0:T(8,128)(2,1)}, u32[]{:S(2)}, u32[]{:S(2)}) collective-permute-start(bf16[3,256,640]{2,1,0:T(8,128)(2,1)} %get-tuple-element.46.refs_7_), channel_id=1, source_target_pairs={{0,8},{8,0},{16,24},{24,16},{1,9},{9,1},{17,25},{25,17},{2,10},{10... | collective-permute-start | bytes 2949128 | tf_op jit(solution)/shard_map/ppermute | solution.py:40
  267.5 137.1 %collective-permute-start.42 = (bf16[768,1152]{1,0:T(8,128)(2,1)S(1)}, bf16[768,1152]{1,0:T(8,128)(2,1)}, u32[]{:S(2)}, u32[]{:S(2)}) collective-permute-start(bf16[768,1152]{1,0:T(8,128)(2,1)S(1)} %bitcast.145), channel_id=1, source_target_pairs={{0,8},{8,0},{16,24},{24,16},{1,9},{9,1},{17,25},{25,17},{2,10},{10... | collective-permute-start | bytes 5308424 | tf_op jit(solution)/shard_map/ppermute | solution.py:40
  425.6 73.8 %collective-permute-start.75 = (bf16[4,144,2176]{2,1,0:T(8,128)(2,1)}, bf16[4,144,2176]{2,1,0:T(8,128)(2,1)}, u32[]{:S(2)}, u32[]{:S(2)}) collective-permute-start(bf16[4,144,2176]{2,1,0:T(8,128)(2,1)} %bitcast.49), channel_id=1, source_target_pairs={{0,1},{1,0},{2,3},{3,2},{4,5},{5,4},{6,7},{7,6},{8,9},{9,8},{10,11... | collective-permute-start | bytes 7520264 | tf_op jit(solution)/shard_map/ppermute | solution.py:40
  460.7 75.3 %collective-permute-start.70 = (bf16[4,144,2176]{2,1,0:T(8,128)(2,1)}, bf16[4,144,2176]{2,1,0:T(8,128)(2,1)}, u32[]{:S(2)}, u32[]{:S(2)}) collective-permute-start(bf16[4,144,2176]{2,1,0:T(8,128)(2,1)} %bitcast.46), channel_id=1, source_target_pairs={{0,1},{1,0},{2,3},{3,2},{4,5},{5,4},{6,7},{7,6},{8,9},{9,8},{10,11... | collective-permute-start | bytes 7520264 | tf_op jit(solution)/shard_map/ppermute | solution.py:40
  484.1 214.0 %collective-permute-start.64 = (bf16[8,144,640]{2,1,0:T(8,128)(2,1)}, bf16[8,144,640]{2,1,0:T(8,128)(2,1)}, u32[]{:S(2)}, u32[]{:S(2)}) collective-permute-start(bf16[8,144,640]{2,1,0:T(8,128)(2,1)} %broadcast_select_fusion), channel_id=1, source_target_pairs={{0,8},{8,0},{16,24},{24,16},{1,9},{9,1},{17,25},{25,17},{2,10},{10... | collective-permute-start | bytes 4423688 | tf_op jit(solution)/shard_map/ppermute | solution.py:40
  502.8 225.7 %collective-permute-start.76 = (bf16[2,144,2176]{2,1,0:T(8,128)(2,1)}, bf16[2,144,2176]{2,1,0:T(8,128)(2,1)}, u32[]{:S(2)}, u32[]{:S(2)}) collective-permute-start(bf16[2,144,2176]{2,1,0:T(8,128)(2,1)} %slice.593), channel_id=1, source_target_pairs={{0,2},{1,3},{2,0},{3,1},{4,6},{5,7},{6,4},{7,5},{8,10},{9,11},{10,... | collective-permute-start | bytes 3760136 | tf_op jit(solution)/shard_map/ppermute | solution.py:40
  540.9 189.8 %collective-permute-start.71 = (bf16[2,144,2176]{2,1,0:T(8,128)(2,1)}, bf16[2,144,2176]{2,1,0:T(8,128)(2,1)}, u32[]{:S(2)}, u32[]{:S(2)}) collective-permute-start(bf16[2,144,2176]{2,1,0:T(8,128)(2,1)} %slice.584), channel_id=1, source_target_pairs={{0,2},{1,3},{2,0},{3,1},{4,6},{5,7},{6,4},{7,5},{8,10},{9,11},{10,... | collective-permute-start | bytes 3760136 | tf_op jit(solution)/shard_map/ppermute | solution.py:40
  678.9 100.2 %collective-permute-start.58 = (bf16[4,144,1280]{2,1,0:T(8,128)(2,1)}, bf16[4,144,1280]{2,1,0:T(8,128)(2,1)}, u32[]{:S(2)}, u32[]{:S(2)}) collective-permute-start(bf16[4,144,1280]{2,1,0:T(8,128)(2,1)} %bitcast.37), channel_id=1, source_target_pairs={{0,1},{1,0},{2,3},{3,2},{4,5},{5,4},{6,7},{7,6},{8,9},{9,8},{10,11... | collective-permute-start | bytes 4423688 | tf_op jit(solution)/shard_map/ppermute | solution.py:40
  698.1 124.0 %collective-permute-start.46 = (bf16[768,1152]{1,0:T(8,128)(2,1)S(1)}, bf16[768,1152]{1,0:T(8,128)(2,1)S(1)}, u32[]{:S(2)}, u32[]{:S(2)}) collective-permute-start(bf16[768,1152]{1,0:T(8,128)(2,1)S(1)} %copy-done.53), channel_id=1, source_target_pairs={{0,8},{8,0},{16,24},{24,16},{1,9},{9,1},{17,25},{25,17},{2,10},{10... | collective-permute-start | bytes 5308424 | tf_op jit(solution)/shard_map/ppermute | solution.py:40
  728.3 87.1 %collective-permute-start.45 = (bf16[768,1152]{1,0:T(8,128)(2,1)S(1)}, bf16[768,1152]{1,0:T(8,128)(2,1)S(1)}, u32[]{:S(2)}, u32[]{:S(2)}) collective-permute-start(bf16[768,1152]{1,0:T(8,128)(2,1)S(1)} %convolution_convert_fusion.1), channel_id=1, source_target_pairs={{0,8},{8,0},{16,24},{24,16},{1,9},{9,1},{17,25},{25,17},{2,10},{10... | collective-permute-start | bytes 5308424 | tf_op jit(solution)/shard_map/ppermute | solution.py:40
  790.5 95.6 %collective-permute-start.59 = (bf16[2,144,1280]{2,1,0:T(8,128)(2,1)S(1)}, bf16[2,144,1280]{2,1,0:T(8,128)(2,1)S(1)}, u32[]{:S(2)}, u32[]{:S(2)}) collective-permute-start(bf16[2,144,1280]{2,1,0:T(8,128)(2,1)S(1)} %slice.558), channel_id=1, source_target_pairs={{0,2},{1,3},{2,0},{3,1},{4,6},{5,7},{6,4},{7,5},{8,10},{9,11},{10,... | collective-permute-start | bytes 2211848 | tf_op jit(solution)/shard_map/ppermute | solution.py:40
  815.4 73.7 %collective-permute-start.78 = (bf16[144,2176]{1,0:T(8,128)(2,1)S(1)}, bf16[144,2176]{1,0:T(8,128)(2,1)S(1)}, u32[]{:S(2)}, u32[]{:S(2)}) collective-permute-start(bf16[144,2176]{1,0:T(8,128)(2,1)S(1)} %fusion.27), channel_id=1, source_target_pairs={{0,16},{8,24},{16,0},{24,8},{1,17},{9,25},{17,1},{25,9},{2,18},{10... | collective-permute-start | bytes 1880072 | tf_op jit(solution)/shard_map/ppermute | solution.py:40
  822.2 84.9 %collective-permute-start.73 = (bf16[144,2176]{1,0:T(8,128)(2,1)S(1)}, bf16[144,2176]{1,0:T(8,128)(2,1)S(1)}, u32[]{:S(2)}, u32[]{:S(2)}) collective-permute-start(bf16[144,2176]{1,0:T(8,128)(2,1)S(1)} %fusion.26), channel_id=1, source_target_pairs={{0,16},{8,24},{16,0},{24,8},{1,17},{9,25},{17,1},{25,9},{2,18},{10... | collective-permute-start | bytes 1880072 | tf_op jit(solution)/shard_map/ppermute | solution.py:40
  826.4 91.7 %collective-permute-start.47 = (bf16[768,1152]{1,0:T(8,128)(2,1)S(1)}, bf16[768,1152]{1,0:T(8,128)(2,1)}, u32[]{:S(2)}, u32[]{:S(2)}) collective-permute-start(bf16[768,1152]{1,0:T(8,128)(2,1)S(1)} %fusion.8), channel_id=1, source_target_pairs={{0,16},{8,24},{16,0},{24,8},{1,17},{9,25},{17,1},{25,9},{2,18},{10... | collective-permute-start | bytes 5308424 | tf_op jit(solution)/shard_map/ppermute | solution.py:40
  827.1 58.7 %collective-permute-start.68 = (bf16[144,640]{1,0:T(8,128)(2,1)S(1)}, bf16[144,640]{1,0:T(8,128)(2,1)S(1)}, u32[]{:S(2)}, u32[]{:S(2)}) collective-permute-start(bf16[144,640]{1,0:T(8,128)(2,1)S(1)} %fusion.31), channel_id=1, source_target_pairs={{0,16},{8,24},{16,0},{24,8},{1,17},{9,25},{17,1},{25,9},{2,18},{10... | collective-permute-start | bytes 552968 | tf_op jit(solution)/shard_map/ppermute | solution.py:40
  889.3 54.5 %collective-permute-start.79 = (f32[144,2176]{1,0:T(8,128)S(1)}, f32[144,2176]{1,0:T(8,128)}, u32[]{:S(2)}, u32[]{:S(2)}) collective-permute-start(f32[144,2176]{1,0:T(8,128)S(1)} %convert_add_fusion.4), channel_id=1, source_target_pairs={{0,8},{8,0},{16,24},{24,16},{1,9},{9,1},{17,25},{25,17},{2,10},{10... | collective-permute-start | bytes 3760136 | tf_op jit(solution)/shard_map/ppermute | solution.py:40
  (128 other events, 2407.0 us)

commit v2 on v1

v2 whole, which is shorter than its diff:
```python
import functools
import math

import jax
import jax.numpy as jnp
from jax import lax
from jax.experimental import pallas as pl
from jax.experimental.pallas import tpu as pltpu
from jax.sharding import PartitionSpec as P

HEAD_DIM = 72
EPS = 1e-06
GELU_COEF = math.sqrt(2.0 / math.pi)
MASKED = -1e30
F32 = jnp.float32
BF16 = jnp.bfloat16
SCALE = 1.0 / math.sqrt(HEAD_DIM)
WIN = 256
LOG2E = math.log2(math.e)
VMEM = 60 << 20


def round_up(value, step):
    return (value + step - 1) // step * step


def dot(left, right, dims=((1,), (0,))):
    return lax.dot_general(left, right, (dims, ((), ())), preferred_element_type=F32)


NT = ((1,), (1,))
TN = ((0,), (0,))


def params(semantics):
    return pltpu.CompilerParams(dimension_semantics=semantics, vmem_limit_bytes=VMEM)


def swap(array, axis, bits):
    size = lax.axis_size(axis)
    return lax.ppermute(array, axis, [(i, i ^ bits) for i in range(size)])


def bits_of(size):
    return [1 << k for k in reversed(range(size.bit_length() - 1))]


def after(value, *earlier):
    return lax.optimization_barrier((value,) + tuple(earlier))[0]


class Chain:
    def __init__(self):
        self.last = ()

    def __call__(self, *values, wait=()):
        held = lax.optimization_barrier(tuple(values) + tuple(self.last) + tuple(wait))
        return held[: len(values)] if len(values) > 1 else held[0]

    def done(self, *results):
        self.last = results
        return results if len(results) > 1 else results[0]


def gather_all(shard):
    parts = {0: shard}
    for bit in bits_of(lax.axis_size("fsdp")):
        parts.update({d | bit: swap(part, "fsdp", bit) for d, part in list(parts.items())})
    return parts


def gather_direct(shard):
    return {0: shard} | {d: swap(shard, "fsdp", d) for d in range(1, lax.axis_size("fsdp"))}


def in_order(parts, me):
    count = len(parts)
    return jnp.take(jnp.stack([parts[d] for d in range(count)]), me ^ jnp.arange(count), axis=0)


def rel_position(distance, count):
    width = count.bit_length() - 1
    return sum(((distance >> k) & 1) << (width - 1 - k) for k in range(width))


def scatter_step(keep, arrived, rows):
    size = keep.shape[0]
    if size == rows:
        return (keep.astype(F32) + arrived.astype(F32)).astype(BF16), None
    return [
        (keep[part].astype(F32) + arrived[part].astype(F32)).astype(BF16)
        for part in (slice(0, size // 2), slice(size // 2, size))
    ]


def seq_sum(mine):
    for bit in bits_of(lax.axis_size("seq"))[:-1]:
        total = mine.astype(F32) + swap(mine, "seq", bit).astype(F32)
        mine = total.astype(BF16)
    return total


def assemble_kernel(count, rows, single, off_ref, *refs):
    outs = refs[count:]

    def fill(out_ref):
        for distance in range(count):
            start = pl.multiple_of(off_ref[distance], 16)
            out_ref[pl.ds(start, rows), :] = refs[distance][...]

    if single:
        fill(outs[0])
    else:
        pl.when(pl.program_id(0) == 0)(lambda: fill(outs[0]))
        pl.when(pl.program_id(0) > 0)(lambda: fill(outs[1]))


def assemble(parts, me, cut=None):
    count = len(parts)
    rows, cols = parts[0].shape
    if rows % 16:
        full = in_order(parts, me).reshape(count * rows, cols)
        return (full[:, :cut], full[:, cut:]) if cut else full
    offsets = ((me ^ jnp.arange(count, dtype=jnp.int32)) * rows).astype(jnp.int32)
    tile = cut or min(cols, 1152)
    widths = [cut, cols - cut] if cut else [cols]
    maps = [lambda n, off: (0, 0), lambda n, off: (0, jnp.maximum(n - 1, 0))]
    if not cut:
        maps = [lambda n, off: (0, n)]
    outs = pl.pallas_call(
        functools.partial(assemble_kernel, count, rows, not cut),
        out_shape=[jax.ShapeDtypeStruct((count * rows, w), parts[0].dtype) for w in widths],
        grid_spec=pltpu.PrefetchScalarGridSpec(
            num_scalar_prefetch=1,
            grid=(pl.cdiv(cols, tile),),
            in_specs=[pl.BlockSpec((rows, tile), lambda n, off: (0, n))] * count,
            out_specs=[pl.BlockSpec((count * rows, tile), m) for m in maps],
        ),
        compiler_params=params(("arbitrary",)),
        cost_estimate=pl.CostEstimate(
            flops=0, transcendentals=0, bytes_accessed=4 * count * rows * cols
        ),
        name="assemble",
    )(offsets, *[parts[d] for d in range(count)])
    return outs if cut else outs[0]


def weight_grad_kernel(pairs, count, rows, pos_ref, *refs):
    lefts, rights = refs[:pairs], refs[pairs : 2 * pairs]
    keep_ref, send_ref = refs[2 * pairs : 2 * pairs + 2]
    total = dot(lefts[0][...], rights[0][...], TN)
    for i in range(1, pairs):
        total += dot(lefts[i][...], rights[i][...], TN)
    for shard in range(count):
        start = pl.multiple_of(pos_ref[shard], 16)
        block = total[shard * rows : (shard + 1) * rows].astype(BF16)

        @pl.when(pos_ref[count] == shard % 2)
        def _():
            keep_ref[pl.ds(start, rows), :] = block

        @pl.when(pos_ref[count] != shard % 2)
        def _():
            send_ref[pl.ds(start, rows), :] = block


def weight_grad(lefts, rights, me, count):
    width = lefts[0].shape[1]
    cols = rights[0].shape[1]
    rows = width // count
    order = me ^ jnp.arange(count, dtype=jnp.int32)
    table = jnp.array([rel_position(d, count) for d in range(count)], jnp.int32)
    half = count // 2
    if rows % 16:
        total = sum(dot(a, b, TN) for a, b in zip(lefts, rights))
        by_distance = jnp.take(total.astype(BF16).reshape(count, rows, cols), order, axis=0)
        back = [0] * count
        for d in range(count):
            back[rel_position(d, count)] = d
        placed = jnp.take(by_distance, jnp.array(back), axis=0).reshape(width, cols)
        return placed[: width // 2], placed[width // 2 :]
    positions = jnp.concatenate([table[order] % half * rows, (me & 1)[None]]).astype(jnp.int32)
    tile = 256
    pairs = len(lefts)
    flops = sum(2 * a.shape[0] * width * cols for a in lefts)
    moved = sum(2 * a.shape[0] * (width + cols) for a in lefts) + 2 * width * cols
    return pl.pallas_call(
        functools.partial(weight_grad_kernel, pairs, count, rows),
        out_shape=[jax.ShapeDtypeStruct((width // 2, cols), BF16)] * 2,
        grid_spec=pltpu.PrefetchScalarGridSpec(
            num_scalar_prefetch=1,
            grid=(pl.cdiv(cols, tile),),
            in_specs=[
                pl.BlockSpec(a.shape, lambda n, off: (0, 0), pipeline_mode=pl.Buffered(1))
                for a in lefts
            ]
            + [pl.BlockSpec((b.shape[0], tile), lambda n, off: (0, n)) for b in rights],
            out_specs=[pl.BlockSpec((width // 2, tile), lambda n, off: (0, n))] * 2,
        ),
        compiler_params=params(("arbitrary",)),
        cost_estimate=pl.CostEstimate(flops=flops, transcendentals=0, bytes_accessed=moved),
        name="weight_grad",
    )(positions, *lefts, *rights)


def normalized(values):
    center = values - jnp.mean(values, axis=-1, keepdims=True)
    spread = jnp.mean(center * center, axis=-1, keepdims=True)
    inverse = lax.rsqrt(spread + EPS)
    return center * inverse, inverse


def row_block(rows):
    return 256 if rows % 256 == 0 else 128 if rows % 128 == 0 else rows


def norm_kernel(steps, x_refs, gain_ref, shift_ref, out_ref):
    for i, x_ref in enumerate(x_refs):

        @pl.when(pl.program_id(0) // steps == i)
        def _():
            hat, _ = normalized(x_ref[...].astype(F32))
            out_ref[...] = (hat * gain_ref[...] + shift_ref[...]).astype(BF16)


def norm(arrays, gain, shift):
    rows, width = arrays[0].shape
    block = row_block(rows)
    steps, count = rows // block, len(arrays)

    def kernel(*refs):
        norm_kernel(steps, refs[:count], *refs[count:])

    line = pl.BlockSpec((1, width), lambda i: (0, 0))
    return pl.pallas_call(
        kernel,
        out_shape=jax.ShapeDtypeStruct((count * rows, width), BF16),
        grid=(count * steps,),
        in_specs=[
            pl.BlockSpec((block, width), lambda i, k=k: (jnp.clip(i - k * steps, 0, steps - 1), 0))
            for k in range(count)
        ]
        + [line, line],
        out_specs=pl.BlockSpec((block, width), lambda i: (i, 0)),
        compiler_params=params(("arbitrary",)),
        cost_estimate=pl.CostEstimate(
            flops=10 * count * rows * width, transcendentals=0, bytes_accessed=4 * count * rows * width
        ),
        name="norm",
    )(*arrays, gain, shift)


def join_kernel(half, core_ref, own_ref, other_ref, x_ref, w_ref, b_ref, g_ref, s_ref, *outs):
    att_ref, mid_ref, out_ref = outs
    own, other = own_ref[:, :half], other_ref[:, :half]

    @pl.when(core_ref[0] == 0)
    def _():
        att_ref[...] = jnp.concatenate([own, other], axis=1)

    @pl.when(core_ref[0] != 0)
    def _():
        att_ref[...] = jnp.concatenate([other, own], axis=1)

    middle = x_ref[...].astype(F32) + dot(att_ref[...], w_ref[...]) + b_ref[...]
    mid_ref[...] = middle
    hat, _ = normalized(middle)
    out_ref[...] = (hat * g_ref[...] + s_ref[...]).astype(BF16)


def join(core, own, other, inputs, weight, bias, gain, shift, half):
    rows, width = inputs.shape
    padded = own.shape[1]
    block = row_block(rows)
    line = pl.BlockSpec((1, width), lambda i, c: (0, 0))
    wide = pl.BlockSpec((block, width), lambda i, c: (i, 0))
    part = pl.BlockSpec((block, padded), lambda i, c: (i, 0))
    return pl.pallas_call(
        functools.partial(join_kernel, half),
        out_shape=(
            jax.ShapeDtypeStruct((rows, width), BF16),
            jax.ShapeDtypeStruct((rows, width), F32),
            jax.ShapeDtypeStruct((rows, width), BF16),
        ),
        grid_spec=pltpu.PrefetchScalarGridSpec(
            num_scalar_prefetch=1,
            grid=(rows // block,),
            in_specs=[
                part,
                part,
                wide,
                pl.BlockSpec((width, width), lambda i, c: (0, 0), pipeline_mode=pl.Buffered(1)),
                line,
                line,
                line,
            ],
            out_specs=(wide, wide, wide),
        ),
        compiler_params=params(("arbitrary",)),
        cost_estimate=pl.CostEstimate(
            flops=2 * rows * width * width, transcendentals=0, bytes_accessed=14 * rows * width
        ),
        name="join",
    )(core, own, other, inputs, weight, bias, gain, shift)


def norm_back_values(x_ref, grads, gain_ref, add_ref, dg_ref, ds_ref):
    hat, inverse = normalized(x_ref[...].astype(F32))
    grad = grads[0][...].astype(F32)
    for other in grads[1:]:
        grad += other[...].astype(F32)
    scaled = grad * gain_ref[...]
    first = jnp.mean(scaled, axis=-1, keepdims=True)
    second = jnp.mean(scaled * hat, axis=-1, keepdims=True)

    @pl.when(pl.program_id(0) == 0)
    def _():
        dg_ref[...] = jnp.zeros_like(dg_ref)
        ds_ref[...] = jnp.zeros_like(ds_ref)

    dg_ref[...] += jnp.sum(grad * hat, axis=0, keepdims=True)
    ds_ref[...] += jnp.sum(grad, axis=0, keepdims=True)
    return add_ref[...].astype(F32) + inverse * (scaled - first - hat * second)


def first_back(values, grads, gain, add):
    rows, width = values.shape
    block = row_block(rows)
    count = len(grads)

    def kernel(x_ref, *refs):
        gain_ref, add_ref, dx_ref, dg_ref, ds_ref = refs[count:]
        dx_ref[...] = norm_back_values(x_ref, refs[:count], gain_ref, add_ref, dg_ref, ds_ref)

    wide = pl.BlockSpec((block, width), lambda i: (i, 0))
    line = pl.BlockSpec((1, width), lambda i: (0, 0))
    return pl.pallas_call(
        kernel,
        out_shape=(
            jax.ShapeDtypeStruct((rows, width), F32),
            jax.ShapeDtypeStruct((1, width), F32),
            jax.ShapeDtypeStruct((1, width), F32),
        ),
        grid=(rows // block,),
        in_specs=[wide] * (1 + count) + [line, wide],
        out_specs=(wide, line, line),
        compiler_params=params(("arbitrary",)),
        cost_estimate=pl.CostEstimate(
            flops=20 * rows * width, transcendentals=0, bytes_accessed=18 * rows * width
        ),
        name="first_back",
    )(values, *grads, gain, add)


def second_back(core, values, grads, gain, add, weight, half, padded):
    rows, width = values.shape
    block = row_block(rows)
    count = len(grads)

    def kernel(core_ref, x_ref, *refs):
        gain_ref, add_ref, w_ref, dx_ref, low_ref, mine_ref, send_ref, db_ref, dg_ref, ds_ref = refs[count:]
        total = norm_back_values(x_ref, refs[:count], gain_ref, add_ref, dg_ref, ds_ref)
        low = total.astype(BF16)
        dx_ref[...] = total
        low_ref[...] = low

        @pl.when(pl.program_id(0) == 0)
        def _():
            db_ref[...] = jnp.zeros_like(db_ref)

        db_ref[...] += jnp.sum(low.astype(F32), axis=0, keepdims=True)
        back = dot(low, w_ref[...], NT).astype(BF16)
        empty = jnp.zeros((block, padded - half), BF16)
        halves = [jnp.concatenate([back[:, i * half : (i + 1) * half], empty], axis=1) for i in range(2)]

        @pl.when(core_ref[0] == 0)
        def _():
            mine_ref[...], send_ref[...] = halves[0], halves[1]

        @pl.when(core_ref[0] != 0)
        def _():
            mine_ref[...], send_ref[...] = halves[1], halves[0]

    wide = pl.BlockSpec((block, width), lambda i, c: (i, 0))
    part = pl.BlockSpec((block, padded), lambda i, c: (i, 0))
    line = pl.BlockSpec((1, width), lambda i, c: (0, 0))
    square = pl.BlockSpec((width, width), lambda i, c: (0, 0), pipeline_mode=pl.Buffered(1))
    return pl.pallas_call(
        kernel,
        out_shape=(
            jax.ShapeDtypeStruct((rows, width), F32),
            jax.ShapeDtypeStruct((rows, width), BF16),
            jax.ShapeDtypeStruct((rows, padded), BF16),
            jax.ShapeDtypeStruct((rows, padded), BF16),
            jax.ShapeDtypeStruct((1, width), F32),
            jax.ShapeDtypeStruct((1, width), F32),
            jax.ShapeDtypeStruct((1, width), F32),
        ),
        grid_spec=pltpu.PrefetchScalarGridSpec(
            num_scalar_prefetch=1,
            grid=(rows // block,),
            in_specs=[wide] * (1 + count) + [line, wide, square],
            out_specs=(wide, wide, part, part, line, line, line),
        ),
        compiler_params=params(("arbitrary",)),
        cost_estimate=pl.CostEstimate(
            flops=2 * rows * width * width, transcendentals=0, bytes_accessed=20 * rows * width
        ),
        name="second_back",
    )(core, values, *grads, gain, add, weight)


def hidden(arrays, weight, bias):
    rows, width = arrays[0].shape
    cols = weight.shape[1]
    block = row_block(rows)
    steps, count = rows // block, len(arrays)

    def kernel(*refs):
        w_ref, b_ref, act_ref, slope_ref, x_ref = refs[count:]
        for i in range(count):

            @pl.when(pl.program_id(0) // steps == i)
            def _():
                x_ref[...] = refs[i][...]

        pre = dot(x_ref[...], w_ref[...]) + b_ref[...]
        square = pre * pre
        turn = jnp.tanh(pre * (GELU_COEF + GELU_COEF * 0.044715 * square))
        act_ref[...] = (0.5 * pre * (1.0 + turn)).astype(BF16)
        inner = GELU_COEF + 3.0 * 0.044715 * GELU_COEF * square
        slope_ref[...] = (0.5 * (1.0 + turn) * (1.0 + pre * (1.0 - turn) * inner)).astype(BF16)

    out = pl.BlockSpec((block, cols), lambda i: (i, 0))
    return pl.pallas_call(
        kernel,
        out_shape=(
            jax.ShapeDtypeStruct((count * rows, cols), BF16),
            jax.ShapeDtypeStruct((count * rows, cols), BF16),
            jax.ShapeDtypeStruct((count * rows, width), BF16),
        ),
        grid=(count * steps,),
        in_specs=[
            pl.BlockSpec((block, width), lambda i, k=k: (jnp.clip(i - k * steps, 0, steps - 1), 0))
            for k in range(count)
        ]
        + [
            pl.BlockSpec((width, cols), lambda i: (0, 0), pipeline_mode=pl.Buffered(1)),
            pl.BlockSpec((1, cols), lambda i: (0, 0)),
        ],
        out_specs=(out, out, pl.BlockSpec((block, width), lambda i: (i, 0))),
        compiler_params=params(("arbitrary",)),
        cost_estimate=pl.CostEstimate(
            flops=2 * count * rows * width * cols,
            transcendentals=count * rows * cols,
            bytes_accessed=2 * (2 * count * rows * width + width * cols + 2 * count * rows * cols),
        ),
        name="hidden",
    )(*arrays, weight, bias)


def head_window(head):
    first = head * HEAD_DIM
    start = first // 128 * 128
    return start, round_up(first + HEAD_DIM, 128) - start, first - start


def head_lanes(rows, width, low):
    lane = lax.broadcasted_iota(jnp.int32, (rows, width), 1)
    return (lane >= low) & (lane < low + HEAD_DIM)


def only_head(block, low):
    mine = head_lanes(*block.shape, low)
    return jnp.where(mine, block.astype(F32), 0.0).astype(BF16)


def pick_block(near_ref, far_ref, block):
    return near_ref.at[block, 0] if block < 2 else far_ref.at[block - 2, 0]


def attend_kernel(row, heads, blocks, padded, need_ref, col_ref, row_ref, q_ref, near_ref, far_ref, *refs):
    own_ref, pair_ref, lse_ref, queries, score, peak, total, acc, lses = refs[-9:]
    outs = (own_ref, pair_ref)
    tokens = own_ref.shape[1]
    slot = lax.broadcasted_iota(jnp.int32, (2 * tokens, 128), 1)
    for which in range(2):
        outs[which][...] = jnp.zeros_like(outs[which])
    windows = [head_window(head) for head in range(heads)]
    for head, (start, width, low) in enumerate(windows):
        for which in range(2):
            queries[head, which * tokens : (which + 1) * tokens, :width] = only_head(
                q_ref[which, 0, :, start : start + width], low
            )
    peak[...] = jnp.full_like(peak, MASKED)
    total[...] = jnp.zeros_like(total)
    acc[...] = jnp.zeros_like(acc)
    for block in range(blocks):

        @pl.when(need_ref[row, block] != 0)
        def _():
            side = pick_block(near_ref, far_ref, block)
            seen = col_ref[0] == row_ref[0, block : block + 1]
            for head, (start, width, _) in enumerate(windows):
                key = side[:, start : start + width]
                found = jnp.where(seen, dot(queries[head, :, :width], key, NT), MASKED)
                score[head, block] = found
                top = peak[head]
                for at in range(0, tokens, 128):
                    top = jnp.maximum(top, found[:, at : at + 128])
                peak[head] = top

    for head in range(heads):
        top = jnp.max(peak[head], axis=-1, keepdims=True) * (SCALE * LOG2E)
        peak[head] = jnp.broadcast_to(top, peak.shape[1:])

    for block in range(blocks):

        @pl.when(need_ref[row, block] != 0)
        def _():
            side = pick_block(near_ref, far_ref, block)
            for head, (start, width, _) in enumerate(windows):
                top, share = peak[head], total[head]
                pieces = []
                for at in range(0, tokens, 128):
                    part = jnp.exp2(score[head, block, :, at : at + 128] * (SCALE * LOG2E) - top)
                    share += part
                    pieces.append(part.astype(BF16))
                total[head] = share
                value = side[:, padded + start : padded + start + width]
                acc[head, :, :width] += dot(jnp.concatenate(pieces, axis=1), value)

    for head, (start, width, low) in enumerate(windows):
        norm = jnp.sum(total[head], axis=-1, keepdims=True)
        result = acc[head, :, :width] / norm
        mine = head_lanes(tokens, width, low)
        for which in range(2):
            kept = outs[which][0, :, start : start + width].astype(F32)
            fresh = result[which * tokens : (which + 1) * tokens]
            outs[which][0, :, start : start + width] = jnp.where(mine, fresh, kept).astype(BF16)
        lse = peak[head] + jnp.log2(norm)
        lses[...] = lse if head == 0 else jnp.where(slot == head, lse, lses[...])
    lse_ref[0] = lses[...].T[:heads]


def attend(row, query, near, far, need, seg_col, seg_row, heads, before):
    _, rows, tokens, padded = query.shape
    blocks = 2 + far.shape[0]
    cost = 2 * heads * blocks * tokens * tokens
    narrow = pl.BlockSpec((1, tokens, padded), lambda i, need: (row, 0, 0))
    lines = pl.BlockSpec((1, heads, 2 * tokens), lambda i, need: (row, 0, 0))

    def stack(count, width):
        return pl.BlockSpec((count, 1, tokens, width), lambda i, need: (0, row, 0, 0))

    return pl.pallas_call(
        functools.partial(attend_kernel, row, heads, blocks, padded),
        out_shape=(
            jax.ShapeDtypeStruct((rows, tokens, padded), BF16),
            jax.ShapeDtypeStruct((rows, tokens, padded), BF16),
            jax.ShapeDtypeStruct((rows, heads, 2 * tokens), F32),
        ),
        grid_spec=pltpu.PrefetchScalarGridSpec(
            num_scalar_prefetch=1,
            grid=(1,),
            in_specs=[
                pl.BlockSpec((1, 2 * tokens, 1), lambda i, need: (row, 0, 0)),
                pl.BlockSpec((1, blocks, tokens), lambda i, need: (row, 0, 0)),
                stack(2, padded),
                stack(2, 2 * padded),
                stack(blocks - 2, 2 * padded),
            ]
            + [pl.BlockSpec(memory_space=pl.ANY)] * len(before),
            out_specs=(narrow, narrow, lines),
            scratch_shapes=[
                pltpu.VMEM((heads, 2 * tokens, WIN), BF16),
                pltpu.VMEM((heads, blocks, 2 * tokens, tokens), F32),
                pltpu.VMEM((heads, 2 * tokens, 128), F32),
                pltpu.VMEM((heads, 2 * tokens, 128), F32),
                pltpu.VMEM((heads, 2 * tokens, WIN), F32),
                pltpu.VMEM((2 * tokens, 128), F32),
            ],
        ),
        input_output_aliases={6 + i: i for i in range(len(before))},
        compiler_params=params(("arbitrary",)),
        cost_estimate=pl.CostEstimate(
            flops=8 * cost * WIN,
            transcendentals=cost,
            bytes_accessed=6 * blocks * tokens * padded,
        ),
        name="attend",
    )(need, seg_col, seg_row, query, near, far, *before)


def attend_back_kernel(
    row, heads, blocks, padded, need_ref, col_ref, row_ref, pick_ref, q_ref, near_ref, far_ref, *refs
):
    grads, outs, lse_ref = refs[0:2], refs[2:4], refs[4]
    dq_ref, dnear_ref, dfar_ref, sums, inner_turn, queries, incoming, dq = refs[-8:]
    tokens = grads[0].shape[1]
    sums[...] = jnp.zeros_like(sums)
    for which in range(2):
        dq_ref[which, 0] = jnp.zeros((tokens, padded), BF16)
        product = grads[which][0].astype(F32) * outs[which][0].astype(F32)
        high = product.astype(BF16)
        rest = (product - high.astype(F32)).astype(BF16)
        inner_turn[:, which * tokens : (which + 1) * tokens] = dot(pick_ref[...], high, NT) + dot(
            pick_ref[...], rest, NT
        )
    windows = [head_window(head) for head in range(heads)]
    for head, (start, width, low) in enumerate(windows):
        for which in range(2):
            there = slice(which * tokens, (which + 1) * tokens)
            here = slice(start, start + width)
            queries[head, there, :width] = only_head(q_ref[which, 0, :, here], low)
            incoming[head, there, :width] = only_head(grads[which][0, :, here], low)
    dq[...] = jnp.zeros_like(dq)
    for block in range(blocks):

        @pl.when(need_ref[row, block] != 0)
        def _():
            side = pick_block(near_ref, far_ref, block)
            seen = col_ref[0, block] == row_ref[0]
            for head, (start, width, _) in enumerate(windows):
                end = start + width
                key, value = side[:, start:end], side[:, padded + start : padded + end]
                query, grad = queries[head, :, :width], incoming[head, :, :width]
                found = dot(key, query, NT) * (SCALE * LOG2E) - lse_ref[0, head : head + 1, :]
                prob = jnp.where(seen, jnp.exp2(found), 0.0)
                inner = inner_turn[head : head + 1, :]
                slope = (prob * (dot(value, grad, NT) - inner)).astype(BF16)
                sums[block, :, start:end] += dot(slope, query)
                sums[block, :, padded + start : padded + end] += dot(prob.astype(BF16), grad)
                dq[head, :, :width] += dot(slope, key, TN)

    for head, (start, width, low) in enumerate(windows):
        mine = head_lanes(tokens, width, low)
        for which in range(2):
            kept = dq_ref[which, 0, :, start : start + width].astype(F32)
            fresh = dq[head, which * tokens : (which + 1) * tokens, :width] * SCALE
            dq_ref[which, 0, :, start : start + width] = jnp.where(mine, fresh, kept).astype(BF16)
    for block in range(blocks):
        side = pick_block(dnear_ref, dfar_ref, block)
        side[:, :padded] = (sums[block, :, :padded] * SCALE).astype(BF16)
        side[:, padded:] = sums[block, :, padded:].astype(BF16)


def attend_back(row, query, near, far, grads, outs, lse, need, seg_col, seg_row, heads, before):
    _, rows, tokens, padded = query.shape
    blocks = 2 + far.shape[0]
    cost = 2 * heads * blocks * tokens * tokens
    column = lax.broadcasted_iota(jnp.int32, (heads, padded), 1)
    pick = (column // HEAD_DIM == lax.broadcasted_iota(jnp.int32, (heads, padded), 0)).astype(BF16)
    narrow = pl.BlockSpec((1, tokens, padded), lambda i, need: (row, 0, 0))

    def stack(count, width):
        return pl.BlockSpec((count, 1, tokens, width), lambda i, need: (0, row, 0, 0))

    return pl.pallas_call(
        functools.partial(attend_back_kernel, row, heads, blocks, padded),
        out_shape=tuple(jax.ShapeDtypeStruct(a.shape, BF16) for a in (query, near, far)),
        grid_spec=pltpu.PrefetchScalarGridSpec(
            num_scalar_prefetch=1,
            grid=(1,),
            in_specs=[
                pl.BlockSpec((1, blocks, tokens, 1), lambda i, need: (row, 0, 0, 0)),
                pl.BlockSpec((1, 1, 2 * tokens), lambda i, need: (row, 0, 0)),
                pl.BlockSpec((heads, padded), lambda i, need: (0, 0)),
                stack(2, padded),
                stack(2, 2 * padded),
                stack(blocks - 2, 2 * padded),
            ]
            + [narrow] * 4
            + [pl.BlockSpec((1, heads, 2 * tokens), lambda i, need: (row, 0, 0))]
            + [pl.BlockSpec(memory_space=pl.ANY)] * len(before),
            out_specs=(stack(2, padded), stack(2, 2 * padded), stack(blocks - 2, 2 * padded)),
            scratch_shapes=[
                pltpu.VMEM((blocks, tokens, 2 * padded), F32),
                pltpu.VMEM((heads, 2 * tokens), F32),
                pltpu.VMEM((heads, 2 * tokens, WIN), BF16),
                pltpu.VMEM((heads, 2 * tokens, WIN), BF16),
                pltpu.VMEM((heads, 2 * tokens, WIN), F32),
            ],
        ),
        input_output_aliases={12 + i: i for i in range(len(before))},
        compiler_params=params(("arbitrary",)),
        cost_estimate=pl.CostEstimate(
            flops=20 * cost * WIN,
            transcendentals=cost,
            bytes_accessed=12 * blocks * tokens * padded,
        ),
        name="attend_back",
    )(need, seg_col, seg_row, pick, query, near, far, *grads, *outs, lse, *before)


def column_sum(array):
    return dot(jnp.ones((8, array.shape[0]), BF16), array)[:1]


def local(
    patches,
    lengths,
    first_gain,
    first_shift,
    query_weight,
    query_bias,
    key_weight,
    value_weight,
    value_bias,
    output_weight,
    output_bias,
    second_gain,
    second_shift,
    hidden_weight,
    hidden_bias,
    down_weight,
    down_bias,
    cotangent,
):
    seq_count, shards = lax.axis_size("seq"), lax.axis_size("fsdp")
    place, me = lax.axis_index("seq"), lax.axis_index("fsdp")
    core = place & 1
    is_first = core == 0
    core_flag = core[None].astype(jnp.int32)
    rows, tokens, width = patches.shape
    flat = rows * tokens
    heads = width // HEAD_DIM // 2
    half = heads * HEAD_DIM
    padded = round_up(half, 128)
    ff = hidden_bias.shape[0]
    ff_half = round_up(ff, 256) // 2
    out_cols = padded
    out_cut = width - padded
    shard_rows = width // shards
    chain = Chain()

    def my_half(array, size, padded_size):
        first, second = array[..., :size], array[..., size:]
        grow = [(0, 0)] * (array.ndim - 1)
        first = jnp.pad(first, grow + [(0, padded_size - size)])
        second = jnp.pad(second, grow + [(0, padded_size - second.shape[-1])])
        return jnp.where(is_first, first, second)

    vectors = jnp.stack(
        [
            first_gain,
            first_shift,
            query_bias,
            value_bias,
            output_bias,
            second_gain,
            second_shift,
            down_bias,
        ]
    )
    vector_parts = gather_direct(vectors)
    shard_qkv = jnp.concatenate(
        [my_half(w, half, padded) for w in (query_weight, key_weight, value_weight)], axis=1
    )
    shard_out = jnp.where(is_first, output_weight[:, :out_cols], output_weight[:, out_cut:])
    shard_hidden = my_half(hidden_weight, ff_half, ff_half)
    shard_down = my_half(down_weight.T, ff_half, ff_half)
    inputs = patches.reshape(flat, width)
    incoming = cotangent.reshape(flat, width)
    raw = {0: inputs}
    for bit in bits_of(seq_count):
        raw.update({j | bit: swap(part, "seq", bit) for j, part in list(raw.items())})
    incoming_near = jnp.concatenate([incoming, swap(incoming, "seq", 1)], axis=0)

    staged = shards == 8
    shard_qkv = after(shard_qkv, *vector_parts.values())
    if staged:
        q = {0: shard_qkv}
        q[4], q[1] = swap(q[0], "fsdp", 4), swap(q[0], "fsdp", 1)
        o = {0: after(shard_out, q[1])}
        o[1] = swap(o[0], "fsdp", 1)
        q[2], q[5] = swap(after(q[0], q[4]), "fsdp", 2), swap(q[4], "fsdp", 1)
        q[6], q[3] = swap(after(q[4], q[2]), "fsdp", 2), swap(after(q[2], q[5]), "fsdp", 1)
        o[4], o[5] = swap(after(o[0], q[6]), "fsdp", 4), swap(after(o[1], q[6]), "fsdp", 4)
        q[7] = swap(after(q[6], q[3]), "fsdp", 1)
        h = {0: after(shard_hidden, q[7])}
        h[4], h[1] = swap(h[0], "fsdp", 4), swap(h[0], "fsdp", 1)
    else:
        q, o, h = gather_all(shard_qkv), gather_all(shard_out), gather_all(shard_hidden)

    stacked = in_order(vector_parts, me).transpose(1, 0, 2).reshape(8, width).astype(F32)
    gain_one, shift_one, bias_query, bias_value, bias_output, gain_two, shift_two, bias_down = [
        stacked[i : i + 1] for i in range(8)
    ]

    block_of = place ^ jnp.arange(seq_count, dtype=jnp.int32)
    position = block_of[:, None] * tokens + jnp.arange(tokens, dtype=jnp.int32)[None, :]
    ends = jnp.cumsum(lengths, axis=-1)
    picture = jnp.sum(
        (position[None, :, :, None] >= ends[:, None, None, :]).astype(jnp.int32), axis=-1
    )
    usable = position[None] < ends[:, -1][:, None, None]
    segment = jnp.where(usable, picture, 1000 + position[None])
    low_id = jnp.min(jnp.where(usable, picture, 1 << 20), axis=-1)
    high_id = jnp.max(jnp.where(usable, picture, -1), axis=-1)
    need = (low_id[:, :2, None] <= high_id[:, None, :]) & (low_id[:, None, :] <= high_id[:, :2, None])
    need = need | jnp.eye(2, seq_count, dtype=jnp.bool_)[None]
    need = jnp.any(need, axis=1).astype(jnp.int32)
    near_flat = segment[:, :2].reshape(rows, 2 * tokens)
    seg_rows, seg_cols = segment, segment[..., None]
    seg_near_row, seg_near_col = near_flat[:, None], near_flat[..., None]

    normed_near = norm([raw[0], raw[1]], gain_one, shift_one)
    normed_far = norm([raw[j] for j in range(2, seq_count)], gain_one, shift_one)
    bias_q = my_half(bias_query, half, padded)
    bias_kv = jnp.concatenate([jnp.zeros((1, padded), F32), my_half(bias_value, half, padded)], axis=1)
    w_q, w_kv = chain.done(*assemble(q, me, padded))
    near_in, w_q, w_kv = chain(normed_near, w_q, w_kv)
    query = (dot(near_in, w_q) + bias_q).astype(BF16)
    near = (dot(near_in, w_kv) + bias_kv).astype(BF16)
    chain.done(query, near)
    if staged:
        far_in, w_kv, h[4], h[1], o[4], o[5] = chain(normed_far, w_kv, h[4], h[1], o[4], o[5])
        h[2], h[5] = swap(after(h[0], h[4]), "fsdp", 2), swap(h[4], "fsdp", 1)
        o[2], o[3] = swap(after(o[0], o[4]), "fsdp", 2), swap(after(o[1], o[4]), "fsdp", 2)
        o[6], o[7] = swap(o[4], "fsdp", 2), swap(o[5], "fsdp", 2)
    else:
        far_in = chain(normed_far)
    far = chain.done((dot(far_in, w_kv) + bias_kv).astype(BF16))
    query = query.reshape(2, rows, tokens, padded)
    near = near.reshape(2, rows, tokens, 2 * padded)
    far = far.reshape(seq_count - 2, rows, tokens, 2 * padded)
    gate = after(shard_down, *([h[4], h[1]] if staged else []))
    w_down = lax.all_gather(gate, "fsdp", axis=0, tiled=True)
    found = ()
    for row in range(rows):
        query, near, far = chain(query, near, far)
        if staged and row == 1:
            query, h[2], h[5] = chain(query, h[2], h[5])
            h[6], h[3] = swap(after(h[4], h[2]), "fsdp", 2), swap(after(h[2], h[5]), "fsdp", 1)
        if staged and row == 2:
            query, h[6], h[3] = chain(query, h[6], h[3])
            h[7] = swap(after(h[6], h[3]), "fsdp", 1)
        found = attend(row, query, near, far, need, seg_near_col, seg_rows, heads, found)
        chain.done(*found)
    out_own, out_pair, lse = found
    other_half = swap(out_pair, "seq", 1).reshape(flat, padded)
    o = dict(zip(o, chain(*o.values())))
    w_out_mine = assemble(o, me)
    w_out_other = swap(w_out_mine, "seq", 1)
    w_out = jnp.where(
        is_first,
        jnp.concatenate([w_out_mine[:, :out_cut], w_out_other], axis=1),
        jnp.concatenate([w_out_other[:, :out_cut], w_out_mine], axis=1),
    )
    attended, middle, second = join(
        core_flag,
        out_own.reshape(flat, padded),
        other_half,
        inputs,
        w_out,
        bias_output,
        gain_two,
        shift_two,
        half,
    )
    second_pair = swap(second, "seq", 1)
    chain.done(second)
    h = dict(zip(h, chain(*h.values())))
    w_hidden = chain.done(assemble(h, me))
    bias_hidden = my_half(hidden_bias.astype(F32)[None], ff_half, ff_half)
    second, second_pair, w_hidden = chain(second, second_pair, w_hidden)
    act, slope, second_near = chain.done(*hidden([second, second_pair], w_hidden, bias_hidden))

    incoming_near, act = chain(incoming_near, act)
    grad_down = chain.done(dot(incoming_near, act, TN).astype(BF16))
    part_down = lax.psum_scatter(grad_down, "fsdp", scatter_dimension=0, tiled=True)
    incoming_near, slope = chain(incoming_near, slope)
    grad_pre = chain.done((dot(incoming_near, w_down) * slope.astype(F32)).astype(BF16))
    grad_pre = chain(grad_pre)
    back = chain.done(dot(grad_pre, w_hidden, NT).astype(BF16))
    back_other = swap(back[flat:], "seq", 1)
    second_near, grad_pre = chain(second_near, grad_pre)
    grad_hidden = chain.done(dot(second_near, grad_pre, TN).astype(BF16))
    part_hidden = lax.psum_scatter(grad_hidden, "fsdp", scatter_dimension=0, tiled=True)
    back, back_other = chain(back, back_other)
    grad_middle, branch, grad_mine, grad_send, grad_bias_out, grad_gain_two, grad_shift_two = second_back(
        core_flag, middle, [back[:flat], back_other], gain_two, incoming, w_out, half, padded
    )
    chain.done(branch)
    grad_pair = swap(grad_send, "seq", 1)
    attended, branch = chain(attended, branch)
    out_keep, out_send = chain.done(*weight_grad([attended], [branch], me, shards))

    def core_part(array):
        low, high = array[:, :out_cols], array[:, out_cut:]
        return jnp.where(is_first, low, high), jnp.where(is_first, high, low)

    keep_mine, keep_other = core_part(out_keep)
    send_mine, send_other = core_part(out_send)
    keep_back, send_back = swap(keep_other, "seq", 1), swap(send_other, "seq", 1)
    grad_hidden_bias = column_sum(grad_pre)

    shape = (rows, tokens, padded)
    grads = [grad_mine.reshape(shape), grad_pair.reshape(shape)]
    found = ()
    for row in range(rows):
        query, near, far, *grads = chain(query, near, far, *grads)
        if row == 1:
            keep_back, send_back, query = chain(keep_back, send_back, query)
            out_keep = (keep_mine.astype(F32) + keep_back.astype(F32)).astype(BF16)
            out_send = (send_mine.astype(F32) + send_back.astype(F32)).astype(BF16)
            out_back = swap(out_send, "fsdp", 1)
        if row == 2:
            out_back, query = chain(out_back, query)
            out_keep, out_send = scatter_step(out_keep, out_back, shard_rows)
            out_back = swap(out_send, "fsdp", 2)
        found = attend_back(
            row,
            query,
            near,
            far,
            grads,
            [out_own, out_pair],
            lse,
            need,
            seg_cols,
            seg_near_row,
            heads,
            found,
        )
        chain.done(*found)
    dq, dnear, dfar = [g.reshape(-1, g.shape[-1]) for g in found]
    dfar, w_kv = chain(dfar, w_kv)
    back_far = chain.done(dot(dfar, w_kv, NT).astype(BF16))
    far_parts = {j: back_far[(j - 2) * flat : (j - 1) * flat] for j in range(2, seq_count)}
    far_sent = {j: swap(part, "seq", 1) for j, part in far_parts.items() if j & 1}
    normed_near, normed_far, dnear, dfar = chain(normed_near, normed_far, dnear, dfar)
    kv_keep, kv_send = weight_grad([normed_near, normed_far], [dnear, dfar], me, shards)
    chain.done(kv_keep, kv_send)
    kv_back = swap(kv_send, "fsdp", 1)
    far_sent = {j: chain(part) for j, part in far_sent.items()}
    far_sums = {
        j: (far_parts[j].astype(F32) + far_sent[j | 1].astype(F32)).astype(BF16)
        for j in far_parts
        if not j & 1
    }
    chain.done(*far_sums.values())
    arrived = []
    for bit in bits_of(seq_count)[:-1]:
        moved = {j: swap(part, "seq", bit) for j, part in far_sums.items() if j & bit}
        far_sums = {j: part for j, part in far_sums.items() if not j & bit}
        for j, part in moved.items():
            if j == bit:
                arrived.append(part)
            else:
                far_sums[j ^ bit] = (far_sums[j ^ bit].astype(F32) + part.astype(F32)).astype(BF16)
    normed_near, dq, out_back = chain(normed_near, dq, out_back)
    out_keep, out_send = scatter_step(out_keep, out_back, shard_rows)
    out_back = swap(out_send, "fsdp", 4) if out_send is not None else None
    q_keep, q_send = chain.done(*weight_grad([normed_near], [dq], me, shards))
    q_back = swap(q_send, "fsdp", 1)
    dq, dnear = chain(dq, dnear)
    back_near = chain.done((dot(dq, w_q, NT) + dot(dnear, w_kv, NT)).astype(BF16))
    pair_back = swap(back_near[flat:], "seq", 1)

    def next_bits(keep, back, bits):
        for bit in bits:
            keep, send = scatter_step(keep, back, shard_rows)
            if send is not None:
                back = swap(send, "fsdp", bit)
        return keep

    act, middle = chain(act, middle)
    down_pair = chain.done(dot(act[flat:], w_down, NT).astype(BF16))
    down_back = swap(down_pair, "seq", 1)
    rest = [2 << k for k in range(shards.bit_length() - 2)] + [0]
    kv_back, q_back = chain(kv_back, q_back)
    kv_sum = next_bits(kv_keep, kv_back, rest)
    q_sum = next_bits(q_keep, q_back, rest)
    out_sum = next_bits(out_keep, out_back, rest[2:]) if shards >= 8 else out_keep
    act, down_back = chain(act, down_back)
    result = middle + dot(act[:flat], w_down, NT) + down_back.astype(F32) + bias_down
    layer_output = chain.done(result.astype(BF16)).reshape(rows, tokens, width)
    grad_patches, grad_gain_one, grad_shift_one = first_back(
        inputs, [back_near[:flat], pair_back] + arrived, gain_one, grad_middle
    )

    def widen(own, size):
        own = own[:, :size]
        none = jnp.zeros_like(own)
        return jnp.where(
            is_first, jnp.concatenate([own, none], axis=1), jnp.concatenate([none, own], axis=1)
        )

    grad_bias_value = column_sum(dnear[:, padded:]) + column_sum(dfar[:, padded:])
    early = jnp.concatenate(
        [
            widen(column_sum(dq), half),
            widen(grad_bias_value, half),
            grad_bias_out,
            grad_gain_two,
            grad_shift_two,
            column_sum(incoming),
            widen(grad_hidden_bias, ff_half),
        ],
        axis=1,
    )
    late = jnp.concatenate([grad_gain_one, grad_shift_one], axis=1)

    def everywhere(bundle):
        for axis in ("seq", "fsdp"):
            for bit in bits_of(lax.axis_size(axis)):
                bundle = bundle + swap(bundle, axis, bit)
        return bundle

    early, late = everywhere(early), everywhere(late)

    def owned(bundle, i):
        return lax.dynamic_slice_in_dim(
            bundle[0, i * width : (i + 1) * width], me * shard_rows, shard_rows, 0
        )

    hidden_total = early[0, 6 * width : 6 * width + ff]

    def whole(mine, size, total):
        other = swap(mine, "seq", 1)
        return jnp.where(
            is_first,
            jnp.concatenate([mine[:, :size], other[:, : total - size]], axis=1),
            jnp.concatenate([other[:, :size], mine[:, : total - size]], axis=1),
        )

    full_down = whole(seq_sum(part_down), ff_half, ff).T
    full_hidden = whole(seq_sum(part_hidden), ff_half, ff)
    out_total, q_total, kv_total = seq_sum(out_sum), seq_sum(q_sum), seq_sum(kv_sum)
    other_out = swap(out_total, "seq", 1)
    full_out = jnp.where(
        is_first,
        jnp.concatenate([out_total[:, :out_cut], other_out], axis=1),
        jnp.concatenate([other_out[:, :out_cut], out_total], axis=1),
    )
    full_query = whole(q_total, half, width)
    full_key = whole(kv_total[:, :padded], half, width)
    full_value = whole(kv_total[:, padded:], half, width)
    return (
        layer_output,
        grad_patches.reshape(rows, tokens, width),
        owned(late, 0),
        owned(late, 1),
        full_query,
        owned(early, 0),
        full_key,
        full_value,
        owned(early, 1),
        full_out,
        owned(early, 2),
        owned(early, 3),
        owned(early, 4),
        full_hidden,
        hidden_total,
        full_down,
        owned(early, 5),
    )


def solution(mesh):
    shard, line, tokens = P("fsdp", None), P("fsdp"), P("fsdp", "seq", None)
    in_specs = (
        tokens,
        shard,
        line,
        line,
        shard,
        line,
        shard,
        shard,
        line,
        shard,
        line,
        line,
        line,
        shard,
        P(),
        P(None, "fsdp"),
        line,
        tokens,
    )
    out_specs = (
        tokens,
        tokens,
        line,
        line,
        shard,
        line,
        shard,
        shard,
        line,
        shard,
        line,
        line,
        line,
        shard,
        P(),
        P(None, "fsdp"),
        line,
    )
    return jax.shard_map(local, mesh=mesh, in_specs=in_specs, out_specs=out_specs, check_vma=False)
```

time: 966 us -> 724 us (0.75)
  Pallas kernels: 350 us -> 212 us
  waiting for transfers between devices: 329 us -> 210 us
  between operations: 2.26 us -> 15.1 us
    ppermute x80 -> x73, waiting for transfers between devices: 329 us -> 210 us  [swap(): return lax.ppermute(array, axis, [(i, i ^ bits) for i in range(size)])]
    pallas_call x13 -> x15, Pallas kernels: 275 us -> 178 us  [the longest x3 65.5 us: attend_back(): pl.pallas_call(functools.partial(attend_back_kernel, row, heads, blocks,...]
    pallas_call x5 -> x3, Pallas kernels: 75 us -> 33.6 us  [weight_grad(): pl.pallas_call(functools.partial(weight_grad_kernel, pairs, count, rows),...]
    slice x19 -> x12, local copies, waits for them, and re-layouts: 19.6 us -> 6.54 us  [the longest x1 1.48 us: local(): pair_back = swap(back_near[flat:], 'seq', 1)]
    ppermute x80 -> x73, starting transfers between devices: 68 us -> 62.9 us  [swap(): return lax.ppermute(array, axis, [(i, i ^ bits) for i in range(size)])]
    dot_general x26 -> x17, matrix products: 114 us -> 116 us  [dot(): lax.dot_general(left, right, (dims, ((), ())), preferred_element_type=F32)]
  transfers between devices with their start and end apart: 80 -> 76, of which waited for: 30 -> 23; matrix products, arithmetic and copies ran while one was open for 19% -> 28% of each run, Pallas kernels for 35% -> 29%
where the time goes in v2:
time: 724 us; the launch traced here: 719 us
  Pallas kernels  212 us (29%)
  waiting for transfers between devices  210 us (29%)
  matrix products  116 us (16%)
  starting transfers between devices  63.6 us (9%)
  local copies, waits for them, and re-layouts  53.9 us (7%)
  other arithmetic  48.1 us (7%)
  between operations  15.1 us (2%)
    ppermute x73, waiting for transfers between devices, swap(): return lax.ppermute(array, axis, [(i, i ^ bits) for i in range(size)])  210 us
    dot_general x17, matrix products, dot(): lax.dot_general(left, right, (dims, ((), ())), preferred_element_type=F32)  116 us
    pallas_call x3, Pallas kernels, attend_back(): pl.pallas_call(functools.partial(attend_back_kernel, row, heads, blocks,...  65.5 us
    ppermute x73, starting transfers between devices, swap(): return lax.ppermute(array, axis, [(i, i ^ bits) for i in range(size)])  62.9 us
    pallas_call x3, Pallas kernels, attend(): pl.pallas_call(functools.partial(attend_kernel, row, heads, blocks, padde...  38 us
    pallas_call x3, Pallas kernels, weight_grad(): pl.pallas_call(functools.partial(weight_grad_kernel, pairs, count, rows),...  33.6 us
    pallas_call x1, Pallas kernels, hidden(): pl.pallas_call(kernel, out_shape=(jax.ShapeDtypeStruct((count * rows, col...  18.9 us
    unnamed x139, local copies, waits for them, and re-layouts  14.9 us
  transfers between devices with their start and end apart: 76, of which 23 were waited for; matrix products, arithmetic and copies ran while one was open for 28% of the time, Pallas kernels for 29%

profile of v2, /device:TPU:0, one launch (start us, length us, event | category | flops | bytes accessed | tf_op | source)
XLA Modules:
  0.0 718.6 jit_solution(12849177176616743661)
XLA Ops:
  48.1 21.6 %collective-permute-done.10.refs_4_ = bf16[144,1920]{1,0:T(8,128)(2,1)S(1)} collective-permute-done((bf16[144,1920]{1,0:T(8,128)(2,1)S(1)}, bf16[144,1920]{1,0:T(8,128)(2,1)S(1)}, u32[]{:S(2)}, u32[]{:S(2)}) %collective-permute-start.10) | collective-permute-done | bytes 552992 | tf_op jit(solution)/shard_map/ppermute | solution.py:41
  74.7 9.3 %collective-permute-done.11.refs_2_ = bf16[144,1920]{1,0:T(8,128)(2,1)} collective-permute-done((bf16[144,1920]{1,0:T(8,128)(2,1)S(1)}, bf16[144,1920]{1,0:T(8,128)(2,1)}, u32[]{:S(2)}, u32[]{:S(2)}) %collective-permute-start.11) | collective-permute-done | bytes 552992 | tf_op jit(solution)/shard_map/ppermute | solution.py:41
  133.0 8.7 %fusion.1 = bf16[1536,1280]{1,0:T(8,128)(2,1)} fusion(bf16[1536,1152]{1,0:T(8,128)(2,1)S(1)} %copy-done.10, bf16[1152,1280]{1,0:T(8,128)(2,1)} %get-tuple-element.285, f32[1280]{0:T(1024)S(1)} %copy-done.46), kind=kOutput, calls=%fused_computation.9 | convolution fusion | flops 4533780480 | bytes 10425344 | tf_op jit(solution)/shard_map/dot_general | solution.py:28
  163.3 9.4 %fusion.2 = bf16[1536,1280]{1,0:T(8,128)(2,1)} fusion(bf16[1536,1152]{1,0:T(8,128)(2,1)} %norm.3.refs_1_, bf16[1152,1280]{1,0:T(8,128)(2,1)} %get-tuple-element.285, f32[1280]{0:T(1024)S(1)} %copy-done.46), kind=kOutput, calls=%fused_computation.10 | convolution fusion | flops 4533780480 | bytes 10425344 | tf_op jit(solution)/shard_map/dot_general | solution.py:28
  172.7 12.4 %attend.3 = (bf16[3,256,640]{2,1,0:T(8,128)(2,1)}, bf16[3,256,640]{2,1,0:T(8,128)(2,1)}, f32[3,8,512]{2,1,0:T(8,128)}) custom-call(s32[3,4]{1,0:T(4,128)} %convert_element_type.274.need_ref, s32[3,512,1]{2,1,0:T(8,128)} %broadcast_in_dim_reshape.8.col_ref, s32[3,4,256]{2,1,0:T(4,128)} %copy-done.44, bf16[2,3,256,640]{3,2,1,0:T(8,128)(2,1)} %bitcast.139, ...), custom_call_target="tpu_custom_call" | custom-call | flops 8589934592 | bytes 3932160 | tf_op jit(solution)/shard_map/attend/pallas_call | solution.py:556
  185.0 21.3 %collective-permute-done.23.refs_2_ = bf16[144,2176]{1,0:T(8,128)(2,1)S(1)} collective-permute-done((bf16[144,2176]{1,0:T(8,128)(2,1)S(1)}, bf16[144,2176]{1,0:T(8,128)(2,1)S(1)}, u32[]{:S(2)}, u32[]{:S(2)}) %collective-permute-start.23) | collective-permute-done | bytes 626720 | tf_op jit(solution)/shard_map/ppermute | solution.py:41
  207.0 13.2 %attend.4 = (bf16[3,256,640]{2,1,0:T(8,128)(2,1)}, bf16[3,256,640]{2,1,0:T(8,128)(2,1)}, f32[3,8,512]{2,1,0:T(8,128)}) custom-call(s32[3,4]{1,0:T(4,128)} %convert_element_type.274.need_ref, s32[3,512,1]{2,1,0:T(8,128)} %broadcast_in_dim_reshape.8.col_ref, s32[3,4,256]{2,1,0:T(4,128)} %copy-done.44, ...), custom_call_target="tpu_custom_call", output_to_operand_aliasing={{0}: (6, {}), {1}: (7, {}), {2}: (8, {})} | custom-call | flops 8589934592 | bytes 3932160 | tf_op jit(solution)/shard_map/attend/pallas_call | solution.py:556
  220.2 29.8 %collective-permute-done.25.refs_6_ = bf16[144,2176]{1,0:T(8,128)(2,1)S(1)} collective-permute-done((bf16[144,2176]{1,0:T(8,128)(2,1)}, bf16[144,2176]{1,0:T(8,128)(2,1)S(1)}, u32[]{:S(2)}, u32[]{:S(2)}) %collective-permute-start.25) | collective-permute-done | bytes 626720 | tf_op jit(solution)/shard_map/ppermute | solution.py:41
  250.8 12.5 %attend.5 = (bf16[3,256,640]{2,1,0:T(8,128)(2,1)}, bf16[3,256,640]{2,1,0:T(8,128)(2,1)}, f32[3,8,512]{2,1,0:T(8,128)}) custom-call(s32[3,4]{1,0:T(4,128)} %convert_element_type.274.need_ref, s32[3,512,1]{2,1,0:T(8,128)} %broadcast_in_dim_reshape.8.col_ref, s32[3,4,256]{2,1,0:T(4,128)} %copy-done.44, ...), custom_call_target="tpu_custom_call", output_to_operand_aliasing={{0}: (6, {}), {1}: (7, {}), {2}: (8, {})} | custom-call | flops 8589934592 | bytes 3932160 | tf_op jit(solution)/shard_map/attend/pallas_call | solution.py:556
  293.3 12.4 %collective-permute-done.34.refs_7_ = bf16[144,2176]{1,0:T(8,128)(2,1)S(1)} collective-permute-done((bf16[144,2176]{1,0:T(8,128)(2,1)S(1)}, bf16[144,2176]{1,0:T(8,128)(2,1)S(1)}, u32[]{:S(2)}, u32[]{:S(2)}) %collective-permute-start.34) | collective-permute-done | bytes 626720 | tf_op jit(solution)/shard_map/ppermute | solution.py:41
  311.4 18.9 %hidden.1 = (bf16[1536,2176]{1,0:T(8,128)(2,1)}, bf16[1536,2176]{1,0:T(8,128)(2,1)}, bf16[1536,1152]{1,0:T(8,128)(2,1)}) custom-call(bf16[768,1152]{1,0:T(8,128)(2,1)} %get-tuple-element.233.refs_0_, bf16[768,1152]{1,0:T(8,128)(2,1)} %collective-permute-done.33.refs_1_, bf16[1152,2176]{1,0:T(8,128)(2,1)} %assemble.5.refs_2_, ...), custom_call_target="tpu_custom_call" | custom-call | flops 7700742144 | bytes 25460736 | tf_op jit(solution)/shard_map/hidden/pallas_call | solution.py:435
  330.2 13.0 %convolution_convert_fusion.1 = bf16[1152,2176]{1,0:T(8,128)(2,1)} fusion(bf16[1536,1152]{1,0:T(8,128)(2,1)S(1)} %copy-done.11, bf16[1536,2176]{1,0:T(8,128)(2,1)} %get-tuple-element.303), kind=kOutput, calls=%fused_computation.5 | convolution fusion | flops 7703248896 | bytes 15237120 | tf_op jit(solution)/shard_map/dot_general | solution.py:28
  343.8 12.9 %fusion = bf16[1536,2176]{1,0:T(8,128)(2,1)S(1)} fusion(bf16[1536,2176]{1,0:T(8,128)(2,1)} %get-tuple-element.245, bf16[1536,1152]{1,0:T(8,128)(2,1)S(1)} %copy-done.11, bf16[1152,2176]{1,0:T(8,128)(2,1)} %all-gather.2.cloned.1.call-done), kind=kOutput, calls=%fused_computation.3 | convolution fusion | flops 7710769152 | bytes 21921792 | tf_op jit(solution)/shard_map/dot_general | solution.py:28
  356.7 14.3 %convolution_convert_fusion.3 = bf16[1536,1152]{1,0:T(8,128)(2,1)S(1)} fusion(bf16[1536,2176]{1,0:T(8,128)(2,1)S(1)} %fusion, bf16[1152,2176]{1,0:T(8,128)(2,1)} %assemble.5.refs_2_), kind=kOutput, calls=%fused_computation.13 | convolution fusion | flops 7702511616 | bytes 15237120 | tf_op jit(solution)/shard_map/dot_general | solution.py:28
  373.7 10.1 %convolution_convert_fusion = bf16[1152,2176]{1,0:T(8,128)(2,1)} fusion(bf16[1536,1152]{1,0:T(8,128)(2,1)S(1)} %copy-done.59, bf16[1536,2176]{1,0:T(8,128)(2,1)S(1)} %fusion), kind=kOutput, calls=%fused_computation.4 | convolution fusion | flops 7703248896 | bytes 15237120 | tf_op jit(solution)/shard_map/dot_general | solution.py:28
  385.2 12.0 %second_back.1 = (f32[768,1152]{1,0:T(8,128)}, bf16[768,1152]{1,0:T(8,128)(2,1)}, bf16[768,640]{1,0:T(8,128)(2,1)}, bf16[768,640]{1,0:T(8,128)(2,1)}, f32[1,1152...) custom-call(s32[1]{0:T(128)} %bitcast.1.core_ref, f32[768,1152]{1,0:T(8,128)} %get-tuple-element.301.x_ref, ...), custom_call_target="tpu_custom_call" | custom-call | flops 2038431744 | bytes 17694720 | tf_op jit(solution)/shard_map/second_back/pallas_call | solution.py:388
  409.4 21.6 %attend_back.3 = (bf16[2,3,256,640]{3,2,1,0:T(8,128)(2,1)}, bf16[2,3,256,1280]{3,2,1,0:T(8,128)(2,1)}, bf16[2,3,256,1280]{3,2,1,0:T(8,128)(2,1)}) custom-call(s32[3,4]{1,0:T(4,128)} %convert_element_type.274.need_ref, s32[3,4,256,1]{3,2,1,0:T(8,128)} %compare_select_fusion.col_ref, s32[3,1,512]{2,1,0:T(1,128)} %broadcast_in_dim_reshape.7.row_ref, ...), custom_call_target="tpu_custom_call" | custom-call | flops 21474836480 | bytes 7864320 | tf_op jit(solution)/shard_map/attend_back/pallas_call | solution.py:659
  433.2 22.0 %attend_back.4 = (bf16[2,3,256,640]{3,2,1,0:T(8,128)(2,1)}, bf16[2,3,256,1280]{3,2,1,0:T(8,128)(2,1)}, bf16[2,3,256,1280]{3,2,1,0:T(8,128)(2,1)}) custom-call(s32[3,4]{1,0:T(4,128)} %convert_element_type.274.need_ref, s32[3,4,256,1]{3,2,1,0:T(8,128)} %compare_select_fusion.col_ref, ...), custom_call_target="tpu_custom_call", output_to_operand_aliasing={{0}: (12, {}), {1}: (13, {}), {2}: (14, {})} | custom-call | flops 21474836480 | bytes 7864320 | tf_op jit(solution)/shard_map/attend_back/pallas_call | solution.py:659
  455.3 21.9 %attend_back.5 = (bf16[2,3,256,640]{3,2,1,0:T(8,128)(2,1)}, bf16[2,3,256,1280]{3,2,1,0:T(8,128)(2,1)}, bf16[2,3,256,1280]{3,2,1,0:T(8,128)(2,1)}) custom-call(s32[3,4]{1,0:T(4,128)} %convert_element_type.274.need_ref, s32[3,4,256,1]{3,2,1,0:T(8,128)} %compare_select_fusion.col_ref, ...), custom_call_target="tpu_custom_call", output_to_operand_aliasing={{0}: (12, {}), {1}: (13, {}), {2}: (14, {})} | custom-call | flops 21474836480 | bytes 7864320 | tf_op jit(solution)/shard_map/attend_back/pallas_call | solution.py:659
  493.8 17.0 %weight_grad.4 = (bf16[576,1280]{1,0:T(8,128)(2,1)}, bf16[576,1280]{1,0:T(8,128)(2,1)}) custom-call(s32[9]{0:T(128)} %pad_add_fusion.pos_ref, bf16[1536,1152]{1,0:T(8,128)(2,1)} %norm.2.refs_0_, bf16[1536,1152]{1,0:T(8,128)(2,1)} %norm.3.refs_1_, bf16[1536,1280]{1,0:T(8,128)(2,1)} %bitcast.101, bf16[1536,1280]{1,0:T(8,128)(2,1)} %bitcast.105), custom_call_target="tpu_custom_call" | custom-call | flops 9059696640 | bytes 17891328 | tf_op jit(solution)/shard_map/weight_grad/pallas_call | solution.py:187
  546.0 36.7 %collective-permute-done.56 = f32[1,11264]{1,0:T(1,128)S(1)} collective-permute-done((f32[1,11264]{1,0:T(1,128)S(1)}, f32[1,11264]{1,0:T(1,128)S(1)}, u32[]{:S(2)}, u32[]{:S(2)}) %collective-permute-start.56) | collective-permute-done | bytes 45088 | tf_op jit(solution)/shard_map/ppermute | solution.py:41
  630.8 8.6 %first_back.1 = (f32[768,1152]{1,0:T(8,128)}, f32[1,1152]{1,0:T(1,128)}, f32[1,1152]{1,0:T(1,128)}) custom-call(bf16[768,1152]{1,0:T(8,128)(2,1)} %bitcast.90, bf16[768,1152]{1,0:T(8,128)(2,1)} %get-tuple-element.324.refs_0_, bf16[768,1152]{1,0:T(8,128)(2,1)} %collective-permute-done.43.refs_1_, bf16[768,1152]{1,0:T(8,128)(2,1)} %collective-permute-done.44.refs_2_, ...), custom_call_target="tpu_custom_call" | custom-call | flops 17694720 | bytes 15925248 | tf_op jit(solution)/shard_map/first_back/pallas_call | solution.py:337
  663.3 10.0 %fusion.6 = bf16[768,1152]{1,0:T(8,128)(2,1)} fusion(bf16[768,1152]{1,0:T(8,128)(2,1)} %collective-permute-done.42, f32[768,1152]{1,0:T(8,128)S(1)} %copy-done.9, bf16[1152,2176]{1,0:T(8,128)(2,1)} %all-gather.2.cloned.1.call-done, bf16[1536,2176]{1,0:T(8,128)(2,1)} %get-tuple-element.303, f32[1152]{0:T(1024)S(1)} %add.288), kind=kOutput, calls=%fused_computation.20 | convolution fusion | flops 3854794752 | bytes 15438336 | tf_op jit(solution)/shard_map/dot_general | solution.py:28
  692.8 11.4 %collective-permute-done.69 = bf16[144,2176]{1,0:T(8,128)(2,1)S(1)} collective-permute-done((bf16[144,2176]{1,0:T(8,128)(2,1)}, bf16[144,2176]{1,0:T(8,128)(2,1)S(1)}, u32[]{:S(2)}, u32[]{:S(2)}) %collective-permute-start.69) | collective-permute-done | bytes 626720 | tf_op jit(solution)/shard_map/ppermute | solution.py:41
  (436 shorter events, 322.7 us)
Async XLA Ops:
  7.2 336.5 %all-gather.2.cloned.1.call-start = ((), (), s32[]{:S(2)}) async-start(), calls=%async_computation.2 | async-start | bytes 5640192 | tf_op jit(solution)/shard_map/all_gather | solution.py:829
  40.4 78.9 %collective-permute-start.16 = (bf16[768,1152]{1,0:T(8,128)(2,1)S(1)}, bf16[768,1152]{1,0:T(8,128)(2,1)}, u32[]{:S(2)}, u32[]{:S(2)}) collective-permute-start(bf16[768,1152]{1,0:T(8,128)(2,1)S(1)} %bitcast.91), channel_id=1, source_target_pairs={{0,16},{8,24},{16,0},{24,8},{1,17},{9,25},{17,1},{25,9},{2,18},{10... | collective-permute-start | bytes 5308424 | tf_op jit(solution)/shard_map/ppermute | solution.py:41
  42.0 77.4 %collective-permute-start.1 = (bf16[768,1152]{1,0:T(8,128)(2,1)S(1)}, bf16[768,1152]{1,0:T(8,128)(2,1)}, u32[]{:S(2)}, u32[]{:S(2)}) collective-permute-start(bf16[768,1152]{1,0:T(8,128)(2,1)S(1)} %bitcast.92), channel_id=1, source_target_pairs={{0,8},{8,0},{16,24},{24,16},{1,9},{9,1},{17,25},{25,17},{2,10},{10... | collective-permute-start | bytes 5308424 | tf_op jit(solution)/shard_map/ppermute | solution.py:41
  46.0 57.9 %collective-permute-start.9 = (bf16[144,1920]{1,0:T(8,128)(2,1)S(1)}, bf16[144,1920]{1,0:T(8,128)(2,1)S(1)}, u32[]{:S(2)}, u32[]{:S(2)}) collective-permute-start(bf16[144,1920]{1,0:T(8,128)(2,1)S(1)} %pad_maximum_fusion.1.refs_0_), channel_id=1, source_target_pairs={{0,1},{1,0},{2,3},{3,2},{4,5},{5,4},{6,7},{7,6},{8,9},{9,8},{10,11... | collective-permute-start | bytes 1658888 | tf_op jit(solution)/shard_map/ppermute | solution.py:41
  107.2 45.5 %collective-permute-start.20 = (bf16[144,640]{1,0:T(8,128)(2,1)}, bf16[144,640]{1,0:T(8,128)(2,1)}, u32[]{:S(2)}, u32[]{:S(2)}) collective-permute-start(bf16[144,640]{1,0:T(8,128)(2,1)} %slice_select_fusion.1.refs_0_), channel_id=1, source_target_pairs={{0,4},{1,5},{2,6},{3,7},{4,0},{5,1},{6,2},{7,3},{8,12},{9,13},{10,... | collective-permute-start | bytes 552968 | tf_op jit(solution)/shard_map/ppermute | solution.py:41
  115.9 36.8 %collective-permute-start.22 = (bf16[144,640]{1,0:T(8,128)(2,1)}, bf16[144,640]{1,0:T(8,128)(2,1)}, u32[]{:S(2)}, u32[]{:S(2)}) collective-permute-start(bf16[144,640]{1,0:T(8,128)(2,1)} %collective-permute-done.21.refs_1_), channel_id=1, source_target_pairs={{0,4},{1,5},{2,6},{3,7},{4,0},{5,1},{6,2},{7,3},{8,12},{9,13},{10,... | collective-permute-start | bytes 552968 | tf_op jit(solution)/shard_map/ppermute | solution.py:41
  127.5 30.9 %collective-permute-start.18 = (bf16[144,2176]{1,0:T(8,128)(2,1)}, bf16[144,2176]{1,0:T(8,128)(2,1)}, u32[]{:S(2)}, u32[]{:S(2)}) collective-permute-start(bf16[144,2176]{1,0:T(8,128)(2,1)} %pad_select_fusion.refs_0_), channel_id=1, source_target_pairs={{0,4},{1,5},{2,6},{3,7},{4,0},{5,1},{6,2},{7,3},{8,12},{9,13},{10,... | collective-permute-start | bytes 1880072 | tf_op jit(solution)/shard_map/ppermute | solution.py:41
  158.4 106.3 %collective-permute-start.30 = (bf16[144,640]{1,0:T(8,128)(2,1)}, bf16[144,640]{1,0:T(8,128)(2,1)S(1)}, u32[]{:S(2)}, u32[]{:S(2)}) collective-permute-start(bf16[144,640]{1,0:T(8,128)(2,1)} %collective-permute-done.20.refs_4_), channel_id=1, source_target_pairs={{0,2},{1,3},{2,0},{3,1},{4,6},{5,7},{6,4},{7,5},{8,10},{9,11},{10,... | collective-permute-start | bytes 552968 | tf_op jit(solution)/shard_map/ppermute | solution.py:41
  158.4 47.9 %collective-permute-start.24 = (bf16[144,2176]{1,0:T(8,128)(2,1)}, bf16[144,2176]{1,0:T(8,128)(2,1)S(1)}, u32[]{:S(2)}, u32[]{:S(2)}) collective-permute-start(bf16[144,2176]{1,0:T(8,128)(2,1)} %collective-permute-done.18.refs_4_), channel_id=1, source_target_pairs={{0,1},{1,0},{2,3},{3,2},{4,5},{5,4},{6,7},{7,6},{8,9},{9,8},{10,11... | collective-permute-start | bytes 1880072 | tf_op jit(solution)/shard_map/ppermute | solution.py:41
  159.0 458.0 %reduce-scatter.5.cloned.1.call-start = ((), (), s32[]{:S(2)}) async-start(), calls=%async_computation.4 | async-start | bytes 5640192 | tf_op jit(solution)/shard_map/reduce_scatter | solution.py:872
  159.2 104.1 %collective-permute-start.28 = (bf16[144,640]{1,0:T(8,128)(2,1)}, bf16[144,640]{1,0:T(8,128)(2,1)S(1)}, u32[]{:S(2)}, u32[]{:S(2)}) collective-permute-start(bf16[144,640]{1,0:T(8,128)(2,1)} %slice_select_fusion.1.refs_0_), channel_id=1, source_target_pairs={{0,2},{1,3},{2,0},{3,1},{4,6},{5,7},{6,4},{7,5},{8,10},{9,11},{10,... | collective-permute-start | bytes 552968 | tf_op jit(solution)/shard_map/ppermute | solution.py:41
  161.3 102.1 %collective-permute-start.29 = (bf16[144,640]{1,0:T(8,128)(2,1)}, bf16[144,640]{1,0:T(8,128)(2,1)S(1)}, u32[]{:S(2)}, u32[]{:S(2)}) collective-permute-start(bf16[144,640]{1,0:T(8,128)(2,1)} %collective-permute-done.21.refs_1_), channel_id=1, source_target_pairs={{0,2},{1,3},{2,0},{3,1},{4,6},{5,7},{6,4},{7,5},{8,10},{9,11},{10,... | collective-permute-start | bytes 552968 | tf_op jit(solution)/shard_map/ppermute | solution.py:41
  161.4 45.0 %collective-permute-start.23 = (bf16[144,2176]{1,0:T(8,128)(2,1)S(1)}, bf16[144,2176]{1,0:T(8,128)(2,1)S(1)}, u32[]{:S(2)}, u32[]{:S(2)}) collective-permute-start(bf16[144,2176]{1,0:T(8,128)(2,1)S(1)} %copy-done.14), channel_id=1, source_target_pairs={{0,2},{1,3},{2,0},{3,1},{4,6},{5,7},{6,4},{7,5},{8,10},{9,11},{10,... | collective-permute-start | bytes 1880072 | tf_op jit(solution)/shard_map/ppermute | solution.py:41
  206.4 43.6 %collective-permute-start.25 = (bf16[144,2176]{1,0:T(8,128)(2,1)}, bf16[144,2176]{1,0:T(8,128)(2,1)S(1)}, u32[]{:S(2)}, u32[]{:S(2)}) collective-permute-start(bf16[144,2176]{1,0:T(8,128)(2,1)} %collective-permute-done.18.refs_4_), channel_id=1, source_target_pairs={{0,2},{1,3},{2,0},{3,1},{4,6},{5,7},{6,4},{7,5},{8,10},{9,11},{10,... | collective-permute-start | bytes 1880072 | tf_op jit(solution)/shard_map/ppermute | solution.py:41
  206.4 43.6 %collective-permute-start.26 = (bf16[144,2176]{1,0:T(8,128)(2,1)S(1)}, bf16[144,2176]{1,0:T(8,128)(2,1)S(1)}, u32[]{:S(2)}, u32[]{:S(2)}) collective-permute-start(bf16[144,2176]{1,0:T(8,128)(2,1)S(1)} %collective-permute-done.23.refs_2_), channel_id=1, source_target_pairs={{0,1},{1,0},{2,3},{3,2},{4,5},{5,4},{6,7},{7,6},{8,9},{9,8},{10,11... | collective-permute-start | bytes 1880072 | tf_op jit(solution)/shard_map/ppermute | solution.py:41
  343.3 339.9 %reduce-scatter.3.cloned.1.call-start = ((), (), s32[]{:S(2)}) async-start(), calls=%async_computation.3 | async-start | bytes 5640192 | tf_op jit(solution)/shard_map/reduce_scatter | solution.py:880
  510.8 106.1 %collective-permute-start.50 = (bf16[576,1280]{1,0:T(8,128)(2,1)}, bf16[576,1280]{1,0:T(8,128)(2,1)}, u32[]{:S(2)}, u32[]{:S(2)}) collective-permute-start(bf16[576,1280]{1,0:T(8,128)(2,1)} %get-tuple-element.293), channel_id=1, source_target_pairs={{0,1},{1,0},{2,3},{3,2},{4,5},{5,4},{6,7},{7,6},{8,9},{9,8},{10,11... | collective-permute-start | bytes 4423688 | tf_op jit(solution)/shard_map/ppermute | solution.py:41
  541.8 75.5 %collective-permute-start.51 = (bf16[576,640]{1,0:T(8,128)(2,1)}, bf16[576,640]{1,0:T(8,128)(2,1)}, u32[]{:S(2)}, u32[]{:S(2)}) collective-permute-start(bf16[576,640]{1,0:T(8,128)(2,1)} %get-tuple-element.298), channel_id=1, source_target_pairs={{0,1},{1,0},{2,3},{3,2},{4,5},{5,4},{6,7},{7,6},{8,9},{9,8},{10,11... | collective-permute-start | bytes 2211848 | tf_op jit(solution)/shard_map/ppermute | solution.py:41
  541.8 87.4 %collective-permute-start.44 = (bf16[768,1152]{1,0:T(8,128)(2,1)}, bf16[768,1152]{1,0:T(8,128)(2,1)}, u32[]{:S(2)}, u32[]{:S(2)}) collective-permute-start(bf16[768,1152]{1,0:T(8,128)(2,1)} %add_convert_fusion.1), channel_id=1, source_target_pairs={{0,16},{8,24},{16,0},{24,8},{1,17},{9,25},{17,1},{25,9},{2,18},{10... | collective-permute-start | bytes 5308424 | tf_op jit(solution)/shard_map/ppermute | solution.py:41
  542.9 39.9 %collective-permute-start.56 = (f32[1,11264]{1,0:T(1,128)S(1)}, f32[1,11264]{1,0:T(1,128)S(1)}, u32[]{:S(2)}, u32[]{:S(2)}) collective-permute-start(f32[1,11264]{1,0:T(1,128)S(1)} %constant_dynamic-update-slice_fusion.10), channel_id=1, source_target_pairs={{0,16},{8,24},{16,0},{24,8},{1,17},{9,25},{17,1},{25,9},{2,18},{10... | collective-permute-start | bytes 135176 | tf_op jit(solution)/shard_map/ppermute | solution.py:41
  546.0 56.1 %collective-permute-start.66 = (bf16[144,640]{1,0:T(8,128)(2,1)S(1)}, bf16[144,640]{1,0:T(8,128)(2,1)S(1)}, u32[]{:S(2)}, u32[]{:S(2)}) collective-permute-start(bf16[144,640]{1,0:T(8,128)(2,1)S(1)} %add_convert_fusion.14), channel_id=1, source_target_pairs={{0,4},{1,5},{2,6},{3,7},{4,0},{5,1},{6,2},{7,3},{8,12},{9,13},{10,... | collective-permute-start | bytes 552968 | tf_op jit(solution)/shard_map/ppermute | solution.py:41
  615.5 46.1 %collective-permute-start.42 = (bf16[768,1152]{1,0:T(8,128)(2,1)}, bf16[768,1152]{1,0:T(8,128)(2,1)}, u32[]{:S(2)}, u32[]{:S(2)}) collective-permute-start(bf16[768,1152]{1,0:T(8,128)(2,1)} %convolution_convert_fusion.4), channel_id=1, source_target_pairs={{0,8},{8,0},{16,24},{24,16},{1,9},{9,1},{17,25},{25,17},{2,10},{10... | collective-permute-start | bytes 5308424 | tf_op jit(solution)/shard_map/ppermute | solution.py:41
  617.0 33.5 %collective-permute-start.71 = (bf16[144,2176]{1,0:T(8,128)(2,1)}, bf16[144,2176]{1,0:T(8,128)(2,1)}, u32[]{:S(2)}, u32[]{:S(2)}) collective-permute-start(bf16[144,2176]{1,0:T(8,128)(2,1)} %reduce-scatter.5.cloned.1.call-done), channel_id=1, source_target_pairs={{0,16},{8,24},{16,0},{24,8},{1,17},{9,25},{17,1},{25,9},{2,18},{10... | collective-permute-start | bytes 1880072 | tf_op jit(solution)/shard_map/ppermute | solution.py:41
  651.7 53.5 %collective-permute-start.72 = (f32[144,2176]{1,0:T(8,128)S(1)}, f32[144,2176]{1,0:T(8,128)S(1)}, u32[]{:S(2)}, u32[]{:S(2)}) collective-permute-start(f32[144,2176]{1,0:T(8,128)S(1)} %convert_add_fusion), channel_id=1, source_target_pairs={{0,8},{8,0},{16,24},{24,16},{1,9},{9,1},{17,25},{25,17},{2,10},{10... | collective-permute-start | bytes 3760136 | tf_op jit(solution)/shard_map/ppermute | solution.py:41
  (118 other events, 1607.3 us)
Sparse Core Ops, SparseCore 0:
  159.1 107.7 all-gather.1
  343.4 97.1 reduce-scatter.4
  491.4 121.2 reduce-scatter.2

commit v3 on v2

--- a/solution.py
+++ b/solution.py
@@ -147,10 +147,11 @@
 
 def weight_grad_kernel(pairs, count, rows, pos_ref, *refs):
     lefts, rights = refs[:pairs], refs[pairs : 2 * pairs]
-    keep_ref, send_ref = refs[2 * pairs : 2 * pairs + 2]
+    keep_ref, send_ref, sum_ref = refs[2 * pairs :]
     total = dot(lefts[0][...], rights[0][...], TN)
     for i in range(1, pairs):
         total += dot(lefts[i][...], rights[i][...], TN)
+    sum_ref[...] = sum(dot(jnp.ones((8, r.shape[0]), BF16), r[...]) for r in rights)
     for shard in range(count):
         start = pl.multiple_of(pos_ref[shard], 16)
         block = total[shard * rows : (shard + 1) * rows].astype(BF16)
@@ -178,7 +179,9 @@
         for d in range(count):
             back[rel_position(d, count)] = d
         placed = jnp.take(by_distance, jnp.array(back), axis=0).reshape(width, cols)
-        return placed[: width // 2], placed[width // 2 :]
+        ones = [jnp.ones((8, b.shape[0]), BF16) for b in rights]
+        sums = sum(dot(one, b) for one, b in zip(ones, rights))
+        return placed[: width // 2], placed[width // 2 :], sums
     positions = jnp.concatenate([table[order] % half * rows, (me & 1)[None]]).astype(jnp.int32)
     tile = 256
     pairs = len(lefts)
@@ -186,7 +189,8 @@
     moved = sum(2 * a.shape[0] * (width + cols) for a in lefts) + 2 * width * cols
     return pl.pallas_call(
         functools.partial(weight_grad_kernel, pairs, count, rows),
-        out_shape=[jax.ShapeDtypeStruct((width // 2, cols), BF16)] * 2,
+        out_shape=[jax.ShapeDtypeStruct((width // 2, cols), BF16)] * 2
+        + [jax.ShapeDtypeStruct((8, cols), F32)],
         grid_spec=pltpu.PrefetchScalarGridSpec(
             num_scalar_prefetch=1,
             grid=(pl.cdiv(cols, tile),),
@@ -195,7 +199,8 @@
                 for a in lefts
             ]
             + [pl.BlockSpec((b.shape[0], tile), lambda n, off: (0, n)) for b in rights],
-            out_specs=[pl.BlockSpec((width // 2, tile), lambda n, off: (0, n))] * 2,
+            out_specs=[pl.BlockSpec((width // 2, tile), lambda n, off: (0, n))] * 2
+            + [pl.BlockSpec((8, tile), lambda n, off: (0, n))],
         ),
         compiler_params=params(("arbitrary",)),
         cost_estimate=pl.CostEstimate(flops=flops, transcendentals=0, bytes_accessed=moved),
@@ -304,7 +309,7 @@
     )(core, own, other, inputs, weight, bias, gain, shift)
 
 
-def norm_back_values(x_ref, grads, gain_ref, add_ref, dg_ref, ds_ref):
+def norm_back_values(x_ref, grads, gain_ref, add_ref, lines_ref):
     hat, inverse = normalized(x_ref[...].astype(F32))
     grad = grads[0][...].astype(F32)
     for other in grads[1:]:
@@ -315,41 +320,58 @@
 
     @pl.when(pl.program_id(0) == 0)
     def _():
-        dg_ref[...] = jnp.zeros_like(dg_ref)
-        ds_ref[...] = jnp.zeros_like(ds_ref)
-
-    dg_ref[...] += jnp.sum(grad * hat, axis=0, keepdims=True)
-    ds_ref[...] += jnp.sum(grad, axis=0, keepdims=True)
+        lines_ref[...] = jnp.zeros_like(lines_ref)
+
+    lines_ref[0:1] += jnp.sum(grad * hat, axis=0, keepdims=True)
+    lines_ref[1:2] += jnp.sum(grad, axis=0, keepdims=True)
     return add_ref[...].astype(F32) + inverse * (scaled - first - hat * second)
 
 
-def first_back(values, grads, gain, add):
+def first_back(core, values, grads, gain, add, q_sums, kv_sums, half):
     rows, width = values.shape
     block = row_block(rows)
     count = len(grads)
-
-    def kernel(x_ref, *refs):
-        gain_ref, add_ref, dx_ref, dg_ref, ds_ref = refs[count:]
-        dx_ref[...] = norm_back_values(x_ref, refs[:count], gain_ref, add_ref, dg_ref, ds_ref)
-
-    wide = pl.BlockSpec((block, width), lambda i: (i, 0))
-    line = pl.BlockSpec((1, width), lambda i: (0, 0))
+    padded = q_sums.shape[1]
+
+    def kernel(core_ref, x_ref, *refs):
+        gain_ref, add_ref, q_ref, kv_ref, dx_ref, lines_ref = refs[count:]
+        dx_ref[...] = norm_back_values(x_ref, refs[:count], gain_ref, add_ref, lines_ref)
+        for line, part in ((2, q_ref[0:1, :half]), (3, kv_ref[0:1, padded : padded + half])):
+            none = jnp.zeros_like(part)
+
+            @pl.when(core_ref[0] == 0)
+            def _():
+                lines_ref[line : line + 1] = jnp.concatenate([part, none], axis=1)
+
+            @pl.when(core_ref[0] != 0)
+            def _():
+                lines_ref[line : line + 1] = jnp.concatenate([none, part], axis=1)
+
+    wide = pl.BlockSpec((block, width), lambda i, c: (i, 0))
     return pl.pallas_call(
         kernel,
         out_shape=(
             jax.ShapeDtypeStruct((rows, width), F32),
-            jax.ShapeDtypeStruct((1, width), F32),
-            jax.ShapeDtypeStruct((1, width), F32),
-        ),
-        grid=(rows // block,),
-        in_specs=[wide] * (1 + count) + [line, wide],
-        out_specs=(wide, line, line),
+            jax.ShapeDtypeStruct((8, width), F32),
+        ),
+        grid_spec=pltpu.PrefetchScalarGridSpec(
+            num_scalar_prefetch=1,
+            grid=(rows // block,),
+            in_specs=[wide] * (1 + count)
+            + [
+                pl.BlockSpec((1, width), lambda i, c: (0, 0)),
+                wide,
+                pl.BlockSpec(q_sums.shape, lambda i, c: (0, 0)),
+                pl.BlockSpec(kv_sums.shape, lambda i, c: (0, 0)),
+            ],
+            out_specs=(wide, pl.BlockSpec((8, width), lambda i, c: (0, 0))),
+        ),
         compiler_params=params(("arbitrary",)),
         cost_estimate=pl.CostEstimate(
             flops=20 * rows * width, transcendentals=0, bytes_accessed=18 * rows * width
         ),
         name="first_back",
-    )(values, *grads, gain, add)
+    )(core, values, *grads, gain, add, q_sums, kv_sums)
 
 
 def second_back(core, values, grads, gain, add, weight, half, padded):
@@ -358,17 +380,13 @@
     count = len(grads)
 
     def kernel(core_ref, x_ref, *refs):
-        gain_ref, add_ref, w_ref, dx_ref, low_ref, mine_ref, send_ref, db_ref, dg_ref, ds_ref = refs[count:]
-        total = norm_back_values(x_ref, refs[:count], gain_ref, add_ref, dg_ref, ds_ref)
+        gain_ref, add_ref, w_ref, dx_ref, low_ref, mine_ref, send_ref, lines_ref = refs[count:]
+        total = norm_back_values(x_ref, refs[:count], gain_ref, add_ref, lines_ref)
         low = total.astype(BF16)
         dx_ref[...] = total
         low_ref[...] = low
-
-        @pl.when(pl.program_id(0) == 0)
-        def _():
-            db_ref[...] = jnp.zeros_like(db_ref)
-
-        db_ref[...] += jnp.sum(low.astype(F32), axis=0, keepdims=True)
+        lines_ref[2:3] += jnp.sum(low.astype(F32), axis=0, keepdims=True)
+        lines_ref[3:4] += jnp.sum(add_ref[...].astype(F32), axis=0, keepdims=True)
         back = dot(low, w_ref[...], NT).astype(BF16)
         empty = jnp.zeros((block, padded - half), BF16)
         halves = [jnp.concatenate([back[:, i * half : (i + 1) * half], empty], axis=1) for i in range(2)]
@@ -392,15 +410,13 @@
             jax.ShapeDtypeStruct((rows, width), BF16),
             jax.ShapeDtypeStruct((rows, padded), BF16),
             jax.ShapeDtypeStruct((rows, padded), BF16),
-            jax.ShapeDtypeStruct((1, width), F32),
-            jax.ShapeDtypeStruct((1, width), F32),
-            jax.ShapeDtypeStruct((1, width), F32),
+            jax.ShapeDtypeStruct((8, width), F32),
         ),
         grid_spec=pltpu.PrefetchScalarGridSpec(
             num_scalar_prefetch=1,
             grid=(rows // block,),
             in_specs=[wide] * (1 + count) + [line, wide, square],
-            out_specs=(wide, wide, part, part, line, line, line),
+            out_specs=(wide, wide, part, part, pl.BlockSpec((8, width), lambda i, c: (0, 0))),
         ),
         compiler_params=params(("arbitrary",)),
         cost_estimate=pl.CostEstimate(
@@ -408,6 +424,43 @@
         ),
         name="second_back",
     )(core, values, *grads, gain, add, weight)
+
+
+def shards_kernel(half, padded, cut, core_ref, q_ref, k_ref, v_ref, o_ref, qkv_ref, out_ref):
+    empty = jnp.zeros((q_ref.shape[0], padded - half), BF16)
+    for core in range(2):
+
+        @pl.when(core_ref[0] == core)
+        def _():
+            for i, ref in enumerate((q_ref, k_ref, v_ref)):
+                part = ref[:, core * half : (core + 1) * half]
+                qkv_ref[:, i * padded : (i + 1) * padded] = jnp.concatenate([part, empty], axis=1)
+            out_ref[...] = o_ref[:, core * cut : core * cut + padded]
+
+
+def attention_shards(core, weights, half, padded):
+    rows, width = weights[0].shape
+    return pl.pallas_call(
+        functools.partial(shards_kernel, half, padded, width - padded),
+        out_shape=(
+            jax.ShapeDtypeStruct((rows, 3 * padded), BF16),
+            jax.ShapeDtypeStruct((rows, padded), BF16),
+        ),
+        grid_spec=pltpu.PrefetchScalarGridSpec(
+            num_scalar_prefetch=1,
+            grid=(1,),
+            in_specs=[pl.BlockSpec((rows, width), lambda i, c: (0, 0))] * 4,
+            out_specs=(
+                pl.BlockSpec((rows, 3 * padded), lambda i, c: (0, 0)),
+                pl.BlockSpec((rows, padded), lambda i, c: (0, 0)),
+            ),
+        ),
+        compiler_params=params(("arbitrary",)),
+        cost_estimate=pl.CostEstimate(
+            flops=0, transcendentals=0, bytes_accessed=16 * rows * width
+        ),
+        name="attention_shards",
+    )(core, *weights)
 
 
 def hidden(arrays, weight, bias):
@@ -741,47 +794,52 @@
         second = jnp.pad(second, grow + [(0, padded_size - second.shape[-1])])
         return jnp.where(is_first, first, second)
 
-    vectors = jnp.stack(
-        [
-            first_gain,
-            first_shift,
-            query_bias,
-            value_bias,
-            output_bias,
-            second_gain,
-            second_shift,
-            down_bias,
-        ]
-    )
-    vector_parts = gather_direct(vectors)
-    shard_qkv = jnp.concatenate(
-        [my_half(w, half, padded) for w in (query_weight, key_weight, value_weight)], axis=1
-    )
-    shard_out = jnp.where(is_first, output_weight[:, :out_cols], output_weight[:, out_cut:])
-    shard_hidden = my_half(hidden_weight, ff_half, ff_half)
-    shard_down = my_half(down_weight.T, ff_half, ff_half)
     inputs = patches.reshape(flat, width)
     incoming = cotangent.reshape(flat, width)
+    shard_qkv, shard_out = attention_shards(
+        core_flag, [query_weight, key_weight, value_weight, output_weight], half, padded
+    )
     raw = {0: inputs}
     for bit in bits_of(seq_count):
         raw.update({j | bit: swap(part, "seq", bit) for j, part in list(raw.items())})
-    incoming_near = jnp.concatenate([incoming, swap(incoming, "seq", 1)], axis=0)
-
     staged = shards == 8
-    shard_qkv = after(shard_qkv, *vector_parts.values())
+    y, z, zz = 1, 2, 4
+    q = {0: shard_qkv}
     if staged:
-        q = {0: shard_qkv}
-        q[4], q[1] = swap(q[0], "fsdp", 4), swap(q[0], "fsdp", 1)
-        o = {0: after(shard_out, q[1])}
-        o[1] = swap(o[0], "fsdp", 1)
-        q[2], q[5] = swap(after(q[0], q[4]), "fsdp", 2), swap(q[4], "fsdp", 1)
-        q[6], q[3] = swap(after(q[4], q[2]), "fsdp", 2), swap(after(q[2], q[5]), "fsdp", 1)
-        o[4], o[5] = swap(after(o[0], q[6]), "fsdp", 4), swap(after(o[1], q[6]), "fsdp", 4)
-        q[7] = swap(after(q[6], q[3]), "fsdp", 1)
-        h = {0: after(shard_hidden, q[7])}
-        h[4], h[1] = swap(h[0], "fsdp", 4), swap(h[0], "fsdp", 1)
+        q[z], q[zz], q[y] = (swap(q[0], "fsdp", bit) for bit in (z, zz, y))
+        early = (q[y],)
     else:
-        q, o, h = gather_all(shard_qkv), gather_all(shard_out), gather_all(shard_hidden)
+        q, early = gather_all(shard_qkv), (shard_qkv,)
+    vectors = after(
+        jnp.stack(
+            [
+                first_gain,
+                first_shift,
+                query_bias,
+                value_bias,
+                output_bias,
+                second_gain,
+                second_shift,
+                down_bias,
+            ]
+        ),
+        shard_qkv,
+    )
+    vector_parts = gather_all(vectors)
+    shard_hidden = my_half(after(hidden_weight, shard_qkv), ff_half, ff_half)
+    shard_down = my_half(after(down_weight, shard_qkv).T, ff_half, ff_half)
+    incoming_near = jnp.concatenate([incoming, swap(after(incoming, *early), "seq", 1)], axis=0)
+    if staged:
+        o, h, d = {0: after(shard_out, q[y])}, {0: after(shard_hidden, q[y])}, {0: shard_down}
+        o[y], h[y] = swap(o[0], "fsdp", y), swap(h[0], "fsdp", y)
+        q[zz | z] = swap(after(q[zz], q[z]), "fsdp", z)
+        q[z | y], q[zz | y] = swap(q[z], "fsdp", y), swap(after(q[zz], q[z]), "fsdp", y)
+        o[zz], o[zz | y] = (swap(after(o[k], q[zz]), "fsdp", zz) for k in (0, y))
+        q[zz | z | y] = swap(after(q[zz | z], q[z | y], q[zz | y]), "fsdp", y)
+        h[z], h[zz] = (swap(after(h[0], q[zz | z], o[zz]), "fsdp", bit) for bit in (z, zz))
+        d[y] = swap(after(d[0], q[zz | z | y]), "fsdp", y)
+    else:
+        o, h, d = gather_all(shard_out), gather_all(shard_hidden), gather_all(shard_down)
 
     stacked = in_order(vector_parts, me).transpose(1, 0, 2).reshape(8, width).astype(F32)
     gain_one, shift_one, bias_query, bias_value, bias_output, gain_two, shift_two, bias_down = [
@@ -805,49 +863,55 @@
     seg_rows, seg_cols = segment, segment[..., None]
     seg_near_row, seg_near_col = near_flat[:, None], near_flat[..., None]
 
-    normed_near = norm([raw[0], raw[1]], gain_one, shift_one)
-    normed_far = norm([raw[j] for j in range(2, seq_count)], gain_one, shift_one)
+    raw_near, incoming_near = after(raw[1], incoming_near), after(incoming_near, raw[1])
+    normed_near = norm([raw[0], raw_near], gain_one, shift_one)
+    normed_far = norm([after(raw[j], normed_near) for j in range(2, seq_count)], gain_one, shift_one)
     bias_q = my_half(bias_query, half, padded)
     bias_kv = jnp.concatenate([jnp.zeros((1, padded), F32), my_half(bias_value, half, padded)], axis=1)
+    q = {k: after(part, normed_far) for k, part in q.items()}
     w_q, w_kv = chain.done(*assemble(q, me, padded))
     near_in, w_q, w_kv = chain(normed_near, w_q, w_kv)
+    if staged:
+        h[z], h[zz], near_in = chain(h[z], h[zz], near_in)
+        h[zz | z] = swap(h[zz], "fsdp", z)
+        h[z | y], h[zz | y] = swap(h[z], "fsdp", y), swap(h[zz], "fsdp", y)
+        for k in (0, y, zz, zz | y):
+            o[k | z] = swap(after(o[k], h[zz], h[z]), "fsdp", z)
     query = (dot(near_in, w_q) + bias_q).astype(BF16)
     near = (dot(near_in, w_kv) + bias_kv).astype(BF16)
     chain.done(query, near)
+    far_in, w_kv = chain(normed_far, w_kv)
     if staged:
-        far_in, w_kv, h[4], h[1], o[4], o[5] = chain(normed_far, w_kv, h[4], h[1], o[4], o[5])
-        h[2], h[5] = swap(after(h[0], h[4]), "fsdp", 2), swap(h[4], "fsdp", 1)
-        o[2], o[3] = swap(after(o[0], o[4]), "fsdp", 2), swap(after(o[1], o[4]), "fsdp", 2)
-        o[6], o[7] = swap(o[4], "fsdp", 2), swap(o[5], "fsdp", 2)
-    else:
-        far_in = chain(normed_far)
+        h[zz | z], far_in = chain(h[zz | z], far_in)
+        h[zz | z | y] = swap(h[zz | z], "fsdp", y)
     far = chain.done((dot(far_in, w_kv) + bias_kv).astype(BF16))
     query = query.reshape(2, rows, tokens, padded)
     near = near.reshape(2, rows, tokens, 2 * padded)
     far = far.reshape(seq_count - 2, rows, tokens, 2 * padded)
-    gate = after(shard_down, *([h[4], h[1]] if staged else []))
-    w_down = lax.all_gather(gate, "fsdp", axis=0, tiled=True)
+    if staged:
+        *rest, query = chain(*o.values(), query)
+        o = dict(zip(o, rest))
+        d[z], d[zz] = (swap(after(d[0], *rest), "fsdp", bit) for bit in (z, zz))
     found = ()
     for row in range(rows):
         query, near, far = chain(query, near, far)
-        if staged and row == 1:
-            query, h[2], h[5] = chain(query, h[2], h[5])
-            h[6], h[3] = swap(after(h[4], h[2]), "fsdp", 2), swap(after(h[2], h[5]), "fsdp", 1)
-        if staged and row == 2:
-            query, h[6], h[3] = chain(query, h[6], h[3])
-            h[7] = swap(after(h[6], h[3]), "fsdp", 1)
-        found = attend(row, query, near, far, need, seg_near_col, seg_rows, heads, found)
-        chain.done(*found)
+        found = chain.done(*attend(row, query, near, far, need, seg_near_col, seg_rows, heads, found))
+        if row == rows - 2:
+            o = dict(zip(o, chain(*o.values())))
+            w_out_mine = chain.done(assemble(o, me))
+            w_out_other = swap(w_out_mine, "seq", 1)
     out_own, out_pair, lse = found
     other_half = swap(out_pair, "seq", 1).reshape(flat, padded)
-    o = dict(zip(o, chain(*o.values())))
-    w_out_mine = assemble(o, me)
-    w_out_other = swap(w_out_mine, "seq", 1)
+    w_out_mine, w_out_other = chain(w_out_mine, w_out_other)
     w_out = jnp.where(
         is_first,
         jnp.concatenate([w_out_mine[:, :out_cut], w_out_other], axis=1),
         jnp.concatenate([w_out_other[:, :out_cut], w_out_mine], axis=1),
     )
+    if staged:
+        d[z], d[zz], w_out = chain(d[z], d[zz], w_out)
+        d[zz | z] = swap(d[zz], "fsdp", z)
+        d[z | y], d[zz | y] = swap(d[z], "fsdp", y), swap(d[zz], "fsdp", y)
     attended, middle, second = join(
         core_flag,
         out_own.reshape(flat, padded),
@@ -863,6 +927,9 @@
     chain.done(second)
     h = dict(zip(h, chain(*h.values())))
     w_hidden = chain.done(assemble(h, me))
+    if staged:
+        d[zz | z], w_hidden = chain(d[zz | z], w_hidden)
+        d[zz | z | y] = swap(d[zz | z], "fsdp", y)
     bias_hidden = my_half(hidden_bias.astype(F32)[None], ff_half, ff_half)
     second, second_pair, w_hidden = chain(second, second_pair, w_hidden)
     act, slope, second_near = chain.done(*hidden([second, second_pair], w_hidden, bias_hidden))
@@ -870,7 +937,9 @@
     incoming_near, act = chain(incoming_near, act)
     grad_down = chain.done(dot(incoming_near, act, TN).astype(BF16))
     part_down = lax.psum_scatter(grad_down, "fsdp", scatter_dimension=0, tiled=True)
-    incoming_near, slope = chain(incoming_near, slope)
+    d = dict(zip(d, chain(*d.values())))
+    w_down = chain.done(assemble(d, me))
+    incoming_near, slope, w_down = chain(incoming_near, slope, w_down)
     grad_pre = chain.done((dot(incoming_near, w_down) * slope.astype(F32)).astype(BF16))
     grad_pre = chain(grad_pre)
     back = chain.done(dot(grad_pre, w_hidden, NT).astype(BF16))
@@ -879,13 +948,13 @@
     grad_hidden = chain.done(dot(second_near, grad_pre, TN).astype(BF16))
     part_hidden = lax.psum_scatter(grad_hidden, "fsdp", scatter_dimension=0, tiled=True)
     back, back_other = chain(back, back_other)
-    grad_middle, branch, grad_mine, grad_send, grad_bias_out, grad_gain_two, grad_shift_two = second_back(
+    grad_middle, branch, grad_mine, grad_send, lines = second_back(
         core_flag, middle, [back[:flat], back_other], gain_two, incoming, w_out, half, padded
     )
     chain.done(branch)
     grad_pair = swap(grad_send, "seq", 1)
     attended, branch = chain(attended, branch)
-    out_keep, out_send = chain.done(*weight_grad([attended], [branch], me, shards))
+    out_keep, out_send, _ = chain.done(*weight_grad([attended], [branch], me, shards))
 
     def core_part(array):
         low, high = array[:, :out_cols], array[:, out_cut:]
@@ -894,22 +963,46 @@
     keep_mine, keep_other = core_part(out_keep)
     send_mine, send_other = core_part(out_send)
     keep_back, send_back = swap(keep_other, "seq", 1), swap(send_other, "seq", 1)
-    grad_hidden_bias = column_sum(grad_pre)
-
+    grad_pre = chain(grad_pre)
+    hidden_line = chain.done(column_sum(grad_pre))
+
+    links = [("seq", bit) for bit in bits_of(seq_count)] + [("fsdp", bit) for bit in bits_of(shards)]
+    todo = list(links)
+    small = [lines, hidden_line]
+    moving = []
+
+    def small_step(guard):
+        nonlocal small, moving
+        if moving:
+            *moving, guard = chain(*moving, guard)
+            small = [a + b for a, b in zip(small, moving)]
+            moving = []
+        if todo:
+            axis, bit = todo.pop(0)
+            parts = small if (axis, bit) != ("seq", 1) else small[:1]
+            moving = [swap(part, axis, bit) for part in parts]
+            if len(parts) < len(small):
+                moving.append(jnp.zeros_like(small[1]))
+        return guard
+
+    branch = small_step(branch)
     shape = (rows, tokens, padded)
     grads = [grad_mine.reshape(shape), grad_pair.reshape(shape)]
     found = ()
     for row in range(rows):
         query, near, far, *grads = chain(query, near, far, *grads)
+        if row >= 1:
+            query = small_step(query)
         if row == 1:
             keep_back, send_back, query = chain(keep_back, send_back, query)
             out_keep = (keep_mine.astype(F32) + keep_back.astype(F32)).astype(BF16)
             out_send = (send_mine.astype(F32) + send_back.astype(F32)).astype(BF16)
             out_back = swap(out_send, "fsdp", 1)
         if row == 2:
-            out_back, query = chain(out_back, query)
+            out_back, part_down, query = chain(out_back, part_down, query)
             out_keep, out_send = scatter_step(out_keep, out_back, shard_rows)
             out_back = swap(out_send, "fsdp", 2)
+            down_seq = swap(part_down, "seq", bits_of(seq_count)[0])
         found = attend_back(
             row,
             query,
@@ -926,13 +1019,27 @@
         )
         chain.done(*found)
     dq, dnear, dfar = [g.reshape(-1, g.shape[-1]) for g in found]
-    dfar, w_kv = chain(dfar, w_kv)
+    dfar, w_kv, down_seq, out_back = chain(dfar, w_kv, down_seq, out_back)
+    dfar = small_step(dfar)
+    out_keep, out_send = scatter_step(out_keep, out_back, shard_rows)
+    out_back = swap(out_send, "fsdp", 4) if out_send is not None else None
+
+    def seq_rest(mine, arrived):
+        total = mine.astype(F32) + arrived.astype(F32)
+        for bit in bits_of(seq_count)[1:-1]:
+            mine = total.astype(BF16)
+            total = mine.astype(F32) + swap(mine, "seq", bit).astype(F32)
+        return total
+
+    top = bits_of(seq_count)[0]
+    down_total = seq_rest(part_down, down_seq)
+    down_other = swap(down_total, "seq", 1)
     back_far = chain.done(dot(dfar, w_kv, NT).astype(BF16))
     far_parts = {j: back_far[(j - 2) * flat : (j - 1) * flat] for j in range(2, seq_count)}
     far_sent = {j: swap(part, "seq", 1) for j, part in far_parts.items() if j & 1}
     normed_near, normed_far, dnear, dfar = chain(normed_near, normed_far, dnear, dfar)
-    kv_keep, kv_send = weight_grad([normed_near, normed_far], [dnear, dfar], me, shards)
-    chain.done(kv_keep, kv_send)
+    dnear = small_step(dnear)
+    kv_keep, kv_send, kv_sums = chain.done(*weight_grad([normed_near, normed_far], [dnear, dfar], me, shards))
     kv_back = swap(kv_send, "fsdp", 1)
     far_sent = {j: chain(part) for j, part in far_sent.items()}
     far_sums = {
@@ -950,112 +1057,112 @@
                 arrived.append(part)
             else:
                 far_sums[j ^ bit] = (far_sums[j ^ bit].astype(F32) + part.astype(F32)).astype(BF16)
-    normed_near, dq, out_back = chain(normed_near, dq, out_back)
-    out_keep, out_send = scatter_step(out_keep, out_back, shard_rows)
-    out_back = swap(out_send, "fsdp", 4) if out_send is not None else None
-    q_keep, q_send = chain.done(*weight_grad([normed_near], [dq], me, shards))
+    normed_near, dq = chain(normed_near, dq)
+    dq = small_step(dq)
+    q_keep, q_send, q_sums = chain.done(*weight_grad([normed_near], [dq], me, shards))
     q_back = swap(q_send, "fsdp", 1)
     dq, dnear = chain(dq, dnear)
     back_near = chain.done((dot(dq, w_q, NT) + dot(dnear, w_kv, NT)).astype(BF16))
     pair_back = swap(back_near[flat:], "seq", 1)
-
-    def next_bits(keep, back, bits):
-        for bit in bits:
-            keep, send = scatter_step(keep, back, shard_rows)
-            if send is not None:
-                back = swap(send, "fsdp", bit)
-        return keep
+    while todo or moving:
+        dnear = small_step(dnear)
+
+    lines_all = small
 
     act, middle = chain(act, middle)
     down_pair = chain.done(dot(act[flat:], w_down, NT).astype(BF16))
     down_back = swap(down_pair, "seq", 1)
-    rest = [2 << k for k in range(shards.bit_length() - 2)] + [0]
-    kv_back, q_back = chain(kv_back, q_back)
-    kv_sum = next_bits(kv_keep, kv_back, rest)
-    q_sum = next_bits(q_keep, q_back, rest)
-    out_sum = next_bits(out_keep, out_back, rest[2:]) if shards >= 8 else out_keep
-    act, down_back = chain(act, down_back)
+    act, down_back, middle = chain(act, down_back, middle)
     result = middle + dot(act[:flat], w_down, NT) + down_back.astype(F32) + bias_down
     layer_output = chain.done(result.astype(BF16)).reshape(rows, tokens, width)
-    grad_patches, grad_gain_one, grad_shift_one = first_back(
-        inputs, [back_near[:flat], pair_back] + arrived, gain_one, grad_middle
+
+    later = [2 << k for k in range(shards.bit_length() - 2)]
+
+    def next_step(keep, back, bits):
+        back = chain(back)
+        keep, send = scatter_step(keep, back, shard_rows)
+        chain.done(keep)
+        return keep, swap(send, "fsdp", bits.pop(0)) if bits else None
+
+    kv_bits, q_bits, out_bits = list(later), list(later), list(later[2:])
+    kv_keep, kv_back = next_step(kv_keep, kv_back, kv_bits)
+    if out_back is not None:
+        out_keep, out_back = next_step(out_keep, out_back, out_bits)
+        while out_back is not None:
+            out_keep, out_back = next_step(out_keep, out_back, out_bits)
+    out_seq = swap(out_keep, "seq", top)
+    pair_back, *arrived = chain(pair_back, *arrived)
+    grad_patches, late = first_back(
+        core_flag,
+        inputs,
+        [back_near[:flat], pair_back] + arrived,
+        gain_one,
+        grad_middle,
+        q_sums,
+        kv_sums,
+        half,
     )
-
-    def widen(own, size):
-        own = own[:, :size]
-        none = jnp.zeros_like(own)
-        return jnp.where(
-            is_first, jnp.concatenate([own, none], axis=1), jnp.concatenate([none, own], axis=1)
-        )
-
-    grad_bias_value = column_sum(dnear[:, padded:]) + column_sum(dfar[:, padded:])
-    early = jnp.concatenate(
-        [
-            widen(column_sum(dq), half),
-            widen(grad_bias_value, half),
-            grad_bias_out,
-            grad_gain_two,
-            grad_shift_two,
-            column_sum(incoming),
-            widen(grad_hidden_bias, ff_half),
-        ],
-        axis=1,
-    )
-    late = jnp.concatenate([grad_gain_one, grad_shift_one], axis=1)
-
-    def everywhere(bundle):
-        for axis in ("seq", "fsdp"):
-            for bit in bits_of(lax.axis_size(axis)):
-                bundle = bundle + swap(bundle, axis, bit)
-        return bundle
-
-    early, late = everywhere(early), everywhere(late)
-
-    def owned(bundle, i):
-        return lax.dynamic_slice_in_dim(
-            bundle[0, i * width : (i + 1) * width], me * shard_rows, shard_rows, 0
-        )
-
-    hidden_total = early[0, 6 * width : 6 * width + ff]
-
-    def whole(mine, size, total):
-        other = swap(mine, "seq", 1)
+    chain.done(grad_patches)
+    small, todo, moving = [late], list(links[1:]) + links[:1], []
+    part_hidden = chain(part_hidden)
+    hidden_seq = swap(part_hidden, "seq", top)
+    late_guard = small_step(part_hidden)
+    while q_back is not None or kv_back is not None:
+        if kv_back is not None:
+            kv_keep, kv_back = next_step(kv_keep, kv_back, kv_bits)
+        late_guard = small_step(late_guard)
+        if q_back is not None:
+            q_keep, q_back = next_step(q_keep, q_back, q_bits)
+    kv_seq, q_seq = swap(kv_keep, "seq", top), swap(q_keep, "seq", top)
+    hidden_seq = chain(hidden_seq)
+    hidden_total = chain.done(seq_rest(part_hidden, hidden_seq))
+    hidden_other = swap(hidden_total, "seq", 1)
+    while todo or moving:
+        late_guard = small_step(late_guard)
+    (late,) = small
+
+    own_lines = lax.dynamic_slice_in_dim(lines_all[0], me * shard_rows, shard_rows, 1)
+    late_lines = lax.dynamic_slice_in_dim(late, me * shard_rows, shard_rows, 1)
+
+    def whole(mine, other, size, total):
         return jnp.where(
             is_first,
             jnp.concatenate([mine[:, :size], other[:, : total - size]], axis=1),
             jnp.concatenate([other[:, :size], mine[:, : total - size]], axis=1),
         )
 
-    full_down = whole(seq_sum(part_down), ff_half, ff).T
-    full_hidden = whole(seq_sum(part_hidden), ff_half, ff)
-    out_total, q_total, kv_total = seq_sum(out_sum), seq_sum(q_sum), seq_sum(kv_sum)
-    other_out = swap(out_total, "seq", 1)
+    bias_line = lines_all[1]
+    full_bias = whole(bias_line, swap(bias_line, "seq", 1), ff_half, ff)[0]
+    full_down = whole(down_total, down_other, ff_half, ff).T
+    full_hidden = whole(hidden_total, hidden_other, ff_half, ff)
+    out_total, q_total, kv_total = seq_rest(out_keep, out_seq), seq_rest(q_keep, q_seq), seq_rest(kv_keep, kv_seq)
+    out_other, q_other, kv_other = [swap(a, "seq", 1) for a in (out_total, q_total, kv_total)]
     full_out = jnp.where(
         is_first,
-        jnp.concatenate([out_total[:, :out_cut], other_out], axis=1),
-        jnp.concatenate([other_out[:, :out_cut], out_total], axis=1),
+        jnp.concatenate([out_total[:, :out_cut], out_other], axis=1),
+        jnp.concatenate([out_other[:, :out_cut], out_total], axis=1),
     )
-    full_query = whole(q_total, half, width)
-    full_key = whole(kv_total[:, :padded], half, width)
-    full_value = whole(kv_total[:, padded:], half, width)
+    full_query = whole(q_total, q_other, half, width)
+    full_key = whole(kv_total[:, :padded], kv_other[:, :padded], half, width)
+    full_value = whole(kv_total[:, padded:], kv_other[:, padded:], half, width)
     return (
         layer_output,
         grad_patches.reshape(rows, tokens, width),
-        owned(late, 0),
-        owned(late, 1),
+        late_lines[0],
+        late_lines[1],
         full_query,
-        owned(early, 0),
+        late_lines[2],
         full_key,
         full_value,
-        owned(early, 1),
+        late_lines[3],
         full_out,
-        owned(early, 2),
-        owned(early, 3),
-        owned(early, 4),
+        own_lines[2],
+        own_lines[0],
+        own_lines[1],
         full_hidden,
-        hidden_total,
+        full_bias,
         full_down,
-        owned(early, 5),
+        own_lines[3],
     )
 
 

time: 724 us -> 754 us (1.041)
  waiting for transfers between devices: 210 us -> 239 us
    ppermute x73 -> x84, waiting for transfers between devices: 210 us -> 239 us  [swap(): return lax.ppermute(array, axis, [(i, i ^ bits) for i in range(size)])]
    dot_general x17 -> x13, matrix products: 116 us -> 109 us  [dot(): lax.dot_general(left, right, (dims, ((), ())), preferred_element_type=F32)]
    ppermute x73 -> x84, starting transfers between devices: 62.9 us -> 69.1 us  [swap(): return lax.ppermute(array, axis, [(i, i ^ bits) for i in range(size)])]
    pallas_call x3 -> x4, Pallas kernels: 13.6 us -> 19.1 us  [assemble(): pl.pallas_call(functools.partial(assemble_kernel, count, rows, not cut),...]
    unnamed x139 -> x121, local copies, waits for them, and re-layouts: 14.9 us -> 16 us
  transfers between devices with their start and end apart: 76 -> 86, of which waited for: 23 -> 30; matrix products, arithmetic and copies ran while one was open for 28% -> 25% of each run, Pallas kernels for 29% -> 23%
where the time goes in v3:
time: 754 us; the launch traced here: 747 us
  waiting for transfers between devices  239 us (32%)
  Pallas kernels  207 us (27%)
  matrix products  109 us (14%)
  starting transfers between devices  69.2 us (9%)
  local copies, waits for them, and re-layouts  57 us (8%)
  other arithmetic  50.1 us (7%)
  between operations  15.3 us (2%)
    ppermute x84, waiting for transfers between devices, swap(): return lax.ppermute(array, axis, [(i, i ^ bits) for i in range(size)])  239 us
    dot_general x13, matrix products, dot(): lax.dot_general(left, right, (dims, ((), ())), preferred_element_type=F32)  109 us
    ppermute x84, starting transfers between devices, swap(): return lax.ppermute(array, axis, [(i, i ^ bits) for i in range(size)])  69.1 us
    pallas_call x3, Pallas kernels, attend_back(): pl.pallas_call(functools.partial(attend_back_kernel, row, heads, blocks,...  58.6 us
    pallas_call x3, Pallas kernels, weight_grad(): pl.pallas_call(functools.partial(weight_grad_kernel, pairs, count, rows),...  33.5 us
    pallas_call x3, Pallas kernels, attend(): pl.pallas_call(functools.partial(attend_kernel, row, heads, blocks, padde...  32.9 us
    pallas_call x4, Pallas kernels, assemble(): pl.pallas_call(functools.partial(assemble_kernel, count, rows, not cut),...  19.1 us
    pallas_call x1, Pallas kernels, hidden(): pl.pallas_call(kernel, out_shape=(jax.ShapeDtypeStruct((count * rows, col...  18.9 us
  transfers between devices with their start and end apart: 86, of which 30 were waited for; matrix products, arithmetic and copies ran while one was open for 25% of the time, Pallas kernels for 23%

profile of v3, /device:TPU:0, one launch (start us, length us, event | category | flops | bytes accessed | tf_op | source)
XLA Modules:
  0.0 746.6 jit_solution(6338676362673949747)
XLA Ops:
  69.6 19.5 %collective-permute-done.4.refs_4_ = bf16[144,1920]{1,0:T(8,128)(2,1)} collective-permute-done((bf16[144,1920]{1,0:T(8,128)(2,1)}, bf16[144,1920]{1,0:T(8,128)(2,1)}, u32[]{:S(2)}, u32[]{:S(2)}) %collective-permute-start.4) | collective-permute-done | bytes 552992 | tf_op jit(solution)/shard_map/ppermute | solution.py:41
  120.0 18.0 %collective-permute-done.5.refs_4_ = bf16[144,640]{1,0:T(8,128)(2,1)} collective-permute-done((bf16[144,640]{1,0:T(8,128)(2,1)}, bf16[144,640]{1,0:T(8,128)(2,1)}, u32[]{:S(2)}, u32[]{:S(2)}) %collective-permute-start.5) | collective-permute-done | bytes 184352 | tf_op jit(solution)/shard_map/ppermute | solution.py:41
  199.5 12.5 %attend.3 = (bf16[3,256,640]{2,1,0:T(8,128)(2,1)}, bf16[3,256,640]{2,1,0:T(8,128)(2,1)}, f32[3,8,512]{2,1,0:T(8,128)}) custom-call(s32[3,4]{1,0:T(4,128)} %convert_element_type.267.need_ref, s32[3,512,1]{2,1,0:T(8,128)} %broadcast_in_dim_reshape.8.col_ref, s32[3,4,256]{2,1,0:T(4,128)} %get-tuple-element.479.row_ref, bf16[2,3,256,640]{3,2,1,0:T(8,128)(2,1)} %bitcast.131, ...), custom_call_target="tpu_custom_call" | custom-call | flops 8589934592 | bytes 3932160 | tf_op jit(solution)/shard_map/attend/pallas_call | solution.py:609
  224.9 11.0 %attend.5 = (bf16[3,256,640]{2,1,0:T(8,128)(2,1)}, bf16[3,256,640]{2,1,0:T(8,128)(2,1)}, f32[3,8,512]{2,1,0:T(8,128)}) custom-call(s32[3,4]{1,0:T(4,128)} %convert_element_type.267.need_ref, s32[3,512,1]{2,1,0:T(8,128)} %broadcast_in_dim_reshape.8.col_ref, ...), custom_call_target="tpu_custom_call", output_to_operand_aliasing={{0}: (6, {}), {1}: (7, {}), {2}: (8, {})} | custom-call | flops 8589934592 | bytes 3932160 | tf_op jit(solution)/shard_map/attend/pallas_call | solution.py:609
  246.1 25.2 %collective-permute-done.30.refs_4_ = bf16[144,2176]{1,0:T(8,128)(2,1)} collective-permute-done((bf16[144,2176]{1,0:T(8,128)(2,1)}, bf16[144,2176]{1,0:T(8,128)(2,1)}, u32[]{:S(2)}, u32[]{:S(2)}) %collective-permute-start.30) | collective-permute-done | bytes 626720 | tf_op jit(solution)/shard_map/ppermute | solution.py:41
  288.5 10.2 %collective-permute-done.34.refs_1_ = bf16[144,2176]{1,0:T(8,128)(2,1)S(1)} collective-permute-done((bf16[144,2176]{1,0:T(8,128)(2,1)S(1)}, bf16[144,2176]{1,0:T(8,128)(2,1)S(1)}, u32[]{:S(2)}, u32[]{:S(2)}) %collective-permute-start.34) | collective-permute-done | bytes 626720 | tf_op jit(solution)/shard_map/ppermute | solution.py:41
  299.4 12.8 %collective-permute-done.35.refs_3_ = bf16[144,2176]{1,0:T(8,128)(2,1)S(1)} collective-permute-done((bf16[144,2176]{1,0:T(8,128)(2,1)}, bf16[144,2176]{1,0:T(8,128)(2,1)S(1)}, u32[]{:S(2)}, u32[]{:S(2)}) %collective-permute-start.35) | collective-permute-done | bytes 626720 | tf_op jit(solution)/shard_map/ppermute | solution.py:41
  312.2 13.3 %collective-permute-done.36.refs_5_ = bf16[144,2176]{1,0:T(8,128)(2,1)S(1)} collective-permute-done((bf16[144,2176]{1,0:T(8,128)(2,1)}, bf16[144,2176]{1,0:T(8,128)(2,1)S(1)}, u32[]{:S(2)}, u32[]{:S(2)}) %collective-permute-start.36) | collective-permute-done | bytes 626720 | tf_op jit(solution)/shard_map/ppermute | solution.py:41
  325.6 13.3 %collective-permute-done.37.refs_7_ = bf16[144,2176]{1,0:T(8,128)(2,1)S(1)} collective-permute-done((bf16[144,2176]{1,0:T(8,128)(2,1)S(1)}, bf16[144,2176]{1,0:T(8,128)(2,1)S(1)}, u32[]{:S(2)}, u32[]{:S(2)}) %collective-permute-start.37) | collective-permute-done | bytes 626720 | tf_op jit(solution)/shard_map/ppermute | solution.py:41
  345.9 18.9 %hidden.1 = (bf16[1536,2176]{1,0:T(8,128)(2,1)}, bf16[1536,2176]{1,0:T(8,128)(2,1)}, bf16[1536,1152]{1,0:T(8,128)(2,1)}) custom-call(bf16[768,1152]{1,0:T(8,128)(2,1)} %get-tuple-element.324.refs_0_, bf16[768,1152]{1,0:T(8,128)(2,1)} %collective-permute-done.32.refs_1_, bf16[1152,2176]{1,0:T(8,128)(2,1)} %assemble.6.refs_2_, ...), custom_call_target="tpu_custom_call" | custom-call | flops 7700742144 | bytes 25460736 | tf_op jit(solution)/shard_map/hidden/pallas_call | solution.py:488
  364.8 13.0 %convolution_convert_fusion.1 = bf16[1152,2176]{1,0:T(8,128)(2,1)} fusion(bf16[1536,1152]{1,0:T(8,128)(2,1)S(1)} %copy-done.10, bf16[1536,2176]{1,0:T(8,128)(2,1)} %get-tuple-element.424), kind=kOutput, calls=%fused_computation.5 | convolution fusion | flops 7703248896 | bytes 15237120 | tf_op jit(solution)/shard_map/dot_general | solution.py:28
  379.4 17.8 %collective-permute-done.41.refs_7_ = bf16[144,2176]{1,0:T(8,128)(2,1)} collective-permute-done((bf16[144,2176]{1,0:T(8,128)(2,1)}, bf16[144,2176]{1,0:T(8,128)(2,1)}, u32[]{:S(2)}, u32[]{:S(2)}) %collective-permute-start.41) | collective-permute-done | bytes 626720 | tf_op jit(solution)/shard_map/ppermute | solution.py:41
  402.6 13.6 %fusion = bf16[1536,2176]{1,0:T(8,128)(2,1)S(1)} fusion(bf16[1536,2176]{1,0:T(8,128)(2,1)} %get-tuple-element.346, bf16[1536,1152]{1,0:T(8,128)(2,1)} %pad_maximum_fusion, bf16[1152,2176]{1,0:T(8,128)(2,1)} %assemble.7), kind=kOutput, calls=%fused_computation.3 | convolution fusion | flops 7710769152 | bytes 21921792 | tf_op jit(solution)/shard_map/dot_general | solution.py:28
  416.3 9.5 %convolution_convert_fusion.3 = bf16[1536,1152]{1,0:T(8,128)(2,1)S(1)} fusion(bf16[1536,2176]{1,0:T(8,128)(2,1)S(1)} %fusion, bf16[1152,2176]{1,0:T(8,128)(2,1)S(1)} %bitcast.92), kind=kOutput, calls=%fused_computation.13 | convolution fusion | flops 7702511616 | bytes 15237120 | tf_op jit(solution)/shard_map/dot_general | solution.py:28
  430.3 10.1 %convolution_convert_fusion = bf16[1152,2176]{1,0:T(8,128)(2,1)} fusion(bf16[1536,1152]{1,0:T(8,128)(2,1)S(1)} %copy-done.52, bf16[1536,2176]{1,0:T(8,128)(2,1)S(1)} %fusion), kind=kOutput, calls=%fused_computation.4 | convolution fusion | flops 7703248896 | bytes 15237120 | tf_op jit(solution)/shard_map/dot_general | solution.py:28
  441.7 11.4 %second_back.1 = (f32[768,1152]{1,0:T(8,128)}, bf16[768,1152]{1,0:T(8,128)(2,1)}, bf16[768,640]{1,0:T(8,128)(2,1)}, bf16[768,640]{1,0:T(8,128)(2,1)}, f32[8,1152]{1,0:T(8,128)}) custom-call(s32[1]{0:T(128)} %bitcast.1.core_ref, f32[768,1152]{1,0:T(8,128)} %get-tuple-element.423.x_ref, bf16[768,1152]{1,0:T(8,128)(2,1)} %slice.306.refs_0_, ...), custom_call_target="tpu_custom_call" | custom-call | flops 2038431744 | bytes 17694720 | tf_op jit(solution)/shard_map/second_back/pallas_call | solution.py:406
  468.9 21.7 %attend_back.3 = (bf16[2,3,256,640]{3,2,1,0:T(8,128)(2,1)}, bf16[2,3,256,1280]{3,2,1,0:T(8,128)(2,1)}, bf16[2,3,256,1280]{3,2,1,0:T(8,128)(2,1)}) custom-call(s32[3,4]{1,0:T(4,128)} %convert_element_type.267.need_ref, s32[3,4,256,1]{3,2,1,0:T(8,128)} %compare_select_fusion.col_ref, s32[3,1,512]{2,1,0:T(1,128)} %broadcast_in_dim_reshape.7.row_ref, ...), custom_call_target="tpu_custom_call" | custom-call | flops 21474836480 | bytes 7864320 | tf_op jit(solution)/shard_map/attend_back/pallas_call | solution.py:712
  493.5 18.8 %attend_back.4 = (bf16[2,3,256,640]{3,2,1,0:T(8,128)(2,1)}, bf16[2,3,256,1280]{3,2,1,0:T(8,128)(2,1)}, bf16[2,3,256,1280]{3,2,1,0:T(8,128)(2,1)}) custom-call(s32[3,4]{1,0:T(4,128)} %convert_element_type.267.need_ref, s32[3,4,256,1]{3,2,1,0:T(8,128)} %compare_select_fusion.col_ref, ...), custom_call_target="tpu_custom_call", output_to_operand_aliasing={{0}: (12, {}), {1}: (13, {}), {2}: (14, {})} | custom-call | flops 21474836480 | bytes 7864320 | tf_op jit(solution)/shard_map/attend_back/pallas_call | solution.py:712
  520.3 18.2 %attend_back.5 = (bf16[2,3,256,640]{3,2,1,0:T(8,128)(2,1)}, bf16[2,3,256,1280]{3,2,1,0:T(8,128)(2,1)}, bf16[2,3,256,1280]{3,2,1,0:T(8,128)(2,1)}) custom-call(s32[3,4]{1,0:T(4,128)} %convert_element_type.267.need_ref, s32[3,4,256,1]{3,2,1,0:T(8,128)} %compare_select_fusion.col_ref, ...), custom_call_target="tpu_custom_call", output_to_operand_aliasing={{0}: (12, {}), {1}: (13, {}), {2}: (14, {})} | custom-call | flops 21474836480 | bytes 7864320 | tf_op jit(solution)/shard_map/attend_back/pallas_call | solution.py:712
  538.5 9.9 %convolution_convert_fusion.2 = bf16[1536,1152]{1,0:T(8,128)(2,1)S(1)} fusion(bf16[1536,1280]{1,0:T(8,128)(2,1)} %bitcast.129, bf16[1152,1280]{1,0:T(8,128)(2,1)} %get-tuple-element.401), kind=kOutput, calls=%fused_computation.12 | convolution fusion | flops 4531617792 | bytes 10420224 | tf_op jit(solution)/shard_map/dot_general | solution.py:28
  561.6 17.3 %weight_grad.4 = (bf16[576,1280]{1,0:T(8,128)(2,1)}, bf16[576,1280]{1,0:T(8,128)(2,1)}, f32[8,1280]{1,0:T(8,128)}) custom-call(s32[9]{0:T(128)} %pad_add_fusion.pos_ref, bf16[1536,1152]{1,0:T(8,128)(2,1)} %norm.2.refs_0_, bf16[1536,1152]{1,0:T(8,128)(2,1)} %norm.3.refs_1_, bf16[1536,1280]{1,0:T(8,128)(2,1)} %bitcast.127, bf16[1536,1280]{1,0:T(8,128)(2,1)} %bitcast.130), custom_call_target="tpu_custom_call" | custom-call | flops 9059696640 | bytes 17891328 | tf_op jit(solution)/shard_map/weight_grad/pallas_call | solution.py:190
  631.5 27.1 %collective-permute-done.63 = bf16[576,1280]{1,0:T(8,128)(2,1)S(1)} collective-permute-done((bf16[576,1280]{1,0:T(8,128)(2,1)}, bf16[576,1280]{1,0:T(8,128)(2,1)S(1)}, u32[]{:S(2)}, u32[]{:S(2)}) %collective-permute-start.63) | collective-permute-done | bytes 1474592 | tf_op jit(solution)/shard_map/ppermute | solution.py:41
  687.8 15.2 %collective-permute-done.67 = bf16[144,1280]{1,0:T(8,128)(2,1)S(1)} collective-permute-done((bf16[144,1280]{1,0:T(8,128)(2,1)S(1)}, bf16[144,1280]{1,0:T(8,128)(2,1)S(1)}, u32[]{:S(2)}, u32[]{:S(2)}) %collective-permute-start.67) | collective-permute-done | bytes 368672 | tf_op jit(solution)/shard_map/ppermute | solution.py:41
  703.3 10.2 %collective-permute-done.70 = bf16[288,640]{1,0:T(8,128)(2,1)S(1)} collective-permute-done((bf16[288,640]{1,0:T(8,128)(2,1)S(1)}, bf16[288,640]{1,0:T(8,128)(2,1)S(1)}, u32[]{:S(2)}, u32[]{:S(2)}) %collective-permute-start.70) | collective-permute-done | bytes 368672 | tf_op jit(solution)/shard_map/ppermute | solution.py:41
  (423 shorter events, 362.9 us)
Async XLA Ops:
  7.2 511.0 %reduce-scatter.3.cloned.1.call-start = ((), (), s32[]{:S(2)}) async-start(), calls=%async_computation.2 | async-start | bytes 5640192 | tf_op jit(solution)/shard_map/reduce_scatter | solution.py:939
  25.6 37.2 %collective-permute-start = (bf16[144,1920]{1,0:T(8,128)(2,1)}, bf16[144,1920]{1,0:T(8,128)(2,1)}, u32[]{:S(2)}, u32[]{:S(2)}) collective-permute-start(bf16[144,1920]{1,0:T(8,128)(2,1)} %get-tuple-element.248.refs_0_), channel_id=1, source_target_pairs={{0,1},{1,0},{2,3},{3,2},{4,5},{5,4},{6,7},{7,6},{8,9},{9,8},{10,11... | collective-permute-start | bytes 1658888 | tf_op jit(solution)/shard_map/ppermute | solution.py:41
  26.1 64.5 %collective-permute-start.18 = (bf16[768,1152]{1,0:T(8,128)(2,1)}, bf16[768,1152]{1,0:T(8,128)(2,1)}, u32[]{:S(2)}, u32[]{:S(2)}) collective-permute-start(bf16[768,1152]{1,0:T(8,128)(2,1)} %bitcast.84), channel_id=1, source_target_pairs={{0,16},{8,24},{16,0},{24,8},{1,17},{9,25},{17,1},{25,9},{2,18},{10... | collective-permute-start | bytes 5308424 | tf_op jit(solution)/shard_map/ppermute | solution.py:41
  65.1 73.0 %collective-permute-start.2 = (bf16[768,1152]{1,0:T(8,128)(2,1)S(1)}, bf16[768,1152]{1,0:T(8,128)(2,1)}, u32[]{:S(2)}, u32[]{:S(2)}) collective-permute-start(bf16[768,1152]{1,0:T(8,128)(2,1)S(1)} %bitcast.88), channel_id=1, source_target_pairs={{0,8},{8,0},{16,24},{24,16},{1,9},{9,1},{17,25},{25,17},{2,10},{10... | collective-permute-start | bytes 5308424 | tf_op jit(solution)/shard_map/ppermute | solution.py:41
  66.4 71.7 %collective-permute-start.1 = (bf16[768,1152]{1,0:T(8,128)(2,1)S(1)}, bf16[768,1152]{1,0:T(8,128)(2,1)}, u32[]{:S(2)}, u32[]{:S(2)}) collective-permute-start(bf16[768,1152]{1,0:T(8,128)(2,1)S(1)} %bitcast.82), channel_id=1, source_target_pairs={{0,8},{8,0},{16,24},{24,16},{1,9},{9,1},{17,25},{25,17},{2,10},{10... | collective-permute-start | bytes 5308424 | tf_op jit(solution)/shard_map/ppermute | solution.py:41
  90.6 58.5 %collective-permute-start.19 = (bf16[768,1152]{1,0:T(8,128)(2,1)}, bf16[768,1152]{1,0:T(8,128)(2,1)}, u32[]{:S(2)}, u32[]{:S(2)}) collective-permute-start(bf16[768,1152]{1,0:T(8,128)(2,1)} %collective-permute-done.18.refs_0_), channel_id=1, source_target_pairs={{0,8},{8,0},{16,24},{24,16},{1,9},{9,1},{17,25},{25,17},{2,10},{10... | collective-permute-start | bytes 5308424 | tf_op jit(solution)/shard_map/ppermute | solution.py:41
  117.1 50.3 %collective-permute-start.6 = (bf16[144,640]{1,0:T(8,128)(2,1)}, bf16[144,640]{1,0:T(8,128)(2,1)}, u32[]{:S(2)}, u32[]{:S(2)}) collective-permute-start(bf16[144,640]{1,0:T(8,128)(2,1)} %collective-permute-done.3.refs_1_), channel_id=1, source_target_pairs={{0,4},{1,5},{2,6},{3,7},{4,0},{5,1},{6,2},{7,3},{8,12},{9,13},{10,... | collective-permute-start | bytes 552968 | tf_op jit(solution)/shard_map/ppermute | solution.py:41
  235.8 35.5 %collective-permute-start.28 = (bf16[3,256,640]{2,1,0:T(8,128)(2,1)}, bf16[3,256,640]{2,1,0:T(8,128)(2,1)}, u32[]{:S(2)}, u32[]{:S(2)}) collective-permute-start(bf16[3,256,640]{2,1,0:T(8,128)(2,1)} %get-tuple-element.305.refs_3_), channel_id=1, source_target_pairs={{0,8},{8,0},{16,24},{24,16},{1,9},{9,1},{17,25},{25,17},{2,10},{10... | collective-permute-start | bytes 2949128 | tf_op jit(solution)/shard_map/ppermute | solution.py:41
  279.7 66.2 %collective-permute-start.32 = (bf16[768,1152]{1,0:T(8,128)(2,1)}, bf16[768,1152]{1,0:T(8,128)(2,1)}, u32[]{:S(2)}, u32[]{:S(2)}) collective-permute-start(bf16[768,1152]{1,0:T(8,128)(2,1)} %get-tuple-element.324.refs_0_), channel_id=1, source_target_pairs={{0,8},{8,0},{16,24},{24,16},{1,9},{9,1},{17,25},{25,17},{2,10},{10... | collective-permute-start | bytes 5308424 | tf_op jit(solution)/shard_map/ppermute | solution.py:41
  286.5 39.1 %collective-permute-start.36 = (bf16[144,2176]{1,0:T(8,128)(2,1)}, bf16[144,2176]{1,0:T(8,128)(2,1)S(1)}, u32[]{:S(2)}, u32[]{:S(2)}) collective-permute-start(bf16[144,2176]{1,0:T(8,128)(2,1)} %collective-permute-done.10.refs_4_), channel_id=1, source_target_pairs={{0,1},{1,0},{2,3},{3,2},{4,5},{5,4},{6,7},{7,6},{8,9},{9,8},{10,11... | collective-permute-start | bytes 1880072 | tf_op jit(solution)/shard_map/ppermute | solution.py:41
  286.5 52.5 %collective-permute-start.37 = (bf16[144,2176]{1,0:T(8,128)(2,1)S(1)}, bf16[144,2176]{1,0:T(8,128)(2,1)S(1)}, u32[]{:S(2)}, u32[]{:S(2)}) collective-permute-start(bf16[144,2176]{1,0:T(8,128)(2,1)S(1)} %copy-done.24), channel_id=1, source_target_pairs={{0,1},{1,0},{2,3},{3,2},{4,5},{5,4},{6,7},{7,6},{8,9},{9,8},{10,11... | collective-permute-start | bytes 1880072 | tf_op jit(solution)/shard_map/ppermute | solution.py:41
  298.7 45.9 %collective-permute-start.33 = (bf16[144,2176]{1,0:T(8,128)(2,1)}, bf16[144,2176]{1,0:T(8,128)(2,1)}, u32[]{:S(2)}, u32[]{:S(2)}) collective-permute-start(bf16[144,2176]{1,0:T(8,128)(2,1)} %collective-permute-done.30.refs_4_), channel_id=1, source_target_pairs={{0,2},{1,3},{2,0},{3,1},{4,6},{5,7},{6,4},{7,5},{8,10},{9,11},{10,... | collective-permute-start | bytes 1880072 | tf_op jit(solution)/shard_map/ppermute | solution.py:41
  312.1 65.7 %collective-permute-start.38 = (bf16[144,2176]{1,0:T(8,128)(2,1)}, bf16[144,2176]{1,0:T(8,128)(2,1)}, u32[]{:S(2)}, u32[]{:S(2)}) collective-permute-start(bf16[144,2176]{1,0:T(8,128)(2,1)} %slice_select_fusion.refs_0_), channel_id=1, source_target_pairs={{0,1},{1,0},{2,3},{3,2},{4,5},{5,4},{6,7},{7,6},{8,9},{9,8},{10,11... | collective-permute-start | bytes 1880072 | tf_op jit(solution)/shard_map/ppermute | solution.py:41
  325.5 53.8 %collective-permute-start.40 = (bf16[144,2176]{1,0:T(8,128)(2,1)}, bf16[144,2176]{1,0:T(8,128)(2,1)}, u32[]{:S(2)}, u32[]{:S(2)}) collective-permute-start(bf16[144,2176]{1,0:T(8,128)(2,1)} %collective-permute-done.30.refs_4_), channel_id=1, source_target_pairs={{0,1},{1,0},{2,3},{3,2},{4,5},{5,4},{6,7},{7,6},{8,9},{9,8},{10,11... | collective-permute-start | bytes 1880072 | tf_op jit(solution)/shard_map/ppermute | solution.py:41
  339.0 40.4 %collective-permute-start.39 = (bf16[144,2176]{1,0:T(8,128)(2,1)}, bf16[144,2176]{1,0:T(8,128)(2,1)}, u32[]{:S(2)}, u32[]{:S(2)}) collective-permute-start(bf16[144,2176]{1,0:T(8,128)(2,1)} %collective-permute-done.29.refs_2_), channel_id=1, source_target_pairs={{0,1},{1,0},{2,3},{3,2},{4,5},{5,4},{6,7},{7,6},{8,9},{9,8},{10,11... | collective-permute-start | bytes 1880072 | tf_op jit(solution)/shard_map/ppermute | solution.py:41
  344.6 52.6 %collective-permute-start.41 = (bf16[144,2176]{1,0:T(8,128)(2,1)}, bf16[144,2176]{1,0:T(8,128)(2,1)}, u32[]{:S(2)}, u32[]{:S(2)}) collective-permute-start(bf16[144,2176]{1,0:T(8,128)(2,1)} %collective-permute-done.33.refs_6_), channel_id=1, source_target_pairs={{0,1},{1,0},{2,3},{3,2},{4,5},{5,4},{6,7},{7,6},{8,9},{9,8},{10,11... | collective-permute-start | bytes 1880072 | tf_op jit(solution)/shard_map/ppermute | solution.py:41
  377.8 296.7 %reduce-scatter.5.cloned.1.call-start = ((), (), s32[]{:S(2)}) async-start(), calls=%async_computation.3 | async-start | bytes 5640192 | tf_op jit(solution)/shard_map/reduce_scatter | solution.py:949
  555.8 58.7 %collective-permute-start.83 = (f32[144,2176]{1,0:T(8,128)S(1)}, f32[144,2176]{1,0:T(8,128)S(1)}, u32[]{:S(2)}, u32[]{:S(2)}) collective-permute-start(f32[144,2176]{1,0:T(8,128)S(1)} %convert_add_fusion), channel_id=1, source_target_pairs={{0,8},{8,0},{16,24},{24,16},{1,9},{9,1},{17,25},{25,17},{2,10},{10... | collective-permute-start | bytes 3760136 | tf_op jit(solution)/shard_map/ppermute | solution.py:41
  611.2 50.0 %collective-permute-start.62 = (bf16[144,640]{1,0:T(8,128)(2,1)S(1)}, bf16[144,640]{1,0:T(8,128)(2,1)S(1)}, u32[]{:S(2)}, u32[]{:S(2)}) collective-permute-start(bf16[144,640]{1,0:T(8,128)(2,1)S(1)} %add_convert_fusion.18), channel_id=1, source_target_pairs={{0,4},{1,5},{2,6},{3,7},{4,0},{5,1},{6,2},{7,3},{8,12},{9,13},{10,... | collective-permute-start | bytes 552968 | tf_op jit(solution)/shard_map/ppermute | solution.py:41
  612.7 45.9 %collective-permute-start.63 = (bf16[576,1280]{1,0:T(8,128)(2,1)}, bf16[576,1280]{1,0:T(8,128)(2,1)S(1)}, u32[]{:S(2)}, u32[]{:S(2)}) collective-permute-start(bf16[576,1280]{1,0:T(8,128)(2,1)} %get-tuple-element.410), channel_id=1, source_target_pairs={{0,1},{1,0},{2,3},{3,2},{4,5},{5,4},{6,7},{7,6},{8,9},{9,8},{10,11... | collective-permute-start | bytes 4423688 | tf_op jit(solution)/shard_map/ppermute | solution.py:41
  616.6 46.2 %collective-permute-start.61 = (bf16[768,1152]{1,0:T(8,128)(2,1)S(1)}, bf16[768,1152]{1,0:T(8,128)(2,1)S(1)}, u32[]{:S(2)}, u32[]{:S(2)}) collective-permute-start(bf16[768,1152]{1,0:T(8,128)(2,1)S(1)} %copy-done.16), channel_id=1, source_target_pairs={{0,16},{8,24},{16,0},{24,8},{1,17},{9,25},{17,1},{25,9},{2,18},{10... | collective-permute-start | bytes 5308424 | tf_op jit(solution)/shard_map/ppermute | solution.py:41
  619.6 44.7 %collective-permute-start.60 = (bf16[768,1152]{1,0:T(8,128)(2,1)S(1)}, bf16[768,1152]{1,0:T(8,128)(2,1)S(1)}, u32[]{:S(2)}, u32[]{:S(2)}) collective-permute-start(bf16[768,1152]{1,0:T(8,128)(2,1)S(1)} %get-tuple-element.459), channel_id=1, source_target_pairs={{0,8},{8,0},{16,24},{24,16},{1,9},{9,1},{17,25},{25,17},{2,10},{10... | collective-permute-start | bytes 5308424 | tf_op jit(solution)/shard_map/ppermute | solution.py:41
  660.4 53.9 %collective-permute-start.82 = (f32[1,2176]{1,0:T(1,128)S(1)}, f32[1,2176]{1,0:T(1,128)S(1)}, u32[]{:S(2)}, u32[]{:S(2)}) collective-permute-start(f32[1,2176]{1,0:T(1,128)S(1)} %get-tuple-element.458), channel_id=1, source_target_pairs={{0,8},{8,0},{16,24},{24,16},{1,9},{9,1},{17,25},{25,17},{2,10},{10... | collective-permute-start | bytes 26120 | tf_op jit(solution)/shard_map/ppermute | solution.py:41
  680.5 43.5 %collective-permute-start.72 = (bf16[144,2176]{1,0:T(8,128)(2,1)}, bf16[144,2176]{1,0:T(8,128)(2,1)}, u32[]{:S(2)}, u32[]{:S(2)}) collective-permute-start(bf16[144,2176]{1,0:T(8,128)(2,1)} %reduce-scatter.5.cloned.1.call-done), channel_id=1, source_target_pairs={{0,16},{8,24},{16,0},{24,8},{1,17},{9,25},{17,1},{25,9},{2,18},{10... | collective-permute-start | bytes 1880072 | tf_op jit(solution)/shard_map/ppermute | solution.py:41
  (119 other events, 1853.1 us)
Sparse Core Ops, SparseCore 0:
  377.9 102.1 reduce-scatter.2
  551.7 115.0 reduce-scatter.4

commit v4 on v3

--- a/solution.py
+++ b/solution.py
@@ -18,6 +18,7 @@
 WIN = 256
 LOG2E = math.log2(math.e)
 VMEM = 60 << 20
+NOMINAL = pl.CostEstimate(flops=1, transcendentals=0, bytes_accessed=1)
 
 
 def round_up(value, step):
@@ -60,6 +61,32 @@
     def done(self, *results):
         self.last = results
         return results if len(results) > 1 else results[0]
+
+
+class Flights:
+    def __init__(self, chain):
+        self.chain, self.open = chain, []
+
+    def send(self, array, axis, bits):
+        self.open.append([swap(array, axis, bits)])
+        return self.open[-1]
+
+    def land(self, *values, through=None):
+        count = len(self.open)
+        if through is not None:
+            count = 1 + next(i for i, box in enumerate(self.open) if box is through)
+        ready, self.open = self.open[:count], self.open[count:]
+        held = self.chain(*[box[0] for box in ready], *values)
+        held = held if isinstance(held, (tuple, list)) else [held]
+        for box, array in zip(ready, held):
+            box[0] = array
+        rest = list(held[len(ready) :])
+        return rest if len(rest) > 1 else rest[0] if rest else None
+
+
+def in_order(parts, me):
+    count = len(parts)
+    return jnp.take(jnp.stack([parts[d] for d in range(count)]), me ^ jnp.arange(count), axis=0)
 
 
 def gather_all(shard):
@@ -69,35 +96,9 @@
     return parts
 
 
-def gather_direct(shard):
-    return {0: shard} | {d: swap(shard, "fsdp", d) for d in range(1, lax.axis_size("fsdp"))}
-
-
-def in_order(parts, me):
-    count = len(parts)
-    return jnp.take(jnp.stack([parts[d] for d in range(count)]), me ^ jnp.arange(count), axis=0)
-
-
 def rel_position(distance, count):
     width = count.bit_length() - 1
     return sum(((distance >> k) & 1) << (width - 1 - k) for k in range(width))
-
-
-def scatter_step(keep, arrived, rows):
-    size = keep.shape[0]
-    if size == rows:
-        return (keep.astype(F32) + arrived.astype(F32)).astype(BF16), None
-    return [
-        (keep[part].astype(F32) + arrived[part].astype(F32)).astype(BF16)
-        for part in (slice(0, size // 2), slice(size // 2, size))
-    ]
-
-
-def seq_sum(mine):
-    for bit in bits_of(lax.axis_size("seq"))[:-1]:
-        total = mine.astype(F32) + swap(mine, "seq", bit).astype(F32)
-        mine = total.astype(BF16)
-    return total
 
 
 def assemble_kernel(count, rows, single, off_ref, *refs):
@@ -137,9 +138,7 @@
             out_specs=[pl.BlockSpec((count * rows, tile), m) for m in maps],
         ),
         compiler_params=params(("arbitrary",)),
-        cost_estimate=pl.CostEstimate(
-            flops=0, transcendentals=0, bytes_accessed=4 * count * rows * cols
-        ),
+        cost_estimate=NOMINAL,
         name="assemble",
     )(offsets, *[parts[d] for d in range(count)])
     return outs if cut else outs[0]
@@ -185,8 +184,6 @@
     positions = jnp.concatenate([table[order] % half * rows, (me & 1)[None]]).astype(jnp.int32)
     tile = 256
     pairs = len(lefts)
-    flops = sum(2 * a.shape[0] * width * cols for a in lefts)
-    moved = sum(2 * a.shape[0] * (width + cols) for a in lefts) + 2 * width * cols
     return pl.pallas_call(
         functools.partial(weight_grad_kernel, pairs, count, rows),
         out_shape=[jax.ShapeDtypeStruct((width // 2, cols), BF16)] * 2
@@ -203,7 +200,7 @@
             + [pl.BlockSpec((8, tile), lambda n, off: (0, n))],
         ),
         compiler_params=params(("arbitrary",)),
-        cost_estimate=pl.CostEstimate(flops=flops, transcendentals=0, bytes_accessed=moved),
+        cost_estimate=NOMINAL,
         name="weight_grad",
     )(positions, *lefts, *rights)
 
@@ -219,38 +216,36 @@
     return 256 if rows % 256 == 0 else 128 if rows % 128 == 0 else rows
 
 
-def norm_kernel(steps, x_refs, gain_ref, shift_ref, out_ref):
-    for i, x_ref in enumerate(x_refs):
-
-        @pl.when(pl.program_id(0) // steps == i)
-        def _():
-            hat, _ = normalized(x_ref[...].astype(F32))
-            out_ref[...] = (hat * gain_ref[...] + shift_ref[...]).astype(BF16)
-
-
 def norm(arrays, gain, shift):
-    rows, width = arrays[0].shape
-    block = row_block(rows)
-    steps, count = rows // block, len(arrays)
+    width = arrays[0].shape[1]
+    block = min(row_block(a.shape[0]) for a in arrays)
+    steps = [a.shape[0] // block for a in arrays]
+    firsts = [sum(steps[:k]) for k in range(len(steps))]
+    count, total = len(arrays), sum(steps)
 
     def kernel(*refs):
-        norm_kernel(steps, refs[:count], *refs[count:])
+        gain_ref, shift_ref, out_ref = refs[count:]
+        at = pl.program_id(0)
+        for k in range(count):
+
+            @pl.when((at >= firsts[k]) & (at < firsts[k] + steps[k]))
+            def _():
+                hat, _ = normalized(refs[k][...].astype(F32))
+                out_ref[...] = (hat * gain_ref[...] + shift_ref[...]).astype(BF16)
 
     line = pl.BlockSpec((1, width), lambda i: (0, 0))
     return pl.pallas_call(
         kernel,
-        out_shape=jax.ShapeDtypeStruct((count * rows, width), BF16),
-        grid=(count * steps,),
+        out_shape=jax.ShapeDtypeStruct((total * block, width), BF16),
+        grid=(total,),
         in_specs=[
-            pl.BlockSpec((block, width), lambda i, k=k: (jnp.clip(i - k * steps, 0, steps - 1), 0))
+            pl.BlockSpec((block, width), lambda i, k=k: (jnp.clip(i - firsts[k], 0, steps[k] - 1), 0))
             for k in range(count)
         ]
         + [line, line],
         out_specs=pl.BlockSpec((block, width), lambda i: (i, 0)),
         compiler_params=params(("arbitrary",)),
-        cost_estimate=pl.CostEstimate(
-            flops=10 * count * rows * width, transcendentals=0, bytes_accessed=4 * count * rows * width
-        ),
+        cost_estimate=NOMINAL,
         name="norm",
     )(*arrays, gain, shift)
 
@@ -302,9 +297,7 @@
             out_specs=(wide, wide, wide),
         ),
         compiler_params=params(("arbitrary",)),
-        cost_estimate=pl.CostEstimate(
-            flops=2 * rows * width * width, transcendentals=0, bytes_accessed=14 * rows * width
-        ),
+        cost_estimate=NOMINAL,
         name="join",
     )(core, own, other, inputs, weight, bias, gain, shift)
 
@@ -367,26 +360,32 @@
             out_specs=(wide, pl.BlockSpec((8, width), lambda i, c: (0, 0))),
         ),
         compiler_params=params(("arbitrary",)),
-        cost_estimate=pl.CostEstimate(
-            flops=20 * rows * width, transcendentals=0, bytes_accessed=18 * rows * width
-        ),
+        cost_estimate=NOMINAL,
         name="first_back",
     )(core, values, *grads, gain, add, q_sums, kv_sums)
 
 
-def second_back(core, values, grads, gain, add, weight, half, padded):
+def second_back(core, values, grads, gain, add, weight, hidden_line, half, padded):
     rows, width = values.shape
     block = row_block(rows)
     count = len(grads)
 
     def kernel(core_ref, x_ref, *refs):
-        gain_ref, add_ref, w_ref, dx_ref, low_ref, mine_ref, send_ref, lines_ref = refs[count:]
+        gain_ref, add_ref, w_ref, hid_ref, dx_ref, low_ref, mine_ref, send_ref, lines_ref = refs[count:]
         total = norm_back_values(x_ref, refs[:count], gain_ref, add_ref, lines_ref)
         low = total.astype(BF16)
         dx_ref[...] = total
         low_ref[...] = low
         lines_ref[2:3] += jnp.sum(low.astype(F32), axis=0, keepdims=True)
         lines_ref[3:4] += jnp.sum(add_ref[...].astype(F32), axis=0, keepdims=True)
+        spare = hid_ref.shape[1] - width
+        for core in range(2):
+
+            @pl.when(core_ref[0] == core)
+            def _():
+                lines_ref[4 + 2 * core : 5 + 2 * core] = hid_ref[:, :width]
+                lines_ref[5 + 2 * core : 6 + 2 * core, :spare] = hid_ref[:, width:]
+
         back = dot(low, w_ref[...], NT).astype(BF16)
         empty = jnp.zeros((block, padded - half), BF16)
         halves = [jnp.concatenate([back[:, i * half : (i + 1) * half], empty], axis=1) for i in range(2)]
@@ -415,52 +414,314 @@
         grid_spec=pltpu.PrefetchScalarGridSpec(
             num_scalar_prefetch=1,
             grid=(rows // block,),
-            in_specs=[wide] * (1 + count) + [line, wide, square],
+            in_specs=[wide] * (1 + count)
+            + [line, wide, square, pl.BlockSpec(hidden_line.shape, lambda i, c: (0, 0))],
             out_specs=(wide, wide, part, part, pl.BlockSpec((8, width), lambda i, c: (0, 0))),
         ),
         compiler_params=params(("arbitrary",)),
-        cost_estimate=pl.CostEstimate(
-            flops=2 * rows * width * width, transcendentals=0, bytes_accessed=20 * rows * width
-        ),
+        cost_estimate=NOMINAL,
         name="second_back",
-    )(core, values, *grads, gain, add, weight)
-
-
-def shards_kernel(half, padded, cut, core_ref, q_ref, k_ref, v_ref, o_ref, qkv_ref, out_ref):
-    empty = jnp.zeros((q_ref.shape[0], padded - half), BF16)
-    for core in range(2):
-
-        @pl.when(core_ref[0] == core)
-        def _():
-            for i, ref in enumerate((q_ref, k_ref, v_ref)):
-                part = ref[:, core * half : (core + 1) * half]
-                qkv_ref[:, i * padded : (i + 1) * padded] = jnp.concatenate([part, empty], axis=1)
-            out_ref[...] = o_ref[:, core * cut : core * cut + padded]
-
-
-def attention_shards(core, weights, half, padded):
+    )(core, values, *grads, gain, add, weight, hidden_line)
+
+
+def rows_matmul(name, lefts, weights, finish, extras, outs, dims=((1,), (0,)), split=False, first_row=0):
+    rows = outs[0].shape[0]
+    block = row_block(rows)
+    steps = rows // block
+    half = steps // 2
+    count, terms = len(lefts), len(lefts) + len(weights)
+
+    def kernel(*refs):
+        total = dot(refs[0][...], refs[count][...], dims)
+        for i in range(1, count):
+            total += dot(refs[i][...], refs[count + i][...], dims)
+        results = finish(total, *refs[terms : terms + len(extras)])
+        targets = refs[terms + len(extras) :]
+        if split:
+
+            @pl.when(pl.program_id(0) < half)
+            def _():
+                targets[0][...] = results[0]
+
+            @pl.when(pl.program_id(0) >= half)
+            def _():
+                targets[1][...] = results[0]
+
+            targets = targets[1:]
+        else:
+            targets[0][...] = results[0]
+        for target, result in zip(targets[1:], results[1:]):
+
+            @pl.when(pl.program_id(0) == 0)
+            def _():
+                target[...] = jnp.zeros_like(target)
+
+            target[...] += result
+
+    def by_rows(array):
+        return pl.BlockSpec((block, array.shape[1]), lambda i: (i, 0))
+
+    def whole(array):
+        return pl.BlockSpec(array.shape, lambda i: (0, 0), pipeline_mode=pl.Buffered(1))
+
+    first = outs[0]
+    if split:
+        part = jax.ShapeDtypeStruct((rows // 2, first.shape[1]), first.dtype)
+        shapes = [part, part] + list(outs[1:])
+        specs = [
+            pl.BlockSpec((block, first.shape[1]), lambda i: (jnp.minimum(i, half - 1), 0)),
+            pl.BlockSpec((block, first.shape[1]), lambda i: (jnp.maximum(i - half, 0), 0)),
+        ]
+    else:
+        shapes, specs = list(outs), [by_rows(first)]
+    specs += [pl.BlockSpec(out.shape, lambda i: (0, 0)) for out in outs[1:]]
+    return pl.pallas_call(
+        kernel,
+        out_shape=shapes,
+        grid=(steps,),
+        in_specs=[
+            pl.BlockSpec((block, a.shape[1]), lambda i: (i + first_row // block, 0)) for a in lefts
+        ]
+        + [whole(w) for w in weights]
+        + [by_rows(e) if e.shape[0] == rows else whole(e) for e in extras],
+        out_specs=specs,
+        compiler_params=params(("arbitrary",)),
+        cost_estimate=NOMINAL,
+        name=name,
+    )(*lefts, *weights, *extras)
+
+
+def like(rows, cols, kind=BF16):
+    return jax.ShapeDtypeStruct((rows, cols), kind)
+
+
+def plain(total):
+    return (total.astype(BF16),)
+
+
+def with_bias(total, bias_ref):
+    return ((total + bias_ref[...]).astype(BF16),)
+
+
+def with_slope(total, slope_ref):
+    low = (total * slope_ref[...].astype(F32)).astype(BF16)
+    return low, jnp.sum(low.astype(F32), axis=0, keepdims=True)
+
+
+def layer_end(total, middle_ref, other_ref, bias_ref):
+    return ((middle_ref[...] + total + other_ref[...].astype(F32) + bias_ref[...]).astype(BF16),)
+
+
+def small_call(kernel, outs, scalars, arrays, name):
+    vmem = pl.BlockSpec(memory_space=pltpu.VMEM)
+    return pl.pallas_call(
+        kernel,
+        out_shape=outs,
+        in_specs=[pl.BlockSpec(memory_space=pltpu.SMEM)] * len(scalars) + [vmem] * len(arrays),
+        out_specs=[vmem] * len(outs),
+        compiler_params=pltpu.CompilerParams(vmem_limit_bytes=VMEM),
+        cost_estimate=NOMINAL,
+        name=name,
+    )(*scalars, *arrays)
+
+
+def add_rows(left, right, kind=BF16, pieces=1):
+    rows, cols = left.shape
+    size = rows // pieces
+
+    def kernel(left_ref, right_ref, *outs):
+        for i, out_ref in enumerate(outs):
+            part = slice(i * size, (i + 1) * size)
+            out_ref[...] = (left_ref[part].astype(F32) + right_ref[part].astype(F32)).astype(kind)
+
+    return small_call(kernel, [like(size, cols, kind)] * pieces, [], [left, right], "add_rows")
+
+
+def scatter_step(keep, arrived, rows):
+    if keep.shape[0] == rows:
+        return add_rows(keep, arrived)[0], None
+    return add_rows(keep, arrived, BF16, 2)
+
+
+def both_cores(core, mine, other, size, total, start=0, turn=False):
+    rows = mine.shape[0]
+
+    def kernel(core_ref, mine_ref, other_ref, out_ref):
+        for at, refs in ((0, (mine_ref, other_ref)), (1, (other_ref, mine_ref))):
+
+            @pl.when(core_ref[0] == at)
+            def _():
+                first = refs[0][:, start : start + size]
+                second = refs[1][:, start : start + total - size]
+                if turn:
+                    out_ref[:size], out_ref[size:] = first.T, second.T
+                else:
+                    out_ref[...] = jnp.concatenate([first, second], axis=1)
+
+    shape = like(total, rows, mine.dtype) if turn else like(rows, total, mine.dtype)
+    return small_call(kernel, [shape], [core], [mine, other], "both_cores")[0]
+
+
+def core_columns(core, arrays, cols):
+    rows, width = arrays[0].shape
+
+    def kernel(core_ref, *refs):
+        for at in range(2):
+
+            @pl.when(core_ref[0] == at)
+            def _():
+                for i in range(len(arrays)):
+                    for k, where in enumerate((at, 1 - at)):
+                        low = where * (width - cols)
+                        refs[len(arrays) * (1 + k) + i][...] = refs[i][:, low : low + cols]
+
+    return small_call(kernel, [like(rows, cols)] * (2 * len(arrays)), [core], arrays, "core_columns")
+
+
+def stack_rows(first, second):
+    rows, cols = first.shape
+    block = row_block(rows)
+    steps = rows // block
+
+    def kernel(first_ref, second_ref, out_ref):
+        for i, ref in enumerate((first_ref, second_ref)):
+
+            @pl.when(pl.program_id(0) // steps == i)
+            def _():
+                out_ref[...] = ref[...]
+
+    return pl.pallas_call(
+        kernel,
+        out_shape=like(2 * rows, cols),
+        grid=(2 * steps,),
+        in_specs=[
+            pl.BlockSpec((block, cols), lambda i: (jnp.minimum(i, steps - 1), 0)),
+            pl.BlockSpec((block, cols), lambda i: (jnp.maximum(i - steps, 0), 0)),
+        ],
+        out_specs=pl.BlockSpec((block, cols), lambda i: (i, 0)),
+        compiler_params=params(("arbitrary",)),
+        cost_estimate=NOMINAL,
+        name="stack_rows",
+    )(first, second)
+
+
+def mask_kernel(rows, tokens, blocks, len_ref, place_ref, need_ref, row_ref, col_ref, near_row, near_col):
+    place = place_ref[0]
+    for row in range(rows):
+        ends = [len_ref[row, 0]]
+        for p in range(1, len_ref.shape[1]):
+            ends.append(ends[-1] + len_ref[row, p])
+
+        def pictures(position):
+            return sum((position >= end).astype(jnp.int32) for end in ends)
+
+        def segment(position):
+            return jnp.where(position < ends[-1], pictures(position), 1000 + position)
+
+        spans = []
+        for block in range(blocks):
+            start = jnp.bitwise_xor(place, block) * tokens
+            across = segment(start + lax.broadcasted_iota(jnp.int32, (1, tokens), 1))
+            down = segment(start + lax.broadcasted_iota(jnp.int32, (tokens, 1), 0))
+            row_ref[row, block : block + 1] = across
+            col_ref[row, block] = down
+            if block < 2:
+                near_row[row, :, block * tokens : (block + 1) * tokens] = across
+                near_col[row, block * tokens : (block + 1) * tokens] = down
+            last = jnp.minimum(start + tokens, ends[-1]) - 1
+            low = sum(jnp.where(start >= end, 1, 0) for end in ends)
+            high = sum(jnp.where(last >= end, 1, 0) for end in ends)
+            spans.append((start < ends[-1], low, high))
+        for block, (real, low, high) in enumerate(spans):
+            if block < 2:
+                need_ref[row, block] = 1
+            else:
+                need_ref[row, block] = sum(
+                    jnp.where(real & ok & (low <= top) & (bottom <= high), 1, 0) for ok, bottom, top in spans[:2]
+                )
+
+
+def masks(lengths, place, blocks, tokens):
+    rows = lengths.shape[0]
+    shapes = [(rows, blocks, tokens), (rows, blocks, tokens, 1), (rows, 1, 2 * tokens), (rows, 2 * tokens, 1)]
+    smem = pl.BlockSpec(memory_space=pltpu.SMEM)
+    return pl.pallas_call(
+        functools.partial(mask_kernel, rows, tokens, blocks),
+        out_shape=[jax.ShapeDtypeStruct((rows, blocks), jnp.int32)]
+        + [jax.ShapeDtypeStruct(shape, jnp.int32) for shape in shapes],
+        in_specs=[smem, smem],
+        out_specs=[smem] + [pl.BlockSpec(memory_space=pltpu.VMEM)] * 4,
+        compiler_params=pltpu.CompilerParams(vmem_limit_bytes=VMEM),
+        cost_estimate=NOMINAL,
+        name="masks",
+    )(lengths, place)
+
+
+def lay_vectors(meta, parts, half, padded):
+    count, lines, size = parts.shape
+
+    def kernel(meta_ref, parts_ref, lines_ref, q_ref, kv_ref):
+        for shard in range(count):
+            block = parts_ref[jnp.bitwise_xor(meta_ref[1], shard)]
+            lines_ref[:, shard * size : (shard + 1) * size] = block.astype(F32)
+        q_ref[...] = jnp.zeros_like(q_ref)
+        kv_ref[...] = jnp.zeros_like(kv_ref)
+        for core in range(2):
+
+            @pl.when(meta_ref[0] == core)
+            def _():
+                q_ref[:, :half] = lines_ref[2:3, core * half : (core + 1) * half]
+                kv_ref[:, padded : padded + half] = lines_ref[3:4, core * half : (core + 1) * half]
+
+    outs = [like(lines, count * size, F32), like(1, padded, F32), like(1, 2 * padded, F32)]
+    return small_call(kernel, outs, [meta], [parts], "lay_vectors")
+
+
+def mlp_shards(core, out_shard, hidden_weight, down_weight, cols):
+    rows, total = hidden_weight.shape
+    before = out_shard.shape[1]
+
+    def kernel(core_ref, part_ref, hidden_ref, down_ref, first_out, down_out):
+        first_out[:, :before] = part_ref[...]
+        for at in range(2):
+
+            @pl.when(core_ref[0] == at)
+            def _():
+                low = at * cols
+                high = min(low + cols, total)
+                size = high - low
+                first_out[:, before : before + size] = hidden_ref[:, low:high]
+                down_out[:, :size] = down_ref[low:high].T
+                if size < cols:
+                    empty = jnp.zeros((rows, cols - size), BF16)
+                    first_out[:, before + size :] = empty
+                    down_out[:, size:] = empty
+
+    outs = [like(rows, before + cols), like(rows, cols)]
+    return small_call(kernel, outs, [core], [out_shard, hidden_weight, down_weight], "mlp_shards")
+
+
+def attention_shards(core, weights, vectors, half, padded):
     rows, width = weights[0].shape
-    return pl.pallas_call(
-        functools.partial(shards_kernel, half, padded, width - padded),
-        out_shape=(
-            jax.ShapeDtypeStruct((rows, 3 * padded), BF16),
-            jax.ShapeDtypeStruct((rows, padded), BF16),
-        ),
-        grid_spec=pltpu.PrefetchScalarGridSpec(
-            num_scalar_prefetch=1,
-            grid=(1,),
-            in_specs=[pl.BlockSpec((rows, width), lambda i, c: (0, 0))] * 4,
-            out_specs=(
-                pl.BlockSpec((rows, 3 * padded), lambda i, c: (0, 0)),
-                pl.BlockSpec((rows, padded), lambda i, c: (0, 0)),
-            ),
-        ),
-        compiler_params=params(("arbitrary",)),
-        cost_estimate=pl.CostEstimate(
-            flops=0, transcendentals=0, bytes_accessed=16 * rows * width
-        ),
-        name="attention_shards",
-    )(core, *weights)
+    cut = width - padded
+
+    def kernel(core_ref, q_ref, k_ref, v_ref, o_ref, *refs):
+        qkv_ref, out_ref, lines_ref = refs[len(vectors) :]
+        empty = jnp.zeros((rows, padded - half), BF16)
+        for at in range(2):
+
+            @pl.when(core_ref[0] == at)
+            def _():
+                for i, ref in enumerate((q_ref, k_ref, v_ref)):
+                    part = ref[:, at * half : (at + 1) * half]
+                    qkv_ref[:, i * padded : (i + 1) * padded] = jnp.concatenate([part, empty], axis=1)
+                out_ref[...] = o_ref[:, at * cut : at * cut + padded]
+
+        for i in range(len(vectors)):
+            lines_ref[i : i + 1] = refs[i][...]
+
+    outs = [like(rows, 3 * padded), like(rows, padded), like(len(vectors), vectors[0].shape[1])]
+    return small_call(kernel, outs, [core], [*weights, *vectors], "attention_shards")
 
 
 def hidden(arrays, weight, bias):
@@ -503,11 +764,7 @@
         ],
         out_specs=(out, out, pl.BlockSpec((block, width), lambda i: (i, 0))),
         compiler_params=params(("arbitrary",)),
-        cost_estimate=pl.CostEstimate(
-            flops=2 * count * rows * width * cols,
-            transcendentals=count * rows * cols,
-            bytes_accessed=2 * (2 * count * rows * width + width * cols + 2 * count * rows * cols),
-        ),
+        cost_estimate=NOMINAL,
         name="hidden",
     )(*arrays, weight, bias)
 
@@ -599,7 +856,6 @@
 def attend(row, query, near, far, need, seg_col, seg_row, heads, before):
     _, rows, tokens, padded = query.shape
     blocks = 2 + far.shape[0]
-    cost = 2 * heads * blocks * tokens * tokens
     narrow = pl.BlockSpec((1, tokens, padded), lambda i, need: (row, 0, 0))
     lines = pl.BlockSpec((1, heads, 2 * tokens), lambda i, need: (row, 0, 0))
 
@@ -636,11 +892,7 @@
         ),
         input_output_aliases={6 + i: i for i in range(len(before))},
         compiler_params=params(("arbitrary",)),
-        cost_estimate=pl.CostEstimate(
-            flops=8 * cost * WIN,
-            transcendentals=cost,
-            bytes_accessed=6 * blocks * tokens * padded,
-        ),
+        cost_estimate=NOMINAL,
         name="attend",
     )(need, seg_col, seg_row, query, near, far, *before)
 
@@ -701,7 +953,6 @@
 def attend_back(row, query, near, far, grads, outs, lse, need, seg_col, seg_row, heads, before):
     _, rows, tokens, padded = query.shape
     blocks = 2 + far.shape[0]
-    cost = 2 * heads * blocks * tokens * tokens
     column = lax.broadcasted_iota(jnp.int32, (heads, padded), 1)
     pick = (column // HEAD_DIM == lax.broadcasted_iota(jnp.int32, (heads, padded), 0)).astype(BF16)
     narrow = pl.BlockSpec((1, tokens, padded), lambda i, need: (row, 0, 0))
@@ -737,17 +988,9 @@
         ),
         input_output_aliases={12 + i: i for i in range(len(before))},
         compiler_params=params(("arbitrary",)),
-        cost_estimate=pl.CostEstimate(
-            flops=20 * cost * WIN,
-            transcendentals=cost,
-            bytes_accessed=12 * blocks * tokens * padded,
-        ),
+        cost_estimate=NOMINAL,
         name="attend_back",
     )(need, seg_col, seg_row, pick, query, near, far, *grads, *outs, lse, *before)
-
-
-def column_sum(array):
-    return dot(jnp.ones((8, array.shape[0]), BF16), array)[:1]
 
 
 def local(
@@ -794,357 +1037,386 @@
         second = jnp.pad(second, grow + [(0, padded_size - second.shape[-1])])
         return jnp.where(is_first, first, second)
 
+    flights = Flights(chain)
+    staged = shards == 8 and seq_count == 4
+    y, z, zz = 1, 2, 4
+    top = bits_of(seq_count)[0]
+
     inputs = patches.reshape(flat, width)
     incoming = cotangent.reshape(flat, width)
-    shard_qkv, shard_out = attention_shards(
-        core_flag, [query_weight, key_weight, value_weight, output_weight], half, padded
+    shard_qkv, shard_out, vectors = chain.done(
+        *attention_shards(
+            core_flag,
+            [query_weight, key_weight, value_weight, output_weight],
+            [
+                vector[None]
+                for vector in (
+                    first_gain,
+                    first_shift,
+                    query_bias,
+                    value_bias,
+                    output_bias,
+                    second_gain,
+                    second_shift,
+                    down_bias,
+                )
+            ],
+            half,
+            padded,
+        )
     )
-    raw = {0: inputs}
-    for bit in bits_of(seq_count):
-        raw.update({j | bit: swap(part, "seq", bit) for j, part in list(raw.items())})
-    staged = shards == 8
-    y, z, zz = 1, 2, 4
-    q = {0: shard_qkv}
+    place_flag = place[None].astype(jnp.int32)
+
+    def over(box_from, bits):
+        return flights.send(box_from[0], "fsdp", bits)
+
+    def both(stacked_lines, arrived):
+        return jnp.concatenate([stacked_lines, arrived], axis=0)
+
+    vectors = vectors[None]
     if staged:
-        q[z], q[zz], q[y] = (swap(q[0], "fsdp", bit) for bit in (z, zz, y))
-        early = (q[y],)
+        q = {0: [shard_qkv]}
+        vec = flights.send(vectors, "fsdp", y)
+        q[y] = over(q[0], y)
+        far_raw = [flights.send(patches[0], "seq", 2)]
+        q[z], q[zz] = over(q[0], z), over(q[0], zz)
+        shard_out, vectors = flights.land(shard_out, vectors, through=vec)
+        vectors = both(vectors, vec[0])
+        vec = flights.send(vectors, "fsdp", z)
+        shard_ho, shard_down = chain.done(
+            *mlp_shards(core_flag, shard_out, hidden_weight, down_weight, ff_half)
+        )
+        h, d = {0: [shard_ho]}, {0: [shard_down]}
+        lengths = flights.land(lengths, through=far_raw[0])
+        h[y] = over(h[0], y)
+        far_raw.append(flights.send(patches[1:].reshape(flat - tokens, width), "seq", 2))
+        need, seg_rows, seg_cols, seg_near_row, seg_near_col = chain.done(
+            *masks(lengths, place_flag, seq_count, tokens)
+        )
+        vectors = flights.land(vectors, through=vec)
+        vectors = both(vectors, vec[0])
+        vec = flights.send(vectors, "fsdp", zz)
+        q[zz | z] = over(q[zz], z)
+        q[z | y] = over(q[z], y)
+        vectors = flights.land(vectors, through=h[y])
+        q[zz | y] = over(q[zz], y)
+        vectors = flights.land(vectors, through=q[zz | z])
+        raw_pair = flights.send(inputs, "seq", 1)
+        q[zz | z | y] = over(q[zz | z], y)
+        h[z] = over(h[0], z)
+        vectors = both(vectors, vec[0])
+        meta = chain(jnp.stack([core, me]).astype(jnp.int32))
+        stacked, bias_q, bias_kv = chain.done(*lay_vectors(meta, vectors, half, padded))
+        gain_one, shift_one = stacked[0:1], stacked[1:2]
+        gain_one = flights.land(gain_one, through=raw_pair)
+        far_pair = [flights.send(box[0], "seq", 1) for box in far_raw]
+        h[zz] = over(h[0], zz)
+        normed_near = chain.done(norm([inputs, raw_pair[0]], gain_one, shift_one))
+        bias_hidden = my_half(after(hidden_bias, gain_one).astype(F32)[None], ff_half, ff_half)
+        gain_one = flights.land(gain_one, through=far_pair[-1])
+        h[z | y], d[y] = over(h[z], y), over(d[0], y)
+        w_q, w_kv = chain.done(*assemble({k: box[0] for k, box in q.items()}, me, padded))
     else:
-        q, early = gather_all(shard_qkv), (shard_qkv,)
-    vectors = after(
-        jnp.stack(
-            [
-                first_gain,
-                first_shift,
-                query_bias,
-                value_bias,
-                output_bias,
-                second_gain,
-                second_shift,
-                down_bias,
-            ]
-        ),
-        shard_qkv,
-    )
-    vector_parts = gather_all(vectors)
-    shard_hidden = my_half(after(hidden_weight, shard_qkv), ff_half, ff_half)
-    shard_down = my_half(after(down_weight, shard_qkv).T, ff_half, ff_half)
-    incoming_near = jnp.concatenate([incoming, swap(after(incoming, *early), "seq", 1)], axis=0)
-    if staged:
-        o, h, d = {0: after(shard_out, q[y])}, {0: after(shard_hidden, q[y])}, {0: shard_down}
-        o[y], h[y] = swap(o[0], "fsdp", y), swap(h[0], "fsdp", y)
-        q[zz | z] = swap(after(q[zz], q[z]), "fsdp", z)
-        q[z | y], q[zz | y] = swap(q[z], "fsdp", y), swap(after(q[zz], q[z]), "fsdp", y)
-        o[zz], o[zz | y] = (swap(after(o[k], q[zz]), "fsdp", zz) for k in (0, y))
-        q[zz | z | y] = swap(after(q[zz | z], q[z | y], q[zz | y]), "fsdp", y)
-        h[z], h[zz] = (swap(after(h[0], q[zz | z], o[zz]), "fsdp", bit) for bit in (z, zz))
-        d[y] = swap(after(d[0], q[zz | z | y]), "fsdp", y)
-    else:
-        o, h, d = gather_all(shard_out), gather_all(shard_hidden), gather_all(shard_down)
-
-    stacked = in_order(vector_parts, me).transpose(1, 0, 2).reshape(8, width).astype(F32)
-    gain_one, shift_one, bias_query, bias_value, bias_output, gain_two, shift_two, bias_down = [
+        parts = gather_all(shard_qkv)
+        for k in range(shards.bit_length() - 1):
+            vectors = both(vectors, swap(vectors, "fsdp", 1 << k))
+        shard_ho, shard_down = mlp_shards(core_flag, shard_out, hidden_weight, down_weight, ff_half)
+        raw = {0: inputs}
+        for bit in bits_of(seq_count):
+            raw.update({j | bit: swap(part, "seq", bit) for j, part in list(raw.items())})
+        need, seg_rows, seg_cols, seg_near_row, seg_near_col = masks(lengths, place_flag, seq_count, tokens)
+        stacked, bias_q, bias_kv = lay_vectors(
+            jnp.stack([core, me]).astype(jnp.int32), vectors, half, padded
+        )
+        gain_one, shift_one = stacked[0:1], stacked[1:2]
+        normed_near = norm([raw[0], raw[1]], gain_one, shift_one)
+        far_raw, far_pair = [[raw[j]] for j in range(2, seq_count)], []
+        bias_hidden = my_half(hidden_bias.astype(F32)[None], ff_half, ff_half)
+        w_q, w_kv = chain.done(*assemble(parts, me, padded))
+    _, _, bias_query, bias_value, bias_output, gain_two, shift_two, bias_down = [
         stacked[i : i + 1] for i in range(8)
     ]
 
-    block_of = place ^ jnp.arange(seq_count, dtype=jnp.int32)
-    position = block_of[:, None] * tokens + jnp.arange(tokens, dtype=jnp.int32)[None, :]
-    ends = jnp.cumsum(lengths, axis=-1)
-    picture = jnp.sum(
-        (position[None, :, :, None] >= ends[:, None, None, :]).astype(jnp.int32), axis=-1
+    near_in, w_q, w_kv = chain(normed_near, w_q, w_kv)
+    (query,) = rows_matmul("query", [near_in], [w_q], with_bias, [bias_q], [like(2 * flat, padded)])
+    near_in = after(near_in, query)
+    (near,) = rows_matmul("near", [near_in], [w_kv], with_bias, [bias_kv], [like(2 * flat, 2 * padded)])
+    chain.done(query, near)
+    gain_one, w_kv = chain(gain_one, w_kv)
+    normed_far = chain.done(norm([box[0] for box in far_raw + far_pair], gain_one, shift_one))
+    if staged:
+        w_kv = flights.land(w_kv, through=h[z | y])
+        h[zz | y], h[zz | z] = over(h[zz], y), over(h[zz], z)
+    far_in, w_kv = chain(normed_far, w_kv)
+    (far,) = rows_matmul(
+        "far", [far_in], [w_kv], with_bias, [bias_kv], [like(normed_far.shape[0], 2 * padded)]
     )
-    usable = position[None] < ends[:, -1][:, None, None]
-    segment = jnp.where(usable, picture, 1000 + position[None])
-    low_id = jnp.min(jnp.where(usable, picture, 1 << 20), axis=-1)
-    high_id = jnp.max(jnp.where(usable, picture, -1), axis=-1)
-    need = (low_id[:, :2, None] <= high_id[:, None, :]) & (low_id[:, None, :] <= high_id[:, :2, None])
-    need = need | jnp.eye(2, seq_count, dtype=jnp.bool_)[None]
-    need = jnp.any(need, axis=1).astype(jnp.int32)
-    near_flat = segment[:, :2].reshape(rows, 2 * tokens)
-    seg_rows, seg_cols = segment, segment[..., None]
-    seg_near_row, seg_near_col = near_flat[:, None], near_flat[..., None]
-
-    raw_near, incoming_near = after(raw[1], incoming_near), after(incoming_near, raw[1])
-    normed_near = norm([raw[0], raw_near], gain_one, shift_one)
-    normed_far = norm([after(raw[j], normed_near) for j in range(2, seq_count)], gain_one, shift_one)
-    bias_q = my_half(bias_query, half, padded)
-    bias_kv = jnp.concatenate([jnp.zeros((1, padded), F32), my_half(bias_value, half, padded)], axis=1)
-    q = {k: after(part, normed_far) for k, part in q.items()}
-    w_q, w_kv = chain.done(*assemble(q, me, padded))
-    near_in, w_q, w_kv = chain(normed_near, w_q, w_kv)
-    if staged:
-        h[z], h[zz], near_in = chain(h[z], h[zz], near_in)
-        h[zz | z] = swap(h[zz], "fsdp", z)
-        h[z | y], h[zz | y] = swap(h[z], "fsdp", y), swap(h[zz], "fsdp", y)
-        for k in (0, y, zz, zz | y):
-            o[k | z] = swap(after(o[k], h[zz], h[z]), "fsdp", z)
-    query = (dot(near_in, w_q) + bias_q).astype(BF16)
-    near = (dot(near_in, w_kv) + bias_kv).astype(BF16)
-    chain.done(query, near)
-    far_in, w_kv = chain(normed_far, w_kv)
-    if staged:
-        h[zz | z], far_in = chain(h[zz | z], far_in)
-        h[zz | z | y] = swap(h[zz | z], "fsdp", y)
-    far = chain.done((dot(far_in, w_kv) + bias_kv).astype(BF16))
+    chain.done(far)
     query = query.reshape(2, rows, tokens, padded)
     near = near.reshape(2, rows, tokens, 2 * padded)
     far = far.reshape(seq_count - 2, rows, tokens, 2 * padded)
-    if staged:
-        *rest, query = chain(*o.values(), query)
-        o = dict(zip(o, rest))
-        d[z], d[zz] = (swap(after(d[0], *rest), "fsdp", bit) for bit in (z, zz))
     found = ()
     for row in range(rows):
         query, near, far = chain(query, near, far)
+        if staged and row == 1:
+            query = flights.land(query)
+            h[zz | z | y] = over(h[zz | z], y)
+            d[z], d[zz] = over(d[0], z), over(d[0], zz)
         found = chain.done(*attend(row, query, near, far, need, seg_near_col, seg_rows, heads, found))
-        if row == rows - 2:
-            o = dict(zip(o, chain(*o.values())))
-            w_out_mine = chain.done(assemble(o, me))
-            w_out_other = swap(w_out_mine, "seq", 1)
     out_own, out_pair, lse = found
-    other_half = swap(out_pair, "seq", 1).reshape(flat, padded)
-    w_out_mine, w_out_other = chain(w_out_mine, w_out_other)
-    w_out = jnp.where(
-        is_first,
-        jnp.concatenate([w_out_mine[:, :out_cut], w_out_other], axis=1),
-        jnp.concatenate([w_out_other[:, :out_cut], w_out_mine], axis=1),
+    if staged:
+        out_own, out_pair = flights.land(out_own, out_pair)
+        h_parts = {k: box[0] for k, box in h.items()}
+    else:
+        out_own, out_pair = flights.land(out_own, out_pair)
+        h_parts = gather_all(chain(shard_ho))
+    w_out_mine, w_hidden = chain.done(*assemble(h_parts, me, out_cols))
+    out_pair, w_out_mine = chain(out_pair, w_out_mine)
+    other_half = flights.send(out_pair, "seq", 1)
+    w_out_other = flights.send(w_out_mine, "seq", 1)
+    incoming_pair = flights.send(incoming, "seq", 1)
+    w_out_mine, w_hidden = flights.land(w_out_mine, w_hidden, through=incoming_pair)
+    if staged:
+        d[zz | z], d[z | y] = over(d[zz], z), over(d[z], y)
+    w_out = chain.done(both_cores(core_flag, w_out_mine, w_out_other[0], out_cut, width))
+    own_half, w_out = chain(out_own.reshape(flat, padded), w_out)
+    attended, middle, second = chain.done(
+        *join(
+            core_flag,
+            own_half,
+            other_half[0].reshape(flat, padded),
+            inputs,
+            w_out,
+            bias_output,
+            gain_two,
+            shift_two,
+            half,
+        )
     )
+    second_pair = flights.send(second, "seq", 1)
+    incoming_own = chain(incoming)
+    incoming_near = chain.done(stack_rows(incoming_own, incoming_pair[0]))
+    second, w_hidden = flights.land(second, w_hidden)
     if staged:
-        d[z], d[zz], w_out = chain(d[z], d[zz], w_out)
-        d[zz | z] = swap(d[zz], "fsdp", z)
-        d[z | y], d[zz | y] = swap(d[z], "fsdp", y), swap(d[zz], "fsdp", y)
-    attended, middle, second = join(
-        core_flag,
-        out_own.reshape(flat, padded),
-        other_half,
-        inputs,
-        w_out,
-        bias_output,
-        gain_two,
-        shift_two,
-        half,
-    )
-    second_pair = swap(second, "seq", 1)
-    chain.done(second)
-    h = dict(zip(h, chain(*h.values())))
-    w_hidden = chain.done(assemble(h, me))
-    if staged:
-        d[zz | z], w_hidden = chain(d[zz | z], w_hidden)
-        d[zz | z | y] = swap(d[zz | z], "fsdp", y)
-    bias_hidden = my_half(hidden_bias.astype(F32)[None], ff_half, ff_half)
-    second, second_pair, w_hidden = chain(second, second_pair, w_hidden)
-    act, slope, second_near = chain.done(*hidden([second, second_pair], w_hidden, bias_hidden))
+        d[zz | y], d[zz | z | y] = over(d[zz], y), over(d[zz | z], y)
+    act, slope, second_near = chain.done(*hidden([second, second_pair[0]], w_hidden, bias_hidden))
 
     incoming_near, act = chain(incoming_near, act)
     grad_down = chain.done(dot(incoming_near, act, TN).astype(BF16))
     part_down = lax.psum_scatter(grad_down, "fsdp", scatter_dimension=0, tiled=True)
-    d = dict(zip(d, chain(*d.values())))
-    w_down = chain.done(assemble(d, me))
+    if staged:
+        slope = flights.land(slope)
+        d_parts = {k: box[0] for k, box in d.items()}
+    else:
+        d_parts = gather_all(chain(shard_down))
+    w_down = chain.done(assemble(d_parts, me))
     incoming_near, slope, w_down = chain(incoming_near, slope, w_down)
-    grad_pre = chain.done((dot(incoming_near, w_down) * slope.astype(F32)).astype(BF16))
+    grad_pre, hidden_line = chain.done(
+        *rows_matmul(
+            "grad_pre",
+            [incoming_near],
+            [w_down],
+            with_slope,
+            [slope],
+            [like(2 * flat, ff_half), like(1, ff_half, F32)],
+        )
+    )
     grad_pre = chain(grad_pre)
-    back = chain.done(dot(grad_pre, w_hidden, NT).astype(BF16))
-    back_other = swap(back[flat:], "seq", 1)
+    back, back_pair = chain.done(
+        *rows_matmul("back", [grad_pre], [w_hidden], plain, [], [like(2 * flat, width)], NT, True)
+    )
+    back_other = flights.send(back_pair, "seq", 1)
     second_near, grad_pre = chain(second_near, grad_pre)
     grad_hidden = chain.done(dot(second_near, grad_pre, TN).astype(BF16))
     part_hidden = lax.psum_scatter(grad_hidden, "fsdp", scatter_dimension=0, tiled=True)
-    back, back_other = chain(back, back_other)
+    back = flights.land(back)
     grad_middle, branch, grad_mine, grad_send, lines = second_back(
-        core_flag, middle, [back[:flat], back_other], gain_two, incoming, w_out, half, padded
+        core_flag, middle, [back, back_other[0]], gain_two, incoming, w_out, hidden_line, half, padded
     )
-    chain.done(branch)
-    grad_pair = swap(grad_send, "seq", 1)
+    chain.done(branch, grad_send)
+    grad_pair = flights.send(grad_send, "seq", 1)
     attended, branch = chain(attended, branch)
     out_keep, out_send, _ = chain.done(*weight_grad([attended], [branch], me, shards))
-
-    def core_part(array):
-        low, high = array[:, :out_cols], array[:, out_cut:]
-        return jnp.where(is_first, low, high), jnp.where(is_first, high, low)
-
-    keep_mine, keep_other = core_part(out_keep)
-    send_mine, send_other = core_part(out_send)
-    keep_back, send_back = swap(keep_other, "seq", 1), swap(send_other, "seq", 1)
-    grad_pre = chain(grad_pre)
-    hidden_line = chain.done(column_sum(grad_pre))
+    out_keep, out_send = chain(out_keep, out_send)
+    keep_mine, send_mine, keep_other, send_other = chain.done(
+        *core_columns(core_flag, [out_keep, out_send], out_cols)
+    )
+    query = flights.land(query)
 
     links = [("seq", bit) for bit in bits_of(seq_count)] + [("fsdp", bit) for bit in bits_of(shards)]
-    todo = list(links)
-    small = [lines, hidden_line]
-    moving = []
-
-    def small_step(guard):
-        nonlocal small, moving
-        if moving:
-            *moving, guard = chain(*moving, guard)
-            small = [a + b for a, b in zip(small, moving)]
-            moving = []
-        if todo:
-            axis, bit = todo.pop(0)
-            parts = small if (axis, bit) != ("seq", 1) else small[:1]
-            moving = [swap(part, axis, bit) for part in parts]
-            if len(parts) < len(small):
-                moving.append(jnp.zeros_like(small[1]))
-        return guard
-
-    branch = small_step(branch)
+
+    class Everywhere:
+        def __init__(self, array, order):
+            self.array, self.todo, self.box = array, list(order), None
+
+        def send(self):
+            if self.todo:
+                self.box = flights.send(self.array, *self.todo.pop(0))
+
+        def step(self):
+            if self.box is not None:
+                self.array = chain.done(*add_rows(self.array, self.box[0], F32))
+                self.box = None
+                self.send()
+
+    small = Everywhere(lines, links)
+    keep_back, send_back = flights.send(keep_other, "seq", 1), flights.send(send_other, "seq", 1)
+    small.send()
     shape = (rows, tokens, padded)
-    grads = [grad_mine.reshape(shape), grad_pair.reshape(shape)]
+    grads = [grad_mine.reshape(shape), grad_pair[0].reshape(shape)]
     found = ()
+    far_bits = [2 << k for k in range(shards.bit_length() - 2)]
+    out_bits = list(far_bits)
+
+    def next_step(keep, box, bits):
+        keep, send = scatter_step(keep, box[0], shard_rows)
+        chain.done(keep)
+        return keep, flights.send(send, "fsdp", bits.pop(0)) if bits else None
+
+    def seq_rest(mine, arrived):
+        for bit in bits_of(seq_count)[1:-1]:
+            (mine,) = add_rows(mine, arrived)
+            arrived = swap(mine, "seq", bit)
+        return chain.done(*add_rows(mine, arrived, F32))
+
     for row in range(rows):
         query, near, far, *grads = chain(query, near, far, *grads)
-        if row >= 1:
-            query = small_step(query)
-        if row == 1:
-            keep_back, send_back, query = chain(keep_back, send_back, query)
-            out_keep = (keep_mine.astype(F32) + keep_back.astype(F32)).astype(BF16)
-            out_send = (send_mine.astype(F32) + send_back.astype(F32)).astype(BF16)
-            out_back = swap(out_send, "fsdp", 1)
-        if row == 2:
-            out_back, part_down, query = chain(out_back, part_down, query)
-            out_keep, out_send = scatter_step(out_keep, out_back, shard_rows)
-            out_back = swap(out_send, "fsdp", 2)
-            down_seq = swap(part_down, "seq", bits_of(seq_count)[0])
         found = attend_back(
-            row,
-            query,
-            near,
-            far,
-            grads,
-            [out_own, out_pair],
-            lse,
-            need,
-            seg_cols,
-            seg_near_row,
-            heads,
-            found,
+            row, query, near, far, grads, [out_own, out_pair], lse, need, seg_cols, seg_near_row, heads, found
         )
         chain.done(*found)
+        query = flights.land(query)
+        small.step()
+        if row == 0:
+            (out_keep,), (out_send,) = add_rows(keep_mine, keep_back[0]), add_rows(send_mine, send_back[0])
+            chain.done(out_keep, out_send)
+            out_box = flights.send(out_send, "fsdp", y)
+        else:
+            out_keep, out_box = next_step(out_keep, out_box, out_bits)
+        if row == 1:
+            part_down = chain(part_down)
+            down_seq = flights.send(part_down, "seq", top)
+        if row == 2:
+            down_total = seq_rest(part_down, down_seq[0])
+            down_other = flights.send(down_total, "seq", 1)
     dq, dnear, dfar = [g.reshape(-1, g.shape[-1]) for g in found]
-    dfar, w_kv, down_seq, out_back = chain(dfar, w_kv, down_seq, out_back)
-    dfar = small_step(dfar)
-    out_keep, out_send = scatter_step(out_keep, out_back, shard_rows)
-    out_back = swap(out_send, "fsdp", 4) if out_send is not None else None
-
-    def seq_rest(mine, arrived):
-        total = mine.astype(F32) + arrived.astype(F32)
-        for bit in bits_of(seq_count)[1:-1]:
-            mine = total.astype(BF16)
-            total = mine.astype(F32) + swap(mine, "seq", bit).astype(F32)
-        return total
-
-    top = bits_of(seq_count)[0]
-    down_total = seq_rest(part_down, down_seq)
-    down_other = swap(down_total, "seq", 1)
-    back_far = chain.done(dot(dfar, w_kv, NT).astype(BF16))
-    far_parts = {j: back_far[(j - 2) * flat : (j - 1) * flat] for j in range(2, seq_count)}
-    far_sent = {j: swap(part, "seq", 1) for j, part in far_parts.items() if j & 1}
-    normed_near, normed_far, dnear, dfar = chain(normed_near, normed_far, dnear, dfar)
-    dnear = small_step(dnear)
-    kv_keep, kv_send, kv_sums = chain.done(*weight_grad([normed_near, normed_far], [dnear, dfar], me, shards))
-    kv_back = swap(kv_send, "fsdp", 1)
-    far_sent = {j: chain(part) for j, part in far_sent.items()}
-    far_sums = {
-        j: (far_parts[j].astype(F32) + far_sent[j | 1].astype(F32)).astype(BF16)
-        for j in far_parts
-        if not j & 1
-    }
+    dfar, w_kv = chain(dfar, w_kv)
+    two = seq_count == 4
+    back_far = rows_matmul("back_far", [dfar], [w_kv], plain, [], [like(dfar.shape[0], width)], NT, two)
+    chain.done(*back_far)
+    dnear = flights.land(dnear)
+    small.step()
+    while out_box is not None:
+        out_keep, out_box = next_step(out_keep, out_box, out_bits)
+        if out_box is not None:
+            dnear = flights.land(dnear)
+    out_seq = flights.send(out_keep, "seq", top)
+    if two:
+        far_parts = {2 + i: part for i, part in enumerate(back_far)}
+    else:
+        far_parts = {j: back_far[0][(j - 2) * flat : (j - 1) * flat] for j in range(2, seq_count)}
+    far_sent = {j: flights.send(part, "seq", 1) for j, part in far_parts.items() if j & 1}
+    normed_near, dnear, dfar = chain(normed_near, dnear, dfar)
+    kv_keep, kv_send, kv_sums = chain.done(
+        *weight_grad([normed_near, normed_far], [dnear, dfar], me, shards)
+    )
+    dq = flights.land(dq)
+    kv_box = flights.send(kv_send, "fsdp", y)
+    far_sums = {j: add_rows(far_parts[j], far_sent[j | 1][0])[0] for j in far_parts if not j & 1}
     chain.done(*far_sums.values())
     arrived = []
     for bit in bits_of(seq_count)[:-1]:
-        moved = {j: swap(part, "seq", bit) for j, part in far_sums.items() if j & bit}
+        moved = {j: flights.send(part, "seq", bit) for j, part in far_sums.items() if j & bit}
         far_sums = {j: part for j, part in far_sums.items() if not j & bit}
-        for j, part in moved.items():
+        for j, box in moved.items():
             if j == bit:
-                arrived.append(part)
+                arrived.append(box)
             else:
-                far_sums[j ^ bit] = (far_sums[j ^ bit].astype(F32) + part.astype(F32)).astype(BF16)
+                (far_sums[j ^ bit],) = add_rows(far_sums[j ^ bit], box[0])
+    small.step()
+    out_total = seq_rest(out_keep, out_seq[0])
+    dq, dnear = chain(dq, dnear)
+    back_own, back_pair = chain.done(
+        *rows_matmul("back_near", [dq, dnear], [w_q, w_kv], plain, [], [like(2 * flat, width)], NT, True)
+    )
+    pair_back = flights.send(back_pair, "seq", 1)
     normed_near, dq = chain(normed_near, dq)
-    dq = small_step(dq)
     q_keep, q_send, q_sums = chain.done(*weight_grad([normed_near], [dq], me, shards))
-    q_back = swap(q_send, "fsdp", 1)
-    dq, dnear = chain(dq, dnear)
-    back_near = chain.done((dot(dq, w_q, NT) + dot(dnear, w_kv, NT)).astype(BF16))
-    pair_back = swap(back_near[flat:], "seq", 1)
-    while todo or moving:
-        dnear = small_step(dnear)
-
-    lines_all = small
-
+    q_box = flights.send(q_send, "fsdp", y)
     act, middle = chain(act, middle)
-    down_pair = chain.done(dot(act[flat:], w_down, NT).astype(BF16))
-    down_back = swap(down_pair, "seq", 1)
-    act, down_back, middle = chain(act, down_back, middle)
-    result = middle + dot(act[:flat], w_down, NT) + down_back.astype(F32) + bias_down
-    layer_output = chain.done(result.astype(BF16)).reshape(rows, tokens, width)
-
-    later = [2 << k for k in range(shards.bit_length() - 2)]
-
-    def next_step(keep, back, bits):
-        back = chain(back)
-        keep, send = scatter_step(keep, back, shard_rows)
-        chain.done(keep)
-        return keep, swap(send, "fsdp", bits.pop(0)) if bits else None
-
-    kv_bits, q_bits, out_bits = list(later), list(later), list(later[2:])
-    kv_keep, kv_back = next_step(kv_keep, kv_back, kv_bits)
-    if out_back is not None:
-        out_keep, out_back = next_step(out_keep, out_back, out_bits)
-        while out_back is not None:
-            out_keep, out_back = next_step(out_keep, out_back, out_bits)
-    out_seq = swap(out_keep, "seq", top)
-    pair_back, *arrived = chain(pair_back, *arrived)
-    grad_patches, late = first_back(
-        core_flag,
-        inputs,
-        [back_near[:flat], pair_back] + arrived,
-        gain_one,
-        grad_middle,
-        q_sums,
-        kv_sums,
-        half,
+    (down_pair,) = rows_matmul(
+        "down_pair", [act], [w_down], plain, [], [like(flat, width)], NT, first_row=flat
     )
-    chain.done(grad_patches)
-    small, todo, moving = [late], list(links[1:]) + links[:1], []
+    chain.done(down_pair)
+    down_back = flights.send(down_pair, "seq", 1)
+    out_other = flights.send(out_total, "seq", 1)
+    kv_bits, q_bits = list(far_bits), list(far_bits)
+    down_total = flights.land(down_total, through=kv_box)
+    kv_keep, kv_box = next_step(kv_keep, kv_box, kv_bits)
+    full_down = chain.done(both_cores(core_flag, chain(down_total), down_other[0], ff_half, ff, turn=True))
+    late_in = flights.land(inputs, through=pair_back)
+    grad_patches, late = chain.done(
+        *first_back(
+            core_flag,
+            late_in,
+            [back_own, pair_back[0]] + [box[0] for box in arrived],
+            gain_one,
+            grad_middle,
+            q_sums,
+            kv_sums,
+            half,
+        )
+    )
+    late = Everywhere(late, links[1:] + links[:1])
+    late.send()
+    out_total = flights.land(out_total, through=out_other)
+    q_keep, q_box = next_step(q_keep, q_box, q_bits)
+    act, middle = chain(act, middle)
+    (layer_output,) = rows_matmul(
+        "down_own", [act], [w_down], layer_end, [middle, down_back[0], bias_down], [like(flat, width)], NT
+    )
+    layer_output = chain.done(layer_output).reshape(rows, tokens, width)
     part_hidden = chain(part_hidden)
-    hidden_seq = swap(part_hidden, "seq", top)
-    late_guard = small_step(part_hidden)
-    while q_back is not None or kv_back is not None:
-        if kv_back is not None:
-            kv_keep, kv_back = next_step(kv_keep, kv_back, kv_bits)
-        late_guard = small_step(late_guard)
-        if q_back is not None:
-            q_keep, q_back = next_step(q_keep, q_back, q_bits)
-    kv_seq, q_seq = swap(kv_keep, "seq", top), swap(q_keep, "seq", top)
-    hidden_seq = chain(hidden_seq)
-    hidden_total = chain.done(seq_rest(part_hidden, hidden_seq))
-    hidden_other = swap(hidden_total, "seq", 1)
-    while todo or moving:
-        late_guard = small_step(late_guard)
-    (late,) = small
-
-    own_lines = lax.dynamic_slice_in_dim(lines_all[0], me * shard_rows, shard_rows, 1)
-    late_lines = lax.dynamic_slice_in_dim(late, me * shard_rows, shard_rows, 1)
-
-    def whole(mine, other, size, total):
-        return jnp.where(
-            is_first,
-            jnp.concatenate([mine[:, :size], other[:, : total - size]], axis=1),
-            jnp.concatenate([other[:, :size], mine[:, : total - size]], axis=1),
-        )
-
-    bias_line = lines_all[1]
-    full_bias = whole(bias_line, swap(bias_line, "seq", 1), ff_half, ff)[0]
-    full_down = whole(down_total, down_other, ff_half, ff).T
-    full_hidden = whole(hidden_total, hidden_other, ff_half, ff)
-    out_total, q_total, kv_total = seq_rest(out_keep, out_seq), seq_rest(q_keep, q_seq), seq_rest(kv_keep, kv_seq)
-    out_other, q_other, kv_other = [swap(a, "seq", 1) for a in (out_total, q_total, kv_total)]
-    full_out = jnp.where(
-        is_first,
-        jnp.concatenate([out_total[:, :out_cut], out_other], axis=1),
-        jnp.concatenate([out_other[:, :out_cut], out_total], axis=1),
-    )
-    full_query = whole(q_total, q_other, half, width)
-    full_key = whole(kv_total[:, :padded], kv_other[:, :padded], half, width)
-    full_value = whole(kv_total[:, padded:], kv_other[:, padded:], half, width)
+    hidden_seq = flights.send(part_hidden, "seq", top)
+    full_out = chain.done(both_cores(core_flag, chain(out_total), out_other[0], out_cut, width))
+    done = {}
+    full_hidden = None
+
+    def finish(name, keep, box):
+        if name not in done:
+            done[name] = [keep, flights.send(keep, "seq", top)]
+        elif len(done[name]) == 2:
+            total = seq_rest(done[name][0], done[name][1][0])
+            done[name] = [total, flights.send(total, "seq", 1), None]
+
+    while flights.open:
+        full_out = flights.land(full_out)
+        late.step()
+        small.step()
+        if kv_box is not None:
+            kv_keep, kv_box = next_step(kv_keep, kv_box, kv_bits)
+        if kv_box is None:
+            finish("kv", kv_keep, kv_box)
+        if q_box is not None:
+            q_keep, q_box = next_step(q_keep, q_box, q_bits)
+        if q_box is None:
+            finish("q", q_keep, q_box)
+        if full_hidden is None and "hidden" in done:
+            total, other, _ = done["hidden"]
+            full_hidden = chain.done(both_cores(core_flag, chain(total), other[0], ff_half, ff))
+        if "hidden" not in done:
+            total = seq_rest(part_hidden, hidden_seq[0])
+            done["hidden"] = [total, flights.send(total, "seq", 1), None]
+    kv_total, kv_other = done["kv"][0], done["kv"][1][0]
+    q_total, q_other = done["q"][0], done["q"][1][0]
+
+    own_lines = lax.dynamic_slice_in_dim(small.array, me * shard_rows, shard_rows, 1)
+    late_lines = lax.dynamic_slice_in_dim(late.array, me * shard_rows, shard_rows, 1)
+    cuts = [width, ff_half - width, width, ff - ff_half - width]
+    full_bias = jnp.concatenate([small.array[4 + i, :size] for i, size in enumerate(cuts)])
+    full_query = both_cores(core_flag, q_total, q_other, half, width)
+    full_key = both_cores(core_flag, kv_total, kv_other, half, width)
+    full_value = both_cores(core_flag, kv_total, kv_other, half, width, padded)
     return (
         layer_output,
         grad_patches.reshape(rows, tokens, width),

time: 754 us -> 731 us (0.969)
  Pallas kernels: 207 us -> 401 us
  matrix products: 109 us -> 26 us
  waiting for transfers between devices: 239 us -> 168 us
  other arithmetic: 50.1 us -> 4.89 us
  local copies, waits for them, and re-layouts: 57 us -> 43 us
  starting transfers between devices: 69.2 us -> 61.1 us
    pallas_call x3 -> x51, Pallas kernels: 15.5 us -> 206 us  [the longest x9 99 us: rows_matmul(): pl.pallas_call(kernel, out_shape=shapes, grid=(steps,), in_specs=[pl.Bloc...]
    dot_general x13 -> x2, matrix products: 109 us -> 26 us  [dot(): lax.dot_general(left, right, (dims, ((), ())), preferred_element_type=F32)]
    ppermute x84 -> x70, waiting for transfers between devices: 239 us -> 168 us  [swap(): return lax.ppermute(array, axis, [(i, i ^ bits) for i in range(size)])]
    convert_element_type x15 -> x0, other arithmetic: 15.8 us -> none  [the longest x6 4.1 us: scatter_step(): (keep[part].astype(F32) + arrived[part].astype(F32)).astype(BF16)]
    another operation x12 -> x0, local copies, waits for them, and re-layouts: 12.4 us -> none  [the longest x9 9 us: local(): jnp.stack([first_gain, first_shift, query_bias, value_bias, output_bias,...]
    select_n x10 -> x1, other arithmetic: 10 us -> 0.01 us  [weight_grad(): table[order] % half * rows]
    broadcast_in_dim x2 -> x9, local copies, waits for them, and re-layouts: 0.02 us -> 9.88 us  [the longest x8 9.87 us: local(): vector[None]]
    ppermute x84 -> x70, starting transfers between devices: 69.1 us -> 60.8 us  [swap(): return lax.ppermute(array, axis, [(i, i ^ bits) for i in range(size)])]
  transfers between devices with their start and end apart: 86 -> 72, of which waited for: 30 -> 25; matrix products, arithmetic and copies ran while one was open for 25% -> 5% of each run, Pallas kernels for 23% -> 50%
where the time goes in v4:
time: 731 us; the launch traced here: 719 us
  Pallas kernels  401 us (55%)
  waiting for transfers between devices  168 us (23%)
  starting transfers between devices  61.1 us (8%)
  local copies, waits for them, and re-layouts  43 us (6%)
  matrix products  26 us (4%)
  between operations  15 us (2%)
    ppermute x70, waiting for transfers between devices, swap(): return lax.ppermute(array, axis, [(i, i ^ bits) for i in range(size)])  168 us
    pallas_call x9, Pallas kernels, rows_matmul(): pl.pallas_call(kernel, out_shape=shapes, grid=(steps,), in_specs=[pl.Bloc...  99 us
    pallas_call x38, Pallas kernels, small_call(): pl.pallas_call(kernel, out_shape=outs, in_specs=[pl.BlockSpec(memory_spac...  85.3 us
    pallas_call x3, Pallas kernels, attend_back(): pl.pallas_call(functools.partial(attend_back_kernel, row, heads, blocks,...  63.2 us
    ppermute x70, starting transfers between devices, swap(): return lax.ppermute(array, axis, [(i, i ^ bits) for i in range(size)])  60.8 us
    pallas_call x3, Pallas kernels, weight_grad(): pl.pallas_call(functools.partial(weight_grad_kernel, pairs, count, rows),...  33.2 us
    pallas_call x3, Pallas kernels, attend(): pl.pallas_call(functools.partial(attend_kernel, row, heads, blocks, padde...  32.9 us
    dot_general x2, matrix products, dot(): lax.dot_general(left, right, (dims, ((), ())), preferred_element_type=F32)  26 us
  transfers between devices with their start and end apart: 72, of which 25 were waited for; matrix products, arithmetic and copies ran while one was open for 5% of the time, Pallas kernels for 50%

profile of v4, /device:TPU:0, one launch (start us, length us, event | category | flops | bytes accessed | tf_op | source)
XLA Modules:
  0.0 718.8 jit_solution(4656377501579126046)
XLA Ops:
  44.8 11.4 %collective-permute-done.5.refs_4_ = bf16[144,1920]{1,0:T(8,128)(2,1)} collective-permute-done((bf16[144,1920]{1,0:T(8,128)(2,1)}, bf16[144,1920]{1,0:T(8,128)(2,1)}, u32[]{:S(2)}, u32[]{:S(2)}) %collective-permute-start.5) | collective-permute-done | bytes 552992 | tf_op jit(solution)/shard_map/ppermute | solution.py:42
  74.4 12.2 %collective-permute-done.17.refs_5_ = bf16[144,1920]{1,0:T(8,128)(2,1)} collective-permute-done((bf16[144,1920]{1,0:T(8,128)(2,1)}, bf16[144,1920]{1,0:T(8,128)(2,1)}, u32[]{:S(2)}, u32[]{:S(2)}) %collective-permute-start.17) | collective-permute-done | bytes 552992 | tf_op jit(solution)/shard_map/ppermute | solution.py:42
  115.9 9.7 %near.1 = bf16[1536,1280]{1,0:T(8,128)(2,1)} custom-call(bf16[1536,1152]{1,0:T(8,128)(2,1)} %norm.2.refs_0_, bf16[1152,1280]{1,0:T(8,128)(2,1)} %get-tuple-element.441.refs_1_.refs_3_, f32[1,1280]{1,0:T(1,128)} %get-tuple-element.294.refs_2_), custom_call_target="tpu_custom_call" | custom-call | flops 1 | bytes 1 | tf_op jit(solution)/shard_map/near/pallas_call | solution.py:478
  135.4 9.7 %far.1 = bf16[1536,1280]{1,0:T(8,128)(2,1)} custom-call(bf16[1536,1152]{1,0:T(8,128)(2,1)} %norm.3.refs_0_.refs_1_, bf16[1152,1280]{1,0:T(8,128)(2,1)} %get-tuple-element.441.refs_1_.refs_3_, f32[1,1280]{1,0:T(1,128)} %get-tuple-element.294.refs_2_), custom_call_target="tpu_custom_call" | custom-call | flops 1 | bytes 1 | tf_op jit(solution)/shard_map/far/pallas_call | solution.py:478
  145.1 12.7 %attend.3 = (bf16[3,256,640]{2,1,0:T(8,128)(2,1)}, bf16[3,256,640]{2,1,0:T(8,128)(2,1)}, f32[3,8,512]{2,1,0:T(8,128)}) custom-call(s32[3,4]{1,0:T(4,128)} %get-tuple-element.276.need_ref, s32[3,512,1]{2,1,0:T(8,128)} %get-tuple-element.280.col_ref, s32[3,4,256]{2,1,0:T(4,128)} %get-tuple-element.277.row_ref, bf16[2,3,256,640]{3,2,1,0:T(8,128)(2,1)} %bitcast.50, ...), custom_call_target="tpu_custom_call" | custom-call | flops 1 | bytes 1 | tf_op jit(solution)/shard_map/attend/pallas_call | solution.py:865
  169.0 11.0 %attend.4 = (bf16[3,256,640]{2,1,0:T(8,128)(2,1)}, bf16[3,256,640]{2,1,0:T(8,128)(2,1)}, f32[3,8,512]{2,1,0:T(8,128)}) custom-call(s32[3,4]{1,0:T(4,128)} %get-tuple-element.276.need_ref, s32[3,512,1]{2,1,0:T(8,128)} %get-tuple-element.280.col_ref, ...), custom_call_target="tpu_custom_call", output_to_operand_aliasing={{0}: (6, {}), {1}: (7, {}), {2}: (8, {})} | custom-call | flops 1 | bytes 1 | tf_op jit(solution)/shard_map/attend/pallas_call | solution.py:865
  180.0 9.2 %attend.5 = (bf16[3,256,640]{2,1,0:T(8,128)(2,1)}, bf16[3,256,640]{2,1,0:T(8,128)(2,1)}, f32[3,8,512]{2,1,0:T(8,128)}) custom-call(s32[3,4]{1,0:T(4,128)} %get-tuple-element.276.need_ref, s32[3,512,1]{2,1,0:T(8,128)} %get-tuple-element.280.col_ref, ...), custom_call_target="tpu_custom_call", output_to_operand_aliasing={{0}: (6, {}), {1}: (7, {}), {2}: (8, {})} | custom-call | flops 1 | bytes 1 | tf_op jit(solution)/shard_map/attend/pallas_call | solution.py:865
  236.7 18.7 %hidden.1 = (bf16[1536,2176]{1,0:T(8,128)(2,1)}, bf16[1536,2176]{1,0:T(8,128)(2,1)}, bf16[1536,1152]{1,0:T(8,128)(2,1)}) custom-call(bf16[768,1152]{1,0:T(8,128)(2,1)} %get-tuple-element.360.refs_0_, bf16[768,1152]{1,0:T(8,128)(2,1)} %collective-permute-done.30.refs_1_, bf16[1152,2176]{1,0:T(8,128)(2,1)} %get-tuple-element.362.refs_2_.refs_1_, ...), custom_call_target="tpu_custom_call" | custom-call | flops 1 | bytes 1 | tf_op jit(solution)/shard_map/hidden/pallas_call | solution.py:749
  255.4 13.0 %convolution_convert_fusion.1 = bf16[1152,2176]{1,0:T(8,128)(2,1)} fusion(bf16[1536,1152]{1,0:T(8,128)(2,1)S(1)} %copy-done.3, bf16[1536,2176]{1,0:T(8,128)(2,1)} %get-tuple-element.481.refs_0_), kind=kOutput, calls=%fused_computation.2 | convolution fusion | flops 7703248896 | bytes 15237120 | tf_op jit(solution)/shard_map/dot_general | solution.py:29
  270.8 22.0 %collective-permute-done.31.refs_5_ = bf16[144,2176]{1,0:T(8,128)(2,1)S(1)} collective-permute-done((bf16[144,2176]{1,0:T(8,128)(2,1)}, bf16[144,2176]{1,0:T(8,128)(2,1)S(1)}, u32[]{:S(2)}, u32[]{:S(2)}) %collective-permute-start.31) | collective-permute-done | bytes 626720 | tf_op jit(solution)/shard_map/ppermute | solution.py:42
  292.8 16.7 %collective-permute-done.32.refs_7_ = bf16[144,2176]{1,0:T(8,128)(2,1)S(1)} collective-permute-done((bf16[144,2176]{1,0:T(8,128)(2,1)}, bf16[144,2176]{1,0:T(8,128)(2,1)S(1)}, u32[]{:S(2)}, u32[]{:S(2)}) %collective-permute-start.32) | collective-permute-done | bytes 626720 | tf_op jit(solution)/shard_map/ppermute | solution.py:42
  315.3 14.7 %grad_pre.1 = (bf16[1536,2176]{1,0:T(8,128)(2,1)}, f32[1,2176]{1,0:T(1,128)}) custom-call(bf16[1536,1152]{1,0:T(8,128)(2,1)} %stack_rows.1.refs_0_, bf16[1152,2176]{1,0:T(8,128)(2,1)} %assemble.5.refs_1_, bf16[1536,2176]{1,0:T(8,128)(2,1)} %get-tuple-element.377.refs_2_), custom_call_target="tpu_custom_call" | custom-call | flops 1 | bytes 1 | tf_op jit(solution)/shard_map/grad_pre/pallas_call | solution.py:478
  330.0 14.9 %back.1 = (bf16[768,1152]{1,0:T(8,128)(2,1)}, bf16[768,1152]{1,0:T(8,128)(2,1)}) custom-call(bf16[1536,2176]{1,0:T(8,128)(2,1)} %get-tuple-element.382.refs_0_, bf16[1152,2176]{1,0:T(8,128)(2,1)} %get-tuple-element.362.refs_2_.refs_1_), custom_call_target="tpu_custom_call" | custom-call | flops 1 | bytes 1 | tf_op jit(solution)/shard_map/back/pallas_call | solution.py:478
  344.9 13.0 %convolution_convert_fusion = bf16[1152,2176]{1,0:T(8,128)(2,1)} fusion(bf16[1536,1152]{1,0:T(8,128)(2,1)S(1)} %copy-done.56, bf16[1536,2176]{1,0:T(8,128)(2,1)} %get-tuple-element.382.refs_0_), kind=kOutput, calls=%fused_computation.1 | convolution fusion | flops 7703248896 | bytes 15237120 | tf_op jit(solution)/shard_map/dot_general | solution.py:29
  364.3 12.3 %second_back.1 = (f32[768,1152]{1,0:T(8,128)}, bf16[768,1152]{1,0:T(8,128)(2,1)}, bf16[768,640]{1,0:T(8,128)(2,1)}, bf16[768,640]{1,0:T(8,128)(2,1)}, f32[8,1152]{1,0:T(8,128)}) custom-call(s32[1]{0:T(128)} %bitcast.1.core_ref, f32[768,1152]{1,0:T(8,128)} %get-tuple-element.482.x_ref.refs_2_, bf16[768,1152]{1,0:T(8,128)(2,1)} %get-tuple-element.383.refs_0_, ...), custom_call_target="tpu_custom_call" | custom-call | flops 1 | bytes 1 | tf_op jit(solution)/shard_map/second_back/pallas_call | solution.py:405
  392.7 21.9 %attend_back.3 = (bf16[2,3,256,640]{3,2,1,0:T(8,128)(2,1)}, bf16[2,3,256,1280]{3,2,1,0:T(8,128)(2,1)}, bf16[2,3,256,1280]{3,2,1,0:T(8,128)(2,1)}) custom-call(s32[3,4]{1,0:T(4,128)} %get-tuple-element.276.need_ref, s32[3,4,256,1]{3,2,1,0:T(8,128)} %get-tuple-element.278.col_ref, s32[3,1,512]{2,1,0:T(1,128)} %get-tuple-element.279.row_ref, ...), custom_call_target="tpu_custom_call" | custom-call | flops 1 | bytes 1 | tf_op jit(solution)/shard_map/attend_back/pallas_call | solution.py:963
  421.9 18.7 %attend_back.4 = (bf16[2,3,256,640]{3,2,1,0:T(8,128)(2,1)}, bf16[2,3,256,1280]{3,2,1,0:T(8,128)(2,1)}, bf16[2,3,256,1280]{3,2,1,0:T(8,128)(2,1)}) custom-call(s32[3,4]{1,0:T(4,128)} %get-tuple-element.276.need_ref, s32[3,4,256,1]{3,2,1,0:T(8,128)} %get-tuple-element.278.col_ref, ...), custom_call_target="tpu_custom_call", output_to_operand_aliasing={{0}: (12, {}), {1}: (13, {}), {2}: (14, {})} | custom-call | flops 1 | bytes 1 | tf_op jit(solution)/shard_map/attend_back/pallas_call | solution.py:963
  452.4 22.6 %attend_back.5 = (bf16[2,3,256,640]{3,2,1,0:T(8,128)(2,1)}, bf16[2,3,256,1280]{3,2,1,0:T(8,128)(2,1)}, bf16[2,3,256,1280]{3,2,1,0:T(8,128)(2,1)}) custom-call(s32[3,4]{1,0:T(4,128)} %get-tuple-element.276.need_ref, s32[3,4,256,1]{3,2,1,0:T(8,128)} %get-tuple-element.278.col_ref, ...), custom_call_target="tpu_custom_call", output_to_operand_aliasing={{0}: (12, {}), {1}: (13, {}), {2}: (14, {})} | custom-call | flops 1 | bytes 1 | tf_op jit(solution)/shard_map/attend_back/pallas_call | solution.py:963
  478.4 10.3 %back_far.1 = (bf16[768,1152]{1,0:T(8,128)(2,1)}, bf16[768,1152]{1,0:T(8,128)(2,1)}) custom-call(bf16[1536,1280]{1,0:T(8,128)(2,1)} %bitcast.58, bf16[1152,1280]{1,0:T(8,128)(2,1)} %get-tuple-element.441.refs_1_.refs_3_), custom_call_target="tpu_custom_call" | custom-call | flops 1 | bytes 1 | tf_op jit(solution)/shard_map/back_far/pallas_call | solution.py:478
  508.1 17.3 %weight_grad.4 = (bf16[576,1280]{1,0:T(8,128)(2,1)}, bf16[576,1280]{1,0:T(8,128)(2,1)}, f32[8,1280]{1,0:T(8,128)}) custom-call(s32[9]{0:T(128)} %pad_add_fusion.1.pos_ref, bf16[1536,1152]{1,0:T(8,128)(2,1)} %norm.2.refs_0_, bf16[1536,1152]{1,0:T(8,128)(2,1)} %norm.3.refs_0_.refs_1_, bf16[1536,1280]{1,0:T(8,128)(2,1)} %bitcast.56, bf16[1536,1280]{1,0:T(8,128)(2,1)} %bitcast.59), custom_call_target="tpu_custom_call" | custom-call | flops 1 | bytes 1 | tf_op jit(solution)/shard_map/weight_grad/pallas_call | solution.py:187
  527.9 13.5 %back_near.1 = (bf16[768,1152]{1,0:T(8,128)(2,1)}, bf16[768,1152]{1,0:T(8,128)(2,1)}) custom-call(bf16[1536,640]{1,0:T(8,128)(2,1)} %bitcast.61, bf16[1536,1280]{1,0:T(8,128)(2,1)} %bitcast.57, bf16[1152,640]{1,0:T(8,128)(2,1)} %get-tuple-element.307.refs_1_.refs_2_, bf16[1152,1280]{1,0:T(8,128)(2,1)} %get-tuple-element.441.refs_1_.refs_3_), custom_call_target="tpu_custom_call" | custom-call | flops 1 | bytes 1 | tf_op jit(solution)/shard_map/back_near/pallas_call | solution.py:478
  565.7 11.2 %collective-permute-done.54.right_ref = bf16[576,1280]{1,0:T(8,128)(2,1)} collective-permute-done((bf16[576,1280]{1,0:T(8,128)(2,1)}, bf16[576,1280]{1,0:T(8,128)(2,1)}, u32[]{:S(2)}, u32[]{:S(2)}) %collective-permute-start.54) | collective-permute-done | bytes 1474592 | tf_op jit(solution)/shard_map/ppermute | solution.py:42
  598.5 10.0 %down_own.1 = bf16[768,1152]{1,0:T(8,128)(2,1)} custom-call(bf16[1536,2176]{1,0:T(8,128)(2,1)} %get-tuple-element.481.refs_0_, bf16[1152,2176]{1,0:T(8,128)(2,1)} %assemble.5.refs_1_, f32[768,1152]{1,0:T(8,128)} %get-tuple-element.482.x_ref.refs_2_, bf16[768,1152]{1,0:T(8,128)(2,1)} %copy-done.8, f32[1,1152]{1,0:T(1,128)} %get-tuple-element.560.refs_4_), custom_call_target="tpu_custom_call" | custom-call | flops 1 | bytes 1 | tf_op jit(solution)/shard_map/down_own/pallas_call | solution.py:478
  637.9 21.3 %collective-permute-done.59.right_ref = f32[8,1152]{1,0:T(8,128)S(1)} collective-permute-done((f32[8,1152]{1,0:T(8,128)}, f32[8,1152]{1,0:T(8,128)S(1)}, u32[]{:S(2)}, u32[]{:S(2)}) %collective-permute-start.59) | collective-permute-done | bytes 36896 | tf_op jit(solution)/shard_map/ppermute | solution.py:42
  (346 shorter events, 355.8 us)
Async XLA Ops:
  7.2 441.7 %reduce-scatter.3.cloned.1.call-start = ((), (), s32[]{:S(2)}) async-start(), calls=%async_computation.2 | async-start | bytes 5640192 | tf_op jit(solution)/shard_map/reduce_scatter | solution.py:1206
  27.5 43.8 %collective-permute-start.3 = (bf16[512,1152]{1,0:T(8,128)(2,1)}, bf16[512,1152]{1,0:T(8,128)(2,1)}, u32[]{:S(2)}, u32[]{:S(2)}) collective-permute-start(bf16[512,1152]{1,0:T(8,128)(2,1)} %bitcast.3), channel_id=1, source_target_pairs={{0,16},{8,24},{16,0},{24,8},{1,17},{9,25},{17,1},{25,9},{2,18},{10... | collective-permute-start | bytes 3538952 | tf_op jit(solution)/shard_map/ppermute | solution.py:42
  41.9 50.8 %collective-permute-start.18 = (bf16[768,1152]{1,0:T(8,128)(2,1)S(1)}, bf16[768,1152]{1,0:T(8,128)(2,1)S(1)}, u32[]{:S(2)}, u32[]{:S(2)}) collective-permute-start(bf16[768,1152]{1,0:T(8,128)(2,1)S(1)} %bitcast.66), channel_id=1, source_target_pairs={{0,8},{8,0},{16,24},{24,16},{1,9},{9,1},{17,25},{25,17},{2,10},{10... | collective-permute-start | bytes 5308424 | tf_op jit(solution)/shard_map/ppermute | solution.py:42
  71.3 29.7 %collective-permute-start.15 = (bf16[512,1152]{1,0:T(8,128)(2,1)}, bf16[512,1152]{1,0:T(8,128)(2,1)}, u32[]{:S(2)}, u32[]{:S(2)}) collective-permute-start(bf16[512,1152]{1,0:T(8,128)(2,1)} %collective-permute-done.3.refs_1_), channel_id=1, source_target_pairs={{0,8},{8,0},{16,24},{24,16},{1,9},{9,1},{17,25},{25,17},{2,10},{10... | collective-permute-start | bytes 3538952 | tf_op jit(solution)/shard_map/ppermute | solution.py:42
  72.9 28.1 %collective-permute-start.13 = (bf16[144,2816]{1,0:T(8,128)(2,1)}, bf16[144,2816]{1,0:T(8,128)(2,1)}, u32[]{:S(2)}, u32[]{:S(2)}) collective-permute-start(bf16[144,2816]{1,0:T(8,128)(2,1)} %get-tuple-element.272.refs_0_), channel_id=1, source_target_pairs={{0,2},{1,3},{2,0},{3,1},{4,6},{5,7},{6,4},{7,5},{8,10},{9,11},{10,... | collective-permute-start | bytes 2433032 | tf_op jit(solution)/shard_map/ppermute | solution.py:42
  92.7 39.9 %collective-permute-start.2 = (bf16[144,2816]{1,0:T(8,128)(2,1)}, bf16[144,2816]{1,0:T(8,128)(2,1)}, u32[]{:S(2)}, u32[]{:S(2)}) collective-permute-start(bf16[144,2816]{1,0:T(8,128)(2,1)} %get-tuple-element.272.refs_0_), channel_id=1, source_target_pairs={{0,4},{1,5},{2,6},{3,7},{4,0},{5,1},{6,2},{7,3},{8,12},{9,13},{10,... | collective-permute-start | bytes 2433032 | tf_op jit(solution)/shard_map/ppermute | solution.py:42
  101.0 31.5 %collective-permute-start.19 = (bf16[144,2816]{1,0:T(8,128)(2,1)}, bf16[144,2816]{1,0:T(8,128)(2,1)S(1)}, u32[]{:S(2)}, u32[]{:S(2)}) collective-permute-start(bf16[144,2816]{1,0:T(8,128)(2,1)} %collective-permute-done.13.refs_2_), channel_id=1, source_target_pairs={{0,1},{1,0},{2,3},{3,2},{4,5},{5,4},{6,7},{7,6},{8,9},{9,8},{10,11... | collective-permute-start | bytes 2433032 | tf_op jit(solution)/shard_map/ppermute | solution.py:42
  132.5 32.8 %collective-permute-start.21 = (bf16[144,2816]{1,0:T(8,128)(2,1)}, bf16[144,2816]{1,0:T(8,128)(2,1)S(1)}, u32[]{:S(2)}, u32[]{:S(2)}) collective-permute-start(bf16[144,2816]{1,0:T(8,128)(2,1)} %collective-permute-done.2.refs_4_), channel_id=1, source_target_pairs={{0,2},{1,3},{2,0},{3,1},{4,6},{5,7},{6,4},{7,5},{8,10},{9,11},{10,... | collective-permute-start | bytes 2433032 | tf_op jit(solution)/shard_map/ppermute | solution.py:42
  133.4 32.0 %collective-permute-start.20 = (bf16[144,2816]{1,0:T(8,128)(2,1)}, bf16[144,2816]{1,0:T(8,128)(2,1)}, u32[]{:S(2)}, u32[]{:S(2)}) collective-permute-start(bf16[144,2816]{1,0:T(8,128)(2,1)} %collective-permute-done.2.refs_4_), channel_id=1, source_target_pairs={{0,1},{1,0},{2,3},{3,2},{4,5},{5,4},{6,7},{7,6},{8,9},{9,8},{10,11... | collective-permute-start | bytes 2433032 | tf_op jit(solution)/shard_map/ppermute | solution.py:42
  133.9 31.5 %collective-permute-start.1 = (bf16[144,2176]{1,0:T(8,128)(2,1)}, bf16[144,2176]{1,0:T(8,128)(2,1)}, u32[]{:S(2)}, u32[]{:S(2)}) collective-permute-start(bf16[144,2176]{1,0:T(8,128)(2,1)} %get-tuple-element.271.refs_0_), channel_id=1, source_target_pairs={{0,1},{1,0},{2,3},{3,2},{4,5},{5,4},{6,7},{7,6},{8,9},{9,8},{10,11... | collective-permute-start | bytes 1880072 | tf_op jit(solution)/shard_map/ppermute | solution.py:42
  165.4 28.7 %collective-permute-start.22 = (bf16[144,2816]{1,0:T(8,128)(2,1)S(1)}, bf16[144,2816]{1,0:T(8,128)(2,1)S(1)}, u32[]{:S(2)}, u32[]{:S(2)}) collective-permute-start(bf16[144,2816]{1,0:T(8,128)(2,1)S(1)} %collective-permute-done.21.refs_6_), channel_id=1, source_target_pairs={{0,1},{1,0},{2,3},{3,2},{4,5},{5,4},{6,7},{7,6},{8,9},{9,8},{10,11... | collective-permute-start | bytes 2433032 | tf_op jit(solution)/shard_map/ppermute | solution.py:42
  166.1 27.9 %collective-permute-start.24 = (bf16[144,2176]{1,0:T(8,128)(2,1)}, bf16[144,2176]{1,0:T(8,128)(2,1)}, u32[]{:S(2)}, u32[]{:S(2)}) collective-permute-start(bf16[144,2176]{1,0:T(8,128)(2,1)} %get-tuple-element.271.refs_0_), channel_id=1, source_target_pairs={{0,4},{1,5},{2,6},{3,7},{4,0},{5,1},{6,2},{7,3},{8,12},{9,13},{10,... | collective-permute-start | bytes 1880072 | tf_op jit(solution)/shard_map/ppermute | solution.py:42
  169.0 33.6 %collective-permute-start.27 = (bf16[768,1152]{1,0:T(8,128)(2,1)S(1)}, bf16[768,1152]{1,0:T(8,128)(2,1)}, u32[]{:S(2)}, u32[]{:S(2)}) collective-permute-start(bf16[768,1152]{1,0:T(8,128)(2,1)S(1)} %bitcast.75), channel_id=1, source_target_pairs={{0,8},{8,0},{16,24},{24,16},{1,9},{9,1},{17,25},{25,17},{2,10},{10... | collective-permute-start | bytes 5308424 | tf_op jit(solution)/shard_map/ppermute | solution.py:42
  268.5 340.0 %reduce-scatter.5.cloned.1.call-start = ((), (), s32[]{:S(2)}) async-start(), calls=%async_computation.3 | async-start | bytes 5640192 | tf_op jit(solution)/shard_map/reduce_scatter | solution.py:1231
  269.7 39.8 %collective-permute-start.32 = (bf16[144,2176]{1,0:T(8,128)(2,1)}, bf16[144,2176]{1,0:T(8,128)(2,1)S(1)}, u32[]{:S(2)}, u32[]{:S(2)}) collective-permute-start(bf16[144,2176]{1,0:T(8,128)(2,1)} %collective-permute-done.28.refs_6_), channel_id=1, source_target_pairs={{0,1},{1,0},{2,3},{3,2},{4,5},{5,4},{6,7},{7,6},{8,9},{9,8},{10,11... | collective-permute-start | bytes 1880072 | tf_op jit(solution)/shard_map/ppermute | solution.py:42
  488.7 36.8 %collective-permute-start.48 = (bf16[768,1152]{1,0:T(8,128)(2,1)}, bf16[768,1152]{1,0:T(8,128)(2,1)S(1)}, u32[]{:S(2)}, u32[]{:S(2)}) collective-permute-start(bf16[768,1152]{1,0:T(8,128)(2,1)} %get-tuple-element.443), channel_id=1, source_target_pairs={{0,8},{8,0},{16,24},{24,16},{1,9},{9,1},{17,25},{25,17},{2,10},{10... | collective-permute-start | bytes 5308424 | tf_op jit(solution)/shard_map/ppermute | solution.py:42
  541.4 38.6 %collective-permute-start.53 = (bf16[768,1152]{1,0:T(8,128)(2,1)}, bf16[768,1152]{1,0:T(8,128)(2,1)S(1)}, u32[]{:S(2)}, u32[]{:S(2)}) collective-permute-start(bf16[768,1152]{1,0:T(8,128)(2,1)} %get-tuple-element.459), channel_id=1, source_target_pairs={{0,8},{8,0},{16,24},{24,16},{1,9},{9,1},{17,25},{25,17},{2,10},{10... | collective-permute-start | bytes 5308424 | tf_op jit(solution)/shard_map/ppermute | solution.py:42
  541.4 35.5 %collective-permute-start.54 = (bf16[576,1280]{1,0:T(8,128)(2,1)}, bf16[576,1280]{1,0:T(8,128)(2,1)}, u32[]{:S(2)}, u32[]{:S(2)}) collective-permute-start(bf16[576,1280]{1,0:T(8,128)(2,1)} %get-tuple-element.452), channel_id=1, source_target_pairs={{0,1},{1,0},{2,3},{3,2},{4,5},{5,4},{6,7},{7,6},{8,9},{9,8},{10,11... | collective-permute-start | bytes 4423688 | tf_op jit(solution)/shard_map/ppermute | solution.py:42
  545.9 41.0 %collective-permute-start.52 = (bf16[768,1152]{1,0:T(8,128)(2,1)}, bf16[768,1152]{1,0:T(8,128)(2,1)}, u32[]{:S(2)}, u32[]{:S(2)}) collective-permute-start(bf16[768,1152]{1,0:T(8,128)(2,1)} %add_rows.38), channel_id=1, source_target_pairs={{0,16},{8,24},{16,0},{24,8},{1,17},{9,25},{17,1},{25,9},{2,18},{10... | collective-permute-start | bytes 5308424 | tf_op jit(solution)/shard_map/ppermute | solution.py:42
  564.1 31.4 %collective-permute-start.50 = (bf16[768,1152]{1,0:T(8,128)(2,1)}, bf16[768,1152]{1,0:T(8,128)(2,1)S(1)}, u32[]{:S(2)}, u32[]{:S(2)}) collective-permute-start(bf16[768,1152]{1,0:T(8,128)(2,1)} %down_pair.1), channel_id=1, source_target_pairs={{0,8},{8,0},{16,24},{24,16},{1,9},{9,1},{17,25},{25,17},{2,10},{10... | collective-permute-start | bytes 5308424 | tf_op jit(solution)/shard_map/ppermute | solution.py:42
  564.1 31.4 %collective-permute-start.49 = (bf16[576,640]{1,0:T(8,128)(2,1)}, bf16[576,640]{1,0:T(8,128)(2,1)}, u32[]{:S(2)}, u32[]{:S(2)}) collective-permute-start(bf16[576,640]{1,0:T(8,128)(2,1)} %get-tuple-element.463), channel_id=1, source_target_pairs={{0,1},{1,0},{2,3},{3,2},{4,5},{5,4},{6,7},{7,6},{8,9},{9,8},{10,11... | collective-permute-start | bytes 2211848 | tf_op jit(solution)/shard_map/ppermute | solution.py:42
  580.0 32.5 %collective-permute-start.55 = (bf16[288,1280]{1,0:T(8,128)(2,1)}, bf16[288,1280]{1,0:T(8,128)(2,1)}, u32[]{:S(2)}, u32[]{:S(2)}) collective-permute-start(bf16[288,1280]{1,0:T(8,128)(2,1)} %get-tuple-element.484), channel_id=1, source_target_pairs={{0,2},{1,3},{2,0},{3,1},{4,6},{5,7},{6,4},{7,5},{8,10},{9,11},{10,... | collective-permute-start | bytes 2211848 | tf_op jit(solution)/shard_map/ppermute | solution.py:42
  627.4 31.8 %collective-permute-start.62 = (f32[144,2176]{1,0:T(8,128)}, f32[144,2176]{1,0:T(8,128)S(1)}, u32[]{:S(2)}, u32[]{:S(2)}) collective-permute-start(f32[144,2176]{1,0:T(8,128)} %add_rows.44.mine_ref), channel_id=1, source_target_pairs={{0,8},{8,0},{16,24},{24,16},{1,9},{9,1},{17,25},{25,17},{2,10},{10... | collective-permute-start | bytes 3760136 | tf_op jit(solution)/shard_map/ppermute | solution.py:42
  629.7 29.5 %collective-permute-start.60 = (bf16[144,1280]{1,0:T(8,128)(2,1)}, bf16[144,1280]{1,0:T(8,128)(2,1)S(1)}, u32[]{:S(2)}, u32[]{:S(2)}) collective-permute-start(bf16[144,1280]{1,0:T(8,128)(2,1)} %get-tuple-element.492), channel_id=1, source_target_pairs={{0,4},{1,5},{2,6},{3,7},{4,0},{5,1},{6,2},{7,3},{8,12},{9,13},{10,... | collective-permute-start | bytes 1105928 | tf_op jit(solution)/shard_map/ppermute | solution.py:42
  (107 other events, 1267.7 us)
Sparse Core Ops, SparseCore 0:
  268.6 103.8 reduce-scatter.2
  376.6 106.1 reduce-scatter.4

commit v5 on v4

--- a/solution.py
+++ b/solution.py
@@ -74,7 +74,7 @@
     def land(self, *values, through=None):
         count = len(self.open)
         if through is not None:
-            count = 1 + next(i for i, box in enumerate(self.open) if box is through)
+            count = sum(i + 1 for i, box in enumerate(self.open) if box is through)
         ready, self.open = self.open[:count], self.open[count:]
         held = self.chain(*[box[0] for box in ready], *values)
         held = held if isinstance(held, (tuple, list)) else [held]
@@ -526,15 +526,9 @@
 
 
 def add_rows(left, right, kind=BF16, pieces=1):
-    rows, cols = left.shape
-    size = rows // pieces
-
-    def kernel(left_ref, right_ref, *outs):
-        for i, out_ref in enumerate(outs):
-            part = slice(i * size, (i + 1) * size)
-            out_ref[...] = (left_ref[part].astype(F32) + right_ref[part].astype(F32)).astype(kind)
-
-    return small_call(kernel, [like(size, cols, kind)] * pieces, [], [left, right], "add_rows")
+    size = left.shape[0] // pieces
+    parts = [slice(i * size, (i + 1) * size) for i in range(pieces)]
+    return [(left[part].astype(F32) + right[part].astype(F32)).astype(kind) for part in parts]
 
 
 def scatter_step(keep, arrived, rows):
@@ -560,6 +554,15 @@
 
     shape = like(total, rows, mine.dtype) if turn else like(rows, total, mine.dtype)
     return small_call(kernel, [shape], [core], [mine, other], "both_cores")[0]
+
+
+def both_columns(is_first, mine, other, size, total, start=0):
+    mine, other = mine[:, start:], other[:, start:]
+    return jnp.where(
+        is_first,
+        jnp.concatenate([mine[:, :size], other[:, : total - size]], axis=1),
+        jnp.concatenate([other[:, :size], mine[:, : total - size]], axis=1),
+    )
 
 
 def core_columns(core, arrays, cols):
@@ -701,12 +704,11 @@
     return small_call(kernel, outs, [core], [out_shard, hidden_weight, down_weight], "mlp_shards")
 
 
-def attention_shards(core, weights, vectors, half, padded):
+def attention_shards(core, weights, half, padded):
     rows, width = weights[0].shape
     cut = width - padded
 
-    def kernel(core_ref, q_ref, k_ref, v_ref, o_ref, *refs):
-        qkv_ref, out_ref, lines_ref = refs[len(vectors) :]
+    def kernel(core_ref, q_ref, k_ref, v_ref, o_ref, qkv_ref, out_ref):
         empty = jnp.zeros((rows, padded - half), BF16)
         for at in range(2):
 
@@ -717,11 +719,8 @@
                     qkv_ref[:, i * padded : (i + 1) * padded] = jnp.concatenate([part, empty], axis=1)
                 out_ref[...] = o_ref[:, at * cut : at * cut + padded]
 
-        for i in range(len(vectors)):
-            lines_ref[i : i + 1] = refs[i][...]
-
-    outs = [like(rows, 3 * padded), like(rows, padded), like(len(vectors), vectors[0].shape[1])]
-    return small_call(kernel, outs, [core], [*weights, *vectors], "attention_shards")
+    outs = [like(rows, 3 * padded), like(rows, padded)]
+    return small_call(kernel, outs, [core], weights, "attention_shards")
 
 
 def hidden(arrays, weight, bias):
@@ -1044,26 +1043,20 @@
 
     inputs = patches.reshape(flat, width)
     incoming = cotangent.reshape(flat, width)
-    shard_qkv, shard_out, vectors = chain.done(
+    shard_qkv, shard_out = chain.done(
         *attention_shards(
-            core_flag,
-            [query_weight, key_weight, value_weight, output_weight],
-            [
-                vector[None]
-                for vector in (
-                    first_gain,
-                    first_shift,
-                    query_bias,
-                    value_bias,
-                    output_bias,
-                    second_gain,
-                    second_shift,
-                    down_bias,
-                )
-            ],
-            half,
-            padded,
+            core_flag, [query_weight, key_weight, value_weight, output_weight], half, padded
         )
+    )
+    vectors = (
+        first_gain,
+        first_shift,
+        query_bias,
+        value_bias,
+        output_bias,
+        second_gain,
+        second_shift,
+        down_bias,
     )
     place_flag = place[None].astype(jnp.int32)
 
@@ -1073,21 +1066,18 @@
     def both(stacked_lines, arrived):
         return jnp.concatenate([stacked_lines, arrived], axis=0)
 
-    vectors = vectors[None]
     if staged:
         q = {0: [shard_qkv]}
-        vec = flights.send(vectors, "fsdp", y)
         q[y] = over(q[0], y)
         far_raw = [flights.send(patches[0], "seq", 2)]
         q[z], q[zz] = over(q[0], z), over(q[0], zz)
-        shard_out, vectors = flights.land(shard_out, vectors, through=vec)
-        vectors = both(vectors, vec[0])
-        vec = flights.send(vectors, "fsdp", z)
         shard_ho, shard_down = chain.done(
             *mlp_shards(core_flag, shard_out, hidden_weight, down_weight, ff_half)
         )
         h, d = {0: [shard_ho]}, {0: [shard_down]}
-        lengths = flights.land(lengths, through=far_raw[0])
+        lengths, *vectors = flights.land(lengths, *vectors, through=far_raw[0])
+        vectors = jnp.stack(vectors)[None]
+        vec = flights.send(vectors, "fsdp", y)
         h[y] = over(h[0], y)
         far_raw.append(flights.send(patches[1:].reshape(flat - tokens, width), "seq", 2))
         need, seg_rows, seg_cols, seg_near_row, seg_near_col = chain.done(
@@ -1095,29 +1085,33 @@
         )
         vectors = flights.land(vectors, through=vec)
         vectors = both(vectors, vec[0])
-        vec = flights.send(vectors, "fsdp", zz)
+        vec = flights.send(vectors, "fsdp", z)
         q[zz | z] = over(q[zz], z)
         q[z | y] = over(q[z], y)
         vectors = flights.land(vectors, through=h[y])
         q[zz | y] = over(q[zz], y)
         vectors = flights.land(vectors, through=q[zz | z])
+        vectors = both(vectors, vec[0])
+        vec = flights.send(vectors, "fsdp", zz)
         raw_pair = flights.send(inputs, "seq", 1)
         q[zz | z | y] = over(q[zz | z], y)
-        h[z] = over(h[0], z)
+        vectors = flights.land(vectors, through=raw_pair)
+        far_pair = [flights.send(box[0], "seq", 1) for box in far_raw]
+        h[z], h[zz] = over(h[0], z), over(h[0], zz)
         vectors = both(vectors, vec[0])
         meta = chain(jnp.stack([core, me]).astype(jnp.int32))
         stacked, bias_q, bias_kv = chain.done(*lay_vectors(meta, vectors, half, padded))
         gain_one, shift_one = stacked[0:1], stacked[1:2]
-        gain_one = flights.land(gain_one, through=raw_pair)
-        far_pair = [flights.send(box[0], "seq", 1) for box in far_raw]
-        h[zz] = over(h[0], zz)
+        gain_one = chain(gain_one)
         normed_near = chain.done(norm([inputs, raw_pair[0]], gain_one, shift_one))
         bias_hidden = my_half(after(hidden_bias, gain_one).astype(F32)[None], ff_half, ff_half)
         gain_one = flights.land(gain_one, through=far_pair[-1])
-        h[z | y], d[y] = over(h[z], y), over(d[0], y)
+        d[y] = over(d[0], y)
+        incoming_pair = flights.send(incoming, "seq", 1)
         w_q, w_kv = chain.done(*assemble({k: box[0] for k, box in q.items()}, me, padded))
     else:
         parts = gather_all(shard_qkv)
+        vectors = jnp.stack(vectors)[None]
         for k in range(shards.bit_length() - 1):
             vectors = both(vectors, swap(vectors, "fsdp", 1 << k))
         shard_ho, shard_down = mlp_shards(core_flag, shard_out, hidden_weight, down_weight, ff_half)
@@ -1131,6 +1125,7 @@
         gain_one, shift_one = stacked[0:1], stacked[1:2]
         normed_near = norm([raw[0], raw[1]], gain_one, shift_one)
         far_raw, far_pair = [[raw[j]] for j in range(2, seq_count)], []
+        incoming_pair = [swap(incoming, "seq", 1)]
         bias_hidden = my_half(hidden_bias.astype(F32)[None], ff_half, ff_half)
         w_q, w_kv = chain.done(*assemble(parts, me, padded))
     _, _, bias_query, bias_value, bias_output, gain_two, shift_two, bias_down = [
@@ -1145,8 +1140,9 @@
     gain_one, w_kv = chain(gain_one, w_kv)
     normed_far = chain.done(norm([box[0] for box in far_raw + far_pair], gain_one, shift_one))
     if staged:
-        w_kv = flights.land(w_kv, through=h[z | y])
-        h[zz | y], h[zz | z] = over(h[zz], y), over(h[zz], z)
+        w_kv, incoming = flights.land(w_kv, incoming)
+        h[z | y], h[zz | y], h[zz | z] = over(h[z], y), over(h[zz], y), over(h[zz], z)
+    incoming_near = jnp.concatenate([incoming, incoming_pair[0]], axis=0)
     far_in, w_kv = chain(normed_far, w_kv)
     (far,) = rows_matmul(
         "far", [far_in], [w_kv], with_bias, [bias_kv], [like(normed_far.shape[0], 2 * padded)]
@@ -1174,8 +1170,7 @@
     out_pair, w_out_mine = chain(out_pair, w_out_mine)
     other_half = flights.send(out_pair, "seq", 1)
     w_out_other = flights.send(w_out_mine, "seq", 1)
-    incoming_pair = flights.send(incoming, "seq", 1)
-    w_out_mine, w_hidden = flights.land(w_out_mine, w_hidden, through=incoming_pair)
+    w_out_mine, w_hidden = flights.land(w_out_mine, w_hidden)
     if staged:
         d[zz | z], d[z | y] = over(d[zz], z), over(d[z], y)
     w_out = chain.done(both_cores(core_flag, w_out_mine, w_out_other[0], out_cut, width))
@@ -1194,13 +1189,14 @@
         )
     )
     second_pair = flights.send(second, "seq", 1)
-    incoming_own = chain(incoming)
-    incoming_near = chain.done(stack_rows(incoming_own, incoming_pair[0]))
     second, w_hidden = flights.land(second, w_hidden)
     if staged:
-        d[zz | y], d[zz | z | y] = over(d[zz], y), over(d[zz | z], y)
+        d[zz | y] = over(d[zz], y)
     act, slope, second_near = chain.done(*hidden([second, second_pair[0]], w_hidden, bias_hidden))
 
+    if staged:
+        incoming_near = flights.land(incoming_near)
+        d[zz | z | y] = over(d[zz | z], y)
     incoming_near, act = chain(incoming_near, act)
     grad_down = chain.done(dot(incoming_near, act, TN).astype(BF16))
     part_down = lax.psum_scatter(grad_down, "fsdp", scatter_dimension=0, tiled=True)
@@ -1243,25 +1239,8 @@
     )
     query = flights.land(query)
 
-    links = [("seq", bit) for bit in bits_of(seq_count)] + [("fsdp", bit) for bit in bits_of(shards)]
-
-    class Everywhere:
-        def __init__(self, array, order):
-            self.array, self.todo, self.box = array, list(order), None
-
-        def send(self):
-            if self.todo:
-                self.box = flights.send(self.array, *self.todo.pop(0))
-
-        def step(self):
-            if self.box is not None:
-                self.array = chain.done(*add_rows(self.array, self.box[0], F32))
-                self.box = None
-                self.send()
-
-    small = Everywhere(lines, links)
+    small = lax.psum(lines, ("seq", "fsdp"))
     keep_back, send_back = flights.send(keep_other, "seq", 1), flights.send(send_other, "seq", 1)
-    small.send()
     shape = (rows, tokens, padded)
     grads = [grad_mine.reshape(shape), grad_pair[0].reshape(shape)]
     found = ()
@@ -1286,7 +1265,6 @@
         )
         chain.done(*found)
         query = flights.land(query)
-        small.step()
         if row == 0:
             (out_keep,), (out_send,) = add_rows(keep_mine, keep_back[0]), add_rows(send_mine, send_back[0])
             chain.done(out_keep, out_send)
@@ -1296,21 +1274,12 @@
         if row == 1:
             part_down = chain(part_down)
             down_seq = flights.send(part_down, "seq", top)
-        if row == 2:
-            down_total = seq_rest(part_down, down_seq[0])
-            down_other = flights.send(down_total, "seq", 1)
     dq, dnear, dfar = [g.reshape(-1, g.shape[-1]) for g in found]
     dfar, w_kv = chain(dfar, w_kv)
     two = seq_count == 4
     back_far = rows_matmul("back_far", [dfar], [w_kv], plain, [], [like(dfar.shape[0], width)], NT, two)
     chain.done(*back_far)
-    dnear = flights.land(dnear)
-    small.step()
-    while out_box is not None:
-        out_keep, out_box = next_step(out_keep, out_box, out_bits)
-        if out_box is not None:
-            dnear = flights.land(dnear)
-    out_seq = flights.send(out_keep, "seq", top)
+    dnear = chain(dnear)
     if two:
         far_parts = {2 + i: part for i, part in enumerate(back_far)}
     else:
@@ -1333,8 +1302,6 @@
                 arrived.append(box)
             else:
                 (far_sums[j ^ bit],) = add_rows(far_sums[j ^ bit], box[0])
-    small.step()
-    out_total = seq_rest(out_keep, out_seq[0])
     dq, dnear = chain(dq, dnear)
     back_own, back_pair = chain.done(
         *rows_matmul("back_near", [dq, dnear], [w_q, w_kv], plain, [], [like(2 * flat, width)], NT, True)
@@ -1349,11 +1316,9 @@
     )
     chain.done(down_pair)
     down_back = flights.send(down_pair, "seq", 1)
-    out_other = flights.send(out_total, "seq", 1)
     kv_bits, q_bits = list(far_bits), list(far_bits)
-    down_total = flights.land(down_total, through=kv_box)
+    act = flights.land(act, through=kv_box)
     kv_keep, kv_box = next_step(kv_keep, kv_box, kv_bits)
-    full_down = chain.done(both_cores(core_flag, chain(down_total), down_other[0], ff_half, ff, turn=True))
     late_in = flights.land(inputs, through=pair_back)
     grad_patches, late = chain.done(
         *first_back(
@@ -1367,56 +1332,54 @@
             half,
         )
     )
-    late = Everywhere(late, links[1:] + links[:1])
-    late.send()
-    out_total = flights.land(out_total, through=out_other)
+    late = lax.psum(late, ("seq", "fsdp"))
+    part_hidden = chain(part_hidden)
+    hidden_seq = flights.send(part_hidden, "seq", top)
+    act = flights.land(act, through=down_back)
     q_keep, q_box = next_step(q_keep, q_box, q_bits)
     act, middle = chain(act, middle)
     (layer_output,) = rows_matmul(
         "down_own", [act], [w_down], layer_end, [middle, down_back[0], bias_down], [like(flat, width)], NT
     )
     layer_output = chain.done(layer_output).reshape(rows, tokens, width)
-    part_hidden = chain(part_hidden)
-    hidden_seq = flights.send(part_hidden, "seq", top)
-    full_out = chain.done(both_cores(core_flag, chain(out_total), out_other[0], out_cut, width))
-    done = {}
-    full_hidden = None
-
-    def finish(name, keep, box):
-        if name not in done:
-            done[name] = [keep, flights.send(keep, "seq", top)]
-        elif len(done[name]) == 2:
-            total = seq_rest(done[name][0], done[name][1][0])
-            done[name] = [total, flights.send(total, "seq", 1), None]
-
-    while flights.open:
-        full_out = flights.land(full_out)
-        late.step()
-        small.step()
-        if kv_box is not None:
-            kv_keep, kv_box = next_step(kv_keep, kv_box, kv_bits)
-        if kv_box is None:
-            finish("kv", kv_keep, kv_box)
-        if q_box is not None:
+    down_total = seq_rest(part_down, down_seq[0])
+    while kv_box is not None:
+        act = flights.land(act, through=kv_box)
+        kv_keep, kv_box = next_step(kv_keep, kv_box, kv_bits)
+        if q_box is not None and kv_box is not None:
+            act = flights.land(act, through=q_box)
             q_keep, q_box = next_step(q_keep, q_box, q_bits)
-        if q_box is None:
-            finish("q", q_keep, q_box)
-        if full_hidden is None and "hidden" in done:
-            total, other, _ = done["hidden"]
-            full_hidden = chain.done(both_cores(core_flag, chain(total), other[0], ff_half, ff))
-        if "hidden" not in done:
-            total = seq_rest(part_hidden, hidden_seq[0])
-            done["hidden"] = [total, flights.send(total, "seq", 1), None]
-    kv_total, kv_other = done["kv"][0], done["kv"][1][0]
-    q_total, q_other = done["q"][0], done["q"][1][0]
-
-    own_lines = lax.dynamic_slice_in_dim(small.array, me * shard_rows, shard_rows, 1)
-    late_lines = lax.dynamic_slice_in_dim(late.array, me * shard_rows, shard_rows, 1)
+    kv_seq = flights.send(kv_keep, "seq", top)
+    while out_box is not None:
+        out_keep, out_box = next_step(out_keep, out_box, out_bits)
+        if out_box is not None:
+            act = flights.land(act)
+    out_seq = flights.send(out_keep, "seq", top)
+    down_other = flights.send(down_total, "seq", 1)
+    hidden_total = seq_rest(part_hidden, hidden_seq[0])
+    while q_box is not None:
+        act = flights.land(act, through=q_box)
+        q_keep, q_box = next_step(q_keep, q_box, q_bits)
+    q_seq = flights.send(q_keep, "seq", top)
+    act = flights.land(act, through=kv_seq)
+    kv_total = seq_rest(kv_keep, kv_seq[0])
+    kv_other = flights.send(kv_total, "seq", 1)
+    hidden_other = flights.send(hidden_total, "seq", 1)
+    act = flights.land(act, through=q_seq)
+    out_total = seq_rest(out_keep, out_seq[0])
+    q_total = seq_rest(q_keep, q_seq[0])
+    q_other, out_other = flights.send(q_total, "seq", 1), flights.send(out_total, "seq", 1)
+    flights.land()
+    own_lines = lax.dynamic_slice_in_dim(small, me * shard_rows, shard_rows, 1)
+    late_lines = lax.dynamic_slice_in_dim(late, me * shard_rows, shard_rows, 1)
     cuts = [width, ff_half - width, width, ff - ff_half - width]
-    full_bias = jnp.concatenate([small.array[4 + i, :size] for i, size in enumerate(cuts)])
-    full_query = both_cores(core_flag, q_total, q_other, half, width)
-    full_key = both_cores(core_flag, kv_total, kv_other, half, width)
-    full_value = both_cores(core_flag, kv_total, kv_other, half, width, padded)
+    full_bias = jnp.concatenate([small[4 + i, :size] for i, size in enumerate(cuts)])
+    full_down = both_columns(is_first, down_total, down_other[0], ff_half, ff).T
+    full_hidden = both_columns(is_first, hidden_total, hidden_other[0], ff_half, ff)
+    full_out = both_columns(is_first, out_total, out_other[0], out_cut, width)
+    full_query = both_columns(is_first, q_total, q_other[0], half, width)
+    full_key = both_columns(is_first, kv_total, kv_other[0], half, width)
+    full_value = both_columns(is_first, kv_total, kv_other[0], half, width, padded)
     return (
         layer_output,
         grad_patches.reshape(rows, tokens, width),

time: 731 us -> 755 us (1.033)
  waiting for transfers between devices: 168 us -> 262 us
  Pallas kernels: 401 us -> 324 us
  other arithmetic: 4.89 us -> 31.5 us
  local copies, waits for them, and re-layouts: 43 us -> 27.5 us
    psum x0 -> x1, waiting for transfers between devices: none -> 96.5 us  [local(): late = lax.psum(late, ('seq', 'fsdp'))]
    pallas_call x38 -> x5, Pallas kernels: 85.3 us -> 14.6 us  [small_call(): pl.pallas_call(kernel, out_shape=outs, in_specs=[pl.BlockSpec(memory_spac...]
    convert_element_type x0 -> x12, other arithmetic: none -> 11.3 us  [add_rows(): (left[part].astype(F32) + right[part].astype(F32)).astype(kind)]
    broadcast_in_dim x8 -> x0, local copies, waits for them, and re-layouts: 9.87 us -> none  [local(): vector[None]]
    unnamed x122 -> x91, local copies, waits for them, and re-layouts: 22.3 us -> 12.9 us
    ppermute x70 -> x60, starting transfers between devices: 60.8 us -> 56.4 us  [swap(): return lax.ppermute(array, axis, [(i, i ^ bits) for i in range(size)])]
    ppermute x70 -> x60, waiting for transfers between devices: 168 us -> 166 us  [swap(): return lax.ppermute(array, axis, [(i, i ^ bits) for i in range(size)])]
  transfers between devices with their start and end apart: 72 -> 63, of which waited for: 25 -> 21; matrix products, arithmetic and copies ran while one was open for 5% -> 7% of each run, Pallas kernels for 50% -> 41%
where the time goes in v5:
time: 755 us; the launch traced here: 742 us
  Pallas kernels  324 us (43%)
  waiting for transfers between devices  262 us (35%)
  starting transfers between devices  56.7 us (8%)
  other arithmetic  31.5 us (4%)
  local copies, waits for them, and re-layouts  27.5 us (4%)
  matrix products  26.1 us (3%)
  between operations  14.6 us (2%)
    ppermute x60, waiting for transfers between devices, swap(): return lax.ppermute(array, axis, [(i, i ^ bits) for i in range(size)])  166 us
    pallas_call x9, Pallas kernels, rows_matmul(): pl.pallas_call(kernel, out_shape=shapes, grid=(steps,), in_specs=[pl.Bloc...  101 us
    psum x1, waiting for transfers between devices, local(): late = lax.psum(late, ('seq', 'fsdp'))  96.5 us
    pallas_call x3, Pallas kernels, attend_back(): pl.pallas_call(functools.partial(attend_back_kernel, row, heads, blocks,...  58.8 us
    ppermute x60, starting transfers between devices, swap(): return lax.ppermute(array, axis, [(i, i ^ bits) for i in range(size)])  56.4 us
    pallas_call x3, Pallas kernels, attend(): pl.pallas_call(functools.partial(attend_kernel, row, heads, blocks, padde...  34.5 us
    pallas_call x3, Pallas kernels, weight_grad(): pl.pallas_call(functools.partial(weight_grad_kernel, pairs, count, rows),...  33.3 us
    dot_general x2, matrix products, dot(): lax.dot_general(left, right, (dims, ((), ())), preferred_element_type=F32)  26.1 us
  transfers between devices with their start and end apart: 63, of which 21 were waited for; matrix products, arithmetic and copies ran while one was open for 7% of the time, Pallas kernels for 41%

profile of v5, /device:TPU:0, one launch (start us, length us, event | category | flops | bytes accessed | tf_op | source)
XLA Modules:
  0.0 742.3 jit_solution(11209212385694986040)
XLA Ops:
  48.8 11.2 %collective-permute-done.8 = bf16[2,8,144]{2,1,0:T(8,128)(2,1)S(1)} collective-permute-done((bf16[2,8,144]{2,1,0:T(8,128)(2,1)S(1)}, bf16[2,8,144]{2,1,0:T(8,128)(2,1)S(1)}, u32[]{:S(2)}, u32[]{:S(2)}) %collective-permute-start.8) | collective-permute-done | bytes 4640 | tf_op jit(solution)/shard_map/ppermute | solution.py:42
  62.3 13.4 %collective-permute-done.5.refs_3_ = bf16[144,1920]{1,0:T(8,128)(2,1)S(1)} collective-permute-done((bf16[144,1920]{1,0:T(8,128)(2,1)}, bf16[144,1920]{1,0:T(8,128)(2,1)S(1)}, u32[]{:S(2)}, u32[]{:S(2)}) %collective-permute-start.5) | collective-permute-done | bytes 552992 | tf_op jit(solution)/shard_map/ppermute | solution.py:42
  154.8 12.6 %attend.3 = (bf16[3,256,640]{2,1,0:T(8,128)(2,1)}, bf16[3,256,640]{2,1,0:T(8,128)(2,1)}, f32[3,8,512]{2,1,0:T(8,128)}) custom-call(s32[3,4]{1,0:T(4,128)} %get-tuple-element.257.need_ref, s32[3,512,1]{2,1,0:T(8,128)} %get-tuple-element.261.col_ref, s32[3,4,256]{2,1,0:T(4,128)} %get-tuple-element.258.row_ref, bf16[2,3,256,640]{3,2,1,0:T(8,128)(2,1)} %bitcast.58, ...), custom_call_target="tpu_custom_call" | custom-call | flops 1 | bytes 1 | tf_op jit(solution)/shard_map/attend/pallas_call | solution.py:864
  167.4 11.5 %collective-permute-done.21.refs_5_ = bf16[144,2816]{1,0:T(8,128)(2,1)S(1)} collective-permute-done((bf16[144,2816]{1,0:T(8,128)(2,1)}, bf16[144,2816]{1,0:T(8,128)(2,1)S(1)}, u32[]{:S(2)}, u32[]{:S(2)}) %collective-permute-start.21) | collective-permute-done | bytes 811040 | tf_op jit(solution)/shard_map/ppermute | solution.py:42
  183.4 10.9 %attend.4 = (bf16[3,256,640]{2,1,0:T(8,128)(2,1)}, bf16[3,256,640]{2,1,0:T(8,128)(2,1)}, f32[3,8,512]{2,1,0:T(8,128)}) custom-call(s32[3,4]{1,0:T(4,128)} %get-tuple-element.257.need_ref, s32[3,512,1]{2,1,0:T(8,128)} %get-tuple-element.261.col_ref, ...), custom_call_target="tpu_custom_call", output_to_operand_aliasing={{0}: (6, {}), {1}: (7, {}), {2}: (8, {})} | custom-call | flops 1 | bytes 1 | tf_op jit(solution)/shard_map/attend/pallas_call | solution.py:864
  194.3 11.0 %attend.5 = (bf16[3,256,640]{2,1,0:T(8,128)(2,1)}, bf16[3,256,640]{2,1,0:T(8,128)(2,1)}, f32[3,8,512]{2,1,0:T(8,128)}) custom-call(s32[3,4]{1,0:T(4,128)} %get-tuple-element.257.need_ref, s32[3,512,1]{2,1,0:T(8,128)} %get-tuple-element.261.col_ref, ...), custom_call_target="tpu_custom_call", output_to_operand_aliasing={{0}: (6, {}), {1}: (7, {}), {2}: (8, {})} | custom-call | flops 1 | bytes 1 | tf_op jit(solution)/shard_map/attend/pallas_call | solution.py:864
  239.2 25.5 %collective-permute-done.30.refs_3_ = bf16[144,2176]{1,0:T(8,128)(2,1)} collective-permute-done((bf16[144,2176]{1,0:T(8,128)(2,1)}, bf16[144,2176]{1,0:T(8,128)(2,1)}, u32[]{:S(2)}, u32[]{:S(2)}) %collective-permute-start.30) | collective-permute-done | bytes 626720 | tf_op jit(solution)/shard_map/ppermute | solution.py:42
  264.8 18.7 %hidden.1 = (bf16[1536,2176]{1,0:T(8,128)(2,1)}, bf16[1536,2176]{1,0:T(8,128)(2,1)}, bf16[1536,1152]{1,0:T(8,128)(2,1)}) custom-call(bf16[768,1152]{1,0:T(8,128)(2,1)} %get-tuple-element.343.refs_0_, bf16[768,1152]{1,0:T(8,128)(2,1)} %collective-permute-done.31.refs_1_, bf16[1152,2176]{1,0:T(8,128)(2,1)} %get-tuple-element.345.refs_2_.refs_1_, ...), custom_call_target="tpu_custom_call" | custom-call | flops 1 | bytes 1 | tf_op jit(solution)/shard_map/hidden/pallas_call | solution.py:748
  283.5 13.0 %convolution_convert_fusion.1 = bf16[1152,2176]{1,0:T(8,128)(2,1)} fusion(bf16[1536,1152]{1,0:T(8,128)(2,1)S(1)} %pad_maximum_fusion.refs_0_, bf16[1536,2176]{1,0:T(8,128)(2,1)} %get-tuple-element.450.refs_0_), kind=kOutput, calls=%fused_computation.2 | convolution fusion | flops 7703248896 | bytes 15237120 | tf_op jit(solution)/shard_map/dot_general | solution.py:29
  297.7 21.3 %collective-permute-done.32.refs_7_ = bf16[144,2176]{1,0:T(8,128)(2,1)S(1)} collective-permute-done((bf16[144,2176]{1,0:T(8,128)(2,1)}, bf16[144,2176]{1,0:T(8,128)(2,1)S(1)}, u32[]{:S(2)}, u32[]{:S(2)}) %collective-permute-start.32) | collective-permute-done | bytes 626720 | tf_op jit(solution)/shard_map/ppermute | solution.py:42
  324.7 14.7 %grad_pre.1 = (bf16[1536,2176]{1,0:T(8,128)(2,1)}, f32[1,2176]{1,0:T(1,128)}) custom-call(bf16[1536,1152]{1,0:T(8,128)(2,1)} %copy-done.3, bf16[1152,2176]{1,0:T(8,128)(2,1)} %assemble.5.refs_1_, bf16[1536,2176]{1,0:T(8,128)(2,1)} %get-tuple-element.361.refs_2_), custom_call_target="tpu_custom_call" | custom-call | flops 1 | bytes 1 | tf_op jit(solution)/shard_map/grad_pre/pallas_call | solution.py:478
  339.4 14.8 %back.1 = (bf16[768,1152]{1,0:T(8,128)(2,1)}, bf16[768,1152]{1,0:T(8,128)(2,1)}) custom-call(bf16[1536,2176]{1,0:T(8,128)(2,1)} %get-tuple-element.366.refs_0_, bf16[1152,2176]{1,0:T(8,128)(2,1)} %get-tuple-element.345.refs_2_.refs_1_), custom_call_target="tpu_custom_call" | custom-call | flops 1 | bytes 1 | tf_op jit(solution)/shard_map/back/pallas_call | solution.py:478
  354.2 13.1 %convolution_convert_fusion = bf16[1152,2176]{1,0:T(8,128)(2,1)} fusion(bf16[1536,1152]{1,0:T(8,128)(2,1)S(1)} %copy-done.34, bf16[1536,2176]{1,0:T(8,128)(2,1)} %get-tuple-element.366.refs_0_), kind=kOutput, calls=%fused_computation.1 | convolution fusion | flops 7703248896 | bytes 15237120 | tf_op jit(solution)/shard_map/dot_general | solution.py:29
  373.7 12.5 %second_back.1 = (f32[768,1152]{1,0:T(8,128)}, bf16[768,1152]{1,0:T(8,128)(2,1)}, bf16[768,640]{1,0:T(8,128)(2,1)}, bf16[768,640]{1,0:T(8,128)(2,1)}, f32[8,1152]{1,0:T(8,128)}) custom-call(s32[1]{0:T(128)} %bitcast.3.core_ref, f32[768,1152]{1,0:T(8,128)} %get-tuple-element.451.x_ref.refs_2_, bf16[768,1152]{1,0:T(8,128)(2,1)} %get-tuple-element.367.refs_0_, ...), custom_call_target="tpu_custom_call" | custom-call | flops 1 | bytes 1 | tf_op jit(solution)/shard_map/second_back/pallas_call | solution.py:405
  400.9 22.0 %attend_back.3 = (bf16[2,3,256,640]{3,2,1,0:T(8,128)(2,1)}, bf16[2,3,256,1280]{3,2,1,0:T(8,128)(2,1)}, bf16[2,3,256,1280]{3,2,1,0:T(8,128)(2,1)}) custom-call(s32[3,4]{1,0:T(4,128)} %get-tuple-element.257.need_ref, s32[3,4,256,1]{3,2,1,0:T(8,128)} %get-tuple-element.259.col_ref, s32[3,1,512]{2,1,0:T(1,128)} %get-tuple-element.260.row_ref, ...), custom_call_target="tpu_custom_call" | custom-call | flops 1 | bytes 1 | tf_op jit(solution)/shard_map/attend_back/pallas_call | solution.py:962
  424.2 18.4 %attend_back.4 = (bf16[2,3,256,640]{3,2,1,0:T(8,128)(2,1)}, bf16[2,3,256,1280]{3,2,1,0:T(8,128)(2,1)}, bf16[2,3,256,1280]{3,2,1,0:T(8,128)(2,1)}) custom-call(s32[3,4]{1,0:T(4,128)} %get-tuple-element.257.need_ref, s32[3,4,256,1]{3,2,1,0:T(8,128)} %get-tuple-element.259.col_ref, ...), custom_call_target="tpu_custom_call", output_to_operand_aliasing={{0}: (12, {}), {1}: (13, {}), {2}: (14, {})} | custom-call | flops 1 | bytes 1 | tf_op jit(solution)/shard_map/attend_back/pallas_call | solution.py:962
  449.6 18.4 %attend_back.5 = (bf16[2,3,256,640]{3,2,1,0:T(8,128)(2,1)}, bf16[2,3,256,1280]{3,2,1,0:T(8,128)(2,1)}, bf16[2,3,256,1280]{3,2,1,0:T(8,128)(2,1)}) custom-call(s32[3,4]{1,0:T(4,128)} %get-tuple-element.257.need_ref, s32[3,4,256,1]{3,2,1,0:T(8,128)} %get-tuple-element.259.col_ref, ...), custom_call_target="tpu_custom_call", output_to_operand_aliasing={{0}: (12, {}), {1}: (13, {}), {2}: (14, {})} | custom-call | flops 1 | bytes 1 | tf_op jit(solution)/shard_map/attend_back/pallas_call | solution.py:962
  468.9 11.6 %back_far.1 = (bf16[768,1152]{1,0:T(8,128)(2,1)}, bf16[768,1152]{1,0:T(8,128)(2,1)}) custom-call(bf16[1536,1280]{1,0:T(8,128)(2,1)} %bitcast.66, bf16[1152,1280]{1,0:T(8,128)(2,1)} %get-tuple-element.417.refs_1_.refs_3_), custom_call_target="tpu_custom_call" | custom-call | flops 1 | bytes 1 | tf_op jit(solution)/shard_map/back_far/pallas_call | solution.py:478
  480.6 17.4 %weight_grad.4 = (bf16[576,1280]{1,0:T(8,128)(2,1)}, bf16[576,1280]{1,0:T(8,128)(2,1)}, f32[8,1280]{1,0:T(8,128)}) custom-call(s32[9]{0:T(128)} %pad_add_fusion.pos_ref, bf16[1536,1152]{1,0:T(8,128)(2,1)} %norm.2.refs_0_, bf16[1536,1152]{1,0:T(8,128)(2,1)} %norm.3.refs_0_.refs_1_, bf16[1536,1280]{1,0:T(8,128)(2,1)} %bitcast.64, bf16[1536,1280]{1,0:T(8,128)(2,1)} %bitcast.67), custom_call_target="tpu_custom_call" | custom-call | flops 1 | bytes 1 | tf_op jit(solution)/shard_map/weight_grad/pallas_call | solution.py:187
  500.8 10.5 %collective-permute-done.40 = bf16[144,640]{1,0:T(8,128)(2,1)S(1)} collective-permute-done((bf16[144,640]{1,0:T(8,128)(2,1)S(1)}, bf16[144,640]{1,0:T(8,128)(2,1)S(1)}, u32[]{:S(2)}, u32[]{:S(2)}) %collective-permute-start.40) | collective-permute-done | bytes 184352 | tf_op jit(solution)/shard_map/ppermute | solution.py:42
  513.6 13.5 %back_near.1 = (bf16[768,1152]{1,0:T(8,128)(2,1)}, bf16[768,1152]{1,0:T(8,128)(2,1)}) custom-call(bf16[1536,640]{1,0:T(8,128)(2,1)} %bitcast.69, bf16[1536,1280]{1,0:T(8,128)(2,1)} %bitcast.65, bf16[1152,640]{1,0:T(8,128)(2,1)} %get-tuple-element.289.refs_1_.refs_2_, bf16[1152,1280]{1,0:T(8,128)(2,1)} %get-tuple-element.417.refs_1_.refs_3_), custom_call_target="tpu_custom_call" | custom-call | flops 1 | bytes 1 | tf_op jit(solution)/shard_map/back_near/pallas_call | solution.py:478
  550.9 17.6 %collective-permute-done.45.refs_2_ = bf16[768,1152]{1,0:T(8,128)(2,1)} collective-permute-done((bf16[768,1152]{1,0:T(8,128)(2,1)}, bf16[768,1152]{1,0:T(8,128)(2,1)}, u32[]{:S(2)}, u32[]{:S(2)}) %collective-permute-start.45) | collective-permute-done | bytes 1769504 | tf_op jit(solution)/shard_map/ppermute | solution.py:42
  597.9 12.5 %collective-permute-done.50 = bf16[144,640]{1,0:T(8,128)(2,1)S(1)} collective-permute-done((bf16[144,640]{1,0:T(8,128)(2,1)S(1)}, bf16[144,640]{1,0:T(8,128)(2,1)S(1)}, u32[]{:S(2)}, u32[]{:S(2)}) %collective-permute-start.50) | collective-permute-done | bytes 184352 | tf_op jit(solution)/shard_map/ppermute | solution.py:42
  614.1 96.5 %all-reduce.4.cloned.1.call-done = (f32[8,1152]{1,0:T(8,128)}, f32[8,1152]{1,0:T(8,128)}) async-done(((f32[8,1152]{1,0:T(8,128)}, f32[8,1152]{1,0:T(8,128)}), (f32[8,1152]{1,0:T(8,128)}, f32[8,1152]{1,0:T(8,128)})) %all-reduce.4.cloned.1.call-update) | async-done | bytes 73744 | tf_op jit(solution)/shard_map/psum | solution.py:1335
  (293 shorter events, 284.8 us)
Async XLA Ops:
  7.2 441.6 %reduce-scatter.3.cloned.1.call-start = ((), (), s32[]{:S(2)}) async-start(), calls=%async_computation.2 | async-start | bytes 5640192 | tf_op jit(solution)/shard_map/reduce_scatter | solution.py:1202
  21.2 40.9 %collective-permute-start.7 = (bf16[512,1152]{1,0:T(8,128)(2,1)}, bf16[512,1152]{1,0:T(8,128)(2,1)}, u32[]{:S(2)}, u32[]{:S(2)}) collective-permute-start(bf16[512,1152]{1,0:T(8,128)(2,1)} %bitcast.7), channel_id=1, source_target_pairs={{0,16},{8,24},{16,0},{24,8},{1,17},{9,25},{17,1},{25,9},{2,18},{10... | collective-permute-start | bytes 3538952 | tf_op jit(solution)/shard_map/ppermute | solution.py:42
  27.8 33.6 %collective-permute-start.10 = (bf16[144,2816]{1,0:T(8,128)(2,1)}, bf16[144,2816]{1,0:T(8,128)(2,1)}, u32[]{:S(2)}, u32[]{:S(2)}) collective-permute-start(bf16[144,2816]{1,0:T(8,128)(2,1)} %get-tuple-element.246.refs_0_), channel_id=1, source_target_pairs={{0,1},{1,0},{2,3},{3,2},{4,5},{5,4},{6,7},{7,6},{8,9},{9,8},{10,11... | collective-permute-start | bytes 2433032 | tf_op jit(solution)/shard_map/ppermute | solution.py:42
  31.0 69.2 %collective-permute-start.12 = (bf16[768,1152]{1,0:T(8,128)(2,1)S(1)}, bf16[768,1152]{1,0:T(8,128)(2,1)}, u32[]{:S(2)}, u32[]{:S(2)}) collective-permute-start(bf16[768,1152]{1,0:T(8,128)(2,1)S(1)} %bitcast.74), channel_id=1, source_target_pairs={{0,8},{8,0},{16,24},{24,16},{1,9},{9,1},{17,25},{25,17},{2,10},{10... | collective-permute-start | bytes 5308424 | tf_op jit(solution)/shard_map/ppermute | solution.py:42
  61.4 81.6 %collective-permute-start.16 = (bf16[768,1152]{1,0:T(8,128)(2,1)S(1)}, bf16[768,1152]{1,0:T(8,128)(2,1)}, u32[]{:S(2)}, u32[]{:S(2)}) collective-permute-start(bf16[768,1152]{1,0:T(8,128)(2,1)S(1)} %bitcast.85), channel_id=1, source_target_pairs={{0,8},{8,0},{16,24},{24,16},{1,9},{9,1},{17,25},{25,17},{2,10},{10... | collective-permute-start | bytes 5308424 | tf_op jit(solution)/shard_map/ppermute | solution.py:42
  93.5 49.5 %collective-permute-start.14 = (bf16[144,2816]{1,0:T(8,128)(2,1)}, bf16[144,2816]{1,0:T(8,128)(2,1)}, u32[]{:S(2)}, u32[]{:S(2)}) collective-permute-start(bf16[144,2816]{1,0:T(8,128)(2,1)} %get-tuple-element.246.refs_0_), channel_id=1, source_target_pairs={{0,4},{1,5},{2,6},{3,7},{4,0},{5,1},{6,2},{7,3},{8,12},{9,13},{10,... | collective-permute-start | bytes 2433032 | tf_op jit(solution)/shard_map/ppermute | solution.py:42
  97.2 45.7 %collective-permute-start.13 = (bf16[144,2816]{1,0:T(8,128)(2,1)}, bf16[144,2816]{1,0:T(8,128)(2,1)}, u32[]{:S(2)}, u32[]{:S(2)}) collective-permute-start(bf16[144,2816]{1,0:T(8,128)(2,1)} %get-tuple-element.246.refs_0_), channel_id=1, source_target_pairs={{0,2},{1,3},{2,0},{3,1},{4,6},{5,7},{6,4},{7,5},{8,10},{9,11},{10,... | collective-permute-start | bytes 2433032 | tf_op jit(solution)/shard_map/ppermute | solution.py:42
  100.2 42.8 %collective-permute-start.15 = (bf16[144,2176]{1,0:T(8,128)(2,1)}, bf16[144,2176]{1,0:T(8,128)(2,1)S(1)}, u32[]{:S(2)}, u32[]{:S(2)}) collective-permute-start(bf16[144,2176]{1,0:T(8,128)(2,1)} %get-tuple-element.247.refs_0_), channel_id=1, source_target_pairs={{0,1},{1,0},{2,3},{3,2},{4,5},{5,4},{6,7},{7,6},{8,9},{9,8},{10,11... | collective-permute-start | bytes 1880072 | tf_op jit(solution)/shard_map/ppermute | solution.py:42
  143.6 35.3 %collective-permute-start.21 = (bf16[144,2816]{1,0:T(8,128)(2,1)}, bf16[144,2816]{1,0:T(8,128)(2,1)S(1)}, u32[]{:S(2)}, u32[]{:S(2)}) collective-permute-start(bf16[144,2816]{1,0:T(8,128)(2,1)} %collective-permute-done.14.refs_4_), channel_id=1, source_target_pairs={{0,1},{1,0},{2,3},{3,2},{4,5},{5,4},{6,7},{7,6},{8,9},{9,8},{10,11... | collective-permute-start | bytes 2433032 | tf_op jit(solution)/shard_map/ppermute | solution.py:42
  232.4 32.3 %collective-permute-start.31 = (bf16[768,1152]{1,0:T(8,128)(2,1)}, bf16[768,1152]{1,0:T(8,128)(2,1)}, u32[]{:S(2)}, u32[]{:S(2)}) collective-permute-start(bf16[768,1152]{1,0:T(8,128)(2,1)} %get-tuple-element.343.refs_0_), channel_id=1, source_target_pairs={{0,8},{8,0},{16,24},{24,16},{1,9},{9,1},{17,25},{25,17},{2,10},{10... | collective-permute-start | bytes 5308424 | tf_op jit(solution)/shard_map/ppermute | solution.py:42
  233.2 31.6 %collective-permute-start.29 = (bf16[144,2176]{1,0:T(8,128)(2,1)}, bf16[144,2176]{1,0:T(8,128)(2,1)}, u32[]{:S(2)}, u32[]{:S(2)}) collective-permute-start(bf16[144,2176]{1,0:T(8,128)(2,1)} %collective-permute-done.25.refs_4_), channel_id=1, source_target_pairs={{0,2},{1,3},{2,0},{3,1},{4,6},{5,7},{6,4},{7,5},{8,10},{9,11},{10,... | collective-permute-start | bytes 1880072 | tf_op jit(solution)/shard_map/ppermute | solution.py:42
  234.9 48.6 %collective-permute-start.28 = (bf16[144,2176]{1,0:T(8,128)(2,1)}, bf16[144,2176]{1,0:T(8,128)(2,1)}, u32[]{:S(2)}, u32[]{:S(2)}) collective-permute-start(bf16[144,2176]{1,0:T(8,128)(2,1)} %collective-permute-done.25.refs_4_), channel_id=1, source_target_pairs={{0,1},{1,0},{2,3},{3,2},{4,5},{5,4},{6,7},{7,6},{8,9},{9,8},{10,11... | collective-permute-start | bytes 1880072 | tf_op jit(solution)/shard_map/ppermute | solution.py:42
  235.8 29.0 %collective-permute-start.30 = (bf16[144,2176]{1,0:T(8,128)(2,1)}, bf16[144,2176]{1,0:T(8,128)(2,1)}, u32[]{:S(2)}, u32[]{:S(2)}) collective-permute-start(bf16[144,2176]{1,0:T(8,128)(2,1)} %collective-permute-done.24.refs_2_), channel_id=1, source_target_pairs={{0,1},{1,0},{2,3},{3,2},{4,5},{5,4},{6,7},{7,6},{8,9},{9,8},{10,11... | collective-permute-start | bytes 1880072 | tf_op jit(solution)/shard_map/ppermute | solution.py:42
  296.6 282.0 %reduce-scatter.5.cloned.1.call-start = ((), (), s32[]{:S(2)}) async-start(), calls=%async_computation.3 | async-start | bytes 5640192 | tf_op jit(solution)/shard_map/reduce_scatter | solution.py:1227
  367.4 343.2 %all-reduce.4.cloned.1.call-start = ((), (), s32[]{:S(2)}) async-start(), calls=%async_computation.4 | async-start | bytes 147456 | tf_op jit(solution)/shard_map/psum | solution.py:1335
  480.6 30.7 %collective-permute-start.41 = (bf16[768,1152]{1,0:T(8,128)(2,1)}, bf16[768,1152]{1,0:T(8,128)(2,1)S(1)}, u32[]{:S(2)}, u32[]{:S(2)}) collective-permute-start(bf16[768,1152]{1,0:T(8,128)(2,1)} %get-tuple-element.419), channel_id=1, source_target_pairs={{0,8},{8,0},{16,24},{24,16},{1,9},{9,1},{17,25},{25,17},{2,10},{10... | collective-permute-start | bytes 5308424 | tf_op jit(solution)/shard_map/ppermute | solution.py:42
  497.9 49.2 %collective-permute-start.44 = (bf16[576,1280]{1,0:T(8,128)(2,1)}, bf16[576,1280]{1,0:T(8,128)(2,1)}, u32[]{:S(2)}, u32[]{:S(2)}) collective-permute-start(bf16[576,1280]{1,0:T(8,128)(2,1)} %get-tuple-element.425), channel_id=1, source_target_pairs={{0,1},{1,0},{2,3},{3,2},{4,5},{5,4},{6,7},{7,6},{8,9},{9,8},{10,11... | collective-permute-start | bytes 4423688 | tf_op jit(solution)/shard_map/ppermute | solution.py:42
  527.2 41.2 %collective-permute-start.45 = (bf16[768,1152]{1,0:T(8,128)(2,1)}, bf16[768,1152]{1,0:T(8,128)(2,1)}, u32[]{:S(2)}, u32[]{:S(2)}) collective-permute-start(bf16[768,1152]{1,0:T(8,128)(2,1)} %add_convert_fusion), channel_id=1, source_target_pairs={{0,16},{8,24},{16,0},{24,8},{1,17},{9,25},{17,1},{25,9},{2,18},{10... | collective-permute-start | bytes 5308424 | tf_op jit(solution)/shard_map/ppermute | solution.py:42
  545.5 33.1 %collective-permute-start.43 = (bf16[768,1152]{1,0:T(8,128)(2,1)}, bf16[768,1152]{1,0:T(8,128)(2,1)}, u32[]{:S(2)}, u32[]{:S(2)}) collective-permute-start(bf16[768,1152]{1,0:T(8,128)(2,1)} %down_pair.1), channel_id=1, source_target_pairs={{0,8},{8,0},{16,24},{24,16},{1,9},{9,1},{17,25},{25,17},{2,10},{10... | collective-permute-start | bytes 5308424 | tf_op jit(solution)/shard_map/ppermute | solution.py:42
  545.6 32.9 %collective-permute-start.42 = (bf16[576,640]{1,0:T(8,128)(2,1)}, bf16[576,640]{1,0:T(8,128)(2,1)}, u32[]{:S(2)}, u32[]{:S(2)}) collective-permute-start(bf16[576,640]{1,0:T(8,128)(2,1)} %get-tuple-element.435), channel_id=1, source_target_pairs={{0,1},{1,0},{2,3},{3,2},{4,5},{5,4},{6,7},{7,6},{8,9},{9,8},{10,11... | collective-permute-start | bytes 2211848 | tf_op jit(solution)/shard_map/ppermute | solution.py:42
  549.7 31.0 %collective-permute-start.49 = (bf16[288,1280]{1,0:T(8,128)(2,1)}, bf16[288,1280]{1,0:T(8,128)(2,1)}, u32[]{:S(2)}, u32[]{:S(2)}) collective-permute-start(bf16[288,1280]{1,0:T(8,128)(2,1)} %get-tuple-element.476), channel_id=1, source_target_pairs={{0,2},{1,3},{2,0},{3,1},{4,6},{5,7},{6,4},{7,5},{8,10},{9,11},{10,... | collective-permute-start | bytes 2211848 | tf_op jit(solution)/shard_map/ppermute | solution.py:42
  550.8 169.6 %collective-permute-start.52 = (f32[144,2176]{1,0:T(8,128)S(1)}, f32[144,2176]{1,0:T(8,128)}, u32[]{:S(2)}, u32[]{:S(2)}) collective-permute-start(f32[144,2176]{1,0:T(8,128)S(1)} %convert_add_fusion.1), channel_id=1, source_target_pairs={{0,8},{8,0},{16,24},{24,16},{1,9},{9,1},{17,25},{25,17},{2,10},{10... | collective-permute-start | bytes 3760136 | tf_op jit(solution)/shard_map/ppermute | solution.py:42
  568.5 151.9 %collective-permute-start.51 = (bf16[144,640]{1,0:T(8,128)(2,1)S(1)}, bf16[144,640]{1,0:T(8,128)(2,1)}, u32[]{:S(2)}, u32[]{:S(2)}) collective-permute-start(bf16[144,640]{1,0:T(8,128)(2,1)S(1)} %add_convert_fusion.12), channel_id=1, source_target_pairs={{0,16},{8,24},{16,0},{24,8},{1,17},{9,25},{17,1},{25,9},{2,18},{10... | collective-permute-start | bytes 552968 | tf_op jit(solution)/shard_map/ppermute | solution.py:42
  612.5 106.7 %collective-permute-start.55 = (bf16[144,1280]{1,0:T(8,128)(2,1)S(1)}, bf16[144,1280]{1,0:T(8,128)(2,1)}, u32[]{:S(2)}, u32[]{:S(2)}) collective-permute-start(bf16[144,1280]{1,0:T(8,128)(2,1)S(1)} %add_convert_fusion.5), channel_id=1, source_target_pairs={{0,16},{8,24},{16,0},{24,8},{1,17},{9,25},{17,1},{25,9},{2,18},{10... | collective-permute-start | bytes 1105928 | tf_op jit(solution)/shard_map/ppermute | solution.py:42
  (83 other events, 1102.1 us)
Sparse Core Ops, SparseCore 0:
  296.7 101.9 reduce-scatter.2
  402.7 101.8 reduce-scatter.4
  580.9 129.6 all-reduce.3

commit v6 on v5

--- a/solution.py
+++ b/solution.py
@@ -71,11 +71,14 @@
         self.open.append([swap(array, axis, bits)])
         return self.open[-1]
 
-    def land(self, *values, through=None):
-        count = len(self.open)
-        if through is not None:
-            count = sum(i + 1 for i, box in enumerate(self.open) if box is through)
-        ready, self.open = self.open[:count], self.open[count:]
+    def land(self, *values, through=None, only=None):
+        if only is None:
+            count = len(self.open)
+            if through is not None:
+                count = sum(i + 1 for i, box in enumerate(self.open) if box is through)
+            only = self.open[:count]
+        ready = [box for box in self.open if any(box is other for other in only)]
+        self.open = [box for box in self.open if not any(box is other for other in ready)]
         held = self.chain(*[box[0] for box in ready], *values)
         held = held if isinstance(held, (tuple, list)) else [held]
         for box, array in zip(ready, held):
@@ -205,6 +208,29 @@
     )(positions, *lefts, *rights)
 
 
+def token_dot(left, right):
+    tokens, width = left.shape
+    cols = right.shape[1]
+    tile = 256
+
+    def kernel(left_ref, right_ref, out_ref):
+        out_ref[...] = dot(left_ref[...], right_ref[...], TN).astype(BF16)
+
+    return pl.pallas_call(
+        kernel,
+        out_shape=jax.ShapeDtypeStruct((width, cols), BF16),
+        grid=(pl.cdiv(cols, tile),),
+        in_specs=[
+            pl.BlockSpec((tokens, width), lambda n: (0, 0), pipeline_mode=pl.Buffered(1)),
+            pl.BlockSpec((tokens, tile), lambda n: (0, n)),
+        ],
+        out_specs=pl.BlockSpec((width, tile), lambda n: (0, n)),
+        compiler_params=params(("arbitrary",)),
+        cost_estimate=NOMINAL,
+        name="token_dot",
+    )(left, right)
+
+
 def normalized(values):
     center = values - jnp.mean(values, axis=-1, keepdims=True)
     spread = jnp.mean(center * center, axis=-1, keepdims=True)
@@ -322,13 +348,21 @@
 
 def first_back(core, values, grads, gain, add, q_sums, kv_sums, half):
     rows, width = values.shape
-    block = row_block(rows)
-    count = len(grads)
     padded = q_sums.shape[1]
+    pieces = [grad for grad in grads if isinstance(grad, tuple)]
+    whole_grads = [grad for grad in grads if not isinstance(grad, tuple)]
+    block = min([row_block(rows)] + [row_block(part.shape[0]) for pair in pieces for part in pair])
+    count = len(whole_grads) + 2 * len(pieces)
+    flat_grads = whole_grads + [part for pair in pieces for part in pair]
 
     def kernel(core_ref, x_ref, *refs):
         gain_ref, add_ref, q_ref, kv_ref, dx_ref, lines_ref = refs[count:]
-        dx_ref[...] = norm_back_values(x_ref, refs[:count], gain_ref, add_ref, lines_ref)
+        sums = list(refs[: len(whole_grads)])
+        for k, pair in enumerate(pieces):
+            low, high = refs[len(whole_grads) + 2 * k : len(whole_grads) + 2 * k + 2]
+            first = pl.program_id(0) < pair[0].shape[0] // block
+            sums.append(jnp.where(first, low[...].astype(F32), high[...].astype(F32)))
+        dx_ref[...] = norm_back_values(x_ref, sums, gain_ref, add_ref, lines_ref)
         for line, part in ((2, q_ref[0:1, :half]), (3, kv_ref[0:1, padded : padded + half])):
             none = jnp.zeros_like(part)
 
@@ -339,6 +373,13 @@
             @pl.when(core_ref[0] != 0)
             def _():
                 lines_ref[line : line + 1] = jnp.concatenate([none, part], axis=1)
+
+    def piece_specs(pair):
+        steps = pair[0].shape[0] // block
+        return [
+            pl.BlockSpec((block, width), lambda i, c: (jnp.minimum(i, steps - 1), 0)),
+            pl.BlockSpec((block, width), lambda i, c: (jnp.maximum(i - steps, 0), 0)),
+        ]
 
     wide = pl.BlockSpec((block, width), lambda i, c: (i, 0))
     return pl.pallas_call(
@@ -350,7 +391,8 @@
         grid_spec=pltpu.PrefetchScalarGridSpec(
             num_scalar_prefetch=1,
             grid=(rows // block,),
-            in_specs=[wide] * (1 + count)
+            in_specs=[wide] * (1 + len(whole_grads))
+            + [spec for pair in pieces for spec in piece_specs(pair)]
             + [
                 pl.BlockSpec((1, width), lambda i, c: (0, 0)),
                 wide,
@@ -362,7 +404,7 @@
         compiler_params=params(("arbitrary",)),
         cost_estimate=NOMINAL,
         name="first_back",
-    )(core, values, *grads, gain, add, q_sums, kv_sums)
+    )(core, values, *flat_grads, gain, add, q_sums, kv_sums)
 
 
 def second_back(core, values, grads, gain, add, weight, hidden_line, half, padded):
@@ -581,33 +623,6 @@
     return small_call(kernel, [like(rows, cols)] * (2 * len(arrays)), [core], arrays, "core_columns")
 
 
-def stack_rows(first, second):
-    rows, cols = first.shape
-    block = row_block(rows)
-    steps = rows // block
-
-    def kernel(first_ref, second_ref, out_ref):
-        for i, ref in enumerate((first_ref, second_ref)):
-
-            @pl.when(pl.program_id(0) // steps == i)
-            def _():
-                out_ref[...] = ref[...]
-
-    return pl.pallas_call(
-        kernel,
-        out_shape=like(2 * rows, cols),
-        grid=(2 * steps,),
-        in_specs=[
-            pl.BlockSpec((block, cols), lambda i: (jnp.minimum(i, steps - 1), 0)),
-            pl.BlockSpec((block, cols), lambda i: (jnp.maximum(i - steps, 0), 0)),
-        ],
-        out_specs=pl.BlockSpec((block, cols), lambda i: (i, 0)),
-        compiler_params=params(("arbitrary",)),
-        cost_estimate=NOMINAL,
-        name="stack_rows",
-    )(first, second)
-
-
 def mask_kernel(rows, tokens, blocks, len_ref, place_ref, need_ref, row_ref, col_ref, near_row, near_col):
     place = place_ref[0]
     for row in range(rows):
@@ -660,24 +675,37 @@
     )(lengths, place)
 
 
-def lay_vectors(meta, parts, half, padded):
-    count, lines, size = parts.shape
-
-    def kernel(meta_ref, parts_ref, lines_ref, q_ref, kv_ref):
-        for shard in range(count):
-            block = parts_ref[jnp.bitwise_xor(meta_ref[1], shard)]
-            lines_ref[:, shard * size : (shard + 1) * size] = block.astype(F32)
+def lay_vectors(core, weight, lines, half, padded):
+    width, cols = weight.shape
+    low = half // 128 * 128
+
+    def kernel(core_ref, weight_ref, lines_ref, q_ref, kv_ref):
+        turned = weight_ref[...].astype(F32).T
+        lines_ref[...] = turned[half - low : half - low + lines]
         q_ref[...] = jnp.zeros_like(q_ref)
         kv_ref[...] = jnp.zeros_like(kv_ref)
-        for core in range(2):
-
-            @pl.when(meta_ref[0] == core)
+        for at in range(2):
+
+            @pl.when(core_ref[0] == at)
             def _():
-                q_ref[:, :half] = lines_ref[2:3, core * half : (core + 1) * half]
-                kv_ref[:, padded : padded + half] = lines_ref[3:4, core * half : (core + 1) * half]
-
-    outs = [like(lines, count * size, F32), like(1, padded, F32), like(1, 2 * padded, F32)]
-    return small_call(kernel, outs, [meta], [parts], "lay_vectors")
+                q_ref[:, :half] = lines_ref[2:3, at * half : (at + 1) * half]
+                kv_ref[:, padded : padded + half] = lines_ref[3:4, at * half : (at + 1) * half]
+
+    outs = [like(lines, width, F32), like(1, padded, F32), like(1, 2 * padded, F32)]
+    block = cols - low
+    return pl.pallas_call(
+        kernel,
+        out_shape=outs,
+        grid=(1,),
+        in_specs=[
+            pl.BlockSpec(memory_space=pltpu.SMEM),
+            pl.BlockSpec((width, block), lambda i: (0, low // block)),
+        ],
+        out_specs=[pl.BlockSpec(out.shape, lambda i: (0, 0)) for out in outs],
+        compiler_params=params(("arbitrary",)),
+        cost_estimate=NOMINAL,
+        name="lay_vectors",
+    )(core, weight)
 
 
 def mlp_shards(core, out_shard, hidden_weight, down_weight, cols):
@@ -704,23 +732,39 @@
     return small_call(kernel, outs, [core], [out_shard, hidden_weight, down_weight], "mlp_shards")
 
 
-def attention_shards(core, weights, half, padded):
+def attention_shards(core, weights, vectors, half, padded):
     rows, width = weights[0].shape
     cut = width - padded
-
-    def kernel(core_ref, q_ref, k_ref, v_ref, o_ref, qkv_ref, out_ref):
+    count = len(vectors)
+
+    def kernel(core_ref, q_ref, k_ref, v_ref, o_ref, *refs):
+        qkv_ref, out_ref, held = refs[count:]
+        for i in range(count):
+            held[i : i + 1] = refs[i][...].astype(F32).reshape(1, rows)
         empty = jnp.zeros((rows, padded - half), BF16)
+        spare = jnp.zeros((rows, padded - half - count), BF16)
+        lines = jnp.concatenate([held[...].T.astype(BF16), spare], axis=1)
         for at in range(2):
 
             @pl.when(core_ref[0] == at)
             def _():
                 for i, ref in enumerate((q_ref, k_ref, v_ref)):
                     part = ref[:, at * half : (at + 1) * half]
-                    qkv_ref[:, i * padded : (i + 1) * padded] = jnp.concatenate([part, empty], axis=1)
+                    rest = empty if i else lines
+                    qkv_ref[:, i * padded : (i + 1) * padded] = jnp.concatenate([part, rest], axis=1)
                 out_ref[...] = o_ref[:, at * cut : at * cut + padded]
 
-    outs = [like(rows, 3 * padded), like(rows, padded)]
-    return small_call(kernel, outs, [core], weights, "attention_shards")
+    vmem = pl.BlockSpec(memory_space=pltpu.VMEM)
+    return pl.pallas_call(
+        kernel,
+        out_shape=[like(rows, 3 * padded), like(rows, padded)],
+        in_specs=[pl.BlockSpec(memory_space=pltpu.SMEM)] + [vmem] * (4 + count),
+        out_specs=[vmem] * 2,
+        scratch_shapes=[pltpu.VMEM((count, rows), F32)],
+        compiler_params=pltpu.CompilerParams(vmem_limit_bytes=VMEM),
+        cost_estimate=NOMINAL,
+        name="attention_shards",
+    )(core, *weights, *vectors)
 
 
 def hidden(arrays, weight, bias):
@@ -1043,12 +1087,7 @@
 
     inputs = patches.reshape(flat, width)
     incoming = cotangent.reshape(flat, width)
-    shard_qkv, shard_out = chain.done(
-        *attention_shards(
-            core_flag, [query_weight, key_weight, value_weight, output_weight], half, padded
-        )
-    )
-    vectors = (
+    vectors = [
         first_gain,
         first_shift,
         query_bias,
@@ -1057,77 +1096,68 @@
         second_gain,
         second_shift,
         down_bias,
+    ]
+    shard_qkv, shard_out = chain.done(
+        *attention_shards(
+            core_flag, [query_weight, key_weight, value_weight, output_weight], vectors, half, padded
+        )
     )
     place_flag = place[None].astype(jnp.int32)
 
     def over(box_from, bits):
         return flights.send(box_from[0], "fsdp", bits)
-
-    def both(stacked_lines, arrived):
-        return jnp.concatenate([stacked_lines, arrived], axis=0)
 
     if staged:
         q = {0: [shard_qkv]}
         q[y] = over(q[0], y)
-        far_raw = [flights.send(patches[0], "seq", 2)]
         q[z], q[zz] = over(q[0], z), over(q[0], zz)
         shard_ho, shard_down = chain.done(
             *mlp_shards(core_flag, shard_out, hidden_weight, down_weight, ff_half)
         )
         h, d = {0: [shard_ho]}, {0: [shard_down]}
-        lengths, *vectors = flights.land(lengths, *vectors, through=far_raw[0])
-        vectors = jnp.stack(vectors)[None]
-        vec = flights.send(vectors, "fsdp", y)
-        h[y] = over(h[0], y)
-        far_raw.append(flights.send(patches[1:].reshape(flat - tokens, width), "seq", 2))
         need, seg_rows, seg_cols, seg_near_row, seg_near_col = chain.done(
-            *masks(lengths, place_flag, seq_count, tokens)
+            *masks(chain(lengths), place_flag, seq_count, tokens)
         )
-        vectors = flights.land(vectors, through=vec)
-        vectors = both(vectors, vec[0])
-        vec = flights.send(vectors, "fsdp", z)
-        q[zz | z] = over(q[zz], z)
-        q[z | y] = over(q[z], y)
-        vectors = flights.land(vectors, through=h[y])
-        q[zz | y] = over(q[zz], y)
-        vectors = flights.land(vectors, through=q[zz | z])
-        vectors = both(vectors, vec[0])
-        vec = flights.send(vectors, "fsdp", zz)
-        raw_pair = flights.send(inputs, "seq", 1)
+        core_flag, raw_own = flights.land(core_flag, inputs)
+        q[zz | z], q[z | y], q[zz | y] = over(q[zz], z), over(q[z], y), over(q[zz], y)
+        far_raw = [flights.send(raw_own, "seq", 2)]
+        raw_pair = flights.send(raw_own, "seq", 1)
+        core_flag = flights.land(core_flag, only=[q[zz | z]])
         q[zz | z | y] = over(q[zz | z], y)
-        vectors = flights.land(vectors, through=raw_pair)
-        far_pair = [flights.send(box[0], "seq", 1) for box in far_raw]
-        h[z], h[zz] = over(h[0], z), over(h[0], zz)
-        vectors = both(vectors, vec[0])
-        meta = chain(jnp.stack([core, me]).astype(jnp.int32))
-        stacked, bias_q, bias_kv = chain.done(*lay_vectors(meta, vectors, half, padded))
+        core_flag, shard_ho = flights.land(core_flag, shard_ho, only=[q[z | y], q[zz | y], raw_pair])
+        h[0] = [shard_ho]
+        h[z], h[y] = over(h[0], z), over(h[0], y)
+        core_flag, shard_ho, shard_down = flights.land(
+            core_flag, shard_ho, shard_down, only=[q[zz | z | y], far_raw[0]]
+        )
+        h[0], d[0] = [shard_ho], [shard_down]
+        far_pair = [flights.send(far_raw[0][0], "seq", 1)]
+        h[zz], d[y] = over(h[0], zz), over(d[0], y)
+        w_q, w_kv = chain.done(*assemble({k: box[0] for k, box in q.items()}, me, padded))
+        stacked, bias_q, bias_kv = chain.done(
+            *lay_vectors(chain(core_flag), w_q, len(vectors), half, padded)
+        )
         gain_one, shift_one = stacked[0:1], stacked[1:2]
         gain_one = chain(gain_one)
         normed_near = chain.done(norm([inputs, raw_pair[0]], gain_one, shift_one))
         bias_hidden = my_half(after(hidden_bias, gain_one).astype(F32)[None], ff_half, ff_half)
-        gain_one = flights.land(gain_one, through=far_pair[-1])
-        d[y] = over(d[0], y)
+        gain_one = flights.land(gain_one, only=[h[z], far_pair[0]])
+        h[z | y] = over(h[z], y)
         incoming_pair = flights.send(incoming, "seq", 1)
-        w_q, w_kv = chain.done(*assemble({k: box[0] for k, box in q.items()}, me, padded))
     else:
         parts = gather_all(shard_qkv)
-        vectors = jnp.stack(vectors)[None]
-        for k in range(shards.bit_length() - 1):
-            vectors = both(vectors, swap(vectors, "fsdp", 1 << k))
         shard_ho, shard_down = mlp_shards(core_flag, shard_out, hidden_weight, down_weight, ff_half)
         raw = {0: inputs}
         for bit in bits_of(seq_count):
             raw.update({j | bit: swap(part, "seq", bit) for j, part in list(raw.items())})
         need, seg_rows, seg_cols, seg_near_row, seg_near_col = masks(lengths, place_flag, seq_count, tokens)
-        stacked, bias_q, bias_kv = lay_vectors(
-            jnp.stack([core, me]).astype(jnp.int32), vectors, half, padded
-        )
+        w_q, w_kv = chain.done(*assemble(parts, me, padded))
+        stacked, bias_q, bias_kv = lay_vectors(core_flag, w_q, len(vectors), half, padded)
         gain_one, shift_one = stacked[0:1], stacked[1:2]
         normed_near = norm([raw[0], raw[1]], gain_one, shift_one)
         far_raw, far_pair = [[raw[j]] for j in range(2, seq_count)], []
         incoming_pair = [swap(incoming, "seq", 1)]
         bias_hidden = my_half(hidden_bias.astype(F32)[None], ff_half, ff_half)
-        w_q, w_kv = chain.done(*assemble(parts, me, padded))
     _, _, bias_query, bias_value, bias_output, gain_two, shift_two, bias_down = [
         stacked[i : i + 1] for i in range(8)
     ]
@@ -1141,7 +1171,7 @@
     normed_far = chain.done(norm([box[0] for box in far_raw + far_pair], gain_one, shift_one))
     if staged:
         w_kv, incoming = flights.land(w_kv, incoming)
-        h[z | y], h[zz | y], h[zz | z] = over(h[z], y), over(h[zz], y), over(h[zz], z)
+        h[zz | y], h[zz | z] = over(h[zz], y), over(h[zz], z)
     incoming_near = jnp.concatenate([incoming, incoming_pair[0]], axis=0)
     far_in, w_kv = chain(normed_far, w_kv)
     (far,) = rows_matmul(
@@ -1170,10 +1200,13 @@
     out_pair, w_out_mine = chain(out_pair, w_out_mine)
     other_half = flights.send(out_pair, "seq", 1)
     w_out_other = flights.send(w_out_mine, "seq", 1)
-    w_out_mine, w_hidden = flights.land(w_out_mine, w_hidden)
     if staged:
         d[zz | z], d[z | y] = over(d[zz], z), over(d[z], y)
+    w_out_mine, w_hidden = flights.land(w_out_mine, w_hidden, only=[other_half, w_out_other])
     w_out = chain.done(both_cores(core_flag, w_out_mine, w_out_other[0], out_cut, width))
+    if staged:
+        w_out = flights.land(w_out, only=[d[zz | z], d[z | y]])
+        d[zz | y], d[zz | z | y] = over(d[zz], y), over(d[zz | z], y)
     own_half, w_out = chain(out_own.reshape(flat, padded), w_out)
     attended, middle, second = chain.done(
         *join(
@@ -1189,22 +1222,17 @@
         )
     )
     second_pair = flights.send(second, "seq", 1)
-    second, w_hidden = flights.land(second, w_hidden)
+    second, w_hidden = flights.land(second, w_hidden, only=[second_pair])
+    act, slope, second_near = chain.done(*hidden([second, second_pair[0]], w_hidden, bias_hidden))
+
+    incoming_near, act = chain(incoming_near, act)
+    grad_down = chain.done(token_dot(incoming_near, act))
     if staged:
-        d[zz | y] = over(d[zz], y)
-    act, slope, second_near = chain.done(*hidden([second, second_pair[0]], w_hidden, bias_hidden))
-
-    if staged:
-        incoming_near = flights.land(incoming_near)
-        d[zz | z | y] = over(d[zz | z], y)
-    incoming_near, act = chain(incoming_near, act)
-    grad_down = chain.done(dot(incoming_near, act, TN).astype(BF16))
-    part_down = lax.psum_scatter(grad_down, "fsdp", scatter_dimension=0, tiled=True)
-    if staged:
-        slope = flights.land(slope)
+        slope, grad_down = flights.land(slope, grad_down)
         d_parts = {k: box[0] for k, box in d.items()}
     else:
         d_parts = gather_all(chain(shard_down))
+    part_down = lax.psum_scatter(grad_down, "fsdp", scatter_dimension=0, tiled=True)
     w_down = chain.done(assemble(d_parts, me))
     incoming_near, slope, w_down = chain(incoming_near, slope, w_down)
     grad_pre, hidden_line = chain.done(
@@ -1232,21 +1260,16 @@
     chain.done(branch, grad_send)
     grad_pair = flights.send(grad_send, "seq", 1)
     attended, branch = chain(attended, branch)
-    out_keep, out_send, _ = chain.done(*weight_grad([attended], [branch], me, shards))
-    out_keep, out_send = chain(out_keep, out_send)
-    keep_mine, send_mine, keep_other, send_other = chain.done(
-        *core_columns(core_flag, [out_keep, out_send], out_cols)
-    )
+    partial_out = chain(chain.done(token_dot(attended, branch)))
+    out_mine, out_other = chain.done(*core_columns(core_flag, [partial_out], out_cols))
     query = flights.land(query)
 
-    small = lax.psum(lines, ("seq", "fsdp"))
-    keep_back, send_back = flights.send(keep_other, "seq", 1), flights.send(send_other, "seq", 1)
+    links = {"x": ("seq", top), "core": ("seq", 1)} | {bit: ("fsdp", bit) for bit in bits_of(shards)}
+    out_back = flights.send(out_other, "seq", 1)
     shape = (rows, tokens, padded)
     grads = [grad_mine.reshape(shape), grad_pair[0].reshape(shape)]
     found = ()
     far_bits = [2 << k for k in range(shards.bit_length() - 2)]
-    out_bits = list(far_bits)
-
     def next_step(keep, box, bits):
         keep, send = scatter_step(keep, box[0], shard_rows)
         chain.done(keep)
@@ -1266,16 +1289,12 @@
         chain.done(*found)
         query = flights.land(query)
         if row == 0:
-            (out_keep,), (out_send,) = add_rows(keep_mine, keep_back[0]), add_rows(send_mine, send_back[0])
-            chain.done(out_keep, out_send)
-            out_box = flights.send(out_send, "fsdp", y)
-        else:
-            out_keep, out_box = next_step(out_keep, out_box, out_bits)
+            out_sum = chain.done(*add_rows(out_mine, out_back[0]))
         if row == 1:
             part_down = chain(part_down)
             down_seq = flights.send(part_down, "seq", top)
     dq, dnear, dfar = [g.reshape(-1, g.shape[-1]) for g in found]
-    dfar, w_kv = chain(dfar, w_kv)
+    dfar, w_kv, down_seq[0] = chain(dfar, w_kv, down_seq[0])
     two = seq_count == 4
     back_far = rows_matmul("back_far", [dfar], [w_kv], plain, [], [like(dfar.shape[0], width)], NT, two)
     chain.done(*back_far)
@@ -1291,40 +1310,49 @@
     )
     dq = flights.land(dq)
     kv_box = flights.send(kv_send, "fsdp", y)
-    far_sums = {j: add_rows(far_parts[j], far_sent[j | 1][0])[0] for j in far_parts if not j & 1}
-    chain.done(*far_sums.values())
+    cut_rows = flat - tokens
+    far_sums = {
+        j: [add_rows(far_parts[j][part], far_sent[j | 1][0][part])[0] for part in (slice(0, cut_rows), slice(cut_rows, flat))]
+        for j in far_parts
+        if not j & 1
+    }
+    chain.done(*[part for parts in far_sums.values() for part in parts])
     arrived = []
     for bit in bits_of(seq_count)[:-1]:
-        moved = {j: flights.send(part, "seq", bit) for j, part in far_sums.items() if j & bit}
-        far_sums = {j: part for j, part in far_sums.items() if not j & bit}
-        for j, box in moved.items():
+        for j in [j for j in far_sums if j & bit]:
+            parts = far_sums.pop(j)
             if j == bit:
-                arrived.append(box)
+                arrived.append([flights.send(parts[0], "seq", bit), parts[1], bit])
             else:
-                (far_sums[j ^ bit],) = add_rows(far_sums[j ^ bit], box[0])
+                pairs = zip(far_sums[j ^ bit], parts)
+                far_sums[j ^ bit] = [add_rows(kept, swap(part, "seq", bit))[0] for kept, part in pairs]
     dq, dnear = chain(dq, dnear)
     back_own, back_pair = chain.done(
         *rows_matmul("back_near", [dq, dnear], [w_q, w_kv], plain, [], [like(2 * flat, width)], NT, True)
     )
     pair_back = flights.send(back_pair, "seq", 1)
+    for entry in arrived:
+        entry[1] = flights.send(chain(entry[1]), "seq", entry[2])
     normed_near, dq = chain(normed_near, dq)
     q_keep, q_send, q_sums = chain.done(*weight_grad([normed_near], [dq], me, shards))
     q_box = flights.send(q_send, "fsdp", y)
-    act, middle = chain(act, middle)
+    kv_bits, q_bits = list(far_bits), list(far_bits)
+    act = flights.land(act, only=[kv_box])
+    kv_keep, kv_box = next_step(kv_keep, kv_box, kv_bits)
+    act, middle = flights.land(act, middle, only=[entry[0] for entry in arrived])
     (down_pair,) = rows_matmul(
         "down_pair", [act], [w_down], plain, [], [like(flat, width)], NT, first_row=flat
     )
     chain.done(down_pair)
     down_back = flights.send(down_pair, "seq", 1)
-    kv_bits, q_bits = list(far_bits), list(far_bits)
-    act = flights.land(act, through=kv_box)
-    kv_keep, kv_box = next_step(kv_keep, kv_box, kv_bits)
-    late_in = flights.land(inputs, through=pair_back)
+    late_in = flights.land(inputs, only=[pair_back, q_box] + [entry[1] for entry in arrived])
+    q_keep, q_box = next_step(q_keep, q_box, q_bits)
+    late_in = chain(late_in)
     grad_patches, late = chain.done(
         *first_back(
             core_flag,
             late_in,
-            [back_own, pair_back[0]] + [box[0] for box in arrived],
+            [back_own, pair_back[0]] + [(entry[0][0], entry[1][0]) for entry in arrived],
             gain_one,
             grad_middle,
             q_sums,
@@ -1332,46 +1360,72 @@
             half,
         )
     )
-    late = lax.psum(late, ("seq", "fsdp"))
+    out_sum = chain(out_sum)
+    part_out = lax.psum_scatter(out_sum, "fsdp", scatter_dimension=0, tiled=True)
+    small = jnp.concatenate([lines, late], axis=0)
+    small_todo = [zz, y, z] if staged else bits_of(shards)
+    small_todo = [("fsdp", bit) for bit in small_todo] + [("seq", bit) for bit in reversed(bits_of(seq_count))]
+    small_box = None
+
+    def small_send():
+        return flights.send(small, *small_todo.pop(0)) if small_todo else None
+
+    def small_step(small, box):
+        return chain.done(*add_rows(small, box[0], F32))
+
+    small_box = small_send()
     part_hidden = chain(part_hidden)
     hidden_seq = flights.send(part_hidden, "seq", top)
-    act = flights.land(act, through=down_back)
-    q_keep, q_box = next_step(q_keep, q_box, q_bits)
+    act = flights.land(act, only=[kv_box, down_back])
+    if kv_box is not None:
+        kv_keep, kv_box = next_step(kv_keep, kv_box, kv_bits)
     act, middle = chain(act, middle)
     (layer_output,) = rows_matmul(
         "down_own", [act], [w_down], layer_end, [middle, down_back[0], bias_down], [like(flat, width)], NT
     )
     layer_output = chain.done(layer_output).reshape(rows, tokens, width)
+    lands = [small_box, hidden_seq, q_box]
+    act = flights.land(act, only=lands)
+    small = small_step(small, small_box)
+    small_box = small_send()
+    if q_box is not None:
+        q_keep, q_box = next_step(q_keep, q_box, q_bits)
+    hidden_total = seq_rest(part_hidden, hidden_seq[0])
+    hidden_other = flights.send(hidden_total, "seq", 1)
     down_total = seq_rest(part_down, down_seq[0])
     while kv_box is not None:
-        act = flights.land(act, through=kv_box)
+        act = flights.land(act, only=[kv_box])
         kv_keep, kv_box = next_step(kv_keep, kv_box, kv_bits)
-        if q_box is not None and kv_box is not None:
-            act = flights.land(act, through=q_box)
-            q_keep, q_box = next_step(q_keep, q_box, q_bits)
     kv_seq = flights.send(kv_keep, "seq", top)
-    while out_box is not None:
-        out_keep, out_box = next_step(out_keep, out_box, out_bits)
-        if out_box is not None:
-            act = flights.land(act)
-    out_seq = flights.send(out_keep, "seq", top)
-    down_other = flights.send(down_total, "seq", 1)
-    hidden_total = seq_rest(part_hidden, hidden_seq[0])
+    act = flights.land(act, only=[small_box, hidden_other])
+    small = small_step(small, small_box)
+    small_box = small_send()
     while q_box is not None:
-        act = flights.land(act, through=q_box)
+        act = flights.land(act, only=[q_box])
         q_keep, q_box = next_step(q_keep, q_box, q_bits)
     q_seq = flights.send(q_keep, "seq", top)
-    act = flights.land(act, through=kv_seq)
+    part_out = chain(part_out)
+    out_seq = flights.send(part_out, "seq", top)
+    act = flights.land(act, only=[kv_seq, small_box])
     kv_total = seq_rest(kv_keep, kv_seq[0])
+    small = small_step(small, small_box)
+    small_box = small_send()
     kv_other = flights.send(kv_total, "seq", 1)
-    hidden_other = flights.send(hidden_total, "seq", 1)
-    act = flights.land(act, through=q_seq)
-    out_total = seq_rest(out_keep, out_seq[0])
+    down_other = flights.send(down_total, "seq", 1)
+    act = flights.land(act, only=[q_seq, out_seq, small_box])
+    small = small_step(small, small_box)
+    small_box = small_send()
     q_total = seq_rest(q_keep, q_seq[0])
+    out_total = seq_rest(part_out, out_seq[0])
     q_other, out_other = flights.send(q_total, "seq", 1), flights.send(out_total, "seq", 1)
+    while small_box is not None:
+        act = flights.land(act)
+        small = small_step(small, small_box)
+        small_box = small_send()
     flights.land()
-    own_lines = lax.dynamic_slice_in_dim(small, me * shard_rows, shard_rows, 1)
-    late_lines = lax.dynamic_slice_in_dim(late, me * shard_rows, shard_rows, 1)
+
+    own_lines = lax.dynamic_slice_in_dim(small[:8], me * shard_rows, shard_rows, 1)
+    late_lines = lax.dynamic_slice_in_dim(small[8:], me * shard_rows, shard_rows, 1)
     cuts = [width, ff_half - width, width, ff - ff_half - width]
     full_bias = jnp.concatenate([small[4 + i, :size] for i, size in enumerate(cuts)])
     full_down = both_columns(is_first, down_total, down_other[0], ff_half, ff).T

time: 755 us -> 646 us (0.86)
  waiting for transfers between devices: 262 us -> 168 us
  Pallas kernels: 324 us -> 347 us
  local copies, waits for them, and re-layouts: 27.5 us -> 11.9 us
  matrix products: 26.1 us -> 14.3 us
  starting transfers between devices: 56.7 us -> 45.3 us
    psum x1 -> x0, waiting for transfers between devices: 96.5 us -> none  [local(): late = lax.psum(late, ('seq', 'fsdp'))]
    pallas_call x0 -> x4, Pallas kernels: none -> 25.2 us  [the longest x2 21 us: token_dot(): pl.pallas_call(kernel, out_shape=jax.ShapeDtypeStruct((width, cols), BF16...]
    reduce_scatter x0 -> x1, waiting for transfers between devices: none -> 24.9 us  [local(): lax.psum_scatter(out_sum, 'fsdp', scatter_dimension=0, tiled=True)]
    ppermute x60 -> x57, waiting for transfers between devices: 166 us -> 143 us  [swap(): return lax.ppermute(array, axis, [(i, i ^ bits) for i in range(size)])]
    dot_general x2 -> x1, matrix products: 26.1 us -> 14.3 us  [dot(): lax.dot_general(left, right, (dims, ((), ())), preferred_element_type=F32)]
    ppermute x60 -> x57, starting transfers between devices: 56.4 us -> 45 us  [swap(): return lax.ppermute(array, axis, [(i, i ^ bits) for i in range(size)])]
    pallas_call x3, Pallas kernels: 58.8 us -> 67.2 us  [attend_back(): pl.pallas_call(functools.partial(attend_back_kernel, row, heads, blocks,...]
    pallas_call x3 -> x2, Pallas kernels: 33.3 us -> 25.6 us  [weight_grad(): pl.pallas_call(functools.partial(weight_grad_kernel, pairs, count, rows),...]
  transfers between devices with their start and end apart: 63 -> 60, of which waited for: 21 -> 23; matrix products, arithmetic and copies ran while one was open for 7% -> 7% of each run, Pallas kernels for 41% -> 52%
where the time goes in v6:
time: 646 us; the launch traced here: 636 us
  Pallas kernels  347 us (54%)
  waiting for transfers between devices  168 us (26%)
  starting transfers between devices  45.3 us (7%)
  other arithmetic  33.9 us (5%)
  between operations  14.6 us (2%)
  matrix products  14.3 us (2%)
  local copies, waits for them, and re-layouts  11.9 us (2%)
    ppermute x57, waiting for transfers between devices, swap(): return lax.ppermute(array, axis, [(i, i ^ bits) for i in range(size)])  143 us
    pallas_call x9, Pallas kernels, rows_matmul(): pl.pallas_call(kernel, out_shape=shapes, grid=(steps,), in_specs=[pl.Bloc...  99.5 us
    pallas_call x3, Pallas kernels, attend_back(): pl.pallas_call(functools.partial(attend_back_kernel, row, heads, blocks,...  67.2 us
    ppermute x57, starting transfers between devices, swap(): return lax.ppermute(array, axis, [(i, i ^ bits) for i in range(size)])  45 us
    pallas_call x3, Pallas kernels, attend(): pl.pallas_call(functools.partial(attend_kernel, row, heads, blocks, padde...  37.8 us
    pallas_call x2, Pallas kernels, weight_grad(): pl.pallas_call(functools.partial(weight_grad_kernel, pairs, count, rows),...  25.6 us
    reduce_scatter x1, waiting for transfers between devices, local(): lax.psum_scatter(out_sum, 'fsdp', scatter_dimension=0, tiled=True)  24.9 us
    pallas_call x2, Pallas kernels, token_dot(): pl.pallas_call(kernel, out_shape=jax.ShapeDtypeStruct((width, cols), BF16...  21 us
  transfers between devices with their start and end apart: 60, of which 23 were waited for; matrix products, arithmetic and copies ran while one was open for 7% of the time, Pallas kernels for 52%

profile of v6, /device:TPU:0, one launch (start us, length us, event | category | flops | bytes accessed | tf_op | source)
XLA Modules:
  0.0 635.7 jit_solution(1710903159654464756)
XLA Ops:
  25.8 12.9 %collective-permute-done.2.refs_4_ = bf16[144,1920]{1,0:T(8,128)(2,1)} collective-permute-done((bf16[144,1920]{1,0:T(8,128)(2,1)}, bf16[144,1920]{1,0:T(8,128)(2,1)}, u32[]{:S(2)}, u32[]{:S(2)}) %collective-permute-start.2) | collective-permute-done | bytes 552992 | tf_op jit(solution)/shard_map/ppermute | solution.py:42
  44.0 11.3 %collective-permute-done.6.refs_6_ = bf16[144,1920]{1,0:T(8,128)(2,1)S(1)} collective-permute-done((bf16[144,1920]{1,0:T(8,128)(2,1)}, bf16[144,1920]{1,0:T(8,128)(2,1)S(1)}, u32[]{:S(2)}, u32[]{:S(2)}) %collective-permute-start.6) | collective-permute-done | bytes 552992 | tf_op jit(solution)/shard_map/ppermute | solution.py:42
  56.9 12.6 %collective-permute-done.3.refs_3_ = bf16[144,1920]{1,0:T(8,128)(2,1)S(1)} collective-permute-done((bf16[144,1920]{1,0:T(8,128)(2,1)}, bf16[144,1920]{1,0:T(8,128)(2,1)S(1)}, u32[]{:S(2)}, u32[]{:S(2)}) %collective-permute-start.3) | collective-permute-done | bytes 552992 | tf_op jit(solution)/shard_map/ppermute | solution.py:42
  69.5 10.7 %collective-permute-done.8.refs_7_ = bf16[144,1920]{1,0:T(8,128)(2,1)S(1)} collective-permute-done((bf16[144,1920]{1,0:T(8,128)(2,1)S(1)}, bf16[144,1920]{1,0:T(8,128)(2,1)S(1)}, u32[]{:S(2)}, u32[]{:S(2)}) %collective-permute-start.8) | collective-permute-done | bytes 552992 | tf_op jit(solution)/shard_map/ppermute | solution.py:42
  152.9 12.6 %attend.3 = (bf16[3,256,640]{2,1,0:T(8,128)(2,1)}, bf16[3,256,640]{2,1,0:T(8,128)(2,1)}, f32[3,8,512]{2,1,0:T(8,128)}) custom-call(s32[3,4]{1,0:T(4,128)} %get-tuple-element.242.need_ref, s32[3,512,1]{2,1,0:T(8,128)} %get-tuple-element.246.col_ref, s32[3,4,256]{2,1,0:T(4,128)} %get-tuple-element.243.row_ref, bf16[2,3,256,640]{3,2,1,0:T(8,128)(2,1)} %bitcast.51, ...), custom_call_target="tpu_custom_call" | custom-call | flops 1 | bytes 1 | tf_op jit(solution)/shard_map/attend/pallas_call | solution.py:908
  168.4 12.5 %attend.4 = (bf16[3,256,640]{2,1,0:T(8,128)(2,1)}, bf16[3,256,640]{2,1,0:T(8,128)(2,1)}, f32[3,8,512]{2,1,0:T(8,128)}) custom-call(s32[3,4]{1,0:T(4,128)} %get-tuple-element.242.need_ref, s32[3,512,1]{2,1,0:T(8,128)} %get-tuple-element.246.col_ref, ...), custom_call_target="tpu_custom_call", output_to_operand_aliasing={{0}: (6, {}), {1}: (7, {}), {2}: (8, {})} | custom-call | flops 1 | bytes 1 | tf_op jit(solution)/shard_map/attend/pallas_call | solution.py:908
  180.9 12.7 %attend.5 = (bf16[3,256,640]{2,1,0:T(8,128)(2,1)}, bf16[3,256,640]{2,1,0:T(8,128)(2,1)}, f32[3,8,512]{2,1,0:T(8,128)}) custom-call(s32[3,4]{1,0:T(4,128)} %get-tuple-element.242.need_ref, s32[3,512,1]{2,1,0:T(8,128)} %get-tuple-element.246.col_ref, ...), custom_call_target="tpu_custom_call", output_to_operand_aliasing={{0}: (6, {}), {1}: (7, {}), {2}: (8, {})} | custom-call | flops 1 | bytes 1 | tf_op jit(solution)/shard_map/attend/pallas_call | solution.py:908
  234.0 18.7 %hidden.1 = (bf16[1536,2176]{1,0:T(8,128)(2,1)}, bf16[1536,2176]{1,0:T(8,128)(2,1)}, bf16[1536,1152]{1,0:T(8,128)(2,1)}) custom-call(bf16[768,1152]{1,0:T(8,128)(2,1)} %get-tuple-element.328.refs_0_, bf16[768,1152]{1,0:T(8,128)(2,1)} %collective-permute-done.25.refs_1_, bf16[1152,2176]{1,0:T(8,128)(2,1)} %get-tuple-element.330.refs_2_.refs_1_, ...), custom_call_target="tpu_custom_call" | custom-call | flops 1 | bytes 1 | tf_op jit(solution)/shard_map/hidden/pallas_call | solution.py:792
  252.7 14.1 %token_dot.2 = bf16[1152,2176]{1,0:T(8,128)(2,1)} custom-call(bf16[1536,1152]{1,0:T(8,128)(2,1)} %pad_maximum_fusion.left_ref.refs_0_, bf16[1536,2176]{1,0:T(8,128)(2,1)} %get-tuple-element.431.right_ref.refs_0_), custom_call_target="tpu_custom_call" | custom-call | flops 1 | bytes 1 | tf_op jit(solution)/shard_map/token_dot/pallas_call | solution.py:219
  272.0 14.9 %grad_pre.1 = (bf16[1536,2176]{1,0:T(8,128)(2,1)}, f32[1,2176]{1,0:T(1,128)}) custom-call(bf16[1536,1152]{1,0:T(8,128)(2,1)} %pad_maximum_fusion.left_ref.refs_0_, bf16[1152,2176]{1,0:T(8,128)(2,1)} %assemble.5.refs_1_, bf16[1536,2176]{1,0:T(8,128)(2,1)} %get-tuple-element.345.refs_2_), custom_call_target="tpu_custom_call" | custom-call | flops 1 | bytes 1 | tf_op jit(solution)/shard_map/grad_pre/pallas_call | solution.py:520
  286.8 14.7 %back.1 = (bf16[768,1152]{1,0:T(8,128)(2,1)}, bf16[768,1152]{1,0:T(8,128)(2,1)}) custom-call(bf16[1536,2176]{1,0:T(8,128)(2,1)} %get-tuple-element.350.refs_0_, bf16[1152,2176]{1,0:T(8,128)(2,1)} %get-tuple-element.330.refs_2_.refs_1_), custom_call_target="tpu_custom_call" | custom-call | flops 1 | bytes 1 | tf_op jit(solution)/shard_map/back/pallas_call | solution.py:520
  301.6 14.3 %convolution_convert_fusion = bf16[1152,2176]{1,0:T(8,128)(2,1)} fusion(bf16[1536,1152]{1,0:T(8,128)(2,1)} %get-tuple-element.349, bf16[1536,2176]{1,0:T(8,128)(2,1)} %get-tuple-element.350.refs_0_), kind=kOutput, calls=%fused_computation.1 | convolution fusion | flops 7703248896 | bytes 15237120 | tf_op jit(solution)/shard_map/dot_general | solution.py:29
  317.1 12.3 %second_back.1 = (f32[768,1152]{1,0:T(8,128)}, bf16[768,1152]{1,0:T(8,128)(2,1)}, bf16[768,640]{1,0:T(8,128)(2,1)}, bf16[768,640]{1,0:T(8,128)(2,1)}, f32[8,1152]{1,0:T(8,128)}) custom-call(s32[1]{0:T(128)} %bitcast.3.core_ref, f32[768,1152]{1,0:T(8,128)} %get-tuple-element.432.x_ref.refs_2_, bf16[768,1152]{1,0:T(8,128)(2,1)} %get-tuple-element.351.refs_0_, ...), custom_call_target="tpu_custom_call" | custom-call | flops 1 | bytes 1 | tf_op jit(solution)/shard_map/second_back/pallas_call | solution.py:447
  345.8 22.0 %attend_back.3 = (bf16[2,3,256,640]{3,2,1,0:T(8,128)(2,1)}, bf16[2,3,256,1280]{3,2,1,0:T(8,128)(2,1)}, bf16[2,3,256,1280]{3,2,1,0:T(8,128)(2,1)}) custom-call(s32[3,4]{1,0:T(4,128)} %get-tuple-element.242.need_ref, s32[3,4,256,1]{3,2,1,0:T(8,128)} %get-tuple-element.244.col_ref, s32[3,1,512]{2,1,0:T(1,128)} %get-tuple-element.245.row_ref, ...), custom_call_target="tpu_custom_call" | custom-call | flops 1 | bytes 1 | tf_op jit(solution)/shard_map/attend_back/pallas_call | solution.py:1006
  369.3 21.8 %attend_back.4 = (bf16[2,3,256,640]{3,2,1,0:T(8,128)(2,1)}, bf16[2,3,256,1280]{3,2,1,0:T(8,128)(2,1)}, bf16[2,3,256,1280]{3,2,1,0:T(8,128)(2,1)}) custom-call(s32[3,4]{1,0:T(4,128)} %get-tuple-element.242.need_ref, s32[3,4,256,1]{3,2,1,0:T(8,128)} %get-tuple-element.244.col_ref, ...), custom_call_target="tpu_custom_call", output_to_operand_aliasing={{0}: (12, {}), {1}: (13, {}), {2}: (14, {})} | custom-call | flops 1 | bytes 1 | tf_op jit(solution)/shard_map/attend_back/pallas_call | solution.py:1006
  393.3 23.4 %attend_back.5 = (bf16[2,3,256,640]{3,2,1,0:T(8,128)(2,1)}, bf16[2,3,256,1280]{3,2,1,0:T(8,128)(2,1)}, bf16[2,3,256,1280]{3,2,1,0:T(8,128)(2,1)}) custom-call(s32[3,4]{1,0:T(4,128)} %get-tuple-element.242.need_ref, s32[3,4,256,1]{3,2,1,0:T(8,128)} %get-tuple-element.244.col_ref, ...), custom_call_target="tpu_custom_call", output_to_operand_aliasing={{0}: (12, {}), {1}: (13, {}), {2}: (14, {})} | custom-call | flops 1 | bytes 1 | tf_op jit(solution)/shard_map/attend_back/pallas_call | solution.py:1006
  416.7 10.5 %back_far.1 = (bf16[768,1152]{1,0:T(8,128)(2,1)}, bf16[768,1152]{1,0:T(8,128)(2,1)}) custom-call(bf16[1536,1280]{1,0:T(8,128)(2,1)} %bitcast.59, bf16[1152,1280]{1,0:T(8,128)(2,1)} %get-tuple-element.394.refs_1_.refs_3_), custom_call_target="tpu_custom_call" | custom-call | flops 1 | bytes 1 | tf_op jit(solution)/shard_map/back_far/pallas_call | solution.py:520
  428.5 17.5 %weight_grad.2 = (bf16[576,1280]{1,0:T(8,128)(2,1)}, bf16[576,1280]{1,0:T(8,128)(2,1)}, f32[8,1280]{1,0:T(8,128)}) custom-call(s32[9]{0:T(128)} %pad_add_fusion.pos_ref, bf16[1536,1152]{1,0:T(8,128)(2,1)} %norm.2.refs_0_, bf16[1536,1152]{1,0:T(8,128)(2,1)} %norm.3.refs_0_.refs_1_, bf16[1536,1280]{1,0:T(8,128)(2,1)} %bitcast.57, bf16[1536,1280]{1,0:T(8,128)(2,1)} %bitcast.60), custom_call_target="tpu_custom_call" | custom-call | flops 1 | bytes 1 | tf_op jit(solution)/shard_map/weight_grad/pallas_call | solution.py:190
  448.5 13.5 %back_near.1 = (bf16[768,1152]{1,0:T(8,128)(2,1)}, bf16[768,1152]{1,0:T(8,128)(2,1)}) custom-call(bf16[1536,640]{1,0:T(8,128)(2,1)} %bitcast.62, bf16[1536,1280]{1,0:T(8,128)(2,1)} %bitcast.58, bf16[1152,640]{1,0:T(8,128)(2,1)} %get-tuple-element.275.weight_ref.refs_1_.refs_2_, bf16[1152,1280]{1,0:T(8,128)(2,1)} %get-tuple-element.394.refs_1_.refs_3_), custom_call_target="tpu_custom_call" | custom-call | flops 1 | bytes 1 | tf_op jit(solution)/shard_map/back_near/pallas_call | solution.py:520
  470.4 14.3 %collective-permute-done.32 = bf16[576,1280]{1,0:T(8,128)(2,1)} collective-permute-done((bf16[576,1280]{1,0:T(8,128)(2,1)}, bf16[576,1280]{1,0:T(8,128)(2,1)}, u32[]{:S(2)}, u32[]{:S(2)}) %collective-permute-start.32) | collective-permute-done | bytes 1474592 | tf_op jit(solution)/shard_map/ppermute | solution.py:42
  498.8 13.1 %collective-permute-done.38.refs_3_ = bf16[256,1152]{1,0:T(8,128)(2,1)S(1)} collective-permute-done((bf16[256,1152]{1,0:T(8,128)(2,1)S(1)}, bf16[256,1152]{1,0:T(8,128)(2,1)S(1)}, u32[]{:S(2)}, u32[]{:S(2)}) %collective-permute-start.38) | collective-permute-done | bytes 589856 | tf_op jit(solution)/shard_map/ppermute | solution.py:42
  532.7 21.6 %collective-permute-done.45 = bf16[144,1280]{1,0:T(8,128)(2,1)} collective-permute-done((bf16[144,1280]{1,0:T(8,128)(2,1)}, bf16[144,1280]{1,0:T(8,128)(2,1)}, u32[]{:S(2)}, u32[]{:S(2)}) %collective-permute-start.45) | collective-permute-done | bytes 368672 | tf_op jit(solution)/shard_map/ppermute | solution.py:42
  555.6 10.3 %down_own.1 = bf16[768,1152]{1,0:T(8,128)(2,1)} custom-call(bf16[1536,2176]{1,0:T(8,128)(2,1)} %get-tuple-element.431.right_ref.refs_0_, bf16[1152,2176]{1,0:T(8,128)(2,1)} %assemble.5.refs_1_, f32[768,1152]{1,0:T(8,128)} %get-tuple-element.432.x_ref.refs_2_, bf16[768,1152]{1,0:T(8,128)(2,1)} %copy-done.5, f32[1,1152]{1,0:T(1,128)} %get-tuple-element.478.refs_4_), custom_call_target="tpu_custom_call" | custom-call | flops 1 | bytes 1 | tf_op jit(solution)/shard_map/down_own/pallas_call | solution.py:520
  578.9 24.9 %reduce-scatter.8.cloned.1.call-done = bf16[144,640]{1,0:T(8,128)(2,1)} async-done(((bf16[1152,640]{1,0:T(8,128)(2,1)}), bf16[144,640]{1,0:T(8,128)(2,1)}) %reduce-scatter.8.cloned.1.call-update) | async-done | bytes 184336 | tf_op jit(solution)/shard_map/reduce_scatter | solution.py:1364
  (259 shorter events, 253.8 us)
Async XLA Ops:
  7.2 384.0 %reduce-scatter.4.cloned.1.call-start = ((), (), s32[]{:S(2)}) async-start(), calls=%async_computation.3 | async-start | bytes 5640192 | tf_op jit(solution)/shard_map/reduce_scatter | solution.py:1235
  9.7 29.0 %collective-permute-start.2 = (bf16[144,1920]{1,0:T(8,128)(2,1)}, bf16[144,1920]{1,0:T(8,128)(2,1)}, u32[]{:S(2)}, u32[]{:S(2)}) collective-permute-start(bf16[144,1920]{1,0:T(8,128)(2,1)} %get-tuple-element.237.refs_0_), channel_id=1, source_target_pairs={{0,4},{1,5},{2,6},{3,7},{4,0},{5,1},{6,2},{7,3},{8,12},{9,13},{10,... | collective-permute-start | bytes 1658888 | tf_op jit(solution)/shard_map/ppermute | solution.py:42
  38.9 30.6 %collective-permute-start.5 = (bf16[768,1152]{1,0:T(8,128)(2,1)S(1)}, bf16[768,1152]{1,0:T(8,128)(2,1)S(1)}, u32[]{:S(2)}, u32[]{:S(2)}) collective-permute-start(bf16[768,1152]{1,0:T(8,128)(2,1)S(1)} %bitcast.67), channel_id=1, source_target_pairs={{0,8},{8,0},{16,24},{24,16},{1,9},{9,1},{17,25},{25,17},{2,10},{10... | collective-permute-start | bytes 5308424 | tf_op jit(solution)/shard_map/ppermute | solution.py:42
  38.9 41.3 %collective-permute-start.7 = (bf16[768,1152]{1,0:T(8,128)(2,1)S(1)}, bf16[768,1152]{1,0:T(8,128)(2,1)}, u32[]{:S(2)}, u32[]{:S(2)}) collective-permute-start(bf16[768,1152]{1,0:T(8,128)(2,1)S(1)} %bitcast.68), channel_id=1, source_target_pairs={{0,16},{8,24},{16,0},{24,8},{1,17},{9,25},{17,1},{25,9},{2,18},{10... | collective-permute-start | bytes 5308424 | tf_op jit(solution)/shard_map/ppermute | solution.py:42
  80.2 53.8 %collective-permute-start.15 = (bf16[768,1152]{1,0:T(8,128)(2,1)S(1)}, bf16[768,1152]{1,0:T(8,128)(2,1)S(1)}, u32[]{:S(2)}, u32[]{:S(2)}) collective-permute-start(bf16[768,1152]{1,0:T(8,128)(2,1)S(1)} %bitcast.78), channel_id=1, source_target_pairs={{0,8},{8,0},{16,24},{24,16},{1,9},{9,1},{17,25},{25,17},{2,10},{10... | collective-permute-start | bytes 5308424 | tf_op jit(solution)/shard_map/ppermute | solution.py:42
  82.7 58.6 %collective-permute-start.9 = (bf16[144,2816]{1,0:T(8,128)(2,1)}, bf16[144,2816]{1,0:T(8,128)(2,1)}, u32[]{:S(2)}, u32[]{:S(2)}) collective-permute-start(bf16[144,2816]{1,0:T(8,128)(2,1)} %get-tuple-element.268.refs_0_), channel_id=1, source_target_pairs={{0,1},{1,0},{2,3},{3,2},{4,5},{5,4},{6,7},{7,6},{8,9},{9,8},{10,11... | collective-permute-start | bytes 2433032 | tf_op jit(solution)/shard_map/ppermute | solution.py:42
  93.1 48.2 %collective-permute-start.10 = (bf16[144,2816]{1,0:T(8,128)(2,1)}, bf16[144,2816]{1,0:T(8,128)(2,1)}, u32[]{:S(2)}, u32[]{:S(2)}) collective-permute-start(bf16[144,2816]{1,0:T(8,128)(2,1)} %get-tuple-element.268.refs_0_), channel_id=1, source_target_pairs={{0,4},{1,5},{2,6},{3,7},{4,0},{5,1},{6,2},{7,3},{8,12},{9,13},{10,... | collective-permute-start | bytes 2433032 | tf_op jit(solution)/shard_map/ppermute | solution.py:42
  107.8 33.5 %collective-permute-start.14 = (bf16[144,2816]{1,0:T(8,128)(2,1)}, bf16[144,2816]{1,0:T(8,128)(2,1)}, u32[]{:S(2)}, u32[]{:S(2)}) collective-permute-start(bf16[144,2816]{1,0:T(8,128)(2,1)} %collective-permute-done.12.refs_2_), channel_id=1, source_target_pairs={{0,1},{1,0},{2,3},{3,2},{4,5},{5,4},{6,7},{7,6},{8,9},{9,8},{10,11... | collective-permute-start | bytes 2433032 | tf_op jit(solution)/shard_map/ppermute | solution.py:42
  110.3 31.0 %collective-permute-start.11 = (bf16[144,2176]{1,0:T(8,128)(2,1)}, bf16[144,2176]{1,0:T(8,128)(2,1)}, u32[]{:S(2)}, u32[]{:S(2)}) collective-permute-start(bf16[144,2176]{1,0:T(8,128)(2,1)} %get-tuple-element.269.refs_0_), channel_id=1, source_target_pairs={{0,1},{1,0},{2,3},{3,2},{4,5},{5,4},{6,7},{7,6},{8,9},{9,8},{10,11... | collective-permute-start | bytes 1880072 | tf_op jit(solution)/shard_map/ppermute | solution.py:42
  165.5 29.8 %collective-permute-start.18 = (bf16[144,2816]{1,0:T(8,128)(2,1)}, bf16[144,2816]{1,0:T(8,128)(2,1)S(1)}, u32[]{:S(2)}, u32[]{:S(2)}) collective-permute-start(bf16[144,2816]{1,0:T(8,128)(2,1)} %collective-permute-done.17.refs_6_), channel_id=1, source_target_pairs={{0,1},{1,0},{2,3},{3,2},{4,5},{5,4},{6,7},{7,6},{8,9},{9,8},{10,11... | collective-permute-start | bytes 2433032 | tf_op jit(solution)/shard_map/ppermute | solution.py:42
  165.6 28.1 %collective-permute-start.20 = (bf16[144,2176]{1,0:T(8,128)(2,1)S(1)}, bf16[144,2176]{1,0:T(8,128)(2,1)}, u32[]{:S(2)}, u32[]{:S(2)}) collective-permute-start(bf16[144,2176]{1,0:T(8,128)(2,1)S(1)} %copy-done.18), channel_id=1, source_target_pairs={{0,4},{1,5},{2,6},{3,7},{4,0},{5,1},{6,2},{7,3},{8,12},{9,13},{10,... | collective-permute-start | bytes 1880072 | tf_op jit(solution)/shard_map/ppermute | solution.py:42
  229.9 36.9 %collective-permute-start.26 = (bf16[144,2176]{1,0:T(8,128)(2,1)}, bf16[144,2176]{1,0:T(8,128)(2,1)}, u32[]{:S(2)}, u32[]{:S(2)}) collective-permute-start(bf16[144,2176]{1,0:T(8,128)(2,1)} %collective-permute-done.20.refs_4_), channel_id=1, source_target_pairs={{0,1},{1,0},{2,3},{3,2},{4,5},{5,4},{6,7},{7,6},{8,9},{9,8},{10,11... | collective-permute-start | bytes 1880072 | tf_op jit(solution)/shard_map/ppermute | solution.py:42
  230.9 35.9 %collective-permute-start.27 = (bf16[144,2176]{1,0:T(8,128)(2,1)}, bf16[144,2176]{1,0:T(8,128)(2,1)}, u32[]{:S(2)}, u32[]{:S(2)}) collective-permute-start(bf16[144,2176]{1,0:T(8,128)(2,1)} %collective-permute-done.21.refs_6_), channel_id=1, source_target_pairs={{0,1},{1,0},{2,3},{3,2},{4,5},{5,4},{6,7},{7,6},{8,9},{9,8},{10,11... | collective-permute-start | bytes 1880072 | tf_op jit(solution)/shard_map/ppermute | solution.py:42
  266.8 262.1 %reduce-scatter.6.cloned.1.call-start = ((), (), s32[]{:S(2)}) async-start(), calls=%async_computation.4 | async-start | bytes 5640192 | tf_op jit(solution)/shard_map/reduce_scatter | solution.py:1255
  315.9 288.0 %reduce-scatter.8.cloned.1.call-start = ((), (), s32[]{:S(2)}) async-start(), calls=%async_computation.5 | async-start | bytes 1658880 | tf_op jit(solution)/shard_map/reduce_scatter | solution.py:1364
  446.0 38.7 %collective-permute-start.32 = (bf16[576,1280]{1,0:T(8,128)(2,1)}, bf16[576,1280]{1,0:T(8,128)(2,1)}, u32[]{:S(2)}, u32[]{:S(2)}) collective-permute-start(bf16[576,1280]{1,0:T(8,128)(2,1)} %get-tuple-element.402), channel_id=1, source_target_pairs={{0,1},{1,0},{2,3},{3,2},{4,5},{5,4},{6,7},{7,6},{8,9},{9,8},{10,11... | collective-permute-start | bytes 4423688 | tf_op jit(solution)/shard_map/ppermute | solution.py:42
  447.3 39.9 %collective-permute-start.35 = (bf16[512,1152]{1,0:T(8,128)(2,1)}, bf16[512,1152]{1,0:T(8,128)(2,1)}, u32[]{:S(2)}, u32[]{:S(2)}) collective-permute-start(bf16[512,1152]{1,0:T(8,128)(2,1)} %add_convert_fusion.1), channel_id=1, source_target_pairs={{0,16},{8,24},{16,0},{24,8},{1,17},{9,25},{17,1},{25,9},{2,18},{10... | collective-permute-start | bytes 3538952 | tf_op jit(solution)/shard_map/ppermute | solution.py:42
  462.0 53.0 %collective-permute-start.37 = (bf16[768,1152]{1,0:T(8,128)(2,1)}, bf16[768,1152]{1,0:T(8,128)(2,1)}, u32[]{:S(2)}, u32[]{:S(2)}) collective-permute-start(bf16[768,1152]{1,0:T(8,128)(2,1)} %get-tuple-element.409), channel_id=1, source_target_pairs={{0,8},{8,0},{16,24},{24,16},{1,9},{9,1},{17,25},{25,17},{2,10},{10... | collective-permute-start | bytes 5308424 | tf_op jit(solution)/shard_map/ppermute | solution.py:42
  496.1 28.6 %collective-permute-start.36 = (bf16[768,1152]{1,0:T(8,128)(2,1)}, bf16[768,1152]{1,0:T(8,128)(2,1)S(1)}, u32[]{:S(2)}, u32[]{:S(2)}) collective-permute-start(bf16[768,1152]{1,0:T(8,128)(2,1)} %down_pair.1), channel_id=1, source_target_pairs={{0,8},{8,0},{16,24},{24,16},{1,9},{9,1},{17,25},{25,17},{2,10},{10... | collective-permute-start | bytes 5308424 | tf_op jit(solution)/shard_map/ppermute | solution.py:42
  529.0 36.9 %collective-permute-start.42 = (bf16[144,2176]{1,0:T(8,128)(2,1)}, bf16[144,2176]{1,0:T(8,128)(2,1)}, u32[]{:S(2)}, u32[]{:S(2)}) collective-permute-start(bf16[144,2176]{1,0:T(8,128)(2,1)} %reduce-scatter.6.cloned.1.call-done), channel_id=1, source_target_pairs={{0,16},{8,24},{16,0},{24,8},{1,17},{9,25},{17,1},{25,9},{2,18},{10... | collective-permute-start | bytes 1880072 | tf_op jit(solution)/shard_map/ppermute | solution.py:42
  530.0 35.9 %collective-permute-start.41 = (f32[16,1152]{1,0:T(8,128)S(1)}, f32[16,1152]{1,0:T(8,128)S(1)}, u32[]{:S(2)}, u32[]{:S(2)}) collective-permute-start(f32[16,1152]{1,0:T(8,128)S(1)} %constant_dynamic-update-slice_fusion), channel_id=1, source_target_pairs={{0,4},{1,5},{2,6},{3,7},{4,0},{5,1},{6,2},{7,3},{8,12},{9,13},{10,... | collective-permute-start | bytes 221192 | tf_op jit(solution)/shard_map/ppermute | solution.py:42
  532.7 33.2 %collective-permute-start.40 = (bf16[288,640]{1,0:T(8,128)(2,1)S(1)}, bf16[288,640]{1,0:T(8,128)(2,1)S(1)}, u32[]{:S(2)}, u32[]{:S(2)}) collective-permute-start(bf16[288,640]{1,0:T(8,128)(2,1)S(1)} %get-tuple-element.462), channel_id=1, source_target_pairs={{0,2},{1,3},{2,0},{3,1},{4,6},{5,7},{6,4},{7,5},{8,10},{9,11},{10,... | collective-permute-start | bytes 1105928 | tf_op jit(solution)/shard_map/ppermute | solution.py:42
  567.9 48.5 %collective-permute-start.53 = (f32[144,2176]{1,0:T(8,128)S(1)}, f32[144,2176]{1,0:T(8,128)}, u32[]{:S(2)}, u32[]{:S(2)}) collective-permute-start(f32[144,2176]{1,0:T(8,128)S(1)} %convert_add_fusion), channel_id=1, source_target_pairs={{0,8},{8,0},{16,24},{24,16},{1,9},{9,1},{17,25},{25,17},{2,10},{10... | collective-permute-start | bytes 3760136 | tf_op jit(solution)/shard_map/ppermute | solution.py:42
  578.1 28.4 %collective-permute-start.49 = (bf16[144,640]{1,0:T(8,128)(2,1)S(1)}, bf16[144,640]{1,0:T(8,128)(2,1)}, u32[]{:S(2)}, u32[]{:S(2)}) collective-permute-start(bf16[144,640]{1,0:T(8,128)(2,1)S(1)} %add_convert_fusion.10), channel_id=1, source_target_pairs={{0,16},{8,24},{16,0},{24,8},{1,17},{9,25},{17,1},{25,9},{2,18},{10... | collective-permute-start | bytes 552968 | tf_op jit(solution)/shard_map/ppermute | solution.py:42
  (72 other events, 999.5 us)
Sparse Core Ops, SparseCore 0:
  267.0 98.4 reduce-scatter.3
  369.5 103.7 reduce-scatter.5
  529.1 74.6 reduce-scatter.7

commit v7 on v6

--- a/solution.py
+++ b/solution.py
@@ -1172,7 +1172,6 @@
     if staged:
         w_kv, incoming = flights.land(w_kv, incoming)
         h[zz | y], h[zz | z] = over(h[zz], y), over(h[zz], z)
-    incoming_near = jnp.concatenate([incoming, incoming_pair[0]], axis=0)
     far_in, w_kv = chain(normed_far, w_kv)
     (far,) = rows_matmul(
         "far", [far_in], [w_kv], with_bias, [bias_kv], [like(normed_far.shape[0], 2 * padded)]
@@ -1204,6 +1203,8 @@
         d[zz | z], d[z | y] = over(d[zz], z), over(d[z], y)
     w_out_mine, w_hidden = flights.land(w_out_mine, w_hidden, only=[other_half, w_out_other])
     w_out = chain.done(both_cores(core_flag, w_out_mine, w_out_other[0], out_cut, width))
+    w_out, incoming_pair[0] = chain(w_out, incoming_pair[0])
+    incoming_near = chain.done(jnp.concatenate([incoming, incoming_pair[0]], axis=0))
     if staged:
         w_out = flights.land(w_out, only=[d[zz | z], d[z | y]])
         d[zz | y], d[zz | z | y] = over(d[zz], y), over(d[zz | z], y)
@@ -1290,6 +1291,7 @@
         query = flights.land(query)
         if row == 0:
             out_sum = chain.done(*add_rows(out_mine, out_back[0]))
+            part_out = lax.psum_scatter(out_sum, "fsdp", scatter_dimension=0, tiled=True)
         if row == 1:
             part_down = chain(part_down)
             down_seq = flights.send(part_down, "seq", top)
@@ -1310,49 +1312,39 @@
     )
     dq = flights.land(dq)
     kv_box = flights.send(kv_send, "fsdp", y)
-    cut_rows = flat - tokens
-    far_sums = {
-        j: [add_rows(far_parts[j][part], far_sent[j | 1][0][part])[0] for part in (slice(0, cut_rows), slice(cut_rows, flat))]
-        for j in far_parts
-        if not j & 1
-    }
-    chain.done(*[part for parts in far_sums.values() for part in parts])
+    far_sums = {j: add_rows(far_parts[j], far_sent[j | 1][0])[0] for j in far_parts if not j & 1}
+    chain.done(*far_sums.values())
     arrived = []
     for bit in bits_of(seq_count)[:-1]:
         for j in [j for j in far_sums if j & bit]:
-            parts = far_sums.pop(j)
+            part = far_sums.pop(j)
             if j == bit:
-                arrived.append([flights.send(parts[0], "seq", bit), parts[1], bit])
+                arrived.append(flights.send(part, "seq", bit))
             else:
-                pairs = zip(far_sums[j ^ bit], parts)
-                far_sums[j ^ bit] = [add_rows(kept, swap(part, "seq", bit))[0] for kept, part in pairs]
+                (far_sums[j ^ bit],) = add_rows(far_sums[j ^ bit], swap(part, "seq", bit))
     dq, dnear = chain(dq, dnear)
     back_own, back_pair = chain.done(
         *rows_matmul("back_near", [dq, dnear], [w_q, w_kv], plain, [], [like(2 * flat, width)], NT, True)
     )
     pair_back = flights.send(back_pair, "seq", 1)
-    for entry in arrived:
-        entry[1] = flights.send(chain(entry[1]), "seq", entry[2])
-    normed_near, dq = chain(normed_near, dq)
-    q_keep, q_send, q_sums = chain.done(*weight_grad([normed_near], [dq], me, shards))
-    q_box = flights.send(q_send, "fsdp", y)
-    kv_bits, q_bits = list(far_bits), list(far_bits)
-    act = flights.land(act, only=[kv_box])
-    kv_keep, kv_box = next_step(kv_keep, kv_box, kv_bits)
-    act, middle = flights.land(act, middle, only=[entry[0] for entry in arrived])
+    act, middle = chain(act, middle)
     (down_pair,) = rows_matmul(
         "down_pair", [act], [w_down], plain, [], [like(flat, width)], NT, first_row=flat
     )
     chain.done(down_pair)
     down_back = flights.send(down_pair, "seq", 1)
-    late_in = flights.land(inputs, only=[pair_back, q_box] + [entry[1] for entry in arrived])
-    q_keep, q_box = next_step(q_keep, q_box, q_bits)
-    late_in = chain(late_in)
+    normed_near, dq = chain(normed_near, dq)
+    q_keep, q_send, q_sums = chain.done(*weight_grad([normed_near], [dq], me, shards))
+    q_box = flights.send(q_send, "fsdp", y)
+    kv_bits, q_bits = list(far_bits), list(far_bits)
+    act, late_in = flights.land(act, inputs, only=[kv_box] + arrived)
+    kv_keep, kv_box = next_step(kv_keep, kv_box, kv_bits)
+    late_in = flights.land(late_in, only=[pair_back])
     grad_patches, late = chain.done(
         *first_back(
             core_flag,
             late_in,
-            [back_own, pair_back[0]] + [(entry[0][0], entry[1][0]) for entry in arrived],
+            [back_own, pair_back[0]] + [box[0] for box in arrived],
             gain_one,
             grad_middle,
             q_sums,
@@ -1360,12 +1352,9 @@
             half,
         )
     )
-    out_sum = chain(out_sum)
-    part_out = lax.psum_scatter(out_sum, "fsdp", scatter_dimension=0, tiled=True)
     small = jnp.concatenate([lines, late], axis=0)
     small_todo = [zz, y, z] if staged else bits_of(shards)
     small_todo = [("fsdp", bit) for bit in small_todo] + [("seq", bit) for bit in reversed(bits_of(seq_count))]
-    small_box = None
 
     def small_send():
         return flights.send(small, *small_todo.pop(0)) if small_todo else None
@@ -1373,55 +1362,57 @@
     def small_step(small, box):
         return chain.done(*add_rows(small, box[0], F32))
 
-    small_box = small_send()
-    part_hidden = chain(part_hidden)
-    hidden_seq = flights.send(part_hidden, "seq", top)
-    act = flights.land(act, only=[kv_box, down_back])
-    if kv_box is not None:
-        kv_keep, kv_box = next_step(kv_keep, kv_box, kv_bits)
+    act, middle = flights.land(act, middle, only=[q_box, down_back])
+    q_keep, q_box = next_step(q_keep, q_box, q_bits)
     act, middle = chain(act, middle)
     (layer_output,) = rows_matmul(
         "down_own", [act], [w_down], layer_end, [middle, down_back[0], bias_down], [like(flat, width)], NT
     )
     layer_output = chain.done(layer_output).reshape(rows, tokens, width)
-    lands = [small_box, hidden_seq, q_box]
-    act = flights.land(act, only=lands)
+    boxes = [box for box in (kv_box, q_box) if box is not None]
+    flights.land(only=boxes)
+    if kv_box is not None:
+        kv_keep, kv_box = next_step(kv_keep, kv_box, kv_bits)
+    if q_box is not None:
+        q_keep, q_box = next_step(q_keep, q_box, q_bits)
+    small, part_hidden = chain(small, part_hidden)
+    hidden_seq = flights.send(part_hidden, "seq", top)
+    small_box = small_send()
+    while kv_box is not None:
+        flights.land(only=[kv_box])
+        kv_keep, kv_box = next_step(kv_keep, kv_box, kv_bits)
+    kv_seq = flights.send(kv_keep, "seq", top)
+    flights.land(only=[hidden_seq, small_box])
     small = small_step(small, small_box)
     small_box = small_send()
-    if q_box is not None:
-        q_keep, q_box = next_step(q_keep, q_box, q_bits)
     hidden_total = seq_rest(part_hidden, hidden_seq[0])
     hidden_other = flights.send(hidden_total, "seq", 1)
-    down_total = seq_rest(part_down, down_seq[0])
-    while kv_box is not None:
-        act = flights.land(act, only=[kv_box])
-        kv_keep, kv_box = next_step(kv_keep, kv_box, kv_bits)
-    kv_seq = flights.send(kv_keep, "seq", top)
-    act = flights.land(act, only=[small_box, hidden_other])
+    part_out = chain(part_out)
+    out_seq = flights.send(part_out, "seq", top)
+    while q_box is not None:
+        flights.land(only=[q_box])
+        q_keep, q_box = next_step(q_keep, q_box, q_bits)
+    q_seq = flights.send(q_keep, "seq", top)
+    flights.land(only=[small_box, kv_seq])
     small = small_step(small, small_box)
     small_box = small_send()
-    while q_box is not None:
-        act = flights.land(act, only=[q_box])
-        q_keep, q_box = next_step(q_keep, q_box, q_bits)
-    q_seq = flights.send(q_keep, "seq", top)
-    part_out = chain(part_out)
-    out_seq = flights.send(part_out, "seq", top)
-    act = flights.land(act, only=[kv_seq, small_box])
     kv_total = seq_rest(kv_keep, kv_seq[0])
+    kv_other = flights.send(kv_total, "seq", 1)
+    down_total = seq_rest(part_down, down_seq[0])
+    flights.land(only=[out_seq, hidden_other, small_box])
     small = small_step(small, small_box)
     small_box = small_send()
-    kv_other = flights.send(kv_total, "seq", 1)
+    out_total = seq_rest(part_out, out_seq[0])
+    out_other = flights.send(out_total, "seq", 1)
     down_other = flights.send(down_total, "seq", 1)
-    act = flights.land(act, only=[q_seq, out_seq, small_box])
-    small = small_step(small, small_box)
-    small_box = small_send()
+    flights.land(only=[q_seq, small_box])
     q_total = seq_rest(q_keep, q_seq[0])
-    out_total = seq_rest(part_out, out_seq[0])
-    q_other, out_other = flights.send(q_total, "seq", 1), flights.send(out_total, "seq", 1)
+    q_other = flights.send(q_total, "seq", 1)
     while small_box is not None:
-        act = flights.land(act)
         small = small_step(small, small_box)
         small_box = small_send()
+        if small_box is not None:
+            flights.land(only=[small_box])
     flights.land()
 
     own_lines = lax.dynamic_slice_in_dim(small[:8], me * shard_rows, shard_rows, 1)

time: 646 us -> 628 us (0.972)
  Pallas kernels: 347 us -> 336 us
  waiting for transfers between devices: 168 us -> 157 us
  other arithmetic: 33.9 us -> 26.8 us
    ppermute x57 -> x56, waiting for transfers between devices: 143 us -> 125 us  [swap(): return lax.ppermute(array, axis, [(i, i ^ bits) for i in range(size)])]
    pallas_call x3, Pallas kernels: 67.2 us -> 58.6 us  [attend_back(): pl.pallas_call(functools.partial(attend_back_kernel, row, heads, blocks,...]
    reduce_scatter x1, waiting for transfers between devices: 24.9 us -> 31.9 us  [local(): lax.psum_scatter(out_sum, 'fsdp', scatter_dimension=0, tiled=True)]
    ppermute x57 -> x56, starting transfers between devices: 45 us -> 51.4 us  [swap(): return lax.ppermute(array, axis, [(i, i ^ bits) for i in range(size)])]
  transfers between devices with their start and end apart: 60 -> 59, of which waited for: 23 -> 21; matrix products, arithmetic and copies ran while one was open for 7% -> 7% of each run, Pallas kernels for 52% -> 52%
where the time goes in v7:
time: 628 us; the launch traced here: 617 us
  Pallas kernels  336 us (54%)
  waiting for transfers between devices  157 us (25%)
  starting transfers between devices  51.7 us (8%)
  other arithmetic  26.8 us (4%)
  local copies, waits for them, and re-layouts  16.9 us (3%)
  between operations  14.5 us (2%)
  matrix products  14.3 us (2%)
    ppermute x56, waiting for transfers between devices, swap(): return lax.ppermute(array, axis, [(i, i ^ bits) for i in range(size)])  125 us
    pallas_call x9, Pallas kernels, rows_matmul(): pl.pallas_call(kernel, out_shape=shapes, grid=(steps,), in_specs=[pl.Bloc...  99.9 us
    pallas_call x3, Pallas kernels, attend_back(): pl.pallas_call(functools.partial(attend_back_kernel, row, heads, blocks,...  58.6 us
    ppermute x56, starting transfers between devices, swap(): return lax.ppermute(array, axis, [(i, i ^ bits) for i in range(size)])  51.4 us
    pallas_call x3, Pallas kernels, attend(): pl.pallas_call(functools.partial(attend_kernel, row, heads, blocks, padde...  34.6 us
    reduce_scatter x1, waiting for transfers between devices, local(): lax.psum_scatter(out_sum, 'fsdp', scatter_dimension=0, tiled=True)  31.9 us
    pallas_call x2, Pallas kernels, weight_grad(): pl.pallas_call(functools.partial(weight_grad_kernel, pairs, count, rows),...  25.4 us
    pallas_call x2, Pallas kernels, token_dot(): pl.pallas_call(kernel, out_shape=jax.ShapeDtypeStruct((width, cols), BF16...  20.9 us
  transfers between devices with their start and end apart: 59, of which 21 were waited for; matrix products, arithmetic and copies ran while one was open for 7% of the time, Pallas kernels for 52%

profile of v7, /device:TPU:0, one launch (start us, length us, event | category | flops | bytes accessed | tf_op | source)
XLA Modules:
  0.0 617.2 jit_solution(11551948257665010618)
XLA Ops:
  25.7 13.0 %collective-permute-done.2.refs_4_ = bf16[144,1920]{1,0:T(8,128)(2,1)} collective-permute-done((bf16[144,1920]{1,0:T(8,128)(2,1)}, bf16[144,1920]{1,0:T(8,128)(2,1)}, u32[]{:S(2)}, u32[]{:S(2)}) %collective-permute-start.2) | collective-permute-done | bytes 552992 | tf_op jit(solution)/shard_map/ppermute | solution.py:42
  44.0 11.3 %collective-permute-done.6.refs_6_ = bf16[144,1920]{1,0:T(8,128)(2,1)S(1)} collective-permute-done((bf16[144,1920]{1,0:T(8,128)(2,1)}, bf16[144,1920]{1,0:T(8,128)(2,1)S(1)}, u32[]{:S(2)}, u32[]{:S(2)}) %collective-permute-start.6) | collective-permute-done | bytes 552992 | tf_op jit(solution)/shard_map/ppermute | solution.py:42
  56.9 12.6 %collective-permute-done.3.refs_3_ = bf16[144,1920]{1,0:T(8,128)(2,1)S(1)} collective-permute-done((bf16[144,1920]{1,0:T(8,128)(2,1)}, bf16[144,1920]{1,0:T(8,128)(2,1)S(1)}, u32[]{:S(2)}, u32[]{:S(2)}) %collective-permute-start.3) | collective-permute-done | bytes 552992 | tf_op jit(solution)/shard_map/ppermute | solution.py:42
  69.5 10.7 %collective-permute-done.9.refs_7_ = bf16[144,1920]{1,0:T(8,128)(2,1)S(1)} collective-permute-done((bf16[144,1920]{1,0:T(8,128)(2,1)S(1)}, bf16[144,1920]{1,0:T(8,128)(2,1)S(1)}, u32[]{:S(2)}, u32[]{:S(2)}) %collective-permute-start.9) | collective-permute-done | bytes 552992 | tf_op jit(solution)/shard_map/ppermute | solution.py:42
  117.9 9.7 %near.1 = bf16[1536,1280]{1,0:T(8,128)(2,1)} custom-call(bf16[1536,1152]{1,0:T(8,128)(2,1)} %norm.2.refs_0_, bf16[1152,1280]{1,0:T(8,128)(2,1)} %get-tuple-element.397.refs_1_.refs_3_, f32[1,1280]{1,0:T(1,128)} %get-tuple-element.269.refs_2_), custom_call_target="tpu_custom_call" | custom-call | flops 1 | bytes 1 | tf_op jit(solution)/shard_map/near/pallas_call | solution.py:520
  143.3 9.7 %far.1 = bf16[1536,1280]{1,0:T(8,128)(2,1)} custom-call(bf16[1536,1152]{1,0:T(8,128)(2,1)} %norm.3.refs_0_.refs_1_, bf16[1152,1280]{1,0:T(8,128)(2,1)} %get-tuple-element.397.refs_1_.refs_3_, f32[1,1280]{1,0:T(1,128)} %get-tuple-element.269.refs_2_), custom_call_target="tpu_custom_call" | custom-call | flops 1 | bytes 1 | tf_op jit(solution)/shard_map/far/pallas_call | solution.py:520
  153.0 12.6 %attend.3 = (bf16[3,256,640]{2,1,0:T(8,128)(2,1)}, bf16[3,256,640]{2,1,0:T(8,128)(2,1)}, f32[3,8,512]{2,1,0:T(8,128)}) custom-call(s32[3,4]{1,0:T(4,128)} %get-tuple-element.243.need_ref, s32[3,512,1]{2,1,0:T(8,128)} %get-tuple-element.247.col_ref, s32[3,4,256]{2,1,0:T(4,128)} %get-tuple-element.244.row_ref, bf16[2,3,256,640]{3,2,1,0:T(8,128)(2,1)} %bitcast.51, ...), custom_call_target="tpu_custom_call" | custom-call | flops 1 | bytes 1 | tf_op jit(solution)/shard_map/attend/pallas_call | solution.py:908
  166.9 10.9 %attend.4 = (bf16[3,256,640]{2,1,0:T(8,128)(2,1)}, bf16[3,256,640]{2,1,0:T(8,128)(2,1)}, f32[3,8,512]{2,1,0:T(8,128)}) custom-call(s32[3,4]{1,0:T(4,128)} %get-tuple-element.243.need_ref, s32[3,512,1]{2,1,0:T(8,128)} %get-tuple-element.247.col_ref, ...), custom_call_target="tpu_custom_call", output_to_operand_aliasing={{0}: (6, {}), {1}: (7, {}), {2}: (8, {})} | custom-call | flops 1 | bytes 1 | tf_op jit(solution)/shard_map/attend/pallas_call | solution.py:908
  177.8 11.1 %attend.5 = (bf16[3,256,640]{2,1,0:T(8,128)(2,1)}, bf16[3,256,640]{2,1,0:T(8,128)(2,1)}, f32[3,8,512]{2,1,0:T(8,128)}) custom-call(s32[3,4]{1,0:T(4,128)} %get-tuple-element.243.need_ref, s32[3,512,1]{2,1,0:T(8,128)} %get-tuple-element.247.col_ref, ...), custom_call_target="tpu_custom_call", output_to_operand_aliasing={{0}: (6, {}), {1}: (7, {}), {2}: (8, {})} | custom-call | flops 1 | bytes 1 | tf_op jit(solution)/shard_map/attend/pallas_call | solution.py:908
  233.4 18.7 %hidden.1 = (bf16[1536,2176]{1,0:T(8,128)(2,1)}, bf16[1536,2176]{1,0:T(8,128)(2,1)}, bf16[1536,1152]{1,0:T(8,128)(2,1)}) custom-call(bf16[768,1152]{1,0:T(8,128)(2,1)} %get-tuple-element.331.refs_0_, bf16[768,1152]{1,0:T(8,128)(2,1)} %copy-done.11, bf16[1152,2176]{1,0:T(8,128)(2,1)} %get-tuple-element.333.refs_2_.refs_1_, f32[1,2176]{1,0:T(1,128)} %broadcast_select_fusion.refs_3_), custom_call_target="tpu_custom_call" | custom-call | flops 1 | bytes 1 | tf_op jit(solution)/shard_map/hidden/pallas_call | solution.py:792
  252.1 14.1 %token_dot.2 = bf16[1152,2176]{1,0:T(8,128)(2,1)} custom-call(bf16[1536,1152]{1,0:T(8,128)(2,1)} %copy-done.3, bf16[1536,2176]{1,0:T(8,128)(2,1)} %get-tuple-element.432.right_ref.refs_0_), custom_call_target="tpu_custom_call" | custom-call | flops 1 | bytes 1 | tf_op jit(solution)/shard_map/token_dot/pallas_call | solution.py:219
  272.3 14.6 %grad_pre.1 = (bf16[1536,2176]{1,0:T(8,128)(2,1)}, f32[1,2176]{1,0:T(1,128)}) custom-call(bf16[1536,1152]{1,0:T(8,128)(2,1)} %copy-done.3, bf16[1152,2176]{1,0:T(8,128)(2,1)} %assemble.5.refs_1_, bf16[1536,2176]{1,0:T(8,128)(2,1)} %get-tuple-element.348.refs_2_), custom_call_target="tpu_custom_call" | custom-call | flops 1 | bytes 1 | tf_op jit(solution)/shard_map/grad_pre/pallas_call | solution.py:520
  286.8 14.6 %back.1 = (bf16[768,1152]{1,0:T(8,128)(2,1)}, bf16[768,1152]{1,0:T(8,128)(2,1)}) custom-call(bf16[1536,2176]{1,0:T(8,128)(2,1)} %get-tuple-element.353.refs_0_, bf16[1152,2176]{1,0:T(8,128)(2,1)} %get-tuple-element.333.refs_2_.refs_1_), custom_call_target="tpu_custom_call" | custom-call | flops 1 | bytes 1 | tf_op jit(solution)/shard_map/back/pallas_call | solution.py:520
  301.7 14.3 %convolution_convert_fusion = bf16[1152,2176]{1,0:T(8,128)(2,1)} fusion(bf16[1536,1152]{1,0:T(8,128)(2,1)} %get-tuple-element.352, bf16[1536,2176]{1,0:T(8,128)(2,1)} %get-tuple-element.353.refs_0_), kind=kOutput, calls=%fused_computation.1 | convolution fusion | flops 7703248896 | bytes 15237120 | tf_op jit(solution)/shard_map/dot_general | solution.py:29
  317.2 12.3 %second_back.1 = (f32[768,1152]{1,0:T(8,128)}, bf16[768,1152]{1,0:T(8,128)(2,1)}, bf16[768,640]{1,0:T(8,128)(2,1)}, bf16[768,640]{1,0:T(8,128)(2,1)}, f32[8,1152]{1,0:T(8,128)}) custom-call(s32[1]{0:T(128)} %bitcast.core_ref, f32[768,1152]{1,0:T(8,128)} %get-tuple-element.433.x_ref.refs_2_, bf16[768,1152]{1,0:T(8,128)(2,1)} %get-tuple-element.354.refs_0_, ...), custom_call_target="tpu_custom_call" | custom-call | flops 1 | bytes 1 | tf_op jit(solution)/shard_map/second_back/pallas_call | solution.py:447
  345.9 21.9 %attend_back.3 = (bf16[2,3,256,640]{3,2,1,0:T(8,128)(2,1)}, bf16[2,3,256,1280]{3,2,1,0:T(8,128)(2,1)}, bf16[2,3,256,1280]{3,2,1,0:T(8,128)(2,1)}) custom-call(s32[3,4]{1,0:T(4,128)} %get-tuple-element.243.need_ref, s32[3,4,256,1]{3,2,1,0:T(8,128)} %get-tuple-element.245.col_ref, s32[3,1,512]{2,1,0:T(1,128)} %get-tuple-element.246.row_ref, ...), custom_call_target="tpu_custom_call" | custom-call | flops 1 | bytes 1 | tf_op jit(solution)/shard_map/attend_back/pallas_call | solution.py:1006
  369.4 18.3 %attend_back.4 = (bf16[2,3,256,640]{3,2,1,0:T(8,128)(2,1)}, bf16[2,3,256,1280]{3,2,1,0:T(8,128)(2,1)}, bf16[2,3,256,1280]{3,2,1,0:T(8,128)(2,1)}) custom-call(s32[3,4]{1,0:T(4,128)} %get-tuple-element.243.need_ref, s32[3,4,256,1]{3,2,1,0:T(8,128)} %get-tuple-element.245.col_ref, ...), custom_call_target="tpu_custom_call", output_to_operand_aliasing={{0}: (12, {}), {1}: (13, {}), {2}: (14, {})} | custom-call | flops 1 | bytes 1 | tf_op jit(solution)/shard_map/attend_back/pallas_call | solution.py:1006
  389.5 18.4 %attend_back.5 = (bf16[2,3,256,640]{3,2,1,0:T(8,128)(2,1)}, bf16[2,3,256,1280]{3,2,1,0:T(8,128)(2,1)}, bf16[2,3,256,1280]{3,2,1,0:T(8,128)(2,1)}) custom-call(s32[3,4]{1,0:T(4,128)} %get-tuple-element.243.need_ref, s32[3,4,256,1]{3,2,1,0:T(8,128)} %get-tuple-element.245.col_ref, ...), custom_call_target="tpu_custom_call", output_to_operand_aliasing={{0}: (12, {}), {1}: (13, {}), {2}: (14, {})} | custom-call | flops 1 | bytes 1 | tf_op jit(solution)/shard_map/attend_back/pallas_call | solution.py:1006
  408.7 11.3 %back_far.1 = (bf16[768,1152]{1,0:T(8,128)(2,1)}, bf16[768,1152]{1,0:T(8,128)(2,1)}) custom-call(bf16[1536,1280]{1,0:T(8,128)(2,1)} %bitcast.59, bf16[1152,1280]{1,0:T(8,128)(2,1)} %get-tuple-element.397.refs_1_.refs_3_), custom_call_target="tpu_custom_call" | custom-call | flops 1 | bytes 1 | tf_op jit(solution)/shard_map/back_far/pallas_call | solution.py:520
  421.3 17.5 %weight_grad.2 = (bf16[576,1280]{1,0:T(8,128)(2,1)}, bf16[576,1280]{1,0:T(8,128)(2,1)}, f32[8,1280]{1,0:T(8,128)}) custom-call(s32[9]{0:T(128)} %pad_add_fusion.pos_ref, bf16[1536,1152]{1,0:T(8,128)(2,1)} %norm.2.refs_0_, bf16[1536,1152]{1,0:T(8,128)(2,1)} %norm.3.refs_0_.refs_1_, bf16[1536,1280]{1,0:T(8,128)(2,1)} %bitcast.57, bf16[1536,1280]{1,0:T(8,128)(2,1)} %bitcast.60), custom_call_target="tpu_custom_call" | custom-call | flops 1 | bytes 1 | tf_op jit(solution)/shard_map/weight_grad/pallas_call | solution.py:190
  443.6 13.6 %back_near.1 = (bf16[768,1152]{1,0:T(8,128)(2,1)}, bf16[768,1152]{1,0:T(8,128)(2,1)}) custom-call(bf16[1536,640]{1,0:T(8,128)(2,1)} %bitcast.62, bf16[1536,1280]{1,0:T(8,128)(2,1)} %bitcast.58, bf16[1152,640]{1,0:T(8,128)(2,1)} %get-tuple-element.276.weight_ref.refs_1_.refs_2_, bf16[1152,1280]{1,0:T(8,128)(2,1)} %get-tuple-element.397.refs_1_.refs_3_), custom_call_target="tpu_custom_call" | custom-call | flops 1 | bytes 1 | tf_op jit(solution)/shard_map/back_near/pallas_call | solution.py:520
  502.4 10.1 %down_own.1 = bf16[768,1152]{1,0:T(8,128)(2,1)} custom-call(bf16[1536,2176]{1,0:T(8,128)(2,1)} %get-tuple-element.432.right_ref.refs_0_, bf16[1152,2176]{1,0:T(8,128)(2,1)} %assemble.5.refs_1_, f32[768,1152]{1,0:T(8,128)} %get-tuple-element.433.x_ref.refs_2_, bf16[768,1152]{1,0:T(8,128)(2,1)} %copy-done.7, f32[1,1152]{1,0:T(1,128)} %get-tuple-element.480.refs_4_), custom_call_target="tpu_custom_call" | custom-call | flops 1 | bytes 1 | tf_op jit(solution)/shard_map/down_own/pallas_call | solution.py:520
  523.3 24.2 %collective-permute-done.42 = bf16[144,1280]{1,0:T(8,128)(2,1)S(1)} collective-permute-done((bf16[144,1280]{1,0:T(8,128)(2,1)S(1)}, bf16[144,1280]{1,0:T(8,128)(2,1)S(1)}, u32[]{:S(2)}, u32[]{:S(2)}) %collective-permute-start.42) | collective-permute-done | bytes 368672 | tf_op jit(solution)/shard_map/ppermute | solution.py:42
  553.1 31.9 %reduce-scatter.8.cloned.1.call-done = bf16[144,640]{1,0:T(8,128)(2,1)} async-done(((bf16[1152,640]{1,0:T(8,128)(2,1)}), bf16[144,640]{1,0:T(8,128)(2,1)}) %reduce-scatter.8.cloned.1.call-update) | async-done | bytes 184336 | tf_op jit(solution)/shard_map/reduce_scatter | solution.py:1294
  (250 shorter events, 245.2 us)
Async XLA Ops:
  7.2 380.5 %reduce-scatter.4.cloned.1.call-start = ((), (), s32[]{:S(2)}) async-start(), calls=%async_computation.3 | async-start | bytes 5640192 | tf_op jit(solution)/shard_map/reduce_scatter | solution.py:1236
  38.9 30.6 %collective-permute-start.5 = (bf16[768,1152]{1,0:T(8,128)(2,1)S(1)}, bf16[768,1152]{1,0:T(8,128)(2,1)S(1)}, u32[]{:S(2)}, u32[]{:S(2)}) collective-permute-start(bf16[768,1152]{1,0:T(8,128)(2,1)S(1)} %bitcast.67), channel_id=1, source_target_pairs={{0,8},{8,0},{16,24},{24,16},{1,9},{9,1},{17,25},{25,17},{2,10},{10... | collective-permute-start | bytes 5308424 | tf_op jit(solution)/shard_map/ppermute | solution.py:42
  38.9 41.3 %collective-permute-start.8 = (bf16[768,1152]{1,0:T(8,128)(2,1)S(1)}, bf16[768,1152]{1,0:T(8,128)(2,1)}, u32[]{:S(2)}, u32[]{:S(2)}) collective-permute-start(bf16[768,1152]{1,0:T(8,128)(2,1)S(1)} %bitcast.68), channel_id=1, source_target_pairs={{0,16},{8,24},{16,0},{24,8},{1,17},{9,25},{17,1},{25,9},{2,18},{10... | collective-permute-start | bytes 5308424 | tf_op jit(solution)/shard_map/ppermute | solution.py:42
  80.3 53.9 %collective-permute-start.15 = (bf16[768,1152]{1,0:T(8,128)(2,1)S(1)}, bf16[768,1152]{1,0:T(8,128)(2,1)S(1)}, u32[]{:S(2)}, u32[]{:S(2)}) collective-permute-start(bf16[768,1152]{1,0:T(8,128)(2,1)S(1)} %bitcast.78), channel_id=1, source_target_pairs={{0,8},{8,0},{16,24},{24,16},{1,9},{9,1},{17,25},{25,17},{2,10},{10... | collective-permute-start | bytes 5308424 | tf_op jit(solution)/shard_map/ppermute | solution.py:42
  82.7 58.7 %collective-permute-start.7 = (bf16[144,2816]{1,0:T(8,128)(2,1)}, bf16[144,2816]{1,0:T(8,128)(2,1)}, u32[]{:S(2)}, u32[]{:S(2)}) collective-permute-start(bf16[144,2816]{1,0:T(8,128)(2,1)} %get-tuple-element.256.refs_0_), channel_id=1, source_target_pairs={{0,1},{1,0},{2,3},{3,2},{4,5},{5,4},{6,7},{7,6},{8,9},{9,8},{10,11... | collective-permute-start | bytes 2433032 | tf_op jit(solution)/shard_map/ppermute | solution.py:42
  93.1 48.3 %collective-permute-start.10 = (bf16[144,2816]{1,0:T(8,128)(2,1)}, bf16[144,2816]{1,0:T(8,128)(2,1)}, u32[]{:S(2)}, u32[]{:S(2)}) collective-permute-start(bf16[144,2816]{1,0:T(8,128)(2,1)} %get-tuple-element.256.refs_0_), channel_id=1, source_target_pairs={{0,4},{1,5},{2,6},{3,7},{4,0},{5,1},{6,2},{7,3},{8,12},{9,13},{10,... | collective-permute-start | bytes 2433032 | tf_op jit(solution)/shard_map/ppermute | solution.py:42
  107.8 33.5 %collective-permute-start.14 = (bf16[144,2816]{1,0:T(8,128)(2,1)}, bf16[144,2816]{1,0:T(8,128)(2,1)}, u32[]{:S(2)}, u32[]{:S(2)}) collective-permute-start(bf16[144,2816]{1,0:T(8,128)(2,1)} %collective-permute-done.12.refs_2_), channel_id=1, source_target_pairs={{0,1},{1,0},{2,3},{3,2},{4,5},{5,4},{6,7},{7,6},{8,9},{9,8},{10,11... | collective-permute-start | bytes 2433032 | tf_op jit(solution)/shard_map/ppermute | solution.py:42
  110.4 31.0 %collective-permute-start.11 = (bf16[144,2176]{1,0:T(8,128)(2,1)}, bf16[144,2176]{1,0:T(8,128)(2,1)}, u32[]{:S(2)}, u32[]{:S(2)}) collective-permute-start(bf16[144,2176]{1,0:T(8,128)(2,1)} %get-tuple-element.257.refs_0_), channel_id=1, source_target_pairs={{0,1},{1,0},{2,3},{3,2},{4,5},{5,4},{6,7},{7,6},{8,9},{9,8},{10,11... | collective-permute-start | bytes 1880072 | tf_op jit(solution)/shard_map/ppermute | solution.py:42
  228.3 37.8 %collective-permute-start.26 = (bf16[144,2176]{1,0:T(8,128)(2,1)}, bf16[144,2176]{1,0:T(8,128)(2,1)S(1)}, u32[]{:S(2)}, u32[]{:S(2)}) collective-permute-start(bf16[144,2176]{1,0:T(8,128)(2,1)} %collective-permute-done.20.refs_4_), channel_id=1, source_target_pairs={{0,1},{1,0},{2,3},{3,2},{4,5},{5,4},{6,7},{7,6},{8,9},{9,8},{10,11... | collective-permute-start | bytes 1880072 | tf_op jit(solution)/shard_map/ppermute | solution.py:42
  228.9 37.2 %collective-permute-start.27 = (bf16[144,2176]{1,0:T(8,128)(2,1)}, bf16[144,2176]{1,0:T(8,128)(2,1)S(1)}, u32[]{:S(2)}, u32[]{:S(2)}) collective-permute-start(bf16[144,2176]{1,0:T(8,128)(2,1)} %collective-permute-done.23.refs_6_), channel_id=1, source_target_pairs={{0,1},{1,0},{2,3},{3,2},{4,5},{5,4},{6,7},{7,6},{8,9},{9,8},{10,11... | collective-permute-start | bytes 1880072 | tf_op jit(solution)/shard_map/ppermute | solution.py:42
  267.2 250.7 %reduce-scatter.6.cloned.1.call-start = ((), (), s32[]{:S(2)}) async-start(), calls=%async_computation.4 | async-start | bytes 5640192 | tf_op jit(solution)/shard_map/reduce_scatter | solution.py:1256
  315.9 269.1 %reduce-scatter.8.cloned.1.call-start = ((), (), s32[]{:S(2)}) async-start(), calls=%async_computation.5 | async-start | bytes 1658880 | tf_op jit(solution)/shard_map/reduce_scatter | solution.py:1294
  440.6 43.3 %collective-permute-start.36 = (bf16[768,1152]{1,0:T(8,128)(2,1)}, bf16[768,1152]{1,0:T(8,128)(2,1)}, u32[]{:S(2)}, u32[]{:S(2)}) collective-permute-start(bf16[768,1152]{1,0:T(8,128)(2,1)} %add_convert_fusion), channel_id=1, source_target_pairs={{0,16},{8,24},{16,0},{24,8},{1,17},{9,25},{17,1},{25,9},{2,18},{10... | collective-permute-start | bytes 5308424 | tf_op jit(solution)/shard_map/ppermute | solution.py:42
  443.6 40.3 %collective-permute-start.35 = (bf16[576,1280]{1,0:T(8,128)(2,1)}, bf16[576,1280]{1,0:T(8,128)(2,1)}, u32[]{:S(2)}, u32[]{:S(2)}) collective-permute-start(bf16[576,1280]{1,0:T(8,128)(2,1)} %get-tuple-element.405), channel_id=1, source_target_pairs={{0,1},{1,0},{2,3},{3,2},{4,5},{5,4},{6,7},{7,6},{8,9},{9,8},{10,11... | collective-permute-start | bytes 4423688 | tf_op jit(solution)/shard_map/ppermute | solution.py:42
  457.1 29.8 %collective-permute-start.37 = (bf16[768,1152]{1,0:T(8,128)(2,1)}, bf16[768,1152]{1,0:T(8,128)(2,1)}, u32[]{:S(2)}, u32[]{:S(2)}) collective-permute-start(bf16[768,1152]{1,0:T(8,128)(2,1)} %get-tuple-element.412), channel_id=1, source_target_pairs={{0,8},{8,0},{16,24},{24,16},{1,9},{9,1},{17,25},{25,17},{2,10},{10... | collective-permute-start | bytes 5308424 | tf_op jit(solution)/shard_map/ppermute | solution.py:42
  466.2 33.0 %collective-permute-start.33 = (bf16[768,1152]{1,0:T(8,128)(2,1)}, bf16[768,1152]{1,0:T(8,128)(2,1)S(1)}, u32[]{:S(2)}, u32[]{:S(2)}) collective-permute-start(bf16[768,1152]{1,0:T(8,128)(2,1)} %down_pair.1), channel_id=1, source_target_pairs={{0,8},{8,0},{16,24},{24,16},{1,9},{9,1},{17,25},{25,17},{2,10},{10... | collective-permute-start | bytes 5308424 | tf_op jit(solution)/shard_map/ppermute | solution.py:42
  517.0 30.5 %collective-permute-start.42 = (bf16[144,1280]{1,0:T(8,128)(2,1)S(1)}, bf16[144,1280]{1,0:T(8,128)(2,1)S(1)}, u32[]{:S(2)}, u32[]{:S(2)}) collective-permute-start(bf16[144,1280]{1,0:T(8,128)(2,1)S(1)} %add_convert_fusion.5), channel_id=1, source_target_pairs={{0,4},{1,5},{2,6},{3,7},{4,0},{5,1},{6,2},{7,3},{8,12},{9,13},{10,... | collective-permute-start | bytes 1105928 | tf_op jit(solution)/shard_map/ppermute | solution.py:42
  517.9 32.9 %collective-permute-start.40 = (bf16[144,2176]{1,0:T(8,128)(2,1)}, bf16[144,2176]{1,0:T(8,128)(2,1)}, u32[]{:S(2)}, u32[]{:S(2)}) collective-permute-start(bf16[144,2176]{1,0:T(8,128)(2,1)} %reduce-scatter.6.cloned.1.call-done), channel_id=1, source_target_pairs={{0,16},{8,24},{16,0},{24,8},{1,17},{9,25},{17,1},{25,9},{2,18},{10... | collective-permute-start | bytes 1880072 | tf_op jit(solution)/shard_map/ppermute | solution.py:42
  520.3 30.5 %collective-permute-start.41 = (f32[16,1152]{1,0:T(8,128)S(1)}, f32[16,1152]{1,0:T(8,128)S(1)}, u32[]{:S(2)}, u32[]{:S(2)}) collective-permute-start(f32[16,1152]{1,0:T(8,128)S(1)} %pad_maximum_fusion), channel_id=1, source_target_pairs={{0,4},{1,5},{2,6},{3,7},{4,0},{5,1},{6,2},{7,3},{8,12},{9,13},{10,... | collective-permute-start | bytes 221192 | tf_op jit(solution)/shard_map/ppermute | solution.py:42
  523.2 29.8 %collective-permute-start.45 = (bf16[144,640]{1,0:T(8,128)(2,1)}, bf16[144,640]{1,0:T(8,128)(2,1)S(1)}, u32[]{:S(2)}, u32[]{:S(2)}) collective-permute-start(bf16[144,640]{1,0:T(8,128)(2,1)} %get-tuple-element.468), channel_id=1, source_target_pairs={{0,4},{1,5},{2,6},{3,7},{4,0},{5,1},{6,2},{7,3},{8,12},{9,13},{10,... | collective-permute-start | bytes 552968 | tf_op jit(solution)/shard_map/ppermute | solution.py:42
  548.6 38.4 %collective-permute-start.43 = (bf16[144,1280]{1,0:T(8,128)(2,1)S(1)}, bf16[144,1280]{1,0:T(8,128)(2,1)}, u32[]{:S(2)}, u32[]{:S(2)}) collective-permute-start(bf16[144,1280]{1,0:T(8,128)(2,1)S(1)} %add_convert_fusion.4), channel_id=1, source_target_pairs={{0,16},{8,24},{16,0},{24,8},{1,17},{9,25},{17,1},{25,9},{2,18},{10... | collective-permute-start | bytes 1105928 | tf_op jit(solution)/shard_map/ppermute | solution.py:42
  552.0 41.7 %collective-permute-start.46 = (f32[144,2176]{1,0:T(8,128)S(1)}, f32[144,2176]{1,0:T(8,128)}, u32[]{:S(2)}, u32[]{:S(2)}) collective-permute-start(f32[144,2176]{1,0:T(8,128)S(1)} %convert_add_fusion.1), channel_id=1, source_target_pairs={{0,8},{8,0},{16,24},{24,16},{1,9},{9,1},{17,25},{25,17},{2,10},{10... | collective-permute-start | bytes 3760136 | tf_op jit(solution)/shard_map/ppermute | solution.py:42
  552.2 51.9 %collective-permute-start.54 = (f32[144,2176]{1,0:T(8,128)S(1)}, f32[144,2176]{1,0:T(8,128)}, u32[]{:S(2)}, u32[]{:S(2)}) collective-permute-start(f32[144,2176]{1,0:T(8,128)S(1)} %convert_add_fusion), channel_id=1, source_target_pairs={{0,8},{8,0},{16,24},{24,16},{1,9},{9,1},{17,25},{25,17},{2,10},{10... | collective-permute-start | bytes 3760136 | tf_op jit(solution)/shard_map/ppermute | solution.py:42
  552.8 33.7 %collective-permute-start.44 = (f32[16,1152]{1,0:T(8,128)S(1)}, f32[16,1152]{1,0:T(8,128)S(1)}, u32[]{:S(2)}, u32[]{:S(2)}) collective-permute-start(f32[16,1152]{1,0:T(8,128)S(1)} %add.114), channel_id=1, source_target_pairs={{0,1},{1,0},{2,3},{3,2},{4,5},{5,4},{6,7},{7,6},{8,9},{9,8},{10,11... | collective-permute-start | bytes 221192 | tf_op jit(solution)/shard_map/ppermute | solution.py:42
  (69 other events, 1016.8 us)
Sparse Core Ops, SparseCore 0:
  266.3 97.9 reduce-scatter.3
  368.4 103.8 reduce-scatter.5
  502.5 82.4 reduce-scatter.7

commit v8 on v7

--- a/solution.py
+++ b/solution.py
@@ -468,7 +468,7 @@
 
 def rows_matmul(name, lefts, weights, finish, extras, outs, dims=((1,), (0,)), split=False, first_row=0):
     rows = outs[0].shape[0]
-    block = row_block(rows)
+    block = 384 if split and rows % 768 == 0 else 512 if not split and rows % 512 == 0 else row_block(rows)
     steps = rows // block
     half = steps // 2
     count, terms = len(lefts), len(lefts) + len(weights)
@@ -1132,7 +1132,7 @@
         )
         h[0], d[0] = [shard_ho], [shard_down]
         far_pair = [flights.send(far_raw[0][0], "seq", 1)]
-        h[zz], d[y] = over(h[0], zz), over(d[0], y)
+        h[zz] = over(h[0], zz)
         w_q, w_kv = chain.done(*assemble({k: box[0] for k, box in q.items()}, me, padded))
         stacked, bias_q, bias_kv = chain.done(
             *lay_vectors(chain(core_flag), w_q, len(vectors), half, padded)
@@ -1186,7 +1186,7 @@
         if staged and row == 1:
             query = flights.land(query)
             h[zz | z | y] = over(h[zz | z], y)
-            d[z], d[zz] = over(d[0], z), over(d[0], zz)
+            d[y], d[z], d[zz] = over(d[0], y), over(d[0], z), over(d[0], zz)
         found = chain.done(*attend(row, query, near, far, need, seg_near_col, seg_rows, heads, found))
     out_own, out_pair, lse = found
     if staged:
@@ -1205,9 +1205,6 @@
     w_out = chain.done(both_cores(core_flag, w_out_mine, w_out_other[0], out_cut, width))
     w_out, incoming_pair[0] = chain(w_out, incoming_pair[0])
     incoming_near = chain.done(jnp.concatenate([incoming, incoming_pair[0]], axis=0))
-    if staged:
-        w_out = flights.land(w_out, only=[d[zz | z], d[z | y]])
-        d[zz | y], d[zz | z | y] = over(d[zz], y), over(d[zz | z], y)
     own_half, w_out = chain(out_own.reshape(flat, padded), w_out)
     attended, middle, second = chain.done(
         *join(
@@ -1222,7 +1219,11 @@
             half,
         )
     )
+    if staged:
+        second = flights.land(second, only=[d[zz | z], d[z | y]])
     second_pair = flights.send(second, "seq", 1)
+    if staged:
+        d[zz | y], d[zz | z | y] = over(d[zz], y), over(d[zz | z], y)
     second, w_hidden = flights.land(second, w_hidden, only=[second_pair])
     act, slope, second_near = chain.done(*hidden([second, second_pair[0]], w_hidden, bias_hidden))
 
@@ -1253,7 +1254,6 @@
     back_other = flights.send(back_pair, "seq", 1)
     second_near, grad_pre = chain(second_near, grad_pre)
     grad_hidden = chain.done(dot(second_near, grad_pre, TN).astype(BF16))
-    part_hidden = lax.psum_scatter(grad_hidden, "fsdp", scatter_dimension=0, tiled=True)
     back = flights.land(back)
     grad_middle, branch, grad_mine, grad_send, lines = second_back(
         core_flag, middle, [back, back_other[0]], gain_two, incoming, w_out, hidden_line, half, padded
@@ -1291,7 +1291,8 @@
         query = flights.land(query)
         if row == 0:
             out_sum = chain.done(*add_rows(out_mine, out_back[0]))
-            part_out = lax.psum_scatter(out_sum, "fsdp", scatter_dimension=0, tiled=True)
+            grad_ho = chain.done(jnp.concatenate([grad_hidden, out_sum], axis=1))
+            part_hidden = lax.psum_scatter(grad_ho, "fsdp", scatter_dimension=0, tiled=True)
         if row == 1:
             part_down = chain(part_down)
             down_seq = flights.send(part_down, "seq", top)
@@ -1387,8 +1388,6 @@
     small_box = small_send()
     hidden_total = seq_rest(part_hidden, hidden_seq[0])
     hidden_other = flights.send(hidden_total, "seq", 1)
-    part_out = chain(part_out)
-    out_seq = flights.send(part_out, "seq", top)
     while q_box is not None:
         flights.land(only=[q_box])
         q_keep, q_box = next_step(q_keep, q_box, q_bits)
@@ -1399,11 +1398,9 @@
     kv_total = seq_rest(kv_keep, kv_seq[0])
     kv_other = flights.send(kv_total, "seq", 1)
     down_total = seq_rest(part_down, down_seq[0])
-    flights.land(only=[out_seq, hidden_other, small_box])
+    flights.land(only=[hidden_other, small_box])
     small = small_step(small, small_box)
     small_box = small_send()
-    out_total = seq_rest(part_out, out_seq[0])
-    out_other = flights.send(out_total, "seq", 1)
     down_other = flights.send(down_total, "seq", 1)
     flights.land(only=[q_seq, small_box])
     q_total = seq_rest(q_keep, q_seq[0])
@@ -1421,7 +1418,7 @@
     full_bias = jnp.concatenate([small[4 + i, :size] for i, size in enumerate(cuts)])
     full_down = both_columns(is_first, down_total, down_other[0], ff_half, ff).T
     full_hidden = both_columns(is_first, hidden_total, hidden_other[0], ff_half, ff)
-    full_out = both_columns(is_first, out_total, out_other[0], out_cut, width)
+    full_out = both_columns(is_first, hidden_total, hidden_other[0], out_cut, width, ff_half)
     full_query = both_columns(is_first, q_total, q_other[0], half, width)
     full_key = both_columns(is_first, kv_total, kv_other[0], half, width)
     full_value = both_columns(is_first, kv_total, kv_other[0], half, width, padded)

time: 628 us -> 601 us (0.957)
  starting transfers between devices: 51.7 us -> 41.2 us
  waiting for transfers between devices: 157 us -> 148 us
  Pallas kernels: 336 us -> 329 us
    reduce_scatter x2 -> x1, waiting for transfers between devices: 31.9 us -> 0.01 us  [local(): lax.psum_scatter(grad_ho, 'fsdp', scatter_dimension=0, tiled=True)]
    ppermute x56 -> x54, waiting for transfers between devices: 125 us -> 148 us  [swap(): return lax.ppermute(array, axis, [(i, i ^ bits) for i in range(size)])]
    ppermute x56 -> x54, starting transfers between devices: 51.4 us -> 41 us  [swap(): return lax.ppermute(array, axis, [(i, i ^ bits) for i in range(size)])]
  transfers between devices with their start and end apart: 59 -> 56, of which waited for: 21 -> 21; matrix products, arithmetic and copies ran while one was open for 7% -> 7% of each run, Pallas kernels for 52% -> 54%
where the time goes in v8:
time: 601 us; the launch traced here: 592 us
  Pallas kernels  329 us (55%)
  waiting for transfers between devices  148 us (25%)
  starting transfers between devices  41.2 us (7%)
  other arithmetic  26.7 us (4%)
  local copies, waits for them, and re-layouts  18.5 us (3%)
  between operations  15 us (2%)
  matrix products  14.2 us (2%)
    ppermute x54, waiting for transfers between devices, swap(): return lax.ppermute(array, axis, [(i, i ^ bits) for i in range(size)])  148 us
    pallas_call x9, Pallas kernels, rows_matmul(): pl.pallas_call(kernel, out_shape=shapes, grid=(steps,), in_specs=[pl.Bloc...  96.6 us
    pallas_call x3, Pallas kernels, attend_back(): pl.pallas_call(functools.partial(attend_back_kernel, row, heads, blocks,...  54.9 us
    ppermute x54, starting transfers between devices, swap(): return lax.ppermute(array, axis, [(i, i ^ bits) for i in range(size)])  41 us
    pallas_call x3, Pallas kernels, attend(): pl.pallas_call(functools.partial(attend_kernel, row, heads, blocks, padde...  32.9 us
    pallas_call x2, Pallas kernels, weight_grad(): pl.pallas_call(functools.partial(weight_grad_kernel, pairs, count, rows),...  25.4 us
    pallas_call x2, Pallas kernels, token_dot(): pl.pallas_call(kernel, out_shape=jax.ShapeDtypeStruct((width, cols), BF16...  21 us
    pallas_call x1, Pallas kernels, hidden(): pl.pallas_call(kernel, out_shape=(jax.ShapeDtypeStruct((count * rows, col...  18.7 us
  transfers between devices with their start and end apart: 56, of which 21 were waited for; matrix products, arithmetic and copies ran while one was open for 7% of the time, Pallas kernels for 54%

profile of v8, /device:TPU:0, one launch (start us, length us, event | category | flops | bytes accessed | tf_op | source)
XLA Modules:
  0.0 592.2 jit_solution(5915448038887222718)
XLA Ops:
  25.8 13.1 %collective-permute-done.1.refs_2_ = bf16[144,1920]{1,0:T(8,128)(2,1)} collective-permute-done((bf16[144,1920]{1,0:T(8,128)(2,1)}, bf16[144,1920]{1,0:T(8,128)(2,1)}, u32[]{:S(2)}, u32[]{:S(2)}) %collective-permute-start.1) | collective-permute-done | bytes 552992 | tf_op jit(solution)/shard_map/ppermute | solution.py:42
  45.2 12.4 %collective-permute-done.6.refs_6_ = bf16[144,1920]{1,0:T(8,128)(2,1)S(1)} collective-permute-done((bf16[144,1920]{1,0:T(8,128)(2,1)}, bf16[144,1920]{1,0:T(8,128)(2,1)S(1)}, u32[]{:S(2)}, u32[]{:S(2)}) %collective-permute-start.6) | collective-permute-done | bytes 552992 | tf_op jit(solution)/shard_map/ppermute | solution.py:42
  58.2 12.5 %collective-permute-done.3.refs_3_ = bf16[144,1920]{1,0:T(8,128)(2,1)S(1)} collective-permute-done((bf16[144,1920]{1,0:T(8,128)(2,1)}, bf16[144,1920]{1,0:T(8,128)(2,1)S(1)}, u32[]{:S(2)}, u32[]{:S(2)}) %collective-permute-start.3) | collective-permute-done | bytes 552992 | tf_op jit(solution)/shard_map/ppermute | solution.py:42
  70.7 10.8 %collective-permute-done.9.refs_7_ = bf16[144,1920]{1,0:T(8,128)(2,1)S(1)} collective-permute-done((bf16[144,1920]{1,0:T(8,128)(2,1)S(1)}, bf16[144,1920]{1,0:T(8,128)(2,1)S(1)}, u32[]{:S(2)}, u32[]{:S(2)}) %collective-permute-start.9) | collective-permute-done | bytes 552992 | tf_op jit(solution)/shard_map/ppermute | solution.py:42
  102.5 17.4 %collective-permute-done.11.refs_2_ = bf16[144,2816]{1,0:T(8,128)(2,1)} collective-permute-done((bf16[144,2816]{1,0:T(8,128)(2,1)}, bf16[144,2816]{1,0:T(8,128)(2,1)}, u32[]{:S(2)}, u32[]{:S(2)}) %collective-permute-start.11) | collective-permute-done | bytes 811040 | tf_op jit(solution)/shard_map/ppermute | solution.py:42
  152.8 12.7 %attend.3 = (bf16[3,256,640]{2,1,0:T(8,128)(2,1)}, bf16[3,256,640]{2,1,0:T(8,128)(2,1)}, f32[3,8,512]{2,1,0:T(8,128)}) custom-call(s32[3,4]{1,0:T(4,128)} %get-tuple-element.240.need_ref, s32[3,512,1]{2,1,0:T(8,128)} %get-tuple-element.244.col_ref, s32[3,4,256]{2,1,0:T(4,128)} %get-tuple-element.241.row_ref, bf16[2,3,256,640]{3,2,1,0:T(8,128)(2,1)} %bitcast.49, ...), custom_call_target="tpu_custom_call" | custom-call | flops 1 | bytes 1 | tf_op jit(solution)/shard_map/attend/pallas_call | solution.py:908
  168.1 11.1 %attend.4 = (bf16[3,256,640]{2,1,0:T(8,128)(2,1)}, bf16[3,256,640]{2,1,0:T(8,128)(2,1)}, f32[3,8,512]{2,1,0:T(8,128)}) custom-call(s32[3,4]{1,0:T(4,128)} %get-tuple-element.240.need_ref, s32[3,512,1]{2,1,0:T(8,128)} %get-tuple-element.244.col_ref, ...), custom_call_target="tpu_custom_call", output_to_operand_aliasing={{0}: (6, {}), {1}: (7, {}), {2}: (8, {})} | custom-call | flops 1 | bytes 1 | tf_op jit(solution)/shard_map/attend/pallas_call | solution.py:908
  188.4 9.5 %collective-permute-done.18.refs_1_ = bf16[144,2176]{1,0:T(8,128)(2,1)} collective-permute-done((bf16[144,2176]{1,0:T(8,128)(2,1)S(1)}, bf16[144,2176]{1,0:T(8,128)(2,1)}, u32[]{:S(2)}, u32[]{:S(2)}) %collective-permute-start.18) | collective-permute-done | bytes 626720 | tf_op jit(solution)/shard_map/ppermute | solution.py:42
  217.0 9.4 %join.1 = (bf16[768,1152]{1,0:T(8,128)(2,1)}, f32[768,1152]{1,0:T(8,128)}, bf16[768,1152]{1,0:T(8,128)(2,1)}) custom-call(s32[1]{0:T(128)} %bitcast.core_ref, bf16[768,640]{1,0:T(8,128)(2,1)} %bitcast.59, bf16[768,640]{1,0:T(8,128)(2,1)} %bitcast.80, bf16[768,1152]{1,0:T(8,128)(2,1)} %bitcast.63, bf16[1152,1152]{1,0:T(8,128)(2,1)} %both_cores.1.w_ref.refs_4_, ...), custom_call_target="tpu_custom_call" | custom-call | flops 1 | bytes 1 | tf_op jit(solution)/shard_map/join/pallas_call | solution.py:304
  231.6 18.7 %hidden.1 = (bf16[1536,2176]{1,0:T(8,128)(2,1)}, bf16[1536,2176]{1,0:T(8,128)(2,1)}, bf16[1536,1152]{1,0:T(8,128)(2,1)}) custom-call(bf16[768,1152]{1,0:T(8,128)(2,1)} %get-tuple-element.328.refs_0_, bf16[768,1152]{1,0:T(8,128)(2,1)} %copy-done.11, bf16[1152,2176]{1,0:T(8,128)(2,1)} %get-tuple-element.330.refs_2_.refs_1_, f32[1,2176]{1,0:T(1,128)} %broadcast_select_fusion.refs_3_), custom_call_target="tpu_custom_call" | custom-call | flops 1 | bytes 1 | tf_op jit(solution)/shard_map/hidden/pallas_call | solution.py:792
  250.4 14.2 %token_dot.2 = bf16[1152,2176]{1,0:T(8,128)(2,1)} custom-call(bf16[1536,1152]{1,0:T(8,128)(2,1)} %copy-done.3, bf16[1536,2176]{1,0:T(8,128)(2,1)} %get-tuple-element.429.right_ref.refs_0_), custom_call_target="tpu_custom_call" | custom-call | flops 1 | bytes 1 | tf_op jit(solution)/shard_map/token_dot/pallas_call | solution.py:219
  270.7 14.6 %grad_pre.1 = (bf16[1536,2176]{1,0:T(8,128)(2,1)}, f32[1,2176]{1,0:T(1,128)}) custom-call(bf16[1536,1152]{1,0:T(8,128)(2,1)} %copy-done.3, bf16[1152,2176]{1,0:T(8,128)(2,1)} %assemble.5.refs_1_, bf16[1536,2176]{1,0:T(8,128)(2,1)} %get-tuple-element.345.refs_2_), custom_call_target="tpu_custom_call" | custom-call | flops 1 | bytes 1 | tf_op jit(solution)/shard_map/grad_pre/pallas_call | solution.py:520
  285.3 14.5 %back.1 = (bf16[768,1152]{1,0:T(8,128)(2,1)}, bf16[768,1152]{1,0:T(8,128)(2,1)}) custom-call(bf16[1536,2176]{1,0:T(8,128)(2,1)} %get-tuple-element.350.refs_0_, bf16[1152,2176]{1,0:T(8,128)(2,1)} %get-tuple-element.330.refs_2_.refs_1_), custom_call_target="tpu_custom_call" | custom-call | flops 1 | bytes 1 | tf_op jit(solution)/shard_map/back/pallas_call | solution.py:520
  300.0 14.2 %convolution_convert_fusion = bf16[1152,2176]{1,0:T(8,128)(2,1)} fusion(bf16[1536,1152]{1,0:T(8,128)(2,1)} %get-tuple-element.349, bf16[1536,2176]{1,0:T(8,128)(2,1)} %get-tuple-element.350.refs_0_), kind=kOutput, calls=%fused_computation.1 | convolution fusion | flops 7703248896 | bytes 15237120 | tf_op jit(solution)/shard_map/dot_general | solution.py:29
  315.4 12.7 %second_back.1 = (f32[768,1152]{1,0:T(8,128)}, bf16[768,1152]{1,0:T(8,128)(2,1)}, bf16[768,640]{1,0:T(8,128)(2,1)}, bf16[768,640]{1,0:T(8,128)(2,1)}, f32[8,1152]{1,0:T(8,128)}) custom-call(s32[1]{0:T(128)} %bitcast.core_ref, f32[768,1152]{1,0:T(8,128)} %get-tuple-element.430.x_ref.refs_2_, bf16[768,1152]{1,0:T(8,128)(2,1)} %get-tuple-element.351.refs_0_, ...), custom_call_target="tpu_custom_call" | custom-call | flops 1 | bytes 1 | tf_op jit(solution)/shard_map/second_back/pallas_call | solution.py:447
  344.3 21.8 %attend_back.3 = (bf16[2,3,256,640]{3,2,1,0:T(8,128)(2,1)}, bf16[2,3,256,1280]{3,2,1,0:T(8,128)(2,1)}, bf16[2,3,256,1280]{3,2,1,0:T(8,128)(2,1)}) custom-call(s32[3,4]{1,0:T(4,128)} %get-tuple-element.240.need_ref, s32[3,4,256,1]{3,2,1,0:T(8,128)} %get-tuple-element.242.col_ref, s32[3,1,512]{2,1,0:T(1,128)} %get-tuple-element.243.row_ref, ...), custom_call_target="tpu_custom_call" | custom-call | flops 1 | bytes 1 | tf_op jit(solution)/shard_map/attend_back/pallas_call | solution.py:1006
  372.1 18.4 %attend_back.4 = (bf16[2,3,256,640]{3,2,1,0:T(8,128)(2,1)}, bf16[2,3,256,1280]{3,2,1,0:T(8,128)(2,1)}, bf16[2,3,256,1280]{3,2,1,0:T(8,128)(2,1)}) custom-call(s32[3,4]{1,0:T(4,128)} %get-tuple-element.240.need_ref, s32[3,4,256,1]{3,2,1,0:T(8,128)} %get-tuple-element.242.col_ref, ...), custom_call_target="tpu_custom_call", output_to_operand_aliasing={{0}: (12, {}), {1}: (13, {}), {2}: (14, {})} | custom-call | flops 1 | bytes 1 | tf_op jit(solution)/shard_map/attend_back/pallas_call | solution.py:1006
  391.8 14.7 %attend_back.5 = (bf16[2,3,256,640]{3,2,1,0:T(8,128)(2,1)}, bf16[2,3,256,1280]{3,2,1,0:T(8,128)(2,1)}, bf16[2,3,256,1280]{3,2,1,0:T(8,128)(2,1)}) custom-call(s32[3,4]{1,0:T(4,128)} %get-tuple-element.240.need_ref, s32[3,4,256,1]{3,2,1,0:T(8,128)} %get-tuple-element.242.col_ref, ...), custom_call_target="tpu_custom_call", output_to_operand_aliasing={{0}: (12, {}), {1}: (13, {}), {2}: (14, {})} | custom-call | flops 1 | bytes 1 | tf_op jit(solution)/shard_map/attend_back/pallas_call | solution.py:1006
  408.0 10.7 %back_far.1 = (bf16[768,1152]{1,0:T(8,128)(2,1)}, bf16[768,1152]{1,0:T(8,128)(2,1)}) custom-call(bf16[1536,1280]{1,0:T(8,128)(2,1)} %bitcast.57, bf16[1152,1280]{1,0:T(8,128)(2,1)} %get-tuple-element.394.refs_1_.refs_3_), custom_call_target="tpu_custom_call" | custom-call | flops 1 | bytes 1 | tf_op jit(solution)/shard_map/back_far/pallas_call | solution.py:520
  420.0 17.5 %weight_grad.2 = (bf16[576,1280]{1,0:T(8,128)(2,1)}, bf16[576,1280]{1,0:T(8,128)(2,1)}, f32[8,1280]{1,0:T(8,128)}) custom-call(s32[9]{0:T(128)} %pad_add_fusion.pos_ref, bf16[1536,1152]{1,0:T(8,128)(2,1)} %norm.2.refs_0_, bf16[1536,1152]{1,0:T(8,128)(2,1)} %norm.3.refs_0_.refs_1_, bf16[1536,1280]{1,0:T(8,128)(2,1)} %bitcast.55, bf16[1536,1280]{1,0:T(8,128)(2,1)} %bitcast.58), custom_call_target="tpu_custom_call" | custom-call | flops 1 | bytes 1 | tf_op jit(solution)/shard_map/weight_grad/pallas_call | solution.py:190
  442.8 13.5 %back_near.1 = (bf16[768,1152]{1,0:T(8,128)(2,1)}, bf16[768,1152]{1,0:T(8,128)(2,1)}) custom-call(bf16[1536,640]{1,0:T(8,128)(2,1)} %bitcast.60, bf16[1536,1280]{1,0:T(8,128)(2,1)} %bitcast.56, bf16[1152,640]{1,0:T(8,128)(2,1)} %get-tuple-element.272.weight_ref.refs_1_.refs_2_, bf16[1152,1280]{1,0:T(8,128)(2,1)} %get-tuple-element.394.refs_1_.refs_3_), custom_call_target="tpu_custom_call" | custom-call | flops 1 | bytes 1 | tf_op jit(solution)/shard_map/back_near/pallas_call | solution.py:520
  473.7 17.8 %collective-permute-done.35 = bf16[576,1280]{1,0:T(8,128)(2,1)} collective-permute-done((bf16[576,1280]{1,0:T(8,128)(2,1)}, bf16[576,1280]{1,0:T(8,128)(2,1)}, u32[]{:S(2)}, u32[]{:S(2)}) %collective-permute-start.35) | collective-permute-done | bytes 1474592 | tf_op jit(solution)/shard_map/ppermute | solution.py:42
  510.9 10.2 %down_own.1 = bf16[768,1152]{1,0:T(8,128)(2,1)} custom-call(bf16[1536,2176]{1,0:T(8,128)(2,1)} %get-tuple-element.429.right_ref.refs_0_, bf16[1152,2176]{1,0:T(8,128)(2,1)} %assemble.5.refs_1_, f32[768,1152]{1,0:T(8,128)} %get-tuple-element.430.x_ref.refs_2_, bf16[768,1152]{1,0:T(8,128)(2,1)} %copy-done.8, f32[1,1152]{1,0:T(1,128)} %get-tuple-element.474.refs_4_), custom_call_target="tpu_custom_call" | custom-call | flops 1 | bytes 1 | tf_op jit(solution)/shard_map/down_own/pallas_call | solution.py:520
  533.8 13.2 %collective-permute-done.42 = bf16[144,1280]{1,0:T(8,128)(2,1)S(1)} collective-permute-done((bf16[144,1280]{1,0:T(8,128)(2,1)S(1)}, bf16[144,1280]{1,0:T(8,128)(2,1)S(1)}, u32[]{:S(2)}, u32[]{:S(2)}) %collective-permute-start.42) | collective-permute-done | bytes 368672 | tf_op jit(solution)/shard_map/ppermute | solution.py:42
  (252 shorter events, 241.4 us)
Async XLA Ops:
  7.2 383.3 %reduce-scatter.3.cloned.1.call-start = ((), (), s32[]{:S(2)}) async-start(), calls=%async_computation.2 | async-start | bytes 5640192 | tf_op jit(solution)/shard_map/reduce_scatter | solution.py:1237
  14.3 27.0 %collective-permute-start.2 = (bf16[144,1920]{1,0:T(8,128)(2,1)}, bf16[144,1920]{1,0:T(8,128)(2,1)}, u32[]{:S(2)}, u32[]{:S(2)}) collective-permute-start(bf16[144,1920]{1,0:T(8,128)(2,1)} %get-tuple-element.235.refs_0_), channel_id=1, source_target_pairs={{0,4},{1,5},{2,6},{3,7},{4,0},{5,1},{6,2},{7,3},{8,12},{9,13},{10,... | collective-permute-start | bytes 1658888 | tf_op jit(solution)/shard_map/ppermute | solution.py:42
  41.3 29.4 %collective-permute-start.5 = (bf16[768,1152]{1,0:T(8,128)(2,1)S(1)}, bf16[768,1152]{1,0:T(8,128)(2,1)S(1)}, u32[]{:S(2)}, u32[]{:S(2)}) collective-permute-start(bf16[768,1152]{1,0:T(8,128)(2,1)S(1)} %bitcast.65), channel_id=1, source_target_pairs={{0,8},{8,0},{16,24},{24,16},{1,9},{9,1},{17,25},{25,17},{2,10},{10... | collective-permute-start | bytes 5308424 | tf_op jit(solution)/shard_map/ppermute | solution.py:42
  41.3 41.1 %collective-permute-start.8 = (bf16[768,1152]{1,0:T(8,128)(2,1)S(1)}, bf16[768,1152]{1,0:T(8,128)(2,1)}, u32[]{:S(2)}, u32[]{:S(2)}) collective-permute-start(bf16[768,1152]{1,0:T(8,128)(2,1)S(1)} %bitcast.66), channel_id=1, source_target_pairs={{0,16},{8,24},{16,0},{24,8},{1,17},{9,25},{17,1},{25,9},{2,18},{10... | collective-permute-start | bytes 5308424 | tf_op jit(solution)/shard_map/ppermute | solution.py:42
  43.2 27.5 %collective-permute-start.4 = (bf16[144,1920]{1,0:T(8,128)(2,1)}, bf16[144,1920]{1,0:T(8,128)(2,1)S(1)}, u32[]{:S(2)}, u32[]{:S(2)}) collective-permute-start(bf16[144,1920]{1,0:T(8,128)(2,1)} %collective-permute-done.2.refs_4_), channel_id=1, source_target_pairs={{0,1},{1,0},{2,3},{3,2},{4,5},{5,4},{6,7},{7,6},{8,9},{9,8},{10,11... | collective-permute-start | bytes 1658888 | tf_op jit(solution)/shard_map/ppermute | solution.py:42
  82.4 37.5 %collective-permute-start.12 = (bf16[768,1152]{1,0:T(8,128)(2,1)}, bf16[768,1152]{1,0:T(8,128)(2,1)}, u32[]{:S(2)}, u32[]{:S(2)}) collective-permute-start(bf16[768,1152]{1,0:T(8,128)(2,1)} %collective-permute-done.8.refs_0_), channel_id=1, source_target_pairs={{0,8},{8,0},{16,24},{24,16},{1,9},{9,1},{17,25},{25,17},{2,10},{10... | collective-permute-start | bytes 5308424 | tf_op jit(solution)/shard_map/ppermute | solution.py:42
  82.4 59.4 %collective-permute-start.14 = (bf16[768,1152]{1,0:T(8,128)(2,1)S(1)}, bf16[768,1152]{1,0:T(8,128)(2,1)S(1)}, u32[]{:S(2)}, u32[]{:S(2)}) collective-permute-start(bf16[768,1152]{1,0:T(8,128)(2,1)S(1)} %bitcast.75), channel_id=1, source_target_pairs={{0,8},{8,0},{16,24},{24,16},{1,9},{9,1},{17,25},{25,17},{2,10},{10... | collective-permute-start | bytes 5308424 | tf_op jit(solution)/shard_map/ppermute | solution.py:42
  83.0 36.9 %collective-permute-start.11 = (bf16[144,2816]{1,0:T(8,128)(2,1)}, bf16[144,2816]{1,0:T(8,128)(2,1)}, u32[]{:S(2)}, u32[]{:S(2)}) collective-permute-start(bf16[144,2816]{1,0:T(8,128)(2,1)} %get-tuple-element.253.refs_0_), channel_id=1, source_target_pairs={{0,2},{1,3},{2,0},{3,1},{4,6},{5,7},{6,4},{7,5},{8,10},{9,11},{10,... | collective-permute-start | bytes 2433032 | tf_op jit(solution)/shard_map/ppermute | solution.py:42
  84.4 57.4 %collective-permute-start.7 = (bf16[144,2816]{1,0:T(8,128)(2,1)}, bf16[144,2816]{1,0:T(8,128)(2,1)}, u32[]{:S(2)}, u32[]{:S(2)}) collective-permute-start(bf16[144,2816]{1,0:T(8,128)(2,1)} %get-tuple-element.253.refs_0_), channel_id=1, source_target_pairs={{0,1},{1,0},{2,3},{3,2},{4,5},{5,4},{6,7},{7,6},{8,9},{9,8},{10,11... | collective-permute-start | bytes 2433032 | tf_op jit(solution)/shard_map/ppermute | solution.py:42
  84.9 56.9 %collective-permute-start.10 = (bf16[144,2816]{1,0:T(8,128)(2,1)}, bf16[144,2816]{1,0:T(8,128)(2,1)}, u32[]{:S(2)}, u32[]{:S(2)}) collective-permute-start(bf16[144,2816]{1,0:T(8,128)(2,1)} %get-tuple-element.253.refs_0_), channel_id=1, source_target_pairs={{0,4},{1,5},{2,6},{3,7},{4,0},{5,1},{6,2},{7,3},{8,12},{9,13},{10,... | collective-permute-start | bytes 2433032 | tf_op jit(solution)/shard_map/ppermute | solution.py:42
  165.5 32.4 %collective-permute-start.17 = (bf16[144,2816]{1,0:T(8,128)(2,1)}, bf16[144,2816]{1,0:T(8,128)(2,1)S(1)}, u32[]{:S(2)}, u32[]{:S(2)}) collective-permute-start(bf16[144,2816]{1,0:T(8,128)(2,1)} %collective-permute-done.16.refs_6_), channel_id=1, source_target_pairs={{0,1},{1,0},{2,3},{3,2},{4,5},{5,4},{6,7},{7,6},{8,9},{9,8},{10,11... | collective-permute-start | bytes 2433032 | tf_op jit(solution)/shard_map/ppermute | solution.py:42
  165.6 32.3 %collective-permute-start.18 = (bf16[144,2176]{1,0:T(8,128)(2,1)S(1)}, bf16[144,2176]{1,0:T(8,128)(2,1)}, u32[]{:S(2)}, u32[]{:S(2)}) collective-permute-start(bf16[144,2176]{1,0:T(8,128)(2,1)S(1)} %copy-done.21), channel_id=1, source_target_pairs={{0,1},{1,0},{2,3},{3,2},{4,5},{5,4},{6,7},{7,6},{8,9},{9,8},{10,11... | collective-permute-start | bytes 1880072 | tf_op jit(solution)/shard_map/ppermute | solution.py:42
  167.6 30.3 %collective-permute-start.19 = (bf16[144,2176]{1,0:T(8,128)(2,1)S(1)}, bf16[144,2176]{1,0:T(8,128)(2,1)}, u32[]{:S(2)}, u32[]{:S(2)}) collective-permute-start(bf16[144,2176]{1,0:T(8,128)(2,1)S(1)} %copy-done.21), channel_id=1, source_target_pairs={{0,2},{1,3},{2,0},{3,1},{4,6},{5,7},{6,4},{7,5},{8,10},{9,11},{10,... | collective-permute-start | bytes 1880072 | tf_op jit(solution)/shard_map/ppermute | solution.py:42
  167.9 29.9 %collective-permute-start.20 = (bf16[144,2176]{1,0:T(8,128)(2,1)S(1)}, bf16[144,2176]{1,0:T(8,128)(2,1)}, u32[]{:S(2)}, u32[]{:S(2)}) collective-permute-start(bf16[144,2176]{1,0:T(8,128)(2,1)S(1)} %copy-done.21), channel_id=1, source_target_pairs={{0,4},{1,5},{2,6},{3,7},{4,0},{5,1},{6,2},{7,3},{8,12},{9,13},{10,... | collective-permute-start | bytes 1880072 | tf_op jit(solution)/shard_map/ppermute | solution.py:42
  226.7 37.9 %collective-permute-start.26 = (bf16[144,2176]{1,0:T(8,128)(2,1)}, bf16[144,2176]{1,0:T(8,128)(2,1)S(1)}, u32[]{:S(2)}, u32[]{:S(2)}) collective-permute-start(bf16[144,2176]{1,0:T(8,128)(2,1)} %collective-permute-done.20.refs_4_), channel_id=1, source_target_pairs={{0,1},{1,0},{2,3},{3,2},{4,5},{5,4},{6,7},{7,6},{8,9},{9,8},{10,11... | collective-permute-start | bytes 1880072 | tf_op jit(solution)/shard_map/ppermute | solution.py:42
  227.0 37.5 %collective-permute-start.27 = (bf16[144,2176]{1,0:T(8,128)(2,1)}, bf16[144,2176]{1,0:T(8,128)(2,1)S(1)}, u32[]{:S(2)}, u32[]{:S(2)}) collective-permute-start(bf16[144,2176]{1,0:T(8,128)(2,1)} %collective-permute-done.23.refs_6_), channel_id=1, source_target_pairs={{0,1},{1,0},{2,3},{3,2},{4,5},{5,4},{6,7},{7,6},{8,9},{9,8},{10,11... | collective-permute-start | bytes 1880072 | tf_op jit(solution)/shard_map/ppermute | solution.py:42
  265.6 266.7 %reduce-scatter.5.cloned.1.call-start = ((), (), s32[]{:S(2)}) async-start(), calls=%async_computation.3 | async-start | bytes 7299072 | tf_op jit(solution)/shard_map/reduce_scatter | solution.py:1295
  338.6 27.5 %collective-permute-start.29 = (bf16[1152,640]{1,0:T(8,128)(2,1)}, bf16[1152,640]{1,0:T(8,128)(2,1)S(1)}, u32[]{:S(2)}, u32[]{:S(2)}) collective-permute-start(bf16[1152,640]{1,0:T(8,128)(2,1)} %get-tuple-element.358), channel_id=1, source_target_pairs={{0,8},{8,0},{16,24},{24,16},{1,9},{9,1},{17,25},{25,17},{2,10},{10... | collective-permute-start | bytes 4423688 | tf_op jit(solution)/shard_map/ppermute | solution.py:42
  439.3 52.2 %collective-permute-start.36 = (bf16[768,1152]{1,0:T(8,128)(2,1)}, bf16[768,1152]{1,0:T(8,128)(2,1)}, u32[]{:S(2)}, u32[]{:S(2)}) collective-permute-start(bf16[768,1152]{1,0:T(8,128)(2,1)} %add_convert_fusion), channel_id=1, source_target_pairs={{0,16},{8,24},{16,0},{24,8},{1,17},{9,25},{17,1},{25,9},{2,18},{10... | collective-permute-start | bytes 5308424 | tf_op jit(solution)/shard_map/ppermute | solution.py:42
  440.0 51.4 %collective-permute-start.35 = (bf16[576,1280]{1,0:T(8,128)(2,1)}, bf16[576,1280]{1,0:T(8,128)(2,1)}, u32[]{:S(2)}, u32[]{:S(2)}) collective-permute-start(bf16[576,1280]{1,0:T(8,128)(2,1)} %get-tuple-element.402), channel_id=1, source_target_pairs={{0,1},{1,0},{2,3},{3,2},{4,5},{5,4},{6,7},{7,6},{8,9},{9,8},{10,11... | collective-permute-start | bytes 4423688 | tf_op jit(solution)/shard_map/ppermute | solution.py:42
  456.4 39.2 %collective-permute-start.37 = (bf16[768,1152]{1,0:T(8,128)(2,1)}, bf16[768,1152]{1,0:T(8,128)(2,1)}, u32[]{:S(2)}, u32[]{:S(2)}) collective-permute-start(bf16[768,1152]{1,0:T(8,128)(2,1)} %get-tuple-element.409), channel_id=1, source_target_pairs={{0,8},{8,0},{16,24},{24,16},{1,9},{9,1},{17,25},{25,17},{2,10},{10... | collective-permute-start | bytes 5308424 | tf_op jit(solution)/shard_map/ppermute | solution.py:42
  465.1 42.1 %collective-permute-start.33 = (bf16[768,1152]{1,0:T(8,128)(2,1)}, bf16[768,1152]{1,0:T(8,128)(2,1)S(1)}, u32[]{:S(2)}, u32[]{:S(2)}) collective-permute-start(bf16[768,1152]{1,0:T(8,128)(2,1)} %down_pair.1), channel_id=1, source_target_pairs={{0,8},{8,0},{16,24},{24,16},{1,9},{9,1},{17,25},{25,17},{2,10},{10... | collective-permute-start | bytes 5308424 | tf_op jit(solution)/shard_map/ppermute | solution.py:42
  473.6 33.6 %collective-permute-start.34 = (bf16[576,640]{1,0:T(8,128)(2,1)}, bf16[576,640]{1,0:T(8,128)(2,1)}, u32[]{:S(2)}, u32[]{:S(2)}) collective-permute-start(bf16[576,640]{1,0:T(8,128)(2,1)} %get-tuple-element.413), channel_id=1, source_target_pairs={{0,1},{1,0},{2,3},{3,2},{4,5},{5,4},{6,7},{7,6},{8,9},{9,8},{10,11... | collective-permute-start | bytes 2211848 | tf_op jit(solution)/shard_map/ppermute | solution.py:42
  494.6 33.4 %collective-permute-start.38 = (bf16[288,1280]{1,0:T(8,128)(2,1)}, bf16[288,1280]{1,0:T(8,128)(2,1)S(1)}, u32[]{:S(2)}, u32[]{:S(2)}) collective-permute-start(bf16[288,1280]{1,0:T(8,128)(2,1)} %get-tuple-element.454), channel_id=1, source_target_pairs={{0,2},{1,3},{2,0},{3,1},{4,6},{5,7},{6,4},{7,5},{8,10},{9,11},{10,... | collective-permute-start | bytes 2211848 | tf_op jit(solution)/shard_map/ppermute | solution.py:42
  (70 other events, 786.8 us)
Sparse Core Ops, SparseCore 0:
  264.7 98.3 reduce-scatter.2
  372.2 138.0 reduce-scatter.4

commit v9 on v8

--- a/solution.py
+++ b/solution.py
@@ -1141,9 +1141,6 @@
         gain_one = chain(gain_one)
         normed_near = chain.done(norm([inputs, raw_pair[0]], gain_one, shift_one))
         bias_hidden = my_half(after(hidden_bias, gain_one).astype(F32)[None], ff_half, ff_half)
-        gain_one = flights.land(gain_one, only=[h[z], far_pair[0]])
-        h[z | y] = over(h[z], y)
-        incoming_pair = flights.send(incoming, "seq", 1)
     else:
         parts = gather_all(shard_qkv)
         shard_ho, shard_down = mlp_shards(core_flag, shard_out, hidden_weight, down_weight, ff_half)
@@ -1167,10 +1164,14 @@
     near_in = after(near_in, query)
     (near,) = rows_matmul("near", [near_in], [w_kv], with_bias, [bias_kv], [like(2 * flat, 2 * padded)])
     chain.done(query, near)
+    if staged:
+        gain_one = flights.land(gain_one, only=[h[z], far_pair[0]])
+        h[z | y] = over(h[z], y)
+        incoming_pair = flights.send(incoming, "seq", 1)
     gain_one, w_kv = chain(gain_one, w_kv)
     normed_far = chain.done(norm([box[0] for box in far_raw + far_pair], gain_one, shift_one))
     if staged:
-        w_kv, incoming = flights.land(w_kv, incoming)
+        w_kv = flights.land(w_kv, only=[h[y], h[zz]])
         h[zz | y], h[zz | z] = over(h[zz], y), over(h[zz], z)
     far_in, w_kv = chain(normed_far, w_kv)
     (far,) = rows_matmul(
@@ -1184,19 +1185,22 @@
     for row in range(rows):
         query, near, far = chain(query, near, far)
         if staged and row == 1:
-            query = flights.land(query)
+            query = flights.land(query, only=[h[zz | z]])
             h[zz | z | y] = over(h[zz | z], y)
             d[y], d[z], d[zz] = over(d[0], y), over(d[0], z), over(d[0], zz)
         found = chain.done(*attend(row, query, near, far, need, seg_near_col, seg_rows, heads, found))
     out_own, out_pair, lse = found
     if staged:
-        out_own, out_pair = flights.land(out_own, out_pair)
+        out_own, out_pair = flights.land(out_own, out_pair, only=[incoming_pair, *h.values()])
         h_parts = {k: box[0] for k, box in h.items()}
     else:
         out_own, out_pair = flights.land(out_own, out_pair)
         h_parts = gather_all(chain(shard_ho))
     w_out_mine, w_hidden = chain.done(*assemble(h_parts, me, out_cols))
-    out_pair, w_out_mine = chain(out_pair, w_out_mine)
+    if staged:
+        out_pair, w_out_mine = flights.land(out_pair, w_out_mine, only=[d[y], d[z], d[zz]])
+    else:
+        out_pair, w_out_mine = chain(out_pair, w_out_mine)
     other_half = flights.send(out_pair, "seq", 1)
     w_out_other = flights.send(w_out_mine, "seq", 1)
     if staged:
@@ -1379,32 +1383,33 @@
     small, part_hidden = chain(small, part_hidden)
     hidden_seq = flights.send(part_hidden, "seq", top)
     small_box = small_send()
-    while kv_box is not None:
-        flights.land(only=[kv_box])
-        kv_keep, kv_box = next_step(kv_keep, kv_box, kv_bits)
+    while kv_box is not None or q_box is not None:
+        flights.land(only=[box for box in (kv_box, q_box) if box is not None])
+        if kv_box is not None:
+            kv_keep, kv_box = next_step(kv_keep, kv_box, kv_bits)
+        if q_box is not None:
+            q_keep, q_box = next_step(q_keep, q_box, q_bits)
     kv_seq = flights.send(kv_keep, "seq", top)
+    q_seq = flights.send(q_keep, "seq", top)
     flights.land(only=[hidden_seq, small_box])
     small = small_step(small, small_box)
     small_box = small_send()
     hidden_total = seq_rest(part_hidden, hidden_seq[0])
     hidden_other = flights.send(hidden_total, "seq", 1)
-    while q_box is not None:
-        flights.land(only=[q_box])
-        q_keep, q_box = next_step(q_keep, q_box, q_bits)
-    q_seq = flights.send(q_keep, "seq", top)
     flights.land(only=[small_box, kv_seq])
     small = small_step(small, small_box)
     small_box = small_send()
     kv_total = seq_rest(kv_keep, kv_seq[0])
     kv_other = flights.send(kv_total, "seq", 1)
     down_total = seq_rest(part_down, down_seq[0])
-    flights.land(only=[hidden_other, small_box])
+    flights.land(only=[q_seq, hidden_other, small_box])
     small = small_step(small, small_box)
     small_box = small_send()
     down_other = flights.send(down_total, "seq", 1)
-    flights.land(only=[q_seq, small_box])
     q_total = seq_rest(q_keep, q_seq[0])
     q_other = flights.send(q_total, "seq", 1)
+    if small_box is not None:
+        flights.land(only=[small_box])
     while small_box is not None:
         small = small_step(small, small_box)
         small_box = small_send()

time: 601 us -> 602 us (level)
    unnamed x70 -> x59, local copies, waits for them, and re-layouts: 12.5 us -> 8.41 us
  transfers between devices with their start and end apart: 56 -> 56, of which waited for: 21 -> 23; matrix products, arithmetic and copies ran while one was open for 7% -> 8% of each run, Pallas kernels for 54% -> 55%
where the time goes in v9:
time: 602 us; the launch traced here: 592 us
  Pallas kernels  328 us (54%)
  waiting for transfers between devices  149 us (25%)
  starting transfers between devices  42.3 us (7%)
  other arithmetic  31 us (5%)
  between operations  15 us (2%)
  matrix products  14.2 us (2%)
  local copies, waits for them, and re-layouts  12.6 us (2%)
    ppermute x54, waiting for transfers between devices, swap(): return lax.ppermute(array, axis, [(i, i ^ bits) for i in range(size)])  149 us
    pallas_call x9, Pallas kernels, rows_matmul(): pl.pallas_call(kernel, out_shape=shapes, grid=(steps,), in_specs=[pl.Bloc...  97.1 us
    pallas_call x3, Pallas kernels, attend_back(): pl.pallas_call(functools.partial(attend_back_kernel, row, heads, blocks,...  54.9 us
    ppermute x54, starting transfers between devices, swap(): return lax.ppermute(array, axis, [(i, i ^ bits) for i in range(size)])  42.1 us
    pallas_call x3, Pallas kernels, attend(): pl.pallas_call(functools.partial(attend_kernel, row, heads, blocks, padde...  32.8 us
    pallas_call x2, Pallas kernels, weight_grad(): pl.pallas_call(functools.partial(weight_grad_kernel, pairs, count, rows),...  25.3 us
    pallas_call x2, Pallas kernels, token_dot(): pl.pallas_call(kernel, out_shape=jax.ShapeDtypeStruct((width, cols), BF16...  20.9 us
    pallas_call x1, Pallas kernels, hidden(): pl.pallas_call(kernel, out_shape=(jax.ShapeDtypeStruct((count * rows, col...  18.7 us
  transfers between devices with their start and end apart: 56, of which 23 were waited for; matrix products, arithmetic and copies ran while one was open for 8% of the time, Pallas kernels for 55%

profile of v9, /device:TPU:0, one launch (start us, length us, event | category | flops | bytes accessed | tf_op | source)
XLA Modules:
  0.0 592.2 jit_solution(11723413504680459146)
XLA Ops:
  25.8 13.1 %collective-permute-done.1.refs_2_ = bf16[144,1920]{1,0:T(8,128)(2,1)} collective-permute-done((bf16[144,1920]{1,0:T(8,128)(2,1)}, bf16[144,1920]{1,0:T(8,128)(2,1)}, u32[]{:S(2)}, u32[]{:S(2)}) %collective-permute-start.1) | collective-permute-done | bytes 552992 | tf_op jit(solution)/shard_map/ppermute | solution.py:42
  45.2 12.4 %collective-permute-done.4.refs_6_ = bf16[144,1920]{1,0:T(8,128)(2,1)S(1)} collective-permute-done((bf16[144,1920]{1,0:T(8,128)(2,1)}, bf16[144,1920]{1,0:T(8,128)(2,1)S(1)}, u32[]{:S(2)}, u32[]{:S(2)}) %collective-permute-start.4) | collective-permute-done | bytes 552992 | tf_op jit(solution)/shard_map/ppermute | solution.py:42
  58.2 12.5 %collective-permute-done.6.refs_3_ = bf16[144,1920]{1,0:T(8,128)(2,1)S(1)} collective-permute-done((bf16[144,1920]{1,0:T(8,128)(2,1)}, bf16[144,1920]{1,0:T(8,128)(2,1)S(1)}, u32[]{:S(2)}, u32[]{:S(2)}) %collective-permute-start.6) | collective-permute-done | bytes 552992 | tf_op jit(solution)/shard_map/ppermute | solution.py:42
  70.7 10.8 %collective-permute-done.5.refs_7_ = bf16[144,1920]{1,0:T(8,128)(2,1)S(1)} collective-permute-done((bf16[144,1920]{1,0:T(8,128)(2,1)S(1)}, bf16[144,1920]{1,0:T(8,128)(2,1)S(1)}, u32[]{:S(2)}, u32[]{:S(2)}) %collective-permute-start.5) | collective-permute-done | bytes 552992 | tf_op jit(solution)/shard_map/ppermute | solution.py:42
  108.4 8.9 %near.1 = bf16[1536,1280]{1,0:T(8,128)(2,1)} custom-call(bf16[1536,1152]{1,0:T(8,128)(2,1)} %norm.2.refs_0_, bf16[1152,1280]{1,0:T(8,128)(2,1)} %get-tuple-element.392.refs_1_.refs_3_, f32[1,1280]{1,0:T(1,128)} %get-tuple-element.264.refs_2_), custom_call_target="tpu_custom_call" | custom-call | flops 1 | bytes 1 | tf_op jit(solution)/shard_map/near/pallas_call | solution.py:520
  137.9 12.5 %attend.3 = (bf16[3,256,640]{2,1,0:T(8,128)(2,1)}, bf16[3,256,640]{2,1,0:T(8,128)(2,1)}, f32[3,8,512]{2,1,0:T(8,128)}) custom-call(s32[3,4]{1,0:T(4,128)} %get-tuple-element.239.need_ref, s32[3,512,1]{2,1,0:T(8,128)} %get-tuple-element.243.col_ref, s32[3,4,256]{2,1,0:T(4,128)} %get-tuple-element.240.row_ref, bf16[2,3,256,640]{3,2,1,0:T(8,128)(2,1)} %bitcast.49, ...), custom_call_target="tpu_custom_call" | custom-call | flops 1 | bytes 1 | tf_op jit(solution)/shard_map/attend/pallas_call | solution.py:908
  152.7 11.1 %attend.4 = (bf16[3,256,640]{2,1,0:T(8,128)(2,1)}, bf16[3,256,640]{2,1,0:T(8,128)(2,1)}, f32[3,8,512]{2,1,0:T(8,128)}) custom-call(s32[3,4]{1,0:T(4,128)} %get-tuple-element.239.need_ref, s32[3,512,1]{2,1,0:T(8,128)} %get-tuple-element.243.col_ref, ...), custom_call_target="tpu_custom_call", output_to_operand_aliasing={{0}: (6, {}), {1}: (7, {}), {2}: (8, {})} | custom-call | flops 1 | bytes 1 | tf_op jit(solution)/shard_map/attend/pallas_call | solution.py:908
  163.8 9.2 %attend.5 = (bf16[3,256,640]{2,1,0:T(8,128)(2,1)}, bf16[3,256,640]{2,1,0:T(8,128)(2,1)}, f32[3,8,512]{2,1,0:T(8,128)}) custom-call(s32[3,4]{1,0:T(4,128)} %get-tuple-element.239.need_ref, s32[3,512,1]{2,1,0:T(8,128)} %get-tuple-element.243.col_ref, ...), custom_call_target="tpu_custom_call", output_to_operand_aliasing={{0}: (6, {}), {1}: (7, {}), {2}: (8, {})} | custom-call | flops 1 | bytes 1 | tf_op jit(solution)/shard_map/attend/pallas_call | solution.py:908
  173.0 10.0 %collective-permute-done.20.refs_7_ = bf16[144,2816]{1,0:T(8,128)(2,1)} collective-permute-done((bf16[144,2816]{1,0:T(8,128)(2,1)}, bf16[144,2816]{1,0:T(8,128)(2,1)}, u32[]{:S(2)}, u32[]{:S(2)}) %collective-permute-start.20) | collective-permute-done | bytes 811040 | tf_op jit(solution)/shard_map/ppermute | solution.py:42
  221.4 18.7 %hidden.1 = (bf16[1536,2176]{1,0:T(8,128)(2,1)}, bf16[1536,2176]{1,0:T(8,128)(2,1)}, bf16[1536,1152]{1,0:T(8,128)(2,1)}) custom-call(bf16[768,1152]{1,0:T(8,128)(2,1)} %get-tuple-element.326.refs_0_, bf16[768,1152]{1,0:T(8,128)(2,1)} %copy-done.9, bf16[1152,2176]{1,0:T(8,128)(2,1)} %get-tuple-element.328.refs_2_.refs_1_, f32[1,2176]{1,0:T(1,128)} %broadcast_select_fusion.refs_3_), custom_call_target="tpu_custom_call" | custom-call | flops 1 | bytes 1 | tf_op jit(solution)/shard_map/hidden/pallas_call | solution.py:792
  240.1 14.1 %token_dot.2 = bf16[1152,2176]{1,0:T(8,128)(2,1)} custom-call(bf16[1536,1152]{1,0:T(8,128)(2,1)} %pad_maximum_fusion.1.left_ref.refs_0_, bf16[1536,2176]{1,0:T(8,128)(2,1)} %get-tuple-element.427.right_ref.refs_0_), custom_call_target="tpu_custom_call" | custom-call | flops 1 | bytes 1 | tf_op jit(solution)/shard_map/token_dot/pallas_call | solution.py:219
  260.3 14.6 %grad_pre.1 = (bf16[1536,2176]{1,0:T(8,128)(2,1)}, f32[1,2176]{1,0:T(1,128)}) custom-call(bf16[1536,1152]{1,0:T(8,128)(2,1)} %pad_maximum_fusion.1.left_ref.refs_0_, bf16[1152,2176]{1,0:T(8,128)(2,1)} %assemble.5.refs_1_, bf16[1536,2176]{1,0:T(8,128)(2,1)} %get-tuple-element.343.refs_2_), custom_call_target="tpu_custom_call" | custom-call | flops 1 | bytes 1 | tf_op jit(solution)/shard_map/grad_pre/pallas_call | solution.py:520
  274.9 14.5 %back.1 = (bf16[768,1152]{1,0:T(8,128)(2,1)}, bf16[768,1152]{1,0:T(8,128)(2,1)}) custom-call(bf16[1536,2176]{1,0:T(8,128)(2,1)} %get-tuple-element.348.refs_0_, bf16[1152,2176]{1,0:T(8,128)(2,1)} %get-tuple-element.328.refs_2_.refs_1_), custom_call_target="tpu_custom_call" | custom-call | flops 1 | bytes 1 | tf_op jit(solution)/shard_map/back/pallas_call | solution.py:520
  289.5 14.2 %convolution_convert_fusion = bf16[1152,2176]{1,0:T(8,128)(2,1)} fusion(bf16[1536,1152]{1,0:T(8,128)(2,1)} %get-tuple-element.347, bf16[1536,2176]{1,0:T(8,128)(2,1)} %get-tuple-element.348.refs_0_), kind=kOutput, calls=%fused_computation.1 | convolution fusion | flops 7703248896 | bytes 15237120 | tf_op jit(solution)/shard_map/dot_general | solution.py:29
  305.0 12.7 %second_back.1 = (f32[768,1152]{1,0:T(8,128)}, bf16[768,1152]{1,0:T(8,128)(2,1)}, bf16[768,640]{1,0:T(8,128)(2,1)}, bf16[768,640]{1,0:T(8,128)(2,1)}, f32[8,1152]{1,0:T(8,128)}) custom-call(s32[1]{0:T(128)} %bitcast.1.core_ref, f32[768,1152]{1,0:T(8,128)} %get-tuple-element.428.x_ref.refs_2_, bf16[768,1152]{1,0:T(8,128)(2,1)} %get-tuple-element.349.refs_0_, ...), custom_call_target="tpu_custom_call" | custom-call | flops 1 | bytes 1 | tf_op jit(solution)/shard_map/second_back/pallas_call | solution.py:447
  333.9 21.8 %attend_back.3 = (bf16[2,3,256,640]{3,2,1,0:T(8,128)(2,1)}, bf16[2,3,256,1280]{3,2,1,0:T(8,128)(2,1)}, bf16[2,3,256,1280]{3,2,1,0:T(8,128)(2,1)}) custom-call(s32[3,4]{1,0:T(4,128)} %get-tuple-element.239.need_ref, s32[3,4,256,1]{3,2,1,0:T(8,128)} %get-tuple-element.241.col_ref, s32[3,1,512]{2,1,0:T(1,128)} %get-tuple-element.242.row_ref, ...), custom_call_target="tpu_custom_call" | custom-call | flops 1 | bytes 1 | tf_op jit(solution)/shard_map/attend_back/pallas_call | solution.py:1006
  361.7 18.5 %attend_back.4 = (bf16[2,3,256,640]{3,2,1,0:T(8,128)(2,1)}, bf16[2,3,256,1280]{3,2,1,0:T(8,128)(2,1)}, bf16[2,3,256,1280]{3,2,1,0:T(8,128)(2,1)}) custom-call(s32[3,4]{1,0:T(4,128)} %get-tuple-element.239.need_ref, s32[3,4,256,1]{3,2,1,0:T(8,128)} %get-tuple-element.241.col_ref, ...), custom_call_target="tpu_custom_call", output_to_operand_aliasing={{0}: (12, {}), {1}: (13, {}), {2}: (14, {})} | custom-call | flops 1 | bytes 1 | tf_op jit(solution)/shard_map/attend_back/pallas_call | solution.py:1006
  384.9 14.7 %attend_back.5 = (bf16[2,3,256,640]{3,2,1,0:T(8,128)(2,1)}, bf16[2,3,256,1280]{3,2,1,0:T(8,128)(2,1)}, bf16[2,3,256,1280]{3,2,1,0:T(8,128)(2,1)}) custom-call(s32[3,4]{1,0:T(4,128)} %get-tuple-element.239.need_ref, s32[3,4,256,1]{3,2,1,0:T(8,128)} %get-tuple-element.241.col_ref, ...), custom_call_target="tpu_custom_call", output_to_operand_aliasing={{0}: (12, {}), {1}: (13, {}), {2}: (14, {})} | custom-call | flops 1 | bytes 1 | tf_op jit(solution)/shard_map/attend_back/pallas_call | solution.py:1006
  400.6 11.2 %back_far.1 = (bf16[768,1152]{1,0:T(8,128)(2,1)}, bf16[768,1152]{1,0:T(8,128)(2,1)}) custom-call(bf16[1536,1280]{1,0:T(8,128)(2,1)} %bitcast.57, bf16[1152,1280]{1,0:T(8,128)(2,1)} %get-tuple-element.392.refs_1_.refs_3_), custom_call_target="tpu_custom_call" | custom-call | flops 1 | bytes 1 | tf_op jit(solution)/shard_map/back_far/pallas_call | solution.py:520
  413.1 17.4 %weight_grad.2 = (bf16[576,1280]{1,0:T(8,128)(2,1)}, bf16[576,1280]{1,0:T(8,128)(2,1)}, f32[8,1280]{1,0:T(8,128)}) custom-call(s32[9]{0:T(128)} %pad_add_fusion.pos_ref, bf16[1536,1152]{1,0:T(8,128)(2,1)} %norm.2.refs_0_, bf16[1536,1152]{1,0:T(8,128)(2,1)} %norm.3.refs_0_.refs_1_, bf16[1536,1280]{1,0:T(8,128)(2,1)} %bitcast.55, bf16[1536,1280]{1,0:T(8,128)(2,1)} %bitcast.58), custom_call_target="tpu_custom_call" | custom-call | flops 1 | bytes 1 | tf_op jit(solution)/shard_map/weight_grad/pallas_call | solution.py:190
  432.7 13.5 %back_near.1 = (bf16[768,1152]{1,0:T(8,128)(2,1)}, bf16[768,1152]{1,0:T(8,128)(2,1)}) custom-call(bf16[1536,640]{1,0:T(8,128)(2,1)} %bitcast.60, bf16[1536,1280]{1,0:T(8,128)(2,1)} %bitcast.56, bf16[1152,640]{1,0:T(8,128)(2,1)} %get-tuple-element.268.weight_ref.refs_1_.refs_2_, bf16[1152,1280]{1,0:T(8,128)(2,1)} %get-tuple-element.392.refs_1_.refs_3_), custom_call_target="tpu_custom_call" | custom-call | flops 1 | bytes 1 | tf_op jit(solution)/shard_map/back_near/pallas_call | solution.py:520
  465.3 15.4 %collective-permute-done.35 = bf16[576,1280]{1,0:T(8,128)(2,1)} collective-permute-done((bf16[576,1280]{1,0:T(8,128)(2,1)}, bf16[576,1280]{1,0:T(8,128)(2,1)}, u32[]{:S(2)}, u32[]{:S(2)}) %collective-permute-start.35) | collective-permute-done | bytes 1474592 | tf_op jit(solution)/shard_map/ppermute | solution.py:42
  499.9 10.2 %down_own.1 = bf16[768,1152]{1,0:T(8,128)(2,1)} custom-call(bf16[1536,2176]{1,0:T(8,128)(2,1)} %get-tuple-element.427.right_ref.refs_0_, bf16[1152,2176]{1,0:T(8,128)(2,1)} %assemble.5.refs_1_, f32[768,1152]{1,0:T(8,128)} %get-tuple-element.428.x_ref.refs_2_, bf16[768,1152]{1,0:T(8,128)(2,1)} %copy-done.6, f32[1,1152]{1,0:T(1,128)} %get-tuple-element.472.refs_4_), custom_call_target="tpu_custom_call" | custom-call | flops 1 | bytes 1 | tf_op jit(solution)/shard_map/down_own/pallas_call | solution.py:520
  524.1 24.0 %collective-permute-done.43 = bf16[144,640]{1,0:T(8,128)(2,1)} collective-permute-done((bf16[144,640]{1,0:T(8,128)(2,1)}, bf16[144,640]{1,0:T(8,128)(2,1)}, u32[]{:S(2)}, u32[]{:S(2)}) %collective-permute-start.43) | collective-permute-done | bytes 184352 | tf_op jit(solution)/shard_map/ppermute | solution.py:42
  (241 shorter events, 241.1 us)
Async XLA Ops:
  7.2 372.9 %reduce-scatter.3.cloned.1.call-start = ((), (), s32[]{:S(2)}) async-start(), calls=%async_computation.2 | async-start | bytes 5640192 | tf_op jit(solution)/shard_map/reduce_scatter | solution.py:1241
  41.3 29.4 %collective-permute-start.8 = (bf16[768,1152]{1,0:T(8,128)(2,1)S(1)}, bf16[768,1152]{1,0:T(8,128)(2,1)S(1)}, u32[]{:S(2)}, u32[]{:S(2)}) collective-permute-start(bf16[768,1152]{1,0:T(8,128)(2,1)S(1)} %bitcast.65), channel_id=1, source_target_pairs={{0,8},{8,0},{16,24},{24,16},{1,9},{9,1},{17,25},{25,17},{2,10},{10... | collective-permute-start | bytes 5308424 | tf_op jit(solution)/shard_map/ppermute | solution.py:42
  41.3 41.1 %collective-permute-start.3 = (bf16[768,1152]{1,0:T(8,128)(2,1)S(1)}, bf16[768,1152]{1,0:T(8,128)(2,1)}, u32[]{:S(2)}, u32[]{:S(2)}) collective-permute-start(bf16[768,1152]{1,0:T(8,128)(2,1)S(1)} %bitcast.66), channel_id=1, source_target_pairs={{0,16},{8,24},{16,0},{24,8},{1,17},{9,25},{17,1},{25,9},{2,18},{10... | collective-permute-start | bytes 5308424 | tf_op jit(solution)/shard_map/ppermute | solution.py:42
  43.2 27.5 %collective-permute-start.7 = (bf16[144,1920]{1,0:T(8,128)(2,1)}, bf16[144,1920]{1,0:T(8,128)(2,1)S(1)}, u32[]{:S(2)}, u32[]{:S(2)}) collective-permute-start(bf16[144,1920]{1,0:T(8,128)(2,1)} %collective-permute-done.2.refs_4_), channel_id=1, source_target_pairs={{0,1},{1,0},{2,3},{3,2},{4,5},{5,4},{6,7},{7,6},{8,9},{9,8},{10,11... | collective-permute-start | bytes 1658888 | tf_op jit(solution)/shard_map/ppermute | solution.py:42
  82.4 37.8 %collective-permute-start.13 = (bf16[768,1152]{1,0:T(8,128)(2,1)}, bf16[768,1152]{1,0:T(8,128)(2,1)}, u32[]{:S(2)}, u32[]{:S(2)}) collective-permute-start(bf16[768,1152]{1,0:T(8,128)(2,1)} %collective-permute-done.3.refs_0_), channel_id=1, source_target_pairs={{0,8},{8,0},{16,24},{24,16},{1,9},{9,1},{17,25},{25,17},{2,10},{10... | collective-permute-start | bytes 5308424 | tf_op jit(solution)/shard_map/ppermute | solution.py:42
  82.4 37.8 %collective-permute-start.12 = (bf16[144,2816]{1,0:T(8,128)(2,1)}, bf16[144,2816]{1,0:T(8,128)(2,1)}, u32[]{:S(2)}, u32[]{:S(2)}) collective-permute-start(bf16[144,2816]{1,0:T(8,128)(2,1)} %get-tuple-element.272.refs_0_), channel_id=1, source_target_pairs={{0,2},{1,3},{2,0},{3,1},{4,6},{5,7},{6,4},{7,5},{8,10},{9,11},{10,... | collective-permute-start | bytes 2433032 | tf_op jit(solution)/shard_map/ppermute | solution.py:42
  83.2 43.6 %collective-permute-start.16 = (bf16[144,2816]{1,0:T(8,128)(2,1)}, bf16[144,2816]{1,0:T(8,128)(2,1)}, u32[]{:S(2)}, u32[]{:S(2)}) collective-permute-start(bf16[144,2816]{1,0:T(8,128)(2,1)} %get-tuple-element.272.refs_0_), channel_id=1, source_target_pairs={{0,1},{1,0},{2,3},{3,2},{4,5},{5,4},{6,7},{7,6},{8,9},{9,8},{10,11... | collective-permute-start | bytes 2433032 | tf_op jit(solution)/shard_map/ppermute | solution.py:42
  83.7 43.1 %collective-permute-start.17 = (bf16[144,2816]{1,0:T(8,128)(2,1)}, bf16[144,2816]{1,0:T(8,128)(2,1)}, u32[]{:S(2)}, u32[]{:S(2)}) collective-permute-start(bf16[144,2816]{1,0:T(8,128)(2,1)} %get-tuple-element.272.refs_0_), channel_id=1, source_target_pairs={{0,4},{1,5},{2,6},{3,7},{4,0},{5,1},{6,2},{7,3},{8,12},{9,13},{10,... | collective-permute-start | bytes 2433032 | tf_op jit(solution)/shard_map/ppermute | solution.py:42
  86.0 66.4 %collective-permute-start.15 = (bf16[768,1152]{1,0:T(8,128)(2,1)S(1)}, bf16[768,1152]{1,0:T(8,128)(2,1)S(1)}, u32[]{:S(2)}, u32[]{:S(2)}) collective-permute-start(bf16[768,1152]{1,0:T(8,128)(2,1)S(1)} %bitcast.75), channel_id=1, source_target_pairs={{0,8},{8,0},{16,24},{24,16},{1,9},{9,1},{17,25},{25,17},{2,10},{10... | collective-permute-start | bytes 5308424 | tf_op jit(solution)/shard_map/ppermute | solution.py:42
  127.0 46.0 %collective-permute-start.18 = (bf16[144,2816]{1,0:T(8,128)(2,1)}, bf16[144,2816]{1,0:T(8,128)(2,1)}, u32[]{:S(2)}, u32[]{:S(2)}) collective-permute-start(bf16[144,2816]{1,0:T(8,128)(2,1)} %collective-permute-done.17.refs_4_), channel_id=1, source_target_pairs={{0,1},{1,0},{2,3},{3,2},{4,5},{5,4},{6,7},{7,6},{8,9},{9,8},{10,11... | collective-permute-start | bytes 2433032 | tf_op jit(solution)/shard_map/ppermute | solution.py:42
  150.4 32.6 %collective-permute-start.20 = (bf16[144,2816]{1,0:T(8,128)(2,1)}, bf16[144,2816]{1,0:T(8,128)(2,1)}, u32[]{:S(2)}, u32[]{:S(2)}) collective-permute-start(bf16[144,2816]{1,0:T(8,128)(2,1)} %collective-permute-done.19.refs_6_), channel_id=1, source_target_pairs={{0,1},{1,0},{2,3},{3,2},{4,5},{5,4},{6,7},{7,6},{8,9},{9,8},{10,11... | collective-permute-start | bytes 2433032 | tf_op jit(solution)/shard_map/ppermute | solution.py:42
  150.4 44.8 %collective-permute-start.9 = (bf16[144,2176]{1,0:T(8,128)(2,1)}, bf16[144,2176]{1,0:T(8,128)(2,1)}, u32[]{:S(2)}, u32[]{:S(2)}) collective-permute-start(bf16[144,2176]{1,0:T(8,128)(2,1)} %get-tuple-element.253.refs_0_), channel_id=1, source_target_pairs={{0,1},{1,0},{2,3},{3,2},{4,5},{5,4},{6,7},{7,6},{8,9},{9,8},{10,11... | collective-permute-start | bytes 1880072 | tf_op jit(solution)/shard_map/ppermute | solution.py:42
  152.4 42.8 %collective-permute-start.10 = (bf16[144,2176]{1,0:T(8,128)(2,1)}, bf16[144,2176]{1,0:T(8,128)(2,1)}, u32[]{:S(2)}, u32[]{:S(2)}) collective-permute-start(bf16[144,2176]{1,0:T(8,128)(2,1)} %get-tuple-element.253.refs_0_), channel_id=1, source_target_pairs={{0,2},{1,3},{2,0},{3,1},{4,6},{5,7},{6,4},{7,5},{8,10},{9,11},{10,... | collective-permute-start | bytes 1880072 | tf_op jit(solution)/shard_map/ppermute | solution.py:42
  152.4 42.7 %collective-permute-start.11 = (bf16[144,2176]{1,0:T(8,128)(2,1)}, bf16[144,2176]{1,0:T(8,128)(2,1)}, u32[]{:S(2)}, u32[]{:S(2)}) collective-permute-start(bf16[144,2176]{1,0:T(8,128)(2,1)} %get-tuple-element.253.refs_0_), channel_id=1, source_target_pairs={{0,4},{1,5},{2,6},{3,7},{4,0},{5,1},{6,2},{7,3},{8,12},{9,13},{10,... | collective-permute-start | bytes 1880072 | tf_op jit(solution)/shard_map/ppermute | solution.py:42
  216.4 37.8 %collective-permute-start.26 = (bf16[144,2176]{1,0:T(8,128)(2,1)}, bf16[144,2176]{1,0:T(8,128)(2,1)S(1)}, u32[]{:S(2)}, u32[]{:S(2)}) collective-permute-start(bf16[144,2176]{1,0:T(8,128)(2,1)} %collective-permute-done.11.refs_4_), channel_id=1, source_target_pairs={{0,1},{1,0},{2,3},{3,2},{4,5},{5,4},{6,7},{7,6},{8,9},{9,8},{10,11... | collective-permute-start | bytes 1880072 | tf_op jit(solution)/shard_map/ppermute | solution.py:42
  216.8 37.4 %collective-permute-start.27 = (bf16[144,2176]{1,0:T(8,128)(2,1)S(1)}, bf16[144,2176]{1,0:T(8,128)(2,1)}, u32[]{:S(2)}, u32[]{:S(2)}) collective-permute-start(bf16[144,2176]{1,0:T(8,128)(2,1)S(1)} %collective-permute-done.23.refs_6_), channel_id=1, source_target_pairs={{0,1},{1,0},{2,3},{3,2},{4,5},{5,4},{6,7},{7,6},{8,9},{9,8},{10,11... | collective-permute-start | bytes 1880072 | tf_op jit(solution)/shard_map/ppermute | solution.py:42
  255.1 263.8 %reduce-scatter.5.cloned.1.call-start = ((), (), s32[]{:S(2)}) async-start(), calls=%async_computation.3 | async-start | bytes 7299072 | tf_op jit(solution)/shard_map/reduce_scatter | solution.py:1299
  432.2 48.5 %collective-permute-start.36 = (bf16[768,1152]{1,0:T(8,128)(2,1)}, bf16[768,1152]{1,0:T(8,128)(2,1)}, u32[]{:S(2)}, u32[]{:S(2)}) collective-permute-start(bf16[768,1152]{1,0:T(8,128)(2,1)} %add_convert_fusion), channel_id=1, source_target_pairs={{0,16},{8,24},{16,0},{24,8},{1,17},{9,25},{17,1},{25,9},{2,18},{10... | collective-permute-start | bytes 5308424 | tf_op jit(solution)/shard_map/ppermute | solution.py:42
  432.7 48.0 %collective-permute-start.35 = (bf16[576,1280]{1,0:T(8,128)(2,1)}, bf16[576,1280]{1,0:T(8,128)(2,1)}, u32[]{:S(2)}, u32[]{:S(2)}) collective-permute-start(bf16[576,1280]{1,0:T(8,128)(2,1)} %get-tuple-element.400), channel_id=1, source_target_pairs={{0,1},{1,0},{2,3},{3,2},{4,5},{5,4},{6,7},{7,6},{8,9},{9,8},{10,11... | collective-permute-start | bytes 4423688 | tf_op jit(solution)/shard_map/ppermute | solution.py:42
  446.2 38.1 %collective-permute-start.37 = (bf16[768,1152]{1,0:T(8,128)(2,1)}, bf16[768,1152]{1,0:T(8,128)(2,1)}, u32[]{:S(2)}, u32[]{:S(2)}) collective-permute-start(bf16[768,1152]{1,0:T(8,128)(2,1)} %get-tuple-element.407), channel_id=1, source_target_pairs={{0,8},{8,0},{16,24},{24,16},{1,9},{9,1},{17,25},{25,17},{2,10},{10... | collective-permute-start | bytes 5308424 | tf_op jit(solution)/shard_map/ppermute | solution.py:42
  455.3 41.0 %collective-permute-start.33 = (bf16[768,1152]{1,0:T(8,128)(2,1)}, bf16[768,1152]{1,0:T(8,128)(2,1)S(1)}, u32[]{:S(2)}, u32[]{:S(2)}) collective-permute-start(bf16[768,1152]{1,0:T(8,128)(2,1)} %down_pair.1), channel_id=1, source_target_pairs={{0,8},{8,0},{16,24},{24,16},{1,9},{9,1},{17,25},{25,17},{2,10},{10... | collective-permute-start | bytes 5308424 | tf_op jit(solution)/shard_map/ppermute | solution.py:42
  463.4 32.8 %collective-permute-start.34 = (bf16[576,640]{1,0:T(8,128)(2,1)}, bf16[576,640]{1,0:T(8,128)(2,1)}, u32[]{:S(2)}, u32[]{:S(2)}) collective-permute-start(bf16[576,640]{1,0:T(8,128)(2,1)} %get-tuple-element.411), channel_id=1, source_target_pairs={{0,1},{1,0},{2,3},{3,2},{4,5},{5,4},{6,7},{7,6},{8,9},{9,8},{10,11... | collective-permute-start | bytes 2211848 | tf_op jit(solution)/shard_map/ppermute | solution.py:42
  483.8 33.2 %collective-permute-start.38 = (bf16[288,1280]{1,0:T(8,128)(2,1)}, bf16[288,1280]{1,0:T(8,128)(2,1)S(1)}, u32[]{:S(2)}, u32[]{:S(2)}) collective-permute-start(bf16[288,1280]{1,0:T(8,128)(2,1)} %get-tuple-element.452), channel_id=1, source_target_pairs={{0,2},{1,3},{2,0},{3,1},{4,6},{5,7},{6,4},{7,5},{8,10},{9,11},{10,... | collective-permute-start | bytes 2211848 | tf_op jit(solution)/shard_map/ppermute | solution.py:42
  518.9 35.3 %collective-permute-start.40 = (bf16[144,2816]{1,0:T(8,128)(2,1)}, bf16[144,2816]{1,0:T(8,128)(2,1)S(1)}, u32[]{:S(2)}, u32[]{:S(2)}) collective-permute-start(bf16[144,2816]{1,0:T(8,128)(2,1)} %reduce-scatter.5.cloned.1.call-done), channel_id=1, source_target_pairs={{0,16},{8,24},{16,0},{24,8},{1,17},{9,25},{17,1},{25,9},{2,18},{10... | collective-permute-start | bytes 2433032 | tf_op jit(solution)/shard_map/ppermute | solution.py:42
  (65 other events, 889.9 us)
Sparse Core Ops, SparseCore 0:
  254.4 98.3 reduce-scatter.2
  361.8 137.7 reduce-scatter.4

commit v10 on v9

--- a/solution.py
+++ b/solution.py
@@ -1111,6 +1111,7 @@
         q = {0: [shard_qkv]}
         q[y] = over(q[0], y)
         q[z], q[zz] = over(q[0], z), over(q[0], zz)
+        incoming_pair = flights.send(incoming, "seq", 1)
         shard_ho, shard_down = chain.done(
             *mlp_shards(core_flag, shard_out, hidden_weight, down_weight, ff_half)
         )
@@ -1122,8 +1123,9 @@
         q[zz | z], q[z | y], q[zz | y] = over(q[zz], z), over(q[z], y), over(q[zz], y)
         far_raw = [flights.send(raw_own, "seq", 2)]
         raw_pair = flights.send(raw_own, "seq", 1)
-        core_flag = flights.land(core_flag, only=[q[zz | z]])
+        core_flag, incoming_pair[0] = flights.land(core_flag, incoming_pair[0], only=[q[zz | z]])
         q[zz | z | y] = over(q[zz | z], y)
+        incoming_near = chain.done(jnp.concatenate([incoming, incoming_pair[0]], axis=0))
         core_flag, shard_ho = flights.land(core_flag, shard_ho, only=[q[z | y], q[zz | y], raw_pair])
         h[0] = [shard_ho]
         h[z], h[y] = over(h[0], z), over(h[0], y)
@@ -1153,7 +1155,7 @@
         gain_one, shift_one = stacked[0:1], stacked[1:2]
         normed_near = norm([raw[0], raw[1]], gain_one, shift_one)
         far_raw, far_pair = [[raw[j]] for j in range(2, seq_count)], []
-        incoming_pair = [swap(incoming, "seq", 1)]
+        incoming_near = jnp.concatenate([incoming, swap(incoming, "seq", 1)], axis=0)
         bias_hidden = my_half(hidden_bias.astype(F32)[None], ff_half, ff_half)
     _, _, bias_query, bias_value, bias_output, gain_two, shift_two, bias_down = [
         stacked[i : i + 1] for i in range(8)
@@ -1167,7 +1169,6 @@
     if staged:
         gain_one = flights.land(gain_one, only=[h[z], far_pair[0]])
         h[z | y] = over(h[z], y)
-        incoming_pair = flights.send(incoming, "seq", 1)
     gain_one, w_kv = chain(gain_one, w_kv)
     normed_far = chain.done(norm([box[0] for box in far_raw + far_pair], gain_one, shift_one))
     if staged:
@@ -1191,7 +1192,7 @@
         found = chain.done(*attend(row, query, near, far, need, seg_near_col, seg_rows, heads, found))
     out_own, out_pair, lse = found
     if staged:
-        out_own, out_pair = flights.land(out_own, out_pair, only=[incoming_pair, *h.values()])
+        out_own, out_pair = flights.land(out_own, out_pair, only=list(h.values()))
         h_parts = {k: box[0] for k, box in h.items()}
     else:
         out_own, out_pair = flights.land(out_own, out_pair)
@@ -1207,8 +1208,6 @@
         d[zz | z], d[z | y] = over(d[zz], z), over(d[z], y)
     w_out_mine, w_hidden = flights.land(w_out_mine, w_hidden, only=[other_half, w_out_other])
     w_out = chain.done(both_cores(core_flag, w_out_mine, w_out_other[0], out_cut, width))
-    w_out, incoming_pair[0] = chain(w_out, incoming_pair[0])
-    incoming_near = chain.done(jnp.concatenate([incoming, incoming_pair[0]], axis=0))
     own_half, w_out = chain(out_own.reshape(flat, padded), w_out)
     attended, middle, second = chain.done(
         *join(
@@ -1265,7 +1264,7 @@
     chain.done(branch, grad_send)
     grad_pair = flights.send(grad_send, "seq", 1)
     attended, branch = chain(attended, branch)
-    partial_out = chain(chain.done(token_dot(attended, branch)))
+    partial_out = flights.land(chain.done(token_dot(attended, branch)))
     out_mine, out_other = chain.done(*core_columns(core_flag, [partial_out], out_cols))
     query = flights.land(query)
 
@@ -1358,8 +1357,10 @@
         )
     )
     small = jnp.concatenate([lines, late], axis=0)
-    small_todo = [zz, y, z] if staged else bits_of(shards)
-    small_todo = [("fsdp", bit) for bit in small_todo] + [("seq", bit) for bit in reversed(bits_of(seq_count))]
+    if staged:
+        small_todo = [("fsdp", zz), ("fsdp", y), ("seq", top), ("fsdp", z), ("seq", 1)]
+    else:
+        small_todo = [("fsdp", bit) for bit in bits_of(shards)] + [("seq", bit) for bit in bits_of(seq_count)]
 
     def small_send():
         return flights.send(small, *small_todo.pop(0)) if small_todo else None
@@ -1367,54 +1368,46 @@
     def small_step(small, box):
         return chain.done(*add_rows(small, box[0], F32))
 
-    act, middle = flights.land(act, middle, only=[q_box, down_back])
+    act, middle, small = flights.land(act, middle, small, only=[q_box, down_back])
     q_keep, q_box = next_step(q_keep, q_box, q_bits)
+    small_box = small_send()
     act, middle = chain(act, middle)
     (layer_output,) = rows_matmul(
         "down_own", [act], [w_down], layer_end, [middle, down_back[0], bias_down], [like(flat, width)], NT
     )
     layer_output = chain.done(layer_output).reshape(rows, tokens, width)
-    boxes = [box for box in (kv_box, q_box) if box is not None]
-    flights.land(only=boxes)
-    if kv_box is not None:
-        kv_keep, kv_box = next_step(kv_keep, kv_box, kv_bits)
-    if q_box is not None:
-        q_keep, q_box = next_step(q_keep, q_box, q_bits)
-    small, part_hidden = chain(small, part_hidden)
-    hidden_seq = flights.send(part_hidden, "seq", top)
-    small_box = small_send()
-    while kv_box is not None or q_box is not None:
-        flights.land(only=[box for box in (kv_box, q_box) if box is not None])
+
+    def move_on(*also):
+        nonlocal small, small_box, kv_keep, kv_box, q_keep, q_box
+        flights.land(only=[box for box in (kv_box, q_box, small_box, *also) if box is not None])
         if kv_box is not None:
             kv_keep, kv_box = next_step(kv_keep, kv_box, kv_bits)
         if q_box is not None:
             q_keep, q_box = next_step(q_keep, q_box, q_bits)
+        if small_box is not None:
+            small = small_step(small, small_box)
+            small_box = small_send()
+
+    move_on()
+    part_hidden = chain(part_hidden)
+    hidden_seq = flights.send(part_hidden, "seq", top)
+    while kv_box is not None or q_box is not None:
+        move_on()
     kv_seq = flights.send(kv_keep, "seq", top)
     q_seq = flights.send(q_keep, "seq", top)
-    flights.land(only=[hidden_seq, small_box])
-    small = small_step(small, small_box)
-    small_box = small_send()
+    flights.land(only=[hidden_seq])
     hidden_total = seq_rest(part_hidden, hidden_seq[0])
     hidden_other = flights.send(hidden_total, "seq", 1)
-    flights.land(only=[small_box, kv_seq])
-    small = small_step(small, small_box)
-    small_box = small_send()
+    move_on(kv_seq, q_seq)
     kv_total = seq_rest(kv_keep, kv_seq[0])
     kv_other = flights.send(kv_total, "seq", 1)
-    down_total = seq_rest(part_down, down_seq[0])
-    flights.land(only=[q_seq, hidden_other, small_box])
-    small = small_step(small, small_box)
-    small_box = small_send()
-    down_other = flights.send(down_total, "seq", 1)
     q_total = seq_rest(q_keep, q_seq[0])
     q_other = flights.send(q_total, "seq", 1)
-    if small_box is not None:
-        flights.land(only=[small_box])
+    flights.land(only=[hidden_other])
+    down_total = seq_rest(part_down, down_seq[0])
+    down_other = flights.send(down_total, "seq", 1)
     while small_box is not None:
-        small = small_step(small, small_box)
-        small_box = small_send()
-        if small_box is not None:
-            flights.land(only=[small_box])
+        move_on()
     flights.land()
 
     own_lines = lax.dynamic_slice_in_dim(small[:8], me * shard_rows, shard_rows, 1)

time: 602 us -> 590 us (0.980)
  waiting for transfers between devices: 149 us -> 125 us
    ppermute x54, waiting for transfers between devices: 149 us -> 125 us  [swap(): return lax.ppermute(array, axis, [(i, i ^ bits) for i in range(size)])]
    unnamed x59 -> x73, local copies, waits for them, and re-layouts: 8.41 us -> 12.6 us
  transfers between devices with their start and end apart: 56 -> 56, of which waited for: 23 -> 23; matrix products, arithmetic and copies ran while one was open for 8% -> 8% of each run, Pallas kernels for 55% -> 57%
where the time goes in v10:
time: 590 us; the launch traced here: 581 us
  Pallas kernels  333 us (56%)
  waiting for transfers between devices  125 us (21%)
  starting transfers between devices  46 us (8%)
  other arithmetic  30.9 us (5%)
  local copies, waits for them, and re-layouts  16.8 us (3%)
  between operations  15 us (3%)
  matrix products  14.2 us (2%)
    ppermute x54, waiting for transfers between devices, swap(): return lax.ppermute(array, axis, [(i, i ^ bits) for i in range(size)])  125 us
    pallas_call x9, Pallas kernels, rows_matmul(): pl.pallas_call(kernel, out_shape=shapes, grid=(steps,), in_specs=[pl.Bloc...  95.4 us
    pallas_call x3, Pallas kernels, attend_back(): pl.pallas_call(functools.partial(attend_back_kernel, row, heads, blocks,...  60 us
    ppermute x54, starting transfers between devices, swap(): return lax.ppermute(array, axis, [(i, i ^ bits) for i in range(size)])  45.7 us
    pallas_call x3, Pallas kernels, attend(): pl.pallas_call(functools.partial(attend_kernel, row, heads, blocks, padde...  34.4 us
    pallas_call x2, Pallas kernels, weight_grad(): pl.pallas_call(functools.partial(weight_grad_kernel, pairs, count, rows),...  25.4 us
    pallas_call x2, Pallas kernels, token_dot(): pl.pallas_call(kernel, out_shape=jax.ShapeDtypeStruct((width, cols), BF16...  20.9 us
    pallas_call x1, Pallas kernels, hidden(): pl.pallas_call(kernel, out_shape=(jax.ShapeDtypeStruct((count * rows, col...  18.7 us
  transfers between devices with their start and end apart: 56, of which 23 were waited for; matrix products, arithmetic and copies ran while one was open for 8% of the time, Pallas kernels for 57%

profile of v10, /device:TPU:0, one launch (start us, length us, event | category | flops | bytes accessed | tf_op | source)
XLA Modules:
  0.0 581.4 jit_solution(14748092168972518333)
XLA Ops:
  26.2 13.3 %collective-permute-done.1.refs_2_ = bf16[144,1920]{1,0:T(8,128)(2,1)} collective-permute-done((bf16[144,1920]{1,0:T(8,128)(2,1)}, bf16[144,1920]{1,0:T(8,128)(2,1)}, u32[]{:S(2)}, u32[]{:S(2)}) %collective-permute-start.1) | collective-permute-done | bytes 552992 | tf_op jit(solution)/shard_map/ppermute | solution.py:42
  45.9 12.4 %collective-permute-done.4.refs_6_ = bf16[144,1920]{1,0:T(8,128)(2,1)S(1)} collective-permute-done((bf16[144,1920]{1,0:T(8,128)(2,1)}, bf16[144,1920]{1,0:T(8,128)(2,1)S(1)}, u32[]{:S(2)}, u32[]{:S(2)}) %collective-permute-start.4) | collective-permute-done | bytes 552992 | tf_op jit(solution)/shard_map/ppermute | solution.py:42
  62.5 8.9 %collective-permute-done.7.refs_3_ = bf16[144,1920]{1,0:T(8,128)(2,1)S(1)} collective-permute-done((bf16[144,1920]{1,0:T(8,128)(2,1)}, bf16[144,1920]{1,0:T(8,128)(2,1)S(1)}, u32[]{:S(2)}, u32[]{:S(2)}) %collective-permute-start.7) | collective-permute-done | bytes 552992 | tf_op jit(solution)/shard_map/ppermute | solution.py:42
  71.4 10.7 %collective-permute-done.6.refs_7_ = bf16[144,1920]{1,0:T(8,128)(2,1)S(1)} collective-permute-done((bf16[144,1920]{1,0:T(8,128)(2,1)S(1)}, bf16[144,1920]{1,0:T(8,128)(2,1)S(1)}, u32[]{:S(2)}, u32[]{:S(2)}) %collective-permute-start.6) | collective-permute-done | bytes 552992 | tf_op jit(solution)/shard_map/ppermute | solution.py:42
  109.2 8.9 %near.1 = bf16[1536,1280]{1,0:T(8,128)(2,1)} custom-call(bf16[1536,1152]{1,0:T(8,128)(2,1)} %norm.2.refs_0_, bf16[1152,1280]{1,0:T(8,128)(2,1)} %get-tuple-element.392.refs_1_.refs_3_, f32[1,1280]{1,0:T(1,128)} %get-tuple-element.266.refs_2_), custom_call_target="tpu_custom_call" | custom-call | flops 1 | bytes 1 | tf_op jit(solution)/shard_map/near/pallas_call | solution.py:520
  139.7 12.5 %attend.3 = (bf16[3,256,640]{2,1,0:T(8,128)(2,1)}, bf16[3,256,640]{2,1,0:T(8,128)(2,1)}, f32[3,8,512]{2,1,0:T(8,128)}) custom-call(s32[3,4]{1,0:T(4,128)} %get-tuple-element.239.need_ref, s32[3,512,1]{2,1,0:T(8,128)} %get-tuple-element.243.col_ref, s32[3,4,256]{2,1,0:T(4,128)} %get-tuple-element.240.row_ref, bf16[2,3,256,640]{3,2,1,0:T(8,128)(2,1)} %bitcast.49, ...), custom_call_target="tpu_custom_call" | custom-call | flops 1 | bytes 1 | tf_op jit(solution)/shard_map/attend/pallas_call | solution.py:908
  154.5 11.1 %attend.4 = (bf16[3,256,640]{2,1,0:T(8,128)(2,1)}, bf16[3,256,640]{2,1,0:T(8,128)(2,1)}, f32[3,8,512]{2,1,0:T(8,128)}) custom-call(s32[3,4]{1,0:T(4,128)} %get-tuple-element.239.need_ref, s32[3,512,1]{2,1,0:T(8,128)} %get-tuple-element.243.col_ref, ...), custom_call_target="tpu_custom_call", output_to_operand_aliasing={{0}: (6, {}), {1}: (7, {}), {2}: (8, {})} | custom-call | flops 1 | bytes 1 | tf_op jit(solution)/shard_map/attend/pallas_call | solution.py:908
  165.6 10.8 %attend.5 = (bf16[3,256,640]{2,1,0:T(8,128)(2,1)}, bf16[3,256,640]{2,1,0:T(8,128)(2,1)}, f32[3,8,512]{2,1,0:T(8,128)}) custom-call(s32[3,4]{1,0:T(4,128)} %get-tuple-element.239.need_ref, s32[3,512,1]{2,1,0:T(8,128)} %get-tuple-element.243.col_ref, ...), custom_call_target="tpu_custom_call", output_to_operand_aliasing={{0}: (6, {}), {1}: (7, {}), {2}: (8, {})} | custom-call | flops 1 | bytes 1 | tf_op jit(solution)/shard_map/attend/pallas_call | solution.py:908
  221.0 18.7 %hidden.1 = (bf16[1536,2176]{1,0:T(8,128)(2,1)}, bf16[1536,2176]{1,0:T(8,128)(2,1)}, bf16[1536,1152]{1,0:T(8,128)(2,1)}) custom-call(bf16[768,1152]{1,0:T(8,128)(2,1)} %get-tuple-element.325.refs_0_, bf16[768,1152]{1,0:T(8,128)(2,1)} %copy-done.9, bf16[1152,2176]{1,0:T(8,128)(2,1)} %get-tuple-element.327.refs_2_.refs_1_, f32[1,2176]{1,0:T(1,128)} %broadcast_select_fusion.refs_3_), custom_call_target="tpu_custom_call" | custom-call | flops 1 | bytes 1 | tf_op jit(solution)/shard_map/hidden/pallas_call | solution.py:792
  239.7 14.1 %token_dot.2 = bf16[1152,2176]{1,0:T(8,128)(2,1)} custom-call(bf16[1536,1152]{1,0:T(8,128)(2,1)} %pad_maximum_fusion.1.left_ref.refs_0_, bf16[1536,2176]{1,0:T(8,128)(2,1)} %get-tuple-element.428.right_ref.refs_0_), custom_call_target="tpu_custom_call" | custom-call | flops 1 | bytes 1 | tf_op jit(solution)/shard_map/token_dot/pallas_call | solution.py:219
  259.8 14.6 %grad_pre.1 = (bf16[1536,2176]{1,0:T(8,128)(2,1)}, f32[1,2176]{1,0:T(1,128)}) custom-call(bf16[1536,1152]{1,0:T(8,128)(2,1)} %pad_maximum_fusion.1.left_ref.refs_0_, bf16[1152,2176]{1,0:T(8,128)(2,1)} %assemble.5.refs_1_, bf16[1536,2176]{1,0:T(8,128)(2,1)} %get-tuple-element.342.refs_2_), custom_call_target="tpu_custom_call" | custom-call | flops 1 | bytes 1 | tf_op jit(solution)/shard_map/grad_pre/pallas_call | solution.py:520
  274.4 14.5 %back.1 = (bf16[768,1152]{1,0:T(8,128)(2,1)}, bf16[768,1152]{1,0:T(8,128)(2,1)}) custom-call(bf16[1536,2176]{1,0:T(8,128)(2,1)} %get-tuple-element.347.refs_0_, bf16[1152,2176]{1,0:T(8,128)(2,1)} %get-tuple-element.327.refs_2_.refs_1_), custom_call_target="tpu_custom_call" | custom-call | flops 1 | bytes 1 | tf_op jit(solution)/shard_map/back/pallas_call | solution.py:520
  289.0 14.2 %convolution_convert_fusion = bf16[1152,2176]{1,0:T(8,128)(2,1)} fusion(bf16[1536,1152]{1,0:T(8,128)(2,1)} %get-tuple-element.346, bf16[1536,2176]{1,0:T(8,128)(2,1)} %get-tuple-element.347.refs_0_), kind=kOutput, calls=%fused_computation.1 | convolution fusion | flops 7703248896 | bytes 15237120 | tf_op jit(solution)/shard_map/dot_general | solution.py:29
  304.5 12.7 %second_back.1 = (f32[768,1152]{1,0:T(8,128)}, bf16[768,1152]{1,0:T(8,128)(2,1)}, bf16[768,640]{1,0:T(8,128)(2,1)}, bf16[768,640]{1,0:T(8,128)(2,1)}, f32[8,1152]{1,0:T(8,128)}) custom-call(s32[1]{0:T(128)} %bitcast.1.core_ref, f32[768,1152]{1,0:T(8,128)} %get-tuple-element.429.x_ref.refs_2_, bf16[768,1152]{1,0:T(8,128)(2,1)} %get-tuple-element.348.refs_0_, ...), custom_call_target="tpu_custom_call" | custom-call | flops 1 | bytes 1 | tf_op jit(solution)/shard_map/second_back/pallas_call | solution.py:447
  329.2 21.8 %attend_back.3 = (bf16[2,3,256,640]{3,2,1,0:T(8,128)(2,1)}, bf16[2,3,256,1280]{3,2,1,0:T(8,128)(2,1)}, bf16[2,3,256,1280]{3,2,1,0:T(8,128)(2,1)}) custom-call(s32[3,4]{1,0:T(4,128)} %get-tuple-element.239.need_ref, s32[3,4,256,1]{3,2,1,0:T(8,128)} %get-tuple-element.241.col_ref, s32[3,1,512]{2,1,0:T(1,128)} %get-tuple-element.242.row_ref, ...), custom_call_target="tpu_custom_call" | custom-call | flops 1 | bytes 1 | tf_op jit(solution)/shard_map/attend_back/pallas_call | solution.py:1006
  357.0 18.5 %attend_back.4 = (bf16[2,3,256,640]{3,2,1,0:T(8,128)(2,1)}, bf16[2,3,256,1280]{3,2,1,0:T(8,128)(2,1)}, bf16[2,3,256,1280]{3,2,1,0:T(8,128)(2,1)}) custom-call(s32[3,4]{1,0:T(4,128)} %get-tuple-element.239.need_ref, s32[3,4,256,1]{3,2,1,0:T(8,128)} %get-tuple-element.241.col_ref, ...), custom_call_target="tpu_custom_call", output_to_operand_aliasing={{0}: (12, {}), {1}: (13, {}), {2}: (14, {})} | custom-call | flops 1 | bytes 1 | tf_op jit(solution)/shard_map/attend_back/pallas_call | solution.py:1006
  376.9 19.7 %attend_back.5 = (bf16[2,3,256,640]{3,2,1,0:T(8,128)(2,1)}, bf16[2,3,256,1280]{3,2,1,0:T(8,128)(2,1)}, bf16[2,3,256,1280]{3,2,1,0:T(8,128)(2,1)}) custom-call(s32[3,4]{1,0:T(4,128)} %get-tuple-element.239.need_ref, s32[3,4,256,1]{3,2,1,0:T(8,128)} %get-tuple-element.241.col_ref, ...), custom_call_target="tpu_custom_call", output_to_operand_aliasing={{0}: (12, {}), {1}: (13, {}), {2}: (14, {})} | custom-call | flops 1 | bytes 1 | tf_op jit(solution)/shard_map/attend_back/pallas_call | solution.py:1006
  397.4 9.7 %back_far.1 = (bf16[768,1152]{1,0:T(8,128)(2,1)}, bf16[768,1152]{1,0:T(8,128)(2,1)}) custom-call(bf16[1536,1280]{1,0:T(8,128)(2,1)} %bitcast.57, bf16[1152,1280]{1,0:T(8,128)(2,1)} %get-tuple-element.392.refs_1_.refs_3_), custom_call_target="tpu_custom_call" | custom-call | flops 1 | bytes 1 | tf_op jit(solution)/shard_map/back_far/pallas_call | solution.py:520
  408.5 17.4 %weight_grad.2 = (bf16[576,1280]{1,0:T(8,128)(2,1)}, bf16[576,1280]{1,0:T(8,128)(2,1)}, f32[8,1280]{1,0:T(8,128)}) custom-call(s32[9]{0:T(128)} %pad_add_fusion.pos_ref, bf16[1536,1152]{1,0:T(8,128)(2,1)} %norm.2.refs_0_, bf16[1536,1152]{1,0:T(8,128)(2,1)} %norm.3.refs_0_.refs_1_, bf16[1536,1280]{1,0:T(8,128)(2,1)} %bitcast.55, bf16[1536,1280]{1,0:T(8,128)(2,1)} %bitcast.58), custom_call_target="tpu_custom_call" | custom-call | flops 1 | bytes 1 | tf_op jit(solution)/shard_map/weight_grad/pallas_call | solution.py:190
  432.0 13.4 %back_near.1 = (bf16[768,1152]{1,0:T(8,128)(2,1)}, bf16[768,1152]{1,0:T(8,128)(2,1)}) custom-call(bf16[1536,640]{1,0:T(8,128)(2,1)} %bitcast.60, bf16[1536,1280]{1,0:T(8,128)(2,1)} %bitcast.56, bf16[1152,640]{1,0:T(8,128)(2,1)} %get-tuple-element.270.weight_ref.refs_1_.refs_2_, bf16[1152,1280]{1,0:T(8,128)(2,1)} %get-tuple-element.392.refs_1_.refs_3_), custom_call_target="tpu_custom_call" | custom-call | flops 1 | bytes 1 | tf_op jit(solution)/shard_map/back_near/pallas_call | solution.py:520
  463.2 12.9 %collective-permute-done.35 = bf16[576,1280]{1,0:T(8,128)(2,1)} collective-permute-done((bf16[576,1280]{1,0:T(8,128)(2,1)}, bf16[576,1280]{1,0:T(8,128)(2,1)}, u32[]{:S(2)}, u32[]{:S(2)}) %collective-permute-start.35) | collective-permute-done | bytes 1474592 | tf_op jit(solution)/shard_map/ppermute | solution.py:42
  498.7 10.2 %down_own.1 = bf16[768,1152]{1,0:T(8,128)(2,1)} custom-call(bf16[1536,2176]{1,0:T(8,128)(2,1)} %get-tuple-element.428.right_ref.refs_0_, bf16[1152,2176]{1,0:T(8,128)(2,1)} %assemble.5.refs_1_, f32[768,1152]{1,0:T(8,128)} %get-tuple-element.429.x_ref.refs_2_, bf16[768,1152]{1,0:T(8,128)(2,1)} %copy-done.6, f32[1,1152]{1,0:T(1,128)} %get-tuple-element.470.refs_4_), custom_call_target="tpu_custom_call" | custom-call | flops 1 | bytes 1 | tf_op jit(solution)/shard_map/down_own/pallas_call | solution.py:520
  523.8 19.4 %collective-permute-done.42 = bf16[144,640]{1,0:T(8,128)(2,1)S(1)} collective-permute-done((bf16[144,640]{1,0:T(8,128)(2,1)}, bf16[144,640]{1,0:T(8,128)(2,1)S(1)}, u32[]{:S(2)}, u32[]{:S(2)}) %collective-permute-start.42) | collective-permute-done | bytes 184352 | tf_op jit(solution)/shard_map/ppermute | solution.py:42
  548.3 11.1 %collective-permute-done.46 = bf16[144,640]{1,0:T(8,128)(2,1)S(1)} collective-permute-done((bf16[144,640]{1,0:T(8,128)(2,1)S(1)}, bf16[144,640]{1,0:T(8,128)(2,1)S(1)}, u32[]{:S(2)}, u32[]{:S(2)}) %collective-permute-start.46) | collective-permute-done | bytes 184352 | tf_op jit(solution)/shard_map/ppermute | solution.py:42
  (253 shorter events, 234.8 us)
Async XLA Ops:
  7.2 368.3 %reduce-scatter.3.cloned.1.call-start = ((), (), s32[]{:S(2)}) async-start(), calls=%async_computation.2 | async-start | bytes 5640192 | tf_op jit(solution)/shard_map/reduce_scatter | solution.py:1240
  7.3 34.7 %collective-permute-start.3 = (bf16[768,1152]{1,0:T(8,128)(2,1)}, bf16[768,1152]{1,0:T(8,128)(2,1)}, u32[]{:S(2)}, u32[]{:S(2)}) collective-permute-start(bf16[768,1152]{1,0:T(8,128)(2,1)} %bitcast.74), channel_id=1, source_target_pairs={{0,8},{8,0},{16,24},{24,16},{1,9},{9,1},{17,25},{25,17},{2,10},{10... | collective-permute-start | bytes 5308424 | tf_op jit(solution)/shard_map/ppermute | solution.py:42
  41.9 29.5 %collective-permute-start.9 = (bf16[768,1152]{1,0:T(8,128)(2,1)S(1)}, bf16[768,1152]{1,0:T(8,128)(2,1)S(1)}, u32[]{:S(2)}, u32[]{:S(2)}) collective-permute-start(bf16[768,1152]{1,0:T(8,128)(2,1)S(1)} %bitcast.65), channel_id=1, source_target_pairs={{0,8},{8,0},{16,24},{24,16},{1,9},{9,1},{17,25},{25,17},{2,10},{10... | collective-permute-start | bytes 5308424 | tf_op jit(solution)/shard_map/ppermute | solution.py:42
  41.9 41.1 %collective-permute-start.5 = (bf16[768,1152]{1,0:T(8,128)(2,1)S(1)}, bf16[768,1152]{1,0:T(8,128)(2,1)}, u32[]{:S(2)}, u32[]{:S(2)}) collective-permute-start(bf16[768,1152]{1,0:T(8,128)(2,1)S(1)} %bitcast.66), channel_id=1, source_target_pairs={{0,16},{8,24},{16,0},{24,8},{1,17},{9,25},{17,1},{25,9},{2,18},{10... | collective-permute-start | bytes 5308424 | tf_op jit(solution)/shard_map/ppermute | solution.py:42
  83.1 37.7 %collective-permute-start.14 = (bf16[768,1152]{1,0:T(8,128)(2,1)}, bf16[768,1152]{1,0:T(8,128)(2,1)S(1)}, u32[]{:S(2)}, u32[]{:S(2)}) collective-permute-start(bf16[768,1152]{1,0:T(8,128)(2,1)} %collective-permute-done.5.refs_0_), channel_id=1, source_target_pairs={{0,8},{8,0},{16,24},{24,16},{1,9},{9,1},{17,25},{25,17},{2,10},{10... | collective-permute-start | bytes 5308424 | tf_op jit(solution)/shard_map/ppermute | solution.py:42
  83.1 37.7 %collective-permute-start.13 = (bf16[144,2816]{1,0:T(8,128)(2,1)}, bf16[144,2816]{1,0:T(8,128)(2,1)S(1)}, u32[]{:S(2)}, u32[]{:S(2)}) collective-permute-start(bf16[144,2816]{1,0:T(8,128)(2,1)} %get-tuple-element.274.refs_0_), channel_id=1, source_target_pairs={{0,2},{1,3},{2,0},{3,1},{4,6},{5,7},{6,4},{7,5},{8,10},{9,11},{10,... | collective-permute-start | bytes 2433032 | tf_op jit(solution)/shard_map/ppermute | solution.py:42
  83.9 44.7 %collective-permute-start.16 = (bf16[144,2816]{1,0:T(8,128)(2,1)}, bf16[144,2816]{1,0:T(8,128)(2,1)S(1)}, u32[]{:S(2)}, u32[]{:S(2)}) collective-permute-start(bf16[144,2816]{1,0:T(8,128)(2,1)} %get-tuple-element.274.refs_0_), channel_id=1, source_target_pairs={{0,1},{1,0},{2,3},{3,2},{4,5},{5,4},{6,7},{7,6},{8,9},{9,8},{10,11... | collective-permute-start | bytes 2433032 | tf_op jit(solution)/shard_map/ppermute | solution.py:42
  84.4 44.2 %collective-permute-start.17 = (bf16[144,2816]{1,0:T(8,128)(2,1)}, bf16[144,2816]{1,0:T(8,128)(2,1)}, u32[]{:S(2)}, u32[]{:S(2)}) collective-permute-start(bf16[144,2816]{1,0:T(8,128)(2,1)} %get-tuple-element.274.refs_0_), channel_id=1, source_target_pairs={{0,4},{1,5},{2,6},{3,7},{4,0},{5,1},{6,2},{7,3},{8,12},{9,13},{10,... | collective-permute-start | bytes 2433032 | tf_op jit(solution)/shard_map/ppermute | solution.py:42
  128.7 47.7 %collective-permute-start.18 = (bf16[144,2816]{1,0:T(8,128)(2,1)}, bf16[144,2816]{1,0:T(8,128)(2,1)}, u32[]{:S(2)}, u32[]{:S(2)}) collective-permute-start(bf16[144,2816]{1,0:T(8,128)(2,1)} %collective-permute-done.17.refs_4_), channel_id=1, source_target_pairs={{0,1},{1,0},{2,3},{3,2},{4,5},{5,4},{6,7},{7,6},{8,9},{9,8},{10,11... | collective-permute-start | bytes 2433032 | tf_op jit(solution)/shard_map/ppermute | solution.py:42
  152.2 32.3 %collective-permute-start.20 = (bf16[144,2816]{1,0:T(8,128)(2,1)S(1)}, bf16[144,2816]{1,0:T(8,128)(2,1)S(1)}, u32[]{:S(2)}, u32[]{:S(2)}) collective-permute-start(bf16[144,2816]{1,0:T(8,128)(2,1)S(1)} %collective-permute-done.19.refs_6_), channel_id=1, source_target_pairs={{0,1},{1,0},{2,3},{3,2},{4,5},{5,4},{6,7},{7,6},{8,9},{9,8},{10,11... | collective-permute-start | bytes 2433032 | tf_op jit(solution)/shard_map/ppermute | solution.py:42
  152.2 44.5 %collective-permute-start.10 = (bf16[144,2176]{1,0:T(8,128)(2,1)}, bf16[144,2176]{1,0:T(8,128)(2,1)}, u32[]{:S(2)}, u32[]{:S(2)}) collective-permute-start(bf16[144,2176]{1,0:T(8,128)(2,1)} %get-tuple-element.254.refs_0_), channel_id=1, source_target_pairs={{0,1},{1,0},{2,3},{3,2},{4,5},{5,4},{6,7},{7,6},{8,9},{9,8},{10,11... | collective-permute-start | bytes 1880072 | tf_op jit(solution)/shard_map/ppermute | solution.py:42
  154.2 42.5 %collective-permute-start.11 = (bf16[144,2176]{1,0:T(8,128)(2,1)}, bf16[144,2176]{1,0:T(8,128)(2,1)}, u32[]{:S(2)}, u32[]{:S(2)}) collective-permute-start(bf16[144,2176]{1,0:T(8,128)(2,1)} %get-tuple-element.254.refs_0_), channel_id=1, source_target_pairs={{0,2},{1,3},{2,0},{3,1},{4,6},{5,7},{6,4},{7,5},{8,10},{9,11},{10,... | collective-permute-start | bytes 1880072 | tf_op jit(solution)/shard_map/ppermute | solution.py:42
  154.5 42.2 %collective-permute-start.12 = (bf16[144,2176]{1,0:T(8,128)(2,1)}, bf16[144,2176]{1,0:T(8,128)(2,1)S(1)}, u32[]{:S(2)}, u32[]{:S(2)}) collective-permute-start(bf16[144,2176]{1,0:T(8,128)(2,1)} %get-tuple-element.254.refs_0_), channel_id=1, source_target_pairs={{0,4},{1,5},{2,6},{3,7},{4,0},{5,1},{6,2},{7,3},{8,12},{9,13},{10,... | collective-permute-start | bytes 1880072 | tf_op jit(solution)/shard_map/ppermute | solution.py:42
  215.9 37.9 %collective-permute-start.26 = (bf16[144,2176]{1,0:T(8,128)(2,1)S(1)}, bf16[144,2176]{1,0:T(8,128)(2,1)S(1)}, u32[]{:S(2)}, u32[]{:S(2)}) collective-permute-start(bf16[144,2176]{1,0:T(8,128)(2,1)S(1)} %copy-done.27), channel_id=1, source_target_pairs={{0,1},{1,0},{2,3},{3,2},{4,5},{5,4},{6,7},{7,6},{8,9},{9,8},{10,11... | collective-permute-start | bytes 1880072 | tf_op jit(solution)/shard_map/ppermute | solution.py:42
  216.2 37.6 %collective-permute-start.27 = (bf16[144,2176]{1,0:T(8,128)(2,1)}, bf16[144,2176]{1,0:T(8,128)(2,1)}, u32[]{:S(2)}, u32[]{:S(2)}) collective-permute-start(bf16[144,2176]{1,0:T(8,128)(2,1)} %collective-permute-done.21.refs_6_), channel_id=1, source_target_pairs={{0,1},{1,0},{2,3},{3,2},{4,5},{5,4},{6,7},{7,6},{8,9},{9,8},{10,11... | collective-permute-start | bytes 1880072 | tf_op jit(solution)/shard_map/ppermute | solution.py:42
  254.6 265.3 %reduce-scatter.5.cloned.1.call-start = ((), (), s32[]{:S(2)}) async-start(), calls=%async_computation.3 | async-start | bytes 7299072 | tf_op jit(solution)/shard_map/reduce_scatter | solution.py:1298
  427.6 48.5 %collective-permute-start.36 = (bf16[768,1152]{1,0:T(8,128)(2,1)}, bf16[768,1152]{1,0:T(8,128)(2,1)}, u32[]{:S(2)}, u32[]{:S(2)}) collective-permute-start(bf16[768,1152]{1,0:T(8,128)(2,1)} %add_convert_fusion), channel_id=1, source_target_pairs={{0,16},{8,24},{16,0},{24,8},{1,17},{9,25},{17,1},{25,9},{2,18},{10... | collective-permute-start | bytes 5308424 | tf_op jit(solution)/shard_map/ppermute | solution.py:42
  428.3 47.8 %collective-permute-start.35 = (bf16[576,1280]{1,0:T(8,128)(2,1)}, bf16[576,1280]{1,0:T(8,128)(2,1)}, u32[]{:S(2)}, u32[]{:S(2)}) collective-permute-start(bf16[576,1280]{1,0:T(8,128)(2,1)} %get-tuple-element.400), channel_id=1, source_target_pairs={{0,1},{1,0},{2,3},{3,2},{4,5},{5,4},{6,7},{7,6},{8,9},{9,8},{10,11... | collective-permute-start | bytes 4423688 | tf_op jit(solution)/shard_map/ppermute | solution.py:42
  445.4 33.8 %collective-permute-start.37 = (bf16[768,1152]{1,0:T(8,128)(2,1)}, bf16[768,1152]{1,0:T(8,128)(2,1)}, u32[]{:S(2)}, u32[]{:S(2)}) collective-permute-start(bf16[768,1152]{1,0:T(8,128)(2,1)} %get-tuple-element.407), channel_id=1, source_target_pairs={{0,8},{8,0},{16,24},{24,16},{1,9},{9,1},{17,25},{25,17},{2,10},{10... | collective-permute-start | bytes 5308424 | tf_op jit(solution)/shard_map/ppermute | solution.py:42
  454.2 37.5 %collective-permute-start.33 = (bf16[768,1152]{1,0:T(8,128)(2,1)}, bf16[768,1152]{1,0:T(8,128)(2,1)S(1)}, u32[]{:S(2)}, u32[]{:S(2)}) collective-permute-start(bf16[768,1152]{1,0:T(8,128)(2,1)} %down_pair.1), channel_id=1, source_target_pairs={{0,8},{8,0},{16,24},{24,16},{1,9},{9,1},{17,25},{25,17},{2,10},{10... | collective-permute-start | bytes 5308424 | tf_op jit(solution)/shard_map/ppermute | solution.py:42
  462.7 29.0 %collective-permute-start.34 = (bf16[576,640]{1,0:T(8,128)(2,1)}, bf16[576,640]{1,0:T(8,128)(2,1)S(1)}, u32[]{:S(2)}, u32[]{:S(2)}) collective-permute-start(bf16[576,640]{1,0:T(8,128)(2,1)} %get-tuple-element.411), channel_id=1, source_target_pairs={{0,1},{1,0},{2,3},{3,2},{4,5},{5,4},{6,7},{7,6},{8,9},{9,8},{10,11... | collective-permute-start | bytes 2211848 | tf_op jit(solution)/shard_map/ppermute | solution.py:42
  479.2 34.7 %collective-permute-start.38 = (bf16[288,1280]{1,0:T(8,128)(2,1)}, bf16[288,1280]{1,0:T(8,128)(2,1)}, u32[]{:S(2)}, u32[]{:S(2)}) collective-permute-start(bf16[288,1280]{1,0:T(8,128)(2,1)} %get-tuple-element.452), channel_id=1, source_target_pairs={{0,2},{1,3},{2,0},{3,1},{4,6},{5,7},{6,4},{7,5},{8,10},{9,11},{10,... | collective-permute-start | bytes 2211848 | tf_op jit(solution)/shard_map/ppermute | solution.py:42
  520.0 28.1 %collective-permute-start.47 = (bf16[144,2816]{1,0:T(8,128)(2,1)}, bf16[144,2816]{1,0:T(8,128)(2,1)S(1)}, u32[]{:S(2)}, u32[]{:S(2)}) collective-permute-start(bf16[144,2816]{1,0:T(8,128)(2,1)} %reduce-scatter.5.cloned.1.call-done), channel_id=1, source_target_pairs={{0,16},{8,24},{16,0},{24,8},{1,17},{9,25},{17,1},{25,9},{2,18},{10... | collective-permute-start | bytes 2433032 | tf_op jit(solution)/shard_map/ppermute | solution.py:42
  521.6 45.0 %collective-permute-start.52 = (f32[144,2176]{1,0:T(8,128)S(1)}, f32[144,2176]{1,0:T(8,128)S(1)}, u32[]{:S(2)}, u32[]{:S(2)}) collective-permute-start(f32[144,2176]{1,0:T(8,128)S(1)} %convert_add_fusion.1), channel_id=1, source_target_pairs={{0,8},{8,0},{16,24},{24,16},{1,9},{9,1},{17,25},{25,17},{2,10},{10... | collective-permute-start | bytes 3760136 | tf_op jit(solution)/shard_map/ppermute | solution.py:42
  (70 other events, 875.3 us)
Sparse Core Ops, SparseCore 0:
  254.0 98.0 reduce-scatter.2
  357.2 137.7 reduce-scatter.4

commit v11 on v10

--- a/solution.py
+++ b/solution.py
@@ -208,7 +208,29 @@
     )(positions, *lefts, *rights)
 
 
-def token_dot(left, right):
+def add_into(array, left, right, first_col):
+    rows, cols = left.shape
+    tile = 128
+    base = first_col // tile
+    part = pl.BlockSpec((rows, tile), lambda n: (0, n))
+
+    def kernel(left_ref, right_ref, _, out_ref):
+        out_ref[...] = (left_ref[...].astype(F32) + right_ref[...].astype(F32)).astype(BF16)
+
+    return pl.pallas_call(
+        kernel,
+        out_shape=jax.ShapeDtypeStruct(array.shape, BF16),
+        grid=(cols // tile,),
+        in_specs=[part, part, pl.BlockSpec(memory_space=pl.ANY)],
+        out_specs=pl.BlockSpec((rows, tile), lambda n: (0, n + base)),
+        input_output_aliases={2: 0},
+        compiler_params=params(("arbitrary",)),
+        cost_estimate=NOMINAL,
+        name="add_into",
+    )(left, right, array)
+
+
+def token_dot(left, right, room=0):
     tokens, width = left.shape
     cols = right.shape[1]
     tile = 256
@@ -218,7 +240,7 @@
 
     return pl.pallas_call(
         kernel,
-        out_shape=jax.ShapeDtypeStruct((width, cols), BF16),
+        out_shape=jax.ShapeDtypeStruct((width, cols + room), BF16),
         grid=(pl.cdiv(cols, tile),),
         in_specs=[
             pl.BlockSpec((tokens, width), lambda n: (0, 0), pipeline_mode=pl.Buffered(1)),
@@ -1186,7 +1208,7 @@
     for row in range(rows):
         query, near, far = chain(query, near, far)
         if staged and row == 1:
-            query = flights.land(query, only=[h[zz | z]])
+            query = flights.land(query, only=[h[z | y], h[zz | z]])
             h[zz | z | y] = over(h[zz | z], y)
             d[y], d[z], d[zz] = over(d[0], y), over(d[0], z), over(d[0], zz)
         found = chain.done(*attend(row, query, near, far, need, seg_near_col, seg_rows, heads, found))
@@ -1256,7 +1278,7 @@
     )
     back_other = flights.send(back_pair, "seq", 1)
     second_near, grad_pre = chain(second_near, grad_pre)
-    grad_hidden = chain.done(dot(second_near, grad_pre, TN).astype(BF16))
+    grad_hidden = chain.done(token_dot(second_near, grad_pre, out_cols))
     back = flights.land(back)
     grad_middle, branch, grad_mine, grad_send, lines = second_back(
         core_flag, middle, [back, back_other[0]], gain_two, incoming, w_out, hidden_line, half, padded
@@ -1293,8 +1315,7 @@
         chain.done(*found)
         query = flights.land(query)
         if row == 0:
-            out_sum = chain.done(*add_rows(out_mine, out_back[0]))
-            grad_ho = chain.done(jnp.concatenate([grad_hidden, out_sum], axis=1))
+            grad_ho = chain.done(add_into(grad_hidden, out_mine, out_back[0], ff_half))
             part_hidden = lax.psum_scatter(grad_ho, "fsdp", scatter_dimension=0, tiled=True)
         if row == 1:
             part_down = chain(part_down)

time: 590 us -> 589 us (level)
  Pallas kernels: 333 us -> 355 us
  matrix products: 14.2 us -> 0 us
  other arithmetic: 30.9 us -> 24.6 us
    pallas_call x2 -> x4, Pallas kernels: 20.9 us -> 39.8 us  [the longest x3 35.2 us: token_dot(): pl.pallas_call(kernel, out_shape=jax.ShapeDtypeStruct((width, cols + room...]
    dot_general x1 -> x0, matrix products: 14.2 us -> none  [dot(): lax.dot_general(left, right, (dims, ((), ())), preferred_element_type=F32)]
    unnamed x73 -> x75, local copies, waits for them, and re-layouts: 12.6 us -> 13.7 us
    convert_element_type x8 -> x7, other arithmetic: 11.9 us -> 11.3 us  [add_rows(): (left[part].astype(F32) + right[part].astype(F32)).astype(kind)]
  transfers between devices with their start and end apart: 56 -> 56, of which waited for: 23 -> 22; matrix products, arithmetic and copies ran while one was open for 8% -> 5% of each run, Pallas kernels for 57% -> 61%
where the time goes in v11:
time: 589 us; the launch traced here: 578 us
  Pallas kernels  355 us (60%)
  waiting for transfers between devices  122 us (21%)
  starting transfers between devices  43.4 us (7%)
  other arithmetic  24.6 us (4%)
  local copies, waits for them, and re-layouts  17.9 us (3%)
  between operations  14.8 us (3%)
    ppermute x54, waiting for transfers between devices, swap(): return lax.ppermute(array, axis, [(i, i ^ bits) for i in range(size)])  122 us
    pallas_call x9, Pallas kernels, rows_matmul(): pl.pallas_call(kernel, out_shape=shapes, grid=(steps,), in_specs=[pl.Bloc...  95.3 us
    pallas_call x3, Pallas kernels, attend_back(): pl.pallas_call(functools.partial(attend_back_kernel, row, heads, blocks,...  63.6 us
    ppermute x54, starting transfers between devices, swap(): return lax.ppermute(array, axis, [(i, i ^ bits) for i in range(size)])  43.2 us
    pallas_call x3, Pallas kernels, token_dot(): pl.pallas_call(kernel, out_shape=jax.ShapeDtypeStruct((width, cols + room...  35.2 us
    pallas_call x3, Pallas kernels, attend(): pl.pallas_call(functools.partial(attend_kernel, row, heads, blocks, padde...  34.5 us
    pallas_call x2, Pallas kernels, weight_grad(): pl.pallas_call(functools.partial(weight_grad_kernel, pairs, count, rows),...  25.5 us
    pallas_call x1, Pallas kernels, hidden(): pl.pallas_call(kernel, out_shape=(jax.ShapeDtypeStruct((count * rows, col...  18.7 us
  transfers between devices with their start and end apart: 56, of which 22 were waited for; matrix products, arithmetic and copies ran while one was open for 5% of the time, Pallas kernels for 61%

profile of v11, /device:TPU:0, one launch (start us, length us, event | category | flops | bytes accessed | tf_op | source)
XLA Modules:
  0.0 578.3 jit_solution(9181603116365287478)
XLA Ops:
  26.2 13.3 %collective-permute-done.1.refs_2_ = bf16[144,1920]{1,0:T(8,128)(2,1)} collective-permute-done((bf16[144,1920]{1,0:T(8,128)(2,1)}, bf16[144,1920]{1,0:T(8,128)(2,1)}, u32[]{:S(2)}, u32[]{:S(2)}) %collective-permute-start.1) | collective-permute-done | bytes 552992 | tf_op jit(solution)/shard_map/ppermute | solution.py:42
  45.9 12.4 %collective-permute-done.4.refs_6_ = bf16[144,1920]{1,0:T(8,128)(2,1)S(1)} collective-permute-done((bf16[144,1920]{1,0:T(8,128)(2,1)}, bf16[144,1920]{1,0:T(8,128)(2,1)S(1)}, u32[]{:S(2)}, u32[]{:S(2)}) %collective-permute-start.4) | collective-permute-done | bytes 552992 | tf_op jit(solution)/shard_map/ppermute | solution.py:42
  62.4 9.0 %collective-permute-done.7.refs_3_ = bf16[144,1920]{1,0:T(8,128)(2,1)S(1)} collective-permute-done((bf16[144,1920]{1,0:T(8,128)(2,1)}, bf16[144,1920]{1,0:T(8,128)(2,1)S(1)}, u32[]{:S(2)}, u32[]{:S(2)}) %collective-permute-start.7) | collective-permute-done | bytes 552992 | tf_op jit(solution)/shard_map/ppermute | solution.py:42
  71.4 10.7 %collective-permute-done.6.refs_7_ = bf16[144,1920]{1,0:T(8,128)(2,1)S(1)} collective-permute-done((bf16[144,1920]{1,0:T(8,128)(2,1)S(1)}, bf16[144,1920]{1,0:T(8,128)(2,1)S(1)}, u32[]{:S(2)}, u32[]{:S(2)}) %collective-permute-start.6) | collective-permute-done | bytes 552992 | tf_op jit(solution)/shard_map/ppermute | solution.py:42
  109.0 8.9 %near.1 = bf16[1536,1280]{1,0:T(8,128)(2,1)} custom-call(bf16[1536,1152]{1,0:T(8,128)(2,1)} %norm.2.refs_0_, bf16[1152,1280]{1,0:T(8,128)(2,1)} %get-tuple-element.392.refs_1_.refs_3_, f32[1,1280]{1,0:T(1,128)} %get-tuple-element.267.refs_2_), custom_call_target="tpu_custom_call" | custom-call | flops 1 | bytes 1 | tf_op jit(solution)/shard_map/near/pallas_call | solution.py:542
  139.6 12.6 %attend.3 = (bf16[3,256,640]{2,1,0:T(8,128)(2,1)}, bf16[3,256,640]{2,1,0:T(8,128)(2,1)}, f32[3,8,512]{2,1,0:T(8,128)}) custom-call(s32[3,4]{1,0:T(4,128)} %get-tuple-element.239.need_ref, s32[3,512,1]{2,1,0:T(8,128)} %get-tuple-element.243.col_ref, s32[3,4,256]{2,1,0:T(4,128)} %get-tuple-element.240.row_ref, bf16[2,3,256,640]{3,2,1,0:T(8,128)(2,1)} %bitcast.47, ...), custom_call_target="tpu_custom_call" | custom-call | flops 1 | bytes 1 | tf_op jit(solution)/shard_map/attend/pallas_call | solution.py:930
  154.5 10.9 %attend.4 = (bf16[3,256,640]{2,1,0:T(8,128)(2,1)}, bf16[3,256,640]{2,1,0:T(8,128)(2,1)}, f32[3,8,512]{2,1,0:T(8,128)}) custom-call(s32[3,4]{1,0:T(4,128)} %get-tuple-element.239.need_ref, s32[3,512,1]{2,1,0:T(8,128)} %get-tuple-element.243.col_ref, ...), custom_call_target="tpu_custom_call", output_to_operand_aliasing={{0}: (6, {}), {1}: (7, {}), {2}: (8, {})} | custom-call | flops 1 | bytes 1 | tf_op jit(solution)/shard_map/attend/pallas_call | solution.py:930
  165.3 11.1 %attend.5 = (bf16[3,256,640]{2,1,0:T(8,128)(2,1)}, bf16[3,256,640]{2,1,0:T(8,128)(2,1)}, f32[3,8,512]{2,1,0:T(8,128)}) custom-call(s32[3,4]{1,0:T(4,128)} %get-tuple-element.239.need_ref, s32[3,512,1]{2,1,0:T(8,128)} %get-tuple-element.243.col_ref, ...), custom_call_target="tpu_custom_call", output_to_operand_aliasing={{0}: (6, {}), {1}: (7, {}), {2}: (8, {})} | custom-call | flops 1 | bytes 1 | tf_op jit(solution)/shard_map/attend/pallas_call | solution.py:930
  220.4 18.7 %hidden.1 = (bf16[1536,2176]{1,0:T(8,128)(2,1)}, bf16[1536,2176]{1,0:T(8,128)(2,1)}, bf16[1536,1152]{1,0:T(8,128)(2,1)}) custom-call(bf16[768,1152]{1,0:T(8,128)(2,1)} %get-tuple-element.325.refs_0_, bf16[768,1152]{1,0:T(8,128)(2,1)} %copy-done.9, bf16[1152,2176]{1,0:T(8,128)(2,1)} %get-tuple-element.327.refs_2_.refs_1_, f32[1,2176]{1,0:T(1,128)} %broadcast_select_fusion.refs_3_), custom_call_target="tpu_custom_call" | custom-call | flops 1 | bytes 1 | tf_op jit(solution)/shard_map/hidden/pallas_call | solution.py:814
  239.1 14.1 %token_dot.3 = bf16[1152,2176]{1,0:T(8,128)(2,1)} custom-call(bf16[1536,1152]{1,0:T(8,128)(2,1)} %pad_maximum_fusion.left_ref.refs_0_, bf16[1536,2176]{1,0:T(8,128)(2,1)} %get-tuple-element.428.right_ref.refs_0_), custom_call_target="tpu_custom_call" | custom-call | flops 1 | bytes 1 | tf_op jit(solution)/shard_map/token_dot/pallas_call | solution.py:241
  259.3 14.6 %grad_pre.1 = (bf16[1536,2176]{1,0:T(8,128)(2,1)}, f32[1,2176]{1,0:T(1,128)}) custom-call(bf16[1536,1152]{1,0:T(8,128)(2,1)} %pad_maximum_fusion.left_ref.refs_0_, bf16[1152,2176]{1,0:T(8,128)(2,1)} %assemble.5.refs_1_, bf16[1536,2176]{1,0:T(8,128)(2,1)} %get-tuple-element.342.refs_2_), custom_call_target="tpu_custom_call" | custom-call | flops 1 | bytes 1 | tf_op jit(solution)/shard_map/grad_pre/pallas_call | solution.py:542
  273.8 14.5 %back.1 = (bf16[768,1152]{1,0:T(8,128)(2,1)}, bf16[768,1152]{1,0:T(8,128)(2,1)}) custom-call(bf16[1536,2176]{1,0:T(8,128)(2,1)} %get-tuple-element.347.refs_0_.right_ref, bf16[1152,2176]{1,0:T(8,128)(2,1)} %get-tuple-element.327.refs_2_.refs_1_), custom_call_target="tpu_custom_call" | custom-call | flops 1 | bytes 1 | tf_op jit(solution)/shard_map/back/pallas_call | solution.py:542
  288.5 14.3 %token_dot.4._ = bf16[1152,2816]{1,0:T(8,128)(2,1)} custom-call(bf16[1536,1152]{1,0:T(8,128)(2,1)} %get-tuple-element.346.left_ref, bf16[1536,2176]{1,0:T(8,128)(2,1)} %get-tuple-element.347.refs_0_.right_ref), custom_call_target="tpu_custom_call" | custom-call | flops 1 | bytes 1 | tf_op jit(solution)/shard_map/token_dot/pallas_call | solution.py:241
  304.0 12.3 %second_back.1 = (f32[768,1152]{1,0:T(8,128)}, bf16[768,1152]{1,0:T(8,128)(2,1)}, bf16[768,640]{1,0:T(8,128)(2,1)}, bf16[768,640]{1,0:T(8,128)(2,1)}, f32[8,1152]{1,0:T(8,128)}) custom-call(s32[1]{0:T(128)} %bitcast.1.core_ref, f32[768,1152]{1,0:T(8,128)} %get-tuple-element.429.x_ref.refs_2_, bf16[768,1152]{1,0:T(8,128)(2,1)} %get-tuple-element.348.refs_0_, ...), custom_call_target="tpu_custom_call" | custom-call | flops 1 | bytes 1 | tf_op jit(solution)/shard_map/second_back/pallas_call | solution.py:469
  328.2 21.9 %attend_back.3 = (bf16[2,3,256,640]{3,2,1,0:T(8,128)(2,1)}, bf16[2,3,256,1280]{3,2,1,0:T(8,128)(2,1)}, bf16[2,3,256,1280]{3,2,1,0:T(8,128)(2,1)}) custom-call(s32[3,4]{1,0:T(4,128)} %get-tuple-element.239.need_ref, s32[3,4,256,1]{3,2,1,0:T(8,128)} %get-tuple-element.241.col_ref, s32[3,1,512]{2,1,0:T(1,128)} %get-tuple-element.242.row_ref, ...), custom_call_target="tpu_custom_call" | custom-call | flops 1 | bytes 1 | tf_op jit(solution)/shard_map/attend_back/pallas_call | solution.py:1028
  355.8 18.3 %attend_back.4 = (bf16[2,3,256,640]{3,2,1,0:T(8,128)(2,1)}, bf16[2,3,256,1280]{3,2,1,0:T(8,128)(2,1)}, bf16[2,3,256,1280]{3,2,1,0:T(8,128)(2,1)}) custom-call(s32[3,4]{1,0:T(4,128)} %get-tuple-element.239.need_ref, s32[3,4,256,1]{3,2,1,0:T(8,128)} %get-tuple-element.241.col_ref, ...), custom_call_target="tpu_custom_call", output_to_operand_aliasing={{0}: (12, {}), {1}: (13, {}), {2}: (14, {})} | custom-call | flops 1 | bytes 1 | tf_op jit(solution)/shard_map/attend_back/pallas_call | solution.py:1028
  375.5 23.4 %attend_back.5 = (bf16[2,3,256,640]{3,2,1,0:T(8,128)(2,1)}, bf16[2,3,256,1280]{3,2,1,0:T(8,128)(2,1)}, bf16[2,3,256,1280]{3,2,1,0:T(8,128)(2,1)}) custom-call(s32[3,4]{1,0:T(4,128)} %get-tuple-element.239.need_ref, s32[3,4,256,1]{3,2,1,0:T(8,128)} %get-tuple-element.241.col_ref, ...), custom_call_target="tpu_custom_call", output_to_operand_aliasing={{0}: (12, {}), {1}: (13, {}), {2}: (14, {})} | custom-call | flops 1 | bytes 1 | tf_op jit(solution)/shard_map/attend_back/pallas_call | solution.py:1028
  399.7 9.7 %back_far.1 = (bf16[768,1152]{1,0:T(8,128)(2,1)}, bf16[768,1152]{1,0:T(8,128)(2,1)}) custom-call(bf16[1536,1280]{1,0:T(8,128)(2,1)} %bitcast.55, bf16[1152,1280]{1,0:T(8,128)(2,1)} %get-tuple-element.392.refs_1_.refs_3_), custom_call_target="tpu_custom_call" | custom-call | flops 1 | bytes 1 | tf_op jit(solution)/shard_map/back_far/pallas_call | solution.py:542
  410.8 17.5 %weight_grad.2 = (bf16[576,1280]{1,0:T(8,128)(2,1)}, bf16[576,1280]{1,0:T(8,128)(2,1)}, f32[8,1280]{1,0:T(8,128)}) custom-call(s32[9]{0:T(128)} %pad_add_fusion.pos_ref, bf16[1536,1152]{1,0:T(8,128)(2,1)} %norm.2.refs_0_, bf16[1536,1152]{1,0:T(8,128)(2,1)} %norm.3.refs_0_.refs_1_, bf16[1536,1280]{1,0:T(8,128)(2,1)} %bitcast.53, bf16[1536,1280]{1,0:T(8,128)(2,1)} %bitcast.56), custom_call_target="tpu_custom_call" | custom-call | flops 1 | bytes 1 | tf_op jit(solution)/shard_map/weight_grad/pallas_call | solution.py:190
  430.6 13.4 %back_near.1 = (bf16[768,1152]{1,0:T(8,128)(2,1)}, bf16[768,1152]{1,0:T(8,128)(2,1)}) custom-call(bf16[1536,640]{1,0:T(8,128)(2,1)} %bitcast.58, bf16[1536,1280]{1,0:T(8,128)(2,1)} %bitcast.54, bf16[1152,640]{1,0:T(8,128)(2,1)} %get-tuple-element.271.weight_ref.refs_1_.refs_2_, bf16[1152,1280]{1,0:T(8,128)(2,1)} %get-tuple-element.392.refs_1_.refs_3_), custom_call_target="tpu_custom_call" | custom-call | flops 1 | bytes 1 | tf_op jit(solution)/shard_map/back_near/pallas_call | solution.py:542
  463.2 12.3 %collective-permute-done.35 = bf16[576,1280]{1,0:T(8,128)(2,1)} collective-permute-done((bf16[576,1280]{1,0:T(8,128)(2,1)}, bf16[576,1280]{1,0:T(8,128)(2,1)}, u32[]{:S(2)}, u32[]{:S(2)}) %collective-permute-start.35) | collective-permute-done | bytes 1474592 | tf_op jit(solution)/shard_map/ppermute | solution.py:42
  498.3 10.1 %down_own.1 = bf16[768,1152]{1,0:T(8,128)(2,1)} custom-call(bf16[1536,2176]{1,0:T(8,128)(2,1)} %get-tuple-element.428.right_ref.refs_0_, bf16[1152,2176]{1,0:T(8,128)(2,1)} %assemble.5.refs_1_, f32[768,1152]{1,0:T(8,128)} %get-tuple-element.429.x_ref.refs_2_, bf16[768,1152]{1,0:T(8,128)(2,1)} %copy-done.6, f32[1,1152]{1,0:T(1,128)} %get-tuple-element.470.refs_4_), custom_call_target="tpu_custom_call" | custom-call | flops 1 | bytes 1 | tf_op jit(solution)/shard_map/down_own/pallas_call | solution.py:542
  520.9 19.3 %collective-permute-done.42 = bf16[144,640]{1,0:T(8,128)(2,1)S(1)} collective-permute-done((bf16[144,640]{1,0:T(8,128)(2,1)}, bf16[144,640]{1,0:T(8,128)(2,1)S(1)}, u32[]{:S(2)}, u32[]{:S(2)}) %collective-permute-start.42) | collective-permute-done | bytes 184352 | tf_op jit(solution)/shard_map/ppermute | solution.py:42
  545.5 11.1 %collective-permute-done.46 = bf16[144,640]{1,0:T(8,128)(2,1)S(1)} collective-permute-done((bf16[144,640]{1,0:T(8,128)(2,1)S(1)}, bf16[144,640]{1,0:T(8,128)(2,1)S(1)}, u32[]{:S(2)}, u32[]{:S(2)}) %collective-permute-start.46) | collective-permute-done | bytes 184352 | tf_op jit(solution)/shard_map/ppermute | solution.py:42
  (254 shorter events, 229.1 us)
Async XLA Ops:
  7.2 367.0 %reduce-scatter.3.cloned.1.call-start = ((), (), s32[]{:S(2)}) async-start(), calls=%async_computation.2 | async-start | bytes 5640192 | tf_op jit(solution)/shard_map/reduce_scatter | solution.py:1262
  7.3 34.7 %collective-permute-start.3 = (bf16[768,1152]{1,0:T(8,128)(2,1)}, bf16[768,1152]{1,0:T(8,128)(2,1)}, u32[]{:S(2)}, u32[]{:S(2)}) collective-permute-start(bf16[768,1152]{1,0:T(8,128)(2,1)} %bitcast.72), channel_id=1, source_target_pairs={{0,8},{8,0},{16,24},{24,16},{1,9},{9,1},{17,25},{25,17},{2,10},{10... | collective-permute-start | bytes 5308424 | tf_op jit(solution)/shard_map/ppermute | solution.py:42
  41.9 29.5 %collective-permute-start.9 = (bf16[768,1152]{1,0:T(8,128)(2,1)S(1)}, bf16[768,1152]{1,0:T(8,128)(2,1)S(1)}, u32[]{:S(2)}, u32[]{:S(2)}) collective-permute-start(bf16[768,1152]{1,0:T(8,128)(2,1)S(1)} %bitcast.63), channel_id=1, source_target_pairs={{0,8},{8,0},{16,24},{24,16},{1,9},{9,1},{17,25},{25,17},{2,10},{10... | collective-permute-start | bytes 5308424 | tf_op jit(solution)/shard_map/ppermute | solution.py:42
  41.9 41.1 %collective-permute-start.5 = (bf16[768,1152]{1,0:T(8,128)(2,1)S(1)}, bf16[768,1152]{1,0:T(8,128)(2,1)}, u32[]{:S(2)}, u32[]{:S(2)}) collective-permute-start(bf16[768,1152]{1,0:T(8,128)(2,1)S(1)} %bitcast.64), channel_id=1, source_target_pairs={{0,16},{8,24},{16,0},{24,8},{1,17},{9,25},{17,1},{25,9},{2,18},{10... | collective-permute-start | bytes 5308424 | tf_op jit(solution)/shard_map/ppermute | solution.py:42
  83.1 37.7 %collective-permute-start.16 = (bf16[768,1152]{1,0:T(8,128)(2,1)}, bf16[768,1152]{1,0:T(8,128)(2,1)S(1)}, u32[]{:S(2)}, u32[]{:S(2)}) collective-permute-start(bf16[768,1152]{1,0:T(8,128)(2,1)} %collective-permute-done.5.refs_0_), channel_id=1, source_target_pairs={{0,8},{8,0},{16,24},{24,16},{1,9},{9,1},{17,25},{25,17},{2,10},{10... | collective-permute-start | bytes 5308424 | tf_op jit(solution)/shard_map/ppermute | solution.py:42
  83.1 37.7 %collective-permute-start.15 = (bf16[144,2816]{1,0:T(8,128)(2,1)}, bf16[144,2816]{1,0:T(8,128)(2,1)S(1)}, u32[]{:S(2)}, u32[]{:S(2)}) collective-permute-start(bf16[144,2816]{1,0:T(8,128)(2,1)} %get-tuple-element.255.refs_0_), channel_id=1, source_target_pairs={{0,2},{1,3},{2,0},{3,1},{4,6},{5,7},{6,4},{7,5},{8,10},{9,11},{10,... | collective-permute-start | bytes 2433032 | tf_op jit(solution)/shard_map/ppermute | solution.py:42
  83.9 44.7 %collective-permute-start.13 = (bf16[144,2816]{1,0:T(8,128)(2,1)}, bf16[144,2816]{1,0:T(8,128)(2,1)S(1)}, u32[]{:S(2)}, u32[]{:S(2)}) collective-permute-start(bf16[144,2816]{1,0:T(8,128)(2,1)} %get-tuple-element.255.refs_0_), channel_id=1, source_target_pairs={{0,1},{1,0},{2,3},{3,2},{4,5},{5,4},{6,7},{7,6},{8,9},{9,8},{10,11... | collective-permute-start | bytes 2433032 | tf_op jit(solution)/shard_map/ppermute | solution.py:42
  84.4 44.2 %collective-permute-start.14 = (bf16[144,2816]{1,0:T(8,128)(2,1)}, bf16[144,2816]{1,0:T(8,128)(2,1)}, u32[]{:S(2)}, u32[]{:S(2)}) collective-permute-start(bf16[144,2816]{1,0:T(8,128)(2,1)} %get-tuple-element.255.refs_0_), channel_id=1, source_target_pairs={{0,4},{1,5},{2,6},{3,7},{4,0},{5,1},{6,2},{7,3},{8,12},{9,13},{10,... | collective-permute-start | bytes 2433032 | tf_op jit(solution)/shard_map/ppermute | solution.py:42
  128.7 47.7 %collective-permute-start.17 = (bf16[144,2816]{1,0:T(8,128)(2,1)}, bf16[144,2816]{1,0:T(8,128)(2,1)}, u32[]{:S(2)}, u32[]{:S(2)}) collective-permute-start(bf16[144,2816]{1,0:T(8,128)(2,1)} %collective-permute-done.14.refs_4_), channel_id=1, source_target_pairs={{0,1},{1,0},{2,3},{3,2},{4,5},{5,4},{6,7},{7,6},{8,9},{9,8},{10,11... | collective-permute-start | bytes 2433032 | tf_op jit(solution)/shard_map/ppermute | solution.py:42
  152.2 32.2 %collective-permute-start.20 = (bf16[144,2816]{1,0:T(8,128)(2,1)S(1)}, bf16[144,2816]{1,0:T(8,128)(2,1)S(1)}, u32[]{:S(2)}, u32[]{:S(2)}) collective-permute-start(bf16[144,2816]{1,0:T(8,128)(2,1)S(1)} %collective-permute-done.19.refs_6_), channel_id=1, source_target_pairs={{0,1},{1,0},{2,3},{3,2},{4,5},{5,4},{6,7},{7,6},{8,9},{9,8},{10,11... | collective-permute-start | bytes 2433032 | tf_op jit(solution)/shard_map/ppermute | solution.py:42
  152.3 44.3 %collective-permute-start.10 = (bf16[144,2176]{1,0:T(8,128)(2,1)S(1)}, bf16[144,2176]{1,0:T(8,128)(2,1)S(1)}, u32[]{:S(2)}, u32[]{:S(2)}) collective-permute-start(bf16[144,2176]{1,0:T(8,128)(2,1)S(1)} %copy-done.26), channel_id=1, source_target_pairs={{0,1},{1,0},{2,3},{3,2},{4,5},{5,4},{6,7},{7,6},{8,9},{9,8},{10,11... | collective-permute-start | bytes 1880072 | tf_op jit(solution)/shard_map/ppermute | solution.py:42
  154.3 42.3 %collective-permute-start.11 = (bf16[144,2176]{1,0:T(8,128)(2,1)S(1)}, bf16[144,2176]{1,0:T(8,128)(2,1)}, u32[]{:S(2)}, u32[]{:S(2)}) collective-permute-start(bf16[144,2176]{1,0:T(8,128)(2,1)S(1)} %copy-done.26), channel_id=1, source_target_pairs={{0,2},{1,3},{2,0},{3,1},{4,6},{5,7},{6,4},{7,5},{8,10},{9,11},{10,... | collective-permute-start | bytes 1880072 | tf_op jit(solution)/shard_map/ppermute | solution.py:42
  154.5 42.1 %collective-permute-start.12 = (bf16[144,2176]{1,0:T(8,128)(2,1)S(1)}, bf16[144,2176]{1,0:T(8,128)(2,1)}, u32[]{:S(2)}, u32[]{:S(2)}) collective-permute-start(bf16[144,2176]{1,0:T(8,128)(2,1)S(1)} %copy-done.26), channel_id=1, source_target_pairs={{0,4},{1,5},{2,6},{3,7},{4,0},{5,1},{6,2},{7,3},{8,12},{9,13},{10,... | collective-permute-start | bytes 1880072 | tf_op jit(solution)/shard_map/ppermute | solution.py:42
  215.4 37.8 %collective-permute-start.26 = (bf16[144,2176]{1,0:T(8,128)(2,1)}, bf16[144,2176]{1,0:T(8,128)(2,1)S(1)}, u32[]{:S(2)}, u32[]{:S(2)}) collective-permute-start(bf16[144,2176]{1,0:T(8,128)(2,1)} %collective-permute-done.12.refs_4_), channel_id=1, source_target_pairs={{0,1},{1,0},{2,3},{3,2},{4,5},{5,4},{6,7},{7,6},{8,9},{9,8},{10,11... | collective-permute-start | bytes 1880072 | tf_op jit(solution)/shard_map/ppermute | solution.py:42
  215.8 37.5 %collective-permute-start.27 = (bf16[144,2176]{1,0:T(8,128)(2,1)S(1)}, bf16[144,2176]{1,0:T(8,128)(2,1)}, u32[]{:S(2)}, u32[]{:S(2)}) collective-permute-start(bf16[144,2176]{1,0:T(8,128)(2,1)S(1)} %collective-permute-done.21.refs_6_), channel_id=1, source_target_pairs={{0,1},{1,0},{2,3},{3,2},{4,5},{5,4},{6,7},{7,6},{8,9},{9,8},{10,11... | collective-permute-start | bytes 1880072 | tf_op jit(solution)/shard_map/ppermute | solution.py:42
  254.1 263.0 %reduce-scatter.5.cloned.1.call-start = ((), (), s32[]{:S(2)}) async-start(), calls=%async_computation.3 | async-start | bytes 7299072 | tf_op jit(solution)/shard_map/reduce_scatter | solution.py:1319
  429.9 45.5 %collective-permute-start.36 = (bf16[768,1152]{1,0:T(8,128)(2,1)}, bf16[768,1152]{1,0:T(8,128)(2,1)}, u32[]{:S(2)}, u32[]{:S(2)}) collective-permute-start(bf16[768,1152]{1,0:T(8,128)(2,1)} %add_convert_fusion), channel_id=1, source_target_pairs={{0,16},{8,24},{16,0},{24,8},{1,17},{9,25},{17,1},{25,9},{2,18},{10... | collective-permute-start | bytes 5308424 | tf_op jit(solution)/shard_map/ppermute | solution.py:42
  430.6 44.9 %collective-permute-start.35 = (bf16[576,1280]{1,0:T(8,128)(2,1)}, bf16[576,1280]{1,0:T(8,128)(2,1)}, u32[]{:S(2)}, u32[]{:S(2)}) collective-permute-start(bf16[576,1280]{1,0:T(8,128)(2,1)} %get-tuple-element.400), channel_id=1, source_target_pairs={{0,1},{1,0},{2,3},{3,2},{4,5},{5,4},{6,7},{7,6},{8,9},{9,8},{10,11... | collective-permute-start | bytes 4423688 | tf_op jit(solution)/shard_map/ppermute | solution.py:42
  444.0 34.5 %collective-permute-start.37 = (bf16[768,1152]{1,0:T(8,128)(2,1)}, bf16[768,1152]{1,0:T(8,128)(2,1)}, u32[]{:S(2)}, u32[]{:S(2)}) collective-permute-start(bf16[768,1152]{1,0:T(8,128)(2,1)} %get-tuple-element.407), channel_id=1, source_target_pairs={{0,8},{8,0},{16,24},{24,16},{1,9},{9,1},{17,25},{25,17},{2,10},{10... | collective-permute-start | bytes 5308424 | tf_op jit(solution)/shard_map/ppermute | solution.py:42
  453.0 37.9 %collective-permute-start.33 = (bf16[768,1152]{1,0:T(8,128)(2,1)}, bf16[768,1152]{1,0:T(8,128)(2,1)S(1)}, u32[]{:S(2)}, u32[]{:S(2)}) collective-permute-start(bf16[768,1152]{1,0:T(8,128)(2,1)} %down_pair.1), channel_id=1, source_target_pairs={{0,8},{8,0},{16,24},{24,16},{1,9},{9,1},{17,25},{25,17},{2,10},{10... | collective-permute-start | bytes 5308424 | tf_op jit(solution)/shard_map/ppermute | solution.py:42
  461.2 29.6 %collective-permute-start.34 = (bf16[576,640]{1,0:T(8,128)(2,1)}, bf16[576,640]{1,0:T(8,128)(2,1)S(1)}, u32[]{:S(2)}, u32[]{:S(2)}) collective-permute-start(bf16[576,640]{1,0:T(8,128)(2,1)} %get-tuple-element.411), channel_id=1, source_target_pairs={{0,1},{1,0},{2,3},{3,2},{4,5},{5,4},{6,7},{7,6},{8,9},{9,8},{10,11... | collective-permute-start | bytes 2211848 | tf_op jit(solution)/shard_map/ppermute | solution.py:42
  478.5 32.6 %collective-permute-start.38 = (bf16[288,1280]{1,0:T(8,128)(2,1)}, bf16[288,1280]{1,0:T(8,128)(2,1)}, u32[]{:S(2)}, u32[]{:S(2)}) collective-permute-start(bf16[288,1280]{1,0:T(8,128)(2,1)} %get-tuple-element.452), channel_id=1, source_target_pairs={{0,2},{1,3},{2,0},{3,1},{4,6},{5,7},{6,4},{7,5},{8,10},{9,11},{10,... | collective-permute-start | bytes 2211848 | tf_op jit(solution)/shard_map/ppermute | solution.py:42
  517.1 28.1 %collective-permute-start.47 = (bf16[144,2816]{1,0:T(8,128)(2,1)}, bf16[144,2816]{1,0:T(8,128)(2,1)S(1)}, u32[]{:S(2)}, u32[]{:S(2)}) collective-permute-start(bf16[144,2816]{1,0:T(8,128)(2,1)} %reduce-scatter.5.cloned.1.call-done), channel_id=1, source_target_pairs={{0,16},{8,24},{16,0},{24,8},{1,17},{9,25},{17,1},{25,9},{2,18},{10... | collective-permute-start | bytes 2433032 | tf_op jit(solution)/shard_map/ppermute | solution.py:42
  518.8 44.9 %collective-permute-start.52 = (f32[144,2176]{1,0:T(8,128)S(1)}, f32[144,2176]{1,0:T(8,128)S(1)}, u32[]{:S(2)}, u32[]{:S(2)}) collective-permute-start(f32[144,2176]{1,0:T(8,128)S(1)} %convert_add_fusion.1), channel_id=1, source_target_pairs={{0,8},{8,0},{16,24},{24,16},{1,9},{9,1},{17,25},{25,17},{2,10},{10... | collective-permute-start | bytes 3760136 | tf_op jit(solution)/shard_map/ppermute | solution.py:42
  (71 other events, 891.3 us)
Sparse Core Ops, SparseCore 0:
  253.4 97.9 reduce-scatter.2
  355.9 133.4 reduce-scatter.4

commit v12 on v11

--- a/solution.py
+++ b/solution.py
@@ -490,7 +490,7 @@
 
 def rows_matmul(name, lefts, weights, finish, extras, outs, dims=((1,), (0,)), split=False, first_row=0):
     rows = outs[0].shape[0]
-    block = 384 if split and rows % 768 == 0 else 512 if not split and rows % 512 == 0 else row_block(rows)
+    block = 512 if not split and rows % 512 == 0 else 384 if rows % 768 == 0 else row_block(rows)
     steps = rows // block
     half = steps // 2
     count, terms = len(lefts), len(lefts) + len(weights)
@@ -792,7 +792,7 @@
 def hidden(arrays, weight, bias):
     rows, width = arrays[0].shape
     cols = weight.shape[1]
-    block = row_block(rows)
+    block = 384 if rows % 384 == 0 else row_block(rows)
     steps, count = rows // block, len(arrays)
 
     def kernel(*refs):

time: 589 us -> 590 us (level)
  waiting for transfers between devices: 122 us -> 130 us
    ppermute x54, waiting for transfers between devices: 122 us -> 130 us  [swap(): return lax.ppermute(array, axis, [(i, i ^ bits) for i in range(size)])]
where the time goes in v12:
time: 590 us; the launch traced here: 580 us
  Pallas kernels  351 us (59%)
  waiting for transfers between devices  130 us (22%)
  starting transfers between devices  41.4 us (7%)
  other arithmetic  24.7 us (4%)
  local copies, waits for them, and re-layouts  17.9 us (3%)
  between operations  14.8 us (3%)
    ppermute x54, waiting for transfers between devices, swap(): return lax.ppermute(array, axis, [(i, i ^ bits) for i in range(size)])  130 us
    pallas_call x9, Pallas kernels, rows_matmul(): pl.pallas_call(kernel, out_shape=shapes, grid=(steps,), in_specs=[pl.Bloc...  96.9 us
    pallas_call x3, Pallas kernels, attend_back(): pl.pallas_call(functools.partial(attend_back_kernel, row, heads, blocks,...  58.7 us
    ppermute x54, starting transfers between devices, swap(): return lax.ppermute(array, axis, [(i, i ^ bits) for i in range(size)])  41.2 us
    pallas_call x3, Pallas kernels, token_dot(): pl.pallas_call(kernel, out_shape=jax.ShapeDtypeStruct((width, cols + room...  35.2 us
    pallas_call x3, Pallas kernels, attend(): pl.pallas_call(functools.partial(attend_kernel, row, heads, blocks, padde...  34.5 us
    pallas_call x2, Pallas kernels, weight_grad(): pl.pallas_call(functools.partial(weight_grad_kernel, pairs, count, rows),...  25.4 us
    pallas_call x1, Pallas kernels, hidden(): pl.pallas_call(kernel, out_shape=(jax.ShapeDtypeStruct((count * rows, col...  17.9 us
  transfers between devices with their start and end apart: 56, of which 22 were waited for; matrix products, arithmetic and copies ran while one was open for 5% of the time, Pallas kernels for 61%

profile of v12, /device:TPU:0, one launch (start us, length us, event | category | flops | bytes accessed | tf_op | source)
XLA Modules:
  0.0 579.5 jit_solution(16836065438365002867)
XLA Ops:
  26.2 13.3 %collective-permute-done.1.refs_2_ = bf16[144,1920]{1,0:T(8,128)(2,1)} collective-permute-done((bf16[144,1920]{1,0:T(8,128)(2,1)}, bf16[144,1920]{1,0:T(8,128)(2,1)}, u32[]{:S(2)}, u32[]{:S(2)}) %collective-permute-start.1) | collective-permute-done | bytes 552992 | tf_op jit(solution)/shard_map/ppermute | solution.py:42
  45.9 12.4 %collective-permute-done.4.refs_6_ = bf16[144,1920]{1,0:T(8,128)(2,1)S(1)} collective-permute-done((bf16[144,1920]{1,0:T(8,128)(2,1)}, bf16[144,1920]{1,0:T(8,128)(2,1)S(1)}, u32[]{:S(2)}, u32[]{:S(2)}) %collective-permute-start.4) | collective-permute-done | bytes 552992 | tf_op jit(solution)/shard_map/ppermute | solution.py:42
  62.4 9.0 %collective-permute-done.7.refs_3_ = bf16[144,1920]{1,0:T(8,128)(2,1)S(1)} collective-permute-done((bf16[144,1920]{1,0:T(8,128)(2,1)}, bf16[144,1920]{1,0:T(8,128)(2,1)S(1)}, u32[]{:S(2)}, u32[]{:S(2)}) %collective-permute-start.7) | collective-permute-done | bytes 552992 | tf_op jit(solution)/shard_map/ppermute | solution.py:42
  71.4 10.7 %collective-permute-done.6.refs_7_ = bf16[144,1920]{1,0:T(8,128)(2,1)S(1)} collective-permute-done((bf16[144,1920]{1,0:T(8,128)(2,1)S(1)}, bf16[144,1920]{1,0:T(8,128)(2,1)S(1)}, u32[]{:S(2)}, u32[]{:S(2)}) %collective-permute-start.6) | collective-permute-done | bytes 552992 | tf_op jit(solution)/shard_map/ppermute | solution.py:42
  109.0 8.9 %near.1 = bf16[1536,1280]{1,0:T(8,128)(2,1)} custom-call(bf16[1536,1152]{1,0:T(8,128)(2,1)} %norm.2.refs_0_, bf16[1152,1280]{1,0:T(8,128)(2,1)} %get-tuple-element.392.refs_1_.refs_3_, f32[1,1280]{1,0:T(1,128)} %get-tuple-element.267.refs_2_), custom_call_target="tpu_custom_call" | custom-call | flops 1 | bytes 1 | tf_op jit(solution)/shard_map/near/pallas_call | solution.py:542
  139.6 12.6 %attend.3 = (bf16[3,256,640]{2,1,0:T(8,128)(2,1)}, bf16[3,256,640]{2,1,0:T(8,128)(2,1)}, f32[3,8,512]{2,1,0:T(8,128)}) custom-call(s32[3,4]{1,0:T(4,128)} %get-tuple-element.239.need_ref, s32[3,512,1]{2,1,0:T(8,128)} %get-tuple-element.243.col_ref, s32[3,4,256]{2,1,0:T(4,128)} %get-tuple-element.240.row_ref, bf16[2,3,256,640]{3,2,1,0:T(8,128)(2,1)} %bitcast.47, ...), custom_call_target="tpu_custom_call" | custom-call | flops 1 | bytes 1 | tf_op jit(solution)/shard_map/attend/pallas_call | solution.py:930
  154.6 10.8 %attend.4 = (bf16[3,256,640]{2,1,0:T(8,128)(2,1)}, bf16[3,256,640]{2,1,0:T(8,128)(2,1)}, f32[3,8,512]{2,1,0:T(8,128)}) custom-call(s32[3,4]{1,0:T(4,128)} %get-tuple-element.239.need_ref, s32[3,512,1]{2,1,0:T(8,128)} %get-tuple-element.243.col_ref, ...), custom_call_target="tpu_custom_call", output_to_operand_aliasing={{0}: (6, {}), {1}: (7, {}), {2}: (8, {})} | custom-call | flops 1 | bytes 1 | tf_op jit(solution)/shard_map/attend/pallas_call | solution.py:930
  165.4 11.1 %attend.5 = (bf16[3,256,640]{2,1,0:T(8,128)(2,1)}, bf16[3,256,640]{2,1,0:T(8,128)(2,1)}, f32[3,8,512]{2,1,0:T(8,128)}) custom-call(s32[3,4]{1,0:T(4,128)} %get-tuple-element.239.need_ref, s32[3,512,1]{2,1,0:T(8,128)} %get-tuple-element.243.col_ref, ...), custom_call_target="tpu_custom_call", output_to_operand_aliasing={{0}: (6, {}), {1}: (7, {}), {2}: (8, {})} | custom-call | flops 1 | bytes 1 | tf_op jit(solution)/shard_map/attend/pallas_call | solution.py:930
  220.4 17.9 %hidden.1 = (bf16[1536,2176]{1,0:T(8,128)(2,1)}, bf16[1536,2176]{1,0:T(8,128)(2,1)}, bf16[1536,1152]{1,0:T(8,128)(2,1)}) custom-call(bf16[768,1152]{1,0:T(8,128)(2,1)} %get-tuple-element.325.refs_0_, bf16[768,1152]{1,0:T(8,128)(2,1)} %copy-done.9, bf16[1152,2176]{1,0:T(8,128)(2,1)} %get-tuple-element.327.refs_2_.refs_1_, f32[1,2176]{1,0:T(1,128)} %broadcast_select_fusion.refs_3_), custom_call_target="tpu_custom_call" | custom-call | flops 1 | bytes 1 | tf_op jit(solution)/shard_map/hidden/pallas_call | solution.py:814
  238.3 14.1 %token_dot.3 = bf16[1152,2176]{1,0:T(8,128)(2,1)} custom-call(bf16[1536,1152]{1,0:T(8,128)(2,1)} %pad_maximum_fusion.left_ref.refs_0_, bf16[1536,2176]{1,0:T(8,128)(2,1)} %get-tuple-element.428.right_ref.refs_0_), custom_call_target="tpu_custom_call" | custom-call | flops 1 | bytes 1 | tf_op jit(solution)/shard_map/token_dot/pallas_call | solution.py:241
  258.4 14.6 %grad_pre.1 = (bf16[1536,2176]{1,0:T(8,128)(2,1)}, f32[1,2176]{1,0:T(1,128)}) custom-call(bf16[1536,1152]{1,0:T(8,128)(2,1)} %pad_maximum_fusion.left_ref.refs_0_, bf16[1152,2176]{1,0:T(8,128)(2,1)} %assemble.5.refs_1_, bf16[1536,2176]{1,0:T(8,128)(2,1)} %get-tuple-element.342.refs_2_), custom_call_target="tpu_custom_call" | custom-call | flops 1 | bytes 1 | tf_op jit(solution)/shard_map/grad_pre/pallas_call | solution.py:542
  273.0 14.5 %back.1 = (bf16[768,1152]{1,0:T(8,128)(2,1)}, bf16[768,1152]{1,0:T(8,128)(2,1)}) custom-call(bf16[1536,2176]{1,0:T(8,128)(2,1)} %get-tuple-element.347.refs_0_.right_ref, bf16[1152,2176]{1,0:T(8,128)(2,1)} %get-tuple-element.327.refs_2_.refs_1_), custom_call_target="tpu_custom_call" | custom-call | flops 1 | bytes 1 | tf_op jit(solution)/shard_map/back/pallas_call | solution.py:542
  287.6 14.3 %token_dot.4._ = bf16[1152,2816]{1,0:T(8,128)(2,1)} custom-call(bf16[1536,1152]{1,0:T(8,128)(2,1)} %get-tuple-element.346.left_ref, bf16[1536,2176]{1,0:T(8,128)(2,1)} %get-tuple-element.347.refs_0_.right_ref), custom_call_target="tpu_custom_call" | custom-call | flops 1 | bytes 1 | tf_op jit(solution)/shard_map/token_dot/pallas_call | solution.py:241
  303.1 12.3 %second_back.1 = (f32[768,1152]{1,0:T(8,128)}, bf16[768,1152]{1,0:T(8,128)(2,1)}, bf16[768,640]{1,0:T(8,128)(2,1)}, bf16[768,640]{1,0:T(8,128)(2,1)}, f32[8,1152]{1,0:T(8,128)}) custom-call(s32[1]{0:T(128)} %bitcast.1.core_ref, f32[768,1152]{1,0:T(8,128)} %get-tuple-element.429.x_ref.refs_2_, bf16[768,1152]{1,0:T(8,128)(2,1)} %get-tuple-element.348.refs_0_, ...), custom_call_target="tpu_custom_call" | custom-call | flops 1 | bytes 1 | tf_op jit(solution)/shard_map/second_back/pallas_call | solution.py:469
  327.4 21.9 %attend_back.3 = (bf16[2,3,256,640]{3,2,1,0:T(8,128)(2,1)}, bf16[2,3,256,1280]{3,2,1,0:T(8,128)(2,1)}, bf16[2,3,256,1280]{3,2,1,0:T(8,128)(2,1)}) custom-call(s32[3,4]{1,0:T(4,128)} %get-tuple-element.239.need_ref, s32[3,4,256,1]{3,2,1,0:T(8,128)} %get-tuple-element.241.col_ref, s32[3,1,512]{2,1,0:T(1,128)} %get-tuple-element.242.row_ref, ...), custom_call_target="tpu_custom_call" | custom-call | flops 1 | bytes 1 | tf_op jit(solution)/shard_map/attend_back/pallas_call | solution.py:1028
  355.0 18.3 %attend_back.4 = (bf16[2,3,256,640]{3,2,1,0:T(8,128)(2,1)}, bf16[2,3,256,1280]{3,2,1,0:T(8,128)(2,1)}, bf16[2,3,256,1280]{3,2,1,0:T(8,128)(2,1)}) custom-call(s32[3,4]{1,0:T(4,128)} %get-tuple-element.239.need_ref, s32[3,4,256,1]{3,2,1,0:T(8,128)} %get-tuple-element.241.col_ref, ...), custom_call_target="tpu_custom_call", output_to_operand_aliasing={{0}: (12, {}), {1}: (13, {}), {2}: (14, {})} | custom-call | flops 1 | bytes 1 | tf_op jit(solution)/shard_map/attend_back/pallas_call | solution.py:1028
  374.6 18.4 %attend_back.5 = (bf16[2,3,256,640]{3,2,1,0:T(8,128)(2,1)}, bf16[2,3,256,1280]{3,2,1,0:T(8,128)(2,1)}, bf16[2,3,256,1280]{3,2,1,0:T(8,128)(2,1)}) custom-call(s32[3,4]{1,0:T(4,128)} %get-tuple-element.239.need_ref, s32[3,4,256,1]{3,2,1,0:T(8,128)} %get-tuple-element.241.col_ref, ...), custom_call_target="tpu_custom_call", output_to_operand_aliasing={{0}: (12, {}), {1}: (13, {}), {2}: (14, {})} | custom-call | flops 1 | bytes 1 | tf_op jit(solution)/shard_map/attend_back/pallas_call | solution.py:1028
  393.9 10.8 %back_far.1 = (bf16[768,1152]{1,0:T(8,128)(2,1)}, bf16[768,1152]{1,0:T(8,128)(2,1)}) custom-call(bf16[1536,1280]{1,0:T(8,128)(2,1)} %bitcast.55, bf16[1152,1280]{1,0:T(8,128)(2,1)} %get-tuple-element.392.refs_1_.refs_3_), custom_call_target="tpu_custom_call" | custom-call | flops 1 | bytes 1 | tf_op jit(solution)/shard_map/back_far/pallas_call | solution.py:542
  406.0 17.4 %weight_grad.2 = (bf16[576,1280]{1,0:T(8,128)(2,1)}, bf16[576,1280]{1,0:T(8,128)(2,1)}, f32[8,1280]{1,0:T(8,128)}) custom-call(s32[9]{0:T(128)} %pad_add_fusion.pos_ref, bf16[1536,1152]{1,0:T(8,128)(2,1)} %norm.2.refs_0_, bf16[1536,1152]{1,0:T(8,128)(2,1)} %norm.3.refs_0_.refs_1_, bf16[1536,1280]{1,0:T(8,128)(2,1)} %bitcast.53, bf16[1536,1280]{1,0:T(8,128)(2,1)} %bitcast.56), custom_call_target="tpu_custom_call" | custom-call | flops 1 | bytes 1 | tf_op jit(solution)/shard_map/weight_grad/pallas_call | solution.py:190
  426.5 13.5 %back_near.1 = (bf16[768,1152]{1,0:T(8,128)(2,1)}, bf16[768,1152]{1,0:T(8,128)(2,1)}) custom-call(bf16[1536,640]{1,0:T(8,128)(2,1)} %bitcast.58, bf16[1536,1280]{1,0:T(8,128)(2,1)} %bitcast.54, bf16[1152,640]{1,0:T(8,128)(2,1)} %get-tuple-element.271.weight_ref.refs_1_.refs_2_, bf16[1152,1280]{1,0:T(8,128)(2,1)} %get-tuple-element.392.refs_1_.refs_3_), custom_call_target="tpu_custom_call" | custom-call | flops 1 | bytes 1 | tf_op jit(solution)/shard_map/back_near/pallas_call | solution.py:542
  458.5 16.0 %collective-permute-done.35 = bf16[576,1280]{1,0:T(8,128)(2,1)} collective-permute-done((bf16[576,1280]{1,0:T(8,128)(2,1)}, bf16[576,1280]{1,0:T(8,128)(2,1)}, u32[]{:S(2)}, u32[]{:S(2)}) %collective-permute-start.35) | collective-permute-done | bytes 1474592 | tf_op jit(solution)/shard_map/ppermute | solution.py:42
  496.4 10.4 %down_own.1 = bf16[768,1152]{1,0:T(8,128)(2,1)} custom-call(bf16[1536,2176]{1,0:T(8,128)(2,1)} %get-tuple-element.428.right_ref.refs_0_, bf16[1152,2176]{1,0:T(8,128)(2,1)} %assemble.5.refs_1_, f32[768,1152]{1,0:T(8,128)} %get-tuple-element.429.x_ref.refs_2_, bf16[768,1152]{1,0:T(8,128)(2,1)} %copy-done.6, f32[1,1152]{1,0:T(1,128)} %get-tuple-element.470.refs_4_), custom_call_target="tpu_custom_call" | custom-call | flops 1 | bytes 1 | tf_op jit(solution)/shard_map/down_own/pallas_call | solution.py:542
  522.1 19.3 %collective-permute-done.42 = bf16[144,640]{1,0:T(8,128)(2,1)S(1)} collective-permute-done((bf16[144,640]{1,0:T(8,128)(2,1)}, bf16[144,640]{1,0:T(8,128)(2,1)S(1)}, u32[]{:S(2)}, u32[]{:S(2)}) %collective-permute-start.42) | collective-permute-done | bytes 184352 | tf_op jit(solution)/shard_map/ppermute | solution.py:42
  546.7 11.1 %collective-permute-done.46 = bf16[144,640]{1,0:T(8,128)(2,1)S(1)} collective-permute-done((bf16[144,640]{1,0:T(8,128)(2,1)S(1)}, bf16[144,640]{1,0:T(8,128)(2,1)S(1)}, u32[]{:S(2)}, u32[]{:S(2)}) %collective-permute-start.46) | collective-permute-done | bytes 184352 | tf_op jit(solution)/shard_map/ppermute | solution.py:42
  (254 shorter events, 231.1 us)
Async XLA Ops:
  7.2 366.1 %reduce-scatter.3.cloned.1.call-start = ((), (), s32[]{:S(2)}) async-start(), calls=%async_computation.2 | async-start | bytes 5640192 | tf_op jit(solution)/shard_map/reduce_scatter | solution.py:1262
  7.3 34.7 %collective-permute-start.3 = (bf16[768,1152]{1,0:T(8,128)(2,1)}, bf16[768,1152]{1,0:T(8,128)(2,1)}, u32[]{:S(2)}, u32[]{:S(2)}) collective-permute-start(bf16[768,1152]{1,0:T(8,128)(2,1)} %bitcast.72), channel_id=1, source_target_pairs={{0,8},{8,0},{16,24},{24,16},{1,9},{9,1},{17,25},{25,17},{2,10},{10... | collective-permute-start | bytes 5308424 | tf_op jit(solution)/shard_map/ppermute | solution.py:42
  41.9 29.5 %collective-permute-start.9 = (bf16[768,1152]{1,0:T(8,128)(2,1)S(1)}, bf16[768,1152]{1,0:T(8,128)(2,1)S(1)}, u32[]{:S(2)}, u32[]{:S(2)}) collective-permute-start(bf16[768,1152]{1,0:T(8,128)(2,1)S(1)} %bitcast.63), channel_id=1, source_target_pairs={{0,8},{8,0},{16,24},{24,16},{1,9},{9,1},{17,25},{25,17},{2,10},{10... | collective-permute-start | bytes 5308424 | tf_op jit(solution)/shard_map/ppermute | solution.py:42
  41.9 41.1 %collective-permute-start.5 = (bf16[768,1152]{1,0:T(8,128)(2,1)S(1)}, bf16[768,1152]{1,0:T(8,128)(2,1)}, u32[]{:S(2)}, u32[]{:S(2)}) collective-permute-start(bf16[768,1152]{1,0:T(8,128)(2,1)S(1)} %bitcast.64), channel_id=1, source_target_pairs={{0,16},{8,24},{16,0},{24,8},{1,17},{9,25},{17,1},{25,9},{2,18},{10... | collective-permute-start | bytes 5308424 | tf_op jit(solution)/shard_map/ppermute | solution.py:42
  83.1 37.7 %collective-permute-start.16 = (bf16[768,1152]{1,0:T(8,128)(2,1)}, bf16[768,1152]{1,0:T(8,128)(2,1)S(1)}, u32[]{:S(2)}, u32[]{:S(2)}) collective-permute-start(bf16[768,1152]{1,0:T(8,128)(2,1)} %collective-permute-done.5.refs_0_), channel_id=1, source_target_pairs={{0,8},{8,0},{16,24},{24,16},{1,9},{9,1},{17,25},{25,17},{2,10},{10... | collective-permute-start | bytes 5308424 | tf_op jit(solution)/shard_map/ppermute | solution.py:42
  83.1 37.7 %collective-permute-start.15 = (bf16[144,2816]{1,0:T(8,128)(2,1)}, bf16[144,2816]{1,0:T(8,128)(2,1)S(1)}, u32[]{:S(2)}, u32[]{:S(2)}) collective-permute-start(bf16[144,2816]{1,0:T(8,128)(2,1)} %get-tuple-element.255.refs_0_), channel_id=1, source_target_pairs={{0,2},{1,3},{2,0},{3,1},{4,6},{5,7},{6,4},{7,5},{8,10},{9,11},{10,... | collective-permute-start | bytes 2433032 | tf_op jit(solution)/shard_map/ppermute | solution.py:42
  83.9 44.7 %collective-permute-start.13 = (bf16[144,2816]{1,0:T(8,128)(2,1)}, bf16[144,2816]{1,0:T(8,128)(2,1)S(1)}, u32[]{:S(2)}, u32[]{:S(2)}) collective-permute-start(bf16[144,2816]{1,0:T(8,128)(2,1)} %get-tuple-element.255.refs_0_), channel_id=1, source_target_pairs={{0,1},{1,0},{2,3},{3,2},{4,5},{5,4},{6,7},{7,6},{8,9},{9,8},{10,11... | collective-permute-start | bytes 2433032 | tf_op jit(solution)/shard_map/ppermute | solution.py:42
  84.4 44.2 %collective-permute-start.14 = (bf16[144,2816]{1,0:T(8,128)(2,1)}, bf16[144,2816]{1,0:T(8,128)(2,1)}, u32[]{:S(2)}, u32[]{:S(2)}) collective-permute-start(bf16[144,2816]{1,0:T(8,128)(2,1)} %get-tuple-element.255.refs_0_), channel_id=1, source_target_pairs={{0,4},{1,5},{2,6},{3,7},{4,0},{5,1},{6,2},{7,3},{8,12},{9,13},{10,... | collective-permute-start | bytes 2433032 | tf_op jit(solution)/shard_map/ppermute | solution.py:42
  128.7 47.8 %collective-permute-start.17 = (bf16[144,2816]{1,0:T(8,128)(2,1)}, bf16[144,2816]{1,0:T(8,128)(2,1)}, u32[]{:S(2)}, u32[]{:S(2)}) collective-permute-start(bf16[144,2816]{1,0:T(8,128)(2,1)} %collective-permute-done.14.refs_4_), channel_id=1, source_target_pairs={{0,1},{1,0},{2,3},{3,2},{4,5},{5,4},{6,7},{7,6},{8,9},{9,8},{10,11... | collective-permute-start | bytes 2433032 | tf_op jit(solution)/shard_map/ppermute | solution.py:42
  152.2 32.2 %collective-permute-start.20 = (bf16[144,2816]{1,0:T(8,128)(2,1)S(1)}, bf16[144,2816]{1,0:T(8,128)(2,1)S(1)}, u32[]{:S(2)}, u32[]{:S(2)}) collective-permute-start(bf16[144,2816]{1,0:T(8,128)(2,1)S(1)} %collective-permute-done.19.refs_6_), channel_id=1, source_target_pairs={{0,1},{1,0},{2,3},{3,2},{4,5},{5,4},{6,7},{7,6},{8,9},{9,8},{10,11... | collective-permute-start | bytes 2433032 | tf_op jit(solution)/shard_map/ppermute | solution.py:42
  152.4 44.1 %collective-permute-start.10 = (bf16[144,2176]{1,0:T(8,128)(2,1)S(1)}, bf16[144,2176]{1,0:T(8,128)(2,1)S(1)}, u32[]{:S(2)}, u32[]{:S(2)}) collective-permute-start(bf16[144,2176]{1,0:T(8,128)(2,1)S(1)} %copy-done.26), channel_id=1, source_target_pairs={{0,1},{1,0},{2,3},{3,2},{4,5},{5,4},{6,7},{7,6},{8,9},{9,8},{10,11... | collective-permute-start | bytes 1880072 | tf_op jit(solution)/shard_map/ppermute | solution.py:42
  154.3 42.3 %collective-permute-start.11 = (bf16[144,2176]{1,0:T(8,128)(2,1)S(1)}, bf16[144,2176]{1,0:T(8,128)(2,1)}, u32[]{:S(2)}, u32[]{:S(2)}) collective-permute-start(bf16[144,2176]{1,0:T(8,128)(2,1)S(1)} %copy-done.26), channel_id=1, source_target_pairs={{0,2},{1,3},{2,0},{3,1},{4,6},{5,7},{6,4},{7,5},{8,10},{9,11},{10,... | collective-permute-start | bytes 1880072 | tf_op jit(solution)/shard_map/ppermute | solution.py:42
  154.3 42.3 %collective-permute-start.12 = (bf16[144,2176]{1,0:T(8,128)(2,1)S(1)}, bf16[144,2176]{1,0:T(8,128)(2,1)}, u32[]{:S(2)}, u32[]{:S(2)}) collective-permute-start(bf16[144,2176]{1,0:T(8,128)(2,1)S(1)} %copy-done.26), channel_id=1, source_target_pairs={{0,4},{1,5},{2,6},{3,7},{4,0},{5,1},{6,2},{7,3},{8,12},{9,13},{10,... | collective-permute-start | bytes 1880072 | tf_op jit(solution)/shard_map/ppermute | solution.py:42
  215.4 37.0 %collective-permute-start.26 = (bf16[144,2176]{1,0:T(8,128)(2,1)}, bf16[144,2176]{1,0:T(8,128)(2,1)S(1)}, u32[]{:S(2)}, u32[]{:S(2)}) collective-permute-start(bf16[144,2176]{1,0:T(8,128)(2,1)} %collective-permute-done.12.refs_4_), channel_id=1, source_target_pairs={{0,1},{1,0},{2,3},{3,2},{4,5},{5,4},{6,7},{7,6},{8,9},{9,8},{10,11... | collective-permute-start | bytes 1880072 | tf_op jit(solution)/shard_map/ppermute | solution.py:42
  215.8 36.6 %collective-permute-start.27 = (bf16[144,2176]{1,0:T(8,128)(2,1)S(1)}, bf16[144,2176]{1,0:T(8,128)(2,1)}, u32[]{:S(2)}, u32[]{:S(2)}) collective-permute-start(bf16[144,2176]{1,0:T(8,128)(2,1)S(1)} %collective-permute-done.21.refs_6_), channel_id=1, source_target_pairs={{0,1},{1,0},{2,3},{3,2},{4,5},{5,4},{6,7},{7,6},{8,9},{9,8},{10,11... | collective-permute-start | bytes 1880072 | tf_op jit(solution)/shard_map/ppermute | solution.py:42
  253.2 265.1 %reduce-scatter.5.cloned.1.call-start = ((), (), s32[]{:S(2)}) async-start(), calls=%async_computation.3 | async-start | bytes 7299072 | tf_op jit(solution)/shard_map/reduce_scatter | solution.py:1319
  425.1 49.4 %collective-permute-start.36 = (bf16[768,1152]{1,0:T(8,128)(2,1)}, bf16[768,1152]{1,0:T(8,128)(2,1)}, u32[]{:S(2)}, u32[]{:S(2)}) collective-permute-start(bf16[768,1152]{1,0:T(8,128)(2,1)} %add_convert_fusion), channel_id=1, source_target_pairs={{0,16},{8,24},{16,0},{24,8},{1,17},{9,25},{17,1},{25,9},{2,18},{10... | collective-permute-start | bytes 5308424 | tf_op jit(solution)/shard_map/ppermute | solution.py:42
  425.8 48.7 %collective-permute-start.35 = (bf16[576,1280]{1,0:T(8,128)(2,1)}, bf16[576,1280]{1,0:T(8,128)(2,1)}, u32[]{:S(2)}, u32[]{:S(2)}) collective-permute-start(bf16[576,1280]{1,0:T(8,128)(2,1)} %get-tuple-element.400), channel_id=1, source_target_pairs={{0,1},{1,0},{2,3},{3,2},{4,5},{5,4},{6,7},{7,6},{8,9},{9,8},{10,11... | collective-permute-start | bytes 4423688 | tf_op jit(solution)/shard_map/ppermute | solution.py:42
  440.0 37.7 %collective-permute-start.37 = (bf16[768,1152]{1,0:T(8,128)(2,1)}, bf16[768,1152]{1,0:T(8,128)(2,1)}, u32[]{:S(2)}, u32[]{:S(2)}) collective-permute-start(bf16[768,1152]{1,0:T(8,128)(2,1)} %get-tuple-element.407), channel_id=1, source_target_pairs={{0,8},{8,0},{16,24},{24,16},{1,9},{9,1},{17,25},{25,17},{2,10},{10... | collective-permute-start | bytes 5308424 | tf_op jit(solution)/shard_map/ppermute | solution.py:42
  448.8 41.1 %collective-permute-start.33 = (bf16[768,1152]{1,0:T(8,128)(2,1)}, bf16[768,1152]{1,0:T(8,128)(2,1)S(1)}, u32[]{:S(2)}, u32[]{:S(2)}) collective-permute-start(bf16[768,1152]{1,0:T(8,128)(2,1)} %down_pair.1), channel_id=1, source_target_pairs={{0,8},{8,0},{16,24},{24,16},{1,9},{9,1},{17,25},{25,17},{2,10},{10... | collective-permute-start | bytes 5308424 | tf_op jit(solution)/shard_map/ppermute | solution.py:42
  457.2 32.7 %collective-permute-start.34 = (bf16[576,640]{1,0:T(8,128)(2,1)}, bf16[576,640]{1,0:T(8,128)(2,1)S(1)}, u32[]{:S(2)}, u32[]{:S(2)}) collective-permute-start(bf16[576,640]{1,0:T(8,128)(2,1)} %get-tuple-element.411), channel_id=1, source_target_pairs={{0,1},{1,0},{2,3},{3,2},{4,5},{5,4},{6,7},{7,6},{8,9},{9,8},{10,11... | collective-permute-start | bytes 2211848 | tf_op jit(solution)/shard_map/ppermute | solution.py:42
  477.6 34.6 %collective-permute-start.38 = (bf16[288,1280]{1,0:T(8,128)(2,1)}, bf16[288,1280]{1,0:T(8,128)(2,1)}, u32[]{:S(2)}, u32[]{:S(2)}) collective-permute-start(bf16[288,1280]{1,0:T(8,128)(2,1)} %get-tuple-element.452), channel_id=1, source_target_pairs={{0,2},{1,3},{2,0},{3,1},{4,6},{5,7},{6,4},{7,5},{8,10},{9,11},{10,... | collective-permute-start | bytes 2211848 | tf_op jit(solution)/shard_map/ppermute | solution.py:42
  518.3 28.1 %collective-permute-start.47 = (bf16[144,2816]{1,0:T(8,128)(2,1)}, bf16[144,2816]{1,0:T(8,128)(2,1)S(1)}, u32[]{:S(2)}, u32[]{:S(2)}) collective-permute-start(bf16[144,2816]{1,0:T(8,128)(2,1)} %reduce-scatter.5.cloned.1.call-done), channel_id=1, source_target_pairs={{0,16},{8,24},{16,0},{24,8},{1,17},{9,25},{17,1},{25,9},{2,18},{10... | collective-permute-start | bytes 2433032 | tf_op jit(solution)/shard_map/ppermute | solution.py:42
  520.0 45.0 %collective-permute-start.52 = (f32[144,2176]{1,0:T(8,128)S(1)}, f32[144,2176]{1,0:T(8,128)S(1)}, u32[]{:S(2)}, u32[]{:S(2)}) collective-permute-start(f32[144,2176]{1,0:T(8,128)S(1)} %convert_add_fusion.1), channel_id=1, source_target_pairs={{0,8},{8,0},{16,24},{24,16},{1,9},{9,1},{17,25},{25,17},{2,10},{10... | collective-permute-start | bytes 3760136 | tf_op jit(solution)/shard_map/ppermute | solution.py:42
  (71 other events, 896.3 us)
Sparse Core Ops, SparseCore 0:
  252.6 98.0 reduce-scatter.2
  355.1 137.9 reduce-scatter.4
